TPU v7x, 32 devices: a whole 2x2x4 slice. The times are simulated.
32 devices in a mesh: fsdp: 8 (over z, y), tp: 4 (over x, core).
Axes of the slice: x: 2, y: 2, z: 4, core: 2. Of those that a mesh axis runs over, the one named last changes fastest.
Arguments:
- layer_in: bfloat16 [8192, 2048], P(('fsdp', 'tp')), may hold values from -6 to 6
- lengths: int32 [4], replicated, may hold values from 1537 to 2048, as said below
- clip_level: int32 [1], replicated, may hold values from 32 to 80
- attn_gain: bfloat16 [2048], replicated, may hold values from 0.5 to 1.5
- w_query: bfloat16 [2048, 2048], P('fsdp', 'tp'), may hold values from -0.70710678 to 0.70710678
- w_key: bfloat16 [2048, 512], P('fsdp', 'tp'), may hold values from -0.375 to 0.375
- w_value: bfloat16 [2048, 512], P('fsdp', 'tp'), may hold values from -0.125 to 0.125
- w_out: bfloat16 [2048, 2048], P('tp', 'fsdp'), may hold values from -6 to 6
- mlp_gain: bfloat16 [2048], replicated, may hold values from 0.5 to 1.5
- w_gate: bfloat16 [2048, 8192], P('fsdp', 'tp'), may hold values from -0.125 to 0.125
- w_up: bfloat16 [2048, 8192], P('fsdp', 'tp'), may hold values from -0.125 to 0.125
- w_down: bfloat16 [8192, 2048], P('tp', 'fsdp'), may hold values from -0.5 to 0.5
- cotangent: bfloat16 [8192, 2048], P(('fsdp', 'tp')), may hold values from -6 to 6
Outputs:
- layer_out: bfloat16 [8192, 2048], P(('fsdp', 'tp'))
- input_grad: bfloat16 [8192, 2048], P(('fsdp', 'tp'))
- attn_gain_grad: float32 [2048], P(('fsdp', 'tp'))
- query_grad: float32 [2048, 2048], P('fsdp', 'tp')
- key_grad: float32 [2048, 512], P('fsdp', 'tp')
- value_grad: float32 [2048, 512], P('fsdp', 'tp')
- out_grad: float32 [2048, 2048], P('tp', 'fsdp')
- mlp_gain_grad: float32 [2048], P(('fsdp', 'tp'))
- gate_grad: float32 [2048, 8192], P('fsdp', 'tp')
- up_grad: float32 [2048, 8192], P('fsdp', 'tp')
- down_grad: float32 [8192, 2048], P('tp', 'fsdp')
- query_clipped: float32 [2048, 2048], P('fsdp', 'tp')
- key_clipped: float32 [2048, 512], P('fsdp', 'tp')
Inputs may be any that keep to these rules, and one draw needn't show every extreme that they name: lengths of the 4 slots; one slot has all 2048 tokens live.
All inputs are finite; a program needn't handle non-finite values.
Results may differ from a plain program's by a relative error of at most 0.02.
The roundings to bfloat16 on the way count: a program that leaves them out, or rounds other values in their place, can miss the bound.
Values may be sent and summed in bfloat16 or wider, within the bound.
No kernel may reach another device: no remote copies, remote signals or barrier semaphores. Data moves between devices by JAX's collectives and lax.ppermute only.
A program may use at most 320 MiB of HBM per device.

v0:
```python
import jax
import jax.numpy as jnp
from jax import lax
from jax.sharding import PartitionSpec as P

HD = 64
SLOT_LEN = 2048


EPSILON = 1e-05
THETA = 10000000.0
MULTIPLIER = 0.015625
RESIDUAL = 0.22
LEVEL_UNIT = 0.125
NEGATIVE = -1e30


def from_behind(x, axis, by):
    peers = lax.axis_size(axis)
    return lax.ppermute(x, axis, [(i, (i + by) % peers) for i in range(peers)])


def rotation_tables(positions):
    half_dim = HD // 2
    freq_table = THETA ** (-(jnp.arange(half_dim, dtype=jnp.float32) * 2.0 / HD))
    angle_table = positions.astype(jnp.float32)[:, None] * freq_table[None, :]
    return (jnp.cos(angle_table), jnp.sin(angle_table))


def rotate(flat_rows, cosine_table, sine_table, direction):
    row_count = flat_rows.shape[0]
    halves = flat_rows.reshape(row_count, -1, 2, HD // 2)
    first_half = halves[:, :, 0, :]
    second_half = halves[:, :, 1, :]
    cos_part = cosine_table[:, None, :]
    sin_part = sine_table[:, None, :]
    turned = jnp.stack(
        (
            first_half * cos_part - direction * second_half * sin_part,
            second_half * cos_part + direction * first_half * sin_part,
        ),
        axis=2,
    )
    return turned.reshape(row_count, -1)


def contract_rows(left, right):
    return lax.dot_general(
        left, right, (((0,), (0,)), ((), ())), preferred_element_type=jnp.float32
    )


def contract_cols(left, right):
    return lax.dot_general(
        left, right, (((1,), (1,)), ((), ())), preferred_element_type=jnp.float32
    )


def arrange(vector, fs_count, tp_count):
    return vector.reshape(fs_count, tp_count, -1).transpose(1, 0, 2).reshape(-1)


def norm_back(values, scale, upstream):
    mean_term = jnp.mean(values * upstream, axis=1, keepdims=True)
    return scale * upstream - values * (scale * scale * scale) * mean_term


def shards(
    layer_in,
    lengths,
    clip_level,
    attn_gain,
    w_query,
    w_key,
    w_value,
    w_out,
    mlp_gain,
    w_gate,
    w_up,
    w_down,
    cotangent,
):
    tok_rows, model_width = layer_in.shape
    tp_count = lax.axis_size("tp")
    fs_count = lax.axis_size("fsdp")
    tp_rank = lax.axis_index("tp")
    fs_rank = lax.axis_index("fsdp")
    group_rows = tok_rows * tp_count
    total_rows = group_rows * fs_count
    lead_rows = group_rows // 2
    slot_span = SLOT_LEN // group_rows
    turn_count = slot_span + 1
    q_cols = w_query.shape[1]
    kv_cols = w_key.shape[1]
    kv_local = kv_cols // HD
    rep_count = q_cols // kv_cols
    block_rows = min(512, group_rows)
    block_count = group_rows // block_rows
    key_count = turn_count * group_rows
    slot_table = jnp.arange(lengths.shape[0], dtype=jnp.int32)

    def place(token_ids):
        packed_ids = (token_ids + lead_rows) % total_rows
        return (packed_ids // SLOT_LEN, packed_ids % SLOT_LEN)

    def live_length(slot_ids):
        return jnp.sum(
            jnp.where(slot_ids[:, None] == slot_table[None, :], lengths[None, :], 0), axis=1
        )

    row_ids = jnp.arange(group_rows, dtype=jnp.int32)
    query_slot, positions = place(fs_rank * group_rows + row_ids)
    query_live = positions < live_length(query_slot)
    own_slot, own_pos = place(
        fs_rank * group_rows + tp_rank * tok_rows + jnp.arange(tok_rows, dtype=jnp.int32)
    )
    own_mask = (own_pos < live_length(own_slot)).astype(jnp.float32)[:, None]
    cosine_table, sine_table = rotation_tables(positions)
    source_dev = (fs_rank - jnp.arange(turn_count, dtype=jnp.int32)) % fs_count
    key_slot, key_pos = place((source_dev[:, None] * group_rows + row_ids[None, :]).reshape(-1))
    full_query, full_key, full_value, full_out, full_gate, full_up, full_down = (
        lax.all_gather(w_query, "fsdp", axis=0, tiled=True),
        lax.all_gather(w_key, "fsdp", axis=0, tiled=True),
        lax.all_gather(w_value, "fsdp", axis=0, tiled=True),
        lax.all_gather(w_out, "fsdp", axis=1, tiled=True),
        lax.all_gather(w_gate, "fsdp", axis=0, tiled=True),
        lax.all_gather(w_up, "fsdp", axis=0, tiled=True),
        lax.all_gather(w_down, "fsdp", axis=1, tiled=True),
    )
    layer_f = layer_in.astype(jnp.float32)
    scale_one = lax.rsqrt(jnp.mean(layer_f * layer_f, axis=1, keepdims=True) + EPSILON)
    normal_one = (layer_f * scale_one).astype(jnp.bfloat16)
    normed_one = lax.all_gather(normal_one, "tp", axis=0, tiled=True)
    gain_one = attn_gain.astype(jnp.float32)
    acts_one = (normed_one.astype(jnp.float32) * gain_one[None, :]).astype(jnp.bfloat16)
    query_b = rotate(
        jnp.dot(acts_one, full_query, preferred_element_type=jnp.float32),
        cosine_table,
        sine_table,
        1.0,
    ).astype(jnp.bfloat16)
    key_b = rotate(
        jnp.dot(acts_one, full_key, preferred_element_type=jnp.float32),
        cosine_table,
        sine_table,
        1.0,
    ).astype(jnp.bfloat16)
    value_b = jnp.dot(acts_one, full_value, preferred_element_type=jnp.float32).astype(jnp.bfloat16)
    pair_now = jnp.stack((key_b, value_b))
    stored = jnp.zeros((turn_count, 2, group_rows, kv_cols), jnp.bfloat16)
    stored = lax.dynamic_update_index_in_dim(stored, pair_now, 0, 0)

    def fetch(turn_index, loop_state):
        moving, kept = loop_state
        moving = from_behind(moving, "fsdp", 1)
        kept = lax.dynamic_update_index_in_dim(kept, moving, turn_index, 0)
        return (moving, kept)

    moving, stored = lax.fori_loop(1, turn_count, fetch, (pair_now, stored))
    key_heads = stored[:, 0].reshape(key_count, kv_local, HD)
    value_heads = stored[:, 1].reshape(key_count, kv_local, HD)

    def score_block(query_block, query_pos, query_seg):
        query_heads = query_block.reshape(block_rows, kv_local, rep_count, HD)
        raw_scores = jnp.einsum(
            "qgrd,kgd->grqk", query_heads, key_heads, preferred_element_type=jnp.float32
        )
        allowed = (key_slot[None, :] == query_seg[:, None]) & (
            key_pos[None, :] <= query_pos[:, None]
        )
        return (
            jnp.where(allowed[None, None], MULTIPLIER * raw_scores, NEGATIVE),
            allowed,
            query_heads,
        )

    query_blocks = query_b.reshape(block_count, block_rows, q_cols)
    pos_blocks = positions.reshape(block_count, block_rows)
    seg_blocks = query_slot.reshape(block_count, block_rows)
    live_blocks = query_live.reshape(block_count, block_rows)

    def forward_block(inputs):
        query_block, query_pos, query_seg, live_rows = inputs
        scores, allowed, query_heads = score_block(query_block, query_pos, query_seg)
        row_top = jnp.max(scores, axis=3, keepdims=True)
        row_total = jnp.sum(jnp.exp(scores - row_top), axis=3, keepdims=True)
        log_total = row_top + jnp.log(row_total)
        attn_probs = jnp.exp(scores - log_total).astype(jnp.bfloat16)
        mixed = jnp.einsum(
            "grqk,kgd->qgrd", attn_probs, value_heads, preferred_element_type=jnp.float32
        )
        counted = (live_rows[:, None] & allowed)[None, None]
        head_peak = jnp.max(jnp.where(counted, scores, NEGATIVE), axis=(2, 3))
        return (mixed.reshape(block_rows, q_cols), log_total[..., 0], head_peak)

    mixed_blocks, log_blocks, peak_blocks = lax.map(
        forward_block, (query_blocks, pos_blocks, seg_blocks, live_blocks)
    )
    attn_b = mixed_blocks.reshape(group_rows, q_cols).astype(jnp.bfloat16)
    local_peak = jnp.max(peak_blocks, axis=0).reshape(-1)
    row_part = attn_b
    branch_one = lax.psum_scatter(
        jnp.dot(row_part, full_out, preferred_element_type=jnp.float32),
        "tp",
        scatter_dimension=0,
        tiled=True,
    )
    resid = layer_f + RESIDUAL * own_mask * branch_one
    scale_two = lax.rsqrt(jnp.mean(resid * resid, axis=1, keepdims=True) + EPSILON)
    normal_two = (resid * scale_two).astype(jnp.bfloat16)
    normed_two = lax.all_gather(normal_two, "tp", axis=0, tiled=True)
    gain_two = mlp_gain.astype(jnp.float32)
    acts_two = (normed_two.astype(jnp.float32) * gain_two[None, :]).astype(jnp.bfloat16)
    gate_proj = jnp.dot(acts_two, full_gate, preferred_element_type=jnp.float32)
    up_proj = jnp.dot(acts_two, full_up, preferred_element_type=jnp.float32)
    sigmoid_gate = jax.nn.sigmoid(gate_proj)
    hidden = (gate_proj * sigmoid_gate * up_proj).astype(jnp.bfloat16)
    row_part = hidden
    branch_two = lax.psum_scatter(
        jnp.dot(row_part, full_down, preferred_element_type=jnp.float32).astype(jnp.bfloat16),
        "tp",
        scatter_dimension=0,
        tiled=True,
    ).astype(jnp.float32)
    result = resid + RESIDUAL * own_mask * branch_two
    head_peak = lax.pmax(local_peak, "fsdp")
    level = clip_level[0].astype(jnp.float32) * LEVEL_UNIT
    factor = level / jnp.maximum(level, head_peak)
    query_clipped = w_query.astype(jnp.float32) * jnp.repeat(jnp.sqrt(factor), HD)[None, :]
    kv_factor = jnp.min(factor.reshape(kv_local, rep_count), axis=1)
    key_clipped = w_key.astype(jnp.float32) * jnp.repeat(jnp.sqrt(kv_factor), HD)[None, :]
    grad_out = cotangent.astype(jnp.float32)
    down_input = (RESIDUAL * own_mask * grad_out).astype(jnp.bfloat16)
    down_rows = lax.all_gather(down_input, "tp", axis=0, tiled=True)
    hidden_grad = contract_cols(down_rows, full_down)
    grad_down = contract_rows(hidden, down_rows)
    gate_grad = (
        hidden_grad * up_proj * sigmoid_gate * (1.0 + gate_proj * (1.0 - sigmoid_gate))
    ).astype(jnp.bfloat16)
    up_grad = (hidden_grad * gate_proj * sigmoid_gate).astype(jnp.bfloat16)
    grad_gate = contract_rows(acts_two, gate_grad)
    grad_up = contract_rows(acts_two, up_grad)
    acts_two_grad = contract_cols(gate_grad, full_gate) + contract_cols(up_grad, full_up)
    gain_two_part = jnp.sum(normed_two.astype(jnp.float32) * acts_two_grad, axis=0)
    norm_two_grad, gain_two_share = (
        lax.psum_scatter(acts_two_grad, "tp", scatter_dimension=0, tiled=True),
        lax.psum_scatter(
            arrange(gain_two_part, fs_count, tp_count), "tp", scatter_dimension=0, tiled=True
        ),
    )
    grad_resid = grad_out + norm_back(resid, scale_two, gain_two[None, :] * norm_two_grad)
    mixed_grad = (RESIDUAL * own_mask * grad_resid).astype(jnp.bfloat16)
    mixed_rows = lax.all_gather(mixed_grad, "tp", axis=0, tiled=True)
    grad_outproj = contract_rows(attn_b, mixed_rows)
    heads_grad = contract_cols(mixed_rows, full_out).astype(jnp.bfloat16)
    heads_blocks = heads_grad.reshape(block_count, block_rows, q_cols)

    def backward_block(loop_state, inputs):
        key_acc, value_acc = loop_state
        query_block, query_pos, query_seg, log_block, grad_block = inputs
        scores, allowed, query_heads = score_block(query_block, query_pos, query_seg)
        attn_probs = jnp.exp(scores - log_block[..., None])
        probs_b = attn_probs.astype(jnp.bfloat16)
        grad_heads = grad_block.reshape(block_rows, kv_local, rep_count, HD)
        prob_grad = jnp.einsum(
            "qgrd,kgd->grqk", grad_heads, value_heads, preferred_element_type=jnp.float32
        )
        delta = jnp.sum(attn_probs * prob_grad, axis=3, keepdims=True)
        score_grad = (MULTIPLIER * (attn_probs * (prob_grad - delta))).astype(jnp.bfloat16)
        query_part = jnp.einsum(
            "grqk,kgd->qgrd", score_grad, key_heads, preferred_element_type=jnp.float32
        )
        key_acc = key_acc + jnp.einsum(
            "grqk,qgrd->kgd", score_grad, query_heads, preferred_element_type=jnp.float32
        ).reshape(key_count, kv_cols)
        value_acc = value_acc + jnp.einsum(
            "grqk,qgrd->kgd", probs_b, grad_heads, preferred_element_type=jnp.float32
        ).reshape(key_count, kv_cols)
        return ((key_acc, value_acc), query_part.reshape(block_rows, q_cols))

    zero_acc = jnp.zeros((key_count, kv_cols), jnp.float32)
    (key_acc, value_acc), query_parts = lax.scan(
        backward_block,
        (zero_acc, zero_acc),
        (query_blocks, pos_blocks, seg_blocks, log_blocks, heads_blocks),
    )
    kv_parts = jnp.stack(
        (
            key_acc.reshape(turn_count, group_rows, kv_cols),
            value_acc.reshape(turn_count, group_rows, kv_cols),
        ),
        axis=1,
    )

    def send_back(turn_index, moving):
        moving = from_behind(moving.astype(jnp.bfloat16), "fsdp", -1).astype(moving.dtype)
        return moving + lax.dynamic_index_in_dim(
            kv_parts, slot_span - turn_index, 0, keepdims=False
        )

    kv_total = lax.fori_loop(1, turn_count, send_back, kv_parts[slot_span])
    query_grad = rotate(
        query_parts.reshape(group_rows, q_cols), cosine_table, sine_table, -1.0
    ).astype(jnp.bfloat16)
    key_grad = rotate(kv_total[0], cosine_table, sine_table, -1.0).astype(jnp.bfloat16)
    value_grad = kv_total[1].astype(jnp.bfloat16)
    grad_query = contract_rows(acts_one, query_grad)
    grad_key = contract_rows(acts_one, key_grad)
    grad_value = contract_rows(acts_one, value_grad)
    acts_one_grad = (
        contract_cols(query_grad, full_query)
        + contract_cols(key_grad, full_key)
        + contract_cols(value_grad, full_value)
    )
    gain_one_part = jnp.sum(normed_one.astype(jnp.float32) * acts_one_grad, axis=0)
    norm_one_grad, gain_one_share = (
        lax.psum_scatter(
            acts_one_grad.astype(jnp.bfloat16), "tp", scatter_dimension=0, tiled=True
        ).astype(jnp.float32),
        lax.psum_scatter(
            arrange(gain_one_part, fs_count, tp_count).astype(jnp.bfloat16),
            "tp",
            scatter_dimension=0,
            tiled=True,
        ).astype(jnp.float32),
    )
    grad_input = grad_resid + norm_back(layer_f, scale_one, gain_one[None, :] * norm_one_grad)
    query_sent, key_sent, value_sent, outproj_sent, gain_one_grad = (
        lax.psum_scatter(
            grad_query.astype(jnp.bfloat16), "fsdp", scatter_dimension=0, tiled=True
        ).astype(jnp.float32),
        lax.psum_scatter(
            grad_key.astype(jnp.bfloat16), "fsdp", scatter_dimension=0, tiled=True
        ).astype(jnp.float32),
        lax.psum_scatter(
            grad_value.astype(jnp.bfloat16), "fsdp", scatter_dimension=0, tiled=True
        ).astype(jnp.float32),
        lax.psum_scatter(
            grad_outproj.astype(jnp.bfloat16), "fsdp", scatter_dimension=1, tiled=True
        ).astype(jnp.float32),
        lax.psum_scatter(
            gain_one_share.astype(jnp.bfloat16), "fsdp", scatter_dimension=0, tiled=True
        ).astype(jnp.float32),
    )
    mlp_sent = (
        lax.psum_scatter(
            grad_gate.astype(jnp.bfloat16), "fsdp", scatter_dimension=0, tiled=True
        ).astype(jnp.float32),
        lax.psum_scatter(
            grad_up.astype(jnp.bfloat16), "fsdp", scatter_dimension=0, tiled=True
        ).astype(jnp.float32),
        lax.psum_scatter(
            grad_down.astype(jnp.bfloat16), "fsdp", scatter_dimension=1, tiled=True
        ).astype(jnp.float32),
        lax.psum_scatter(
            gain_two_share.astype(jnp.bfloat16), "fsdp", scatter_dimension=0, tiled=True
        ).astype(jnp.float32),
    )
    gate_sent, up_sent, down_sent, gain_two_grad = mlp_sent
    return (
        result.astype(jnp.bfloat16),
        grad_input.astype(jnp.bfloat16),
        gain_one_grad,
        query_sent,
        key_sent,
        value_sent,
        outproj_sent,
        gain_two_grad,
        gate_sent,
        up_sent,
        down_sent,
        query_clipped,
        key_clipped,
    )


def solution(mesh):
    in_specs = (
        P(("fsdp", "tp"), None),
        P(),
        P(),
        P(),
        P("fsdp", "tp"),
        P("fsdp", "tp"),
        P("fsdp", "tp"),
        P("tp", "fsdp"),
        P(),
        P("fsdp", "tp"),
        P("fsdp", "tp"),
        P("tp", "fsdp"),
        P(("fsdp", "tp"), None),
    )
    out_specs = (
        P(("fsdp", "tp"), None),
        P(("fsdp", "tp"), None),
        P(("fsdp", "tp")),
        P("fsdp", "tp"),
        P("fsdp", "tp"),
        P("fsdp", "tp"),
        P("tp", "fsdp"),
        P(("fsdp", "tp")),
        P("fsdp", "tp"),
        P("fsdp", "tp"),
        P("tp", "fsdp"),
        P("fsdp", "tp"),
        P("fsdp", "tp"),
    )
    return jax.shard_map(shards, mesh=mesh, in_specs=in_specs, out_specs=out_specs, check_vma=False)
```

profile of v0, /device:TPU:0, one launch (start us, length us, event | category | flops | bytes accessed | tf_op | source)
XLA Modules:
  0.0 1938.3 jit_solution(5175736201635258595)
XLA Ops:
  13.7 33.1 %all_gather.36 = bf16[2048,128]{1,0:T(8,128)(2,1)S(1)} all-gather(bf16[256,128]{1,0:T(8,128)(2,1)S(1)} %copy-done.26), channel_id=1, replica_groups=mesh['fsdp'=8,'tp'=4] {'fsdp'}, dimensions={0}, use_global_device_ids=true | all-gather | bytes 589824 | tf_op jit(solution)/shard_map/all_gather | solution.py:124
  46.7 31.8 %all_gather.35 = bf16[2048,128]{1,0:T(8,128)(2,1)S(1)} all-gather(bf16[256,128]{1,0:T(8,128)(2,1)S(1)} %copy-done.16), channel_id=1, replica_groups=mesh['fsdp'=8,'tp'=4] {'fsdp'}, dimensions={0}, use_global_device_ids=true | all-gather | bytes 589824 | tf_op jit(solution)/shard_map/all_gather | solution.py:123
  88.3 36.9 %while.63 = (s32[]{:T(128)}, bf16[2,1024,128]{2,1,0:T(8,128)(2,1)}, bf16[3,2,1024,128]{3,2,1,0:T(8,128)(2,1)S(1)}, s32[]{:T(128)}, s32[]{:T(128)}, /*index=5*/s32[]{:T(128)}) while((s32[]{:T(128)}, bf16[2,1024,128]{2,1,0:T(8,128)(2,1)}, bf16[3,2,1024,128]{3,2,1,0:T(8,128)(2,1)S(1)}, s32[]{:T(128)}, s32[]{:T(128)}, /*index=5*/s32[]{:T(128)}) %tuple.165), condition=%wide.region_4.5_spmd, body=%wide.region_3.4_spmd.sunk | while | flops 5 | bytes 4194451 | solution.py:159
  90.2 21.1 %collective-permute-done = bf16[2,1024,128]{2,1,0:T(8,128)(2,1)S(1)} collective-permute-done((bf16[2,1024,128]{2,1,0:T(8,128)(2,1)}, bf16[2,1024,128]{2,1,0:T(8,128)(2,1)S(1)}, u32[]{:S(2)}, u32[]{:S(2)}) %collective-permute-start) | collective-permute-done | bytes 524320 | tf_op jit(solution)/shard_map/while/body/eval_jaxpr/ppermute | solution.py:20
  112.2 12.1 collective-permute-done
  132.5 5.3 fusion.81
  140.3 145.5 %while.65 = (s32[]{:T(128)}, bf16[2,512,512]{2,1,0:T(8,128)(2,1)}, f32[2,2,4,512]{3,2,1,0:T(4,128)S(1)}, f32[2,2,4]{2,1,0:T(2,128)S(1)}, s32[2,512]{1,0:T(2,128)...) while((s32[]{:T(128)}, bf16[2,512,512]{2,1,0:T(8,128)(2,1)}, ...), condition=%wide.region_9.10_spmd.clone.clone, body=%wide.region_5.9_spmd.clone.clone.sunk | while | flops 3391188992 | bytes 174833392 | solution.py:196
  144.8 21.5 %bitcast_reduce_fusion.2 = (f32[2,4,512]{2,1,0:T(4,128)S(1)}, f32[2,512,4,3072]{3,1,2,0:T(8,128)}) fusion(pred[512,3072]{1,0:T(8,128)(4,1)S(1)} %get-tuple-element.886, bf16[512,2,4,64]{0,3,2,1:T(8,128)(2,1)} %bitcast.275, bf16[3072,2,64]{0,2,1:T(8,128)(2,1)} %get-tuple-element.959), kind=kOutput, calls=%fused_computation.57.clone.1 | convolution fusion | flops 1648357376 | bytes 53231616 | tf_op jit(solution)/shard_map/while/body/eval_jaxpr/qgrd,kgd->grqk/dot_general | solution.py:165
  166.4 26.3 %fusion.165 = (f32[2,4]{1,0:T(2,128)S(1)}, f32[2,4,512]{2,1,0:T(4,128)S(1)}) fusion(f32[2,512,4,3072]{3,1,2,0:T(8,128)} %get-tuple-element.887, pred[512,3072]{1,0:T(8,128)(4,1)S(1)} %get-tuple-element.889, pred[512,3072]{1,0:T(8,128)(4,1)S(1)} %get-tuple-element.886, f32[2,4,512]{2,1,0:T(4,128)S(1)} %get-tuple-element.888), kind=kLoop, calls=%fused_computation.62.clone.1 | loop fusion | flops 75493368 | bytes 53510176 | tf_op jit(solution)/shard_map/while/body/eval_jaxpr/reduce_max | solution.py:193
  192.7 19.2 fusion.166
  217.5 21.4 %bitcast_reduce_fusion.2 = (f32[2,4,512]{2,1,0:T(4,128)S(1)}, f32[2,512,4,3072]{3,1,2,0:T(8,128)}) fusion(pred[512,3072]{1,0:T(8,128)(4,1)S(1)} %get-tuple-element.886, bf16[512,2,4,64]{0,3,2,1:T(8,128)(2,1)} %bitcast.275, bf16[3072,2,64]{0,2,1:T(8,128)(2,1)} %get-tuple-element.959), kind=kOutput, calls=%fused_computation.57.clone.1 | convolution fusion | flops 1648357376 | bytes 53231616 | tf_op jit(solution)/shard_map/while/body/eval_jaxpr/qgrd,kgd->grqk/dot_general | solution.py:165
  238.9 26.3 %fusion.165 = (f32[2,4]{1,0:T(2,128)S(1)}, f32[2,4,512]{2,1,0:T(4,128)S(1)}) fusion(f32[2,512,4,3072]{3,1,2,0:T(8,128)} %get-tuple-element.887, pred[512,3072]{1,0:T(8,128)(4,1)S(1)} %get-tuple-element.889, pred[512,3072]{1,0:T(8,128)(4,1)S(1)} %get-tuple-element.886, f32[2,4,512]{2,1,0:T(4,128)S(1)} %get-tuple-element.888), kind=kLoop, calls=%fused_computation.62.clone.1 | loop fusion | flops 75493368 | bytes 53510176 | tf_op jit(solution)/shard_map/while/body/eval_jaxpr/reduce_max | solution.py:193
  265.3 19.2 fusion.166
  285.8 7.5 fusion.105
  294.2 70.0 %reduce-scatter.12.cloned.1.call-done = f32[256,2048]{1,0:T(8,128)} async-done(((f32[1024,2048]{1,0:T(8,128)}), f32[256,2048]{1,0:T(8,128)}) %reduce-scatter.12.cloned.1.call-update) | async-done | bytes 2097168 | tf_op jit(solution)/shard_map/reduce_scatter | solution.py:202
  371.1 120.2 %all-gather.20.cloned.1.call-done = bf16[2048,2048]{1,0:T(8,128)(2,1)} async-done(((bf16[256,2048]{1,0:T(8,128)(2,1)}), bf16[2048,2048]{1,0:T(8,128)(2,1)}) %all-gather.20.cloned.1.call-update) | async-done | bytes 8388624 | tf_op jit(solution)/shard_map/all_gather | solution.py:127
  491.4 34.8 %all-gather.16.cloned.1.call-done = bf16[1024,2048]{1,0:T(8,128)(2,1)} async-done(((bf16[256,2048]{1,0:T(8,128)(2,1)}), bf16[1024,2048]{1,0:T(8,128)(2,1)}) %all-gather.16.cloned.1.call-update) | async-done | bytes 4194320 | tf_op jit(solution)/shard_map/all_gather | solution.py:211
  526.1 15.0 fusion.62
  541.1 112.3 %all-gather.18.cloned.1.call-done = bf16[2048,2048]{1,0:T(8,128)(2,1)} async-done(((bf16[256,2048]{1,0:T(8,128)(2,1)}), bf16[2048,2048]{1,0:T(8,128)(2,1)}) %all-gather.18.cloned.1.call-update) | async-done | bytes 8388624 | tf_op jit(solution)/shard_map/all_gather | solution.py:126
  653.4 14.5 fusion.64
  667.9 111.3 %all-gather.22.cloned.1.call-done = bf16[2048,2048]{1,0:T(8,128)(2,1)} async-done(((bf16[2048,256]{1,0:T(8,128)(2,1)}), bf16[2048,2048]{1,0:T(8,128)(2,1)}) %all-gather.22.cloned.1.call-update) | async-done | bytes 8388624 | tf_op jit(solution)/shard_map/all_gather | solution.py:128
  779.2 34.9 %all-gather.24.cloned.1.call-done = bf16[1024,2048]{1,0:T(8,128)(2,1)} async-done(((bf16[256,2048]{1,0:T(8,128)(2,1)}), bf16[1024,2048]{1,0:T(8,128)(2,1)}) %all-gather.24.cloned.1.call-update) | async-done | bytes 4194320 | tf_op jit(solution)/shard_map/all_gather | solution.py:234
  814.1 21.9 %multiply_convert_fusion = (bf16[1024,2048]{1,0:T(8,128)(2,1)}, bf16[1024,2048]{1,0:T(8,128)(2,1)}, bf16[1024,2048]{1,0:T(8,128)(2,1)}) fusion(f32[1024,2048]{1,0:T(8,128)} %fusion.64, f32[1024,2048]{1,0:T(8,128)} %fusion.62, bf16[1024,2048]{1,0:T(8,128)(2,1)} %all-gather.24.cloned.1.call-done, bf16[2048,2048]{1,0:T(8,128)(2,1)} %all-gather.22.cloned.1.call-done), kind=kOutput, calls=%fused_computation.103 | convolution fusion | flops 8623489024 | bytes 41943040 | tf_op jit(solution)/shard_map/dot_general | solution.py:54
  836.0 14.9 fusion.106
  851.0 15.3 fusion.59
  866.4 13.9 convolution_convert_fusion.3
  880.4 57.8 %reduce-scatter.16.cloned.1.call-done = f32[256,2048]{1,0:T(8,128)} async-done(((f32[1024,2048]{1,0:T(8,128)}), f32[256,2048]{1,0:T(8,128)}) %reduce-scatter.16.cloned.1.call-update) | async-done | bytes 2097168 | tf_op jit(solution)/shard_map/reduce_scatter | solution.py:246
  940.1 45.2 %reduce-scatter.14.cloned.1.call-done = bf16[256,2048]{1,0:T(8,128)(2,1)} async-done(((bf16[1024,2048]{1,0:T(8,128)(2,1)}), bf16[256,2048]{1,0:T(8,128)(2,1)}) %reduce-scatter.14.cloned.1.call-update) | async-done | bytes 1048592 | tf_op jit(solution)/shard_map/reduce_scatter | solution.py:219
  985.3 4.7 multiply_convert_fusion.3
  990.1 14.3 convolution_convert_fusion.1
  1004.4 14.0 convolution_convert_fusion.2
  1018.5 14.5 convolution_convert_fusion
  1033.2 6.5 convolution_convert_fusion.8
  1039.7 527.4 %while.66 = (s32[]{:T(128)}, f32[3072,128]{0,1:T(8,128)}, f32[3072,128]{0,1:T(8,128)S(1)}, f32[2,512,512]{1,0,2:T(2,128)}, bf16[2,512,512]{1,2,0:T(8,128)(2,1)},...) while((s32[]{:T(128)}, f32[3072,128]{0,1:T(8,128)}, ...), condition=%wide.region_17.18_spmd.clone.clone.clone, body=%wide.region_15.17_spmd.clone.clone.clone.sunk | while | flops 8386623488 | bytes 388427968 | solution.py:282
  1044.9 21.0 %fusion.175 = f32[2,512,4,3072]{3,1,2,0:T(8,128)} fusion(bf16[512,2,4,64]{0,3,2,1:T(8,128)(2,1)S(1)} %bitcast.267, bf16[3072,2,64]{0,2,1:T(8,128)(2,1)} %get-tuple-element.999), kind=kOutput, calls=%fused_computation.26.clone.1 | convolution fusion | flops 1610612736 | bytes 51642368 | tf_op jit(solution)/shard_map/while/body/eval_jaxpr/qgrd,kgd->grqk/dot_general | solution.py:165
  1065.9 22.2 %fusion.176 = f32[2,64,3072,1]{2,1,3,0:T(8,128)} fusion(bf16[512,2,4,64]{0,3,2,1:T(8,128)(2,1)S(1)} %bitcast.265, f32[2,512,4,3072]{3,1,2,0:T(8,128)} %fusion.175, f32[2,4,512]{2,1,0:T(4,128)S(1)} %dynamic-slice_bitcast_fusion.2, pred[512,3072]{1,0:T(8,128)(4,1)} %compare_and_fusion.3), kind=kOutput, calls=%fused_computation.15.clone.1 | convolution fusion | flops 1660944384 | bytes 54018048 | tf_op jit(solution)/shard_map/while/body/eval_jaxpr/grqk,qgrd->kgd/dot_general | solution.py:276
  1088.1 20.0 %fusion.177 = f32[2,512,4,3072]{3,1,2,0:T(8,128)} fusion(bf16[512,2,4,64]{0,3,2,1:T(8,128)(2,1)S(1)} %bitcast.266, bf16[3072,2,64]{0,2,1:T(8,128)(2,1)S(1)} %get-tuple-element.1002), kind=kOutput, calls=%fused_computation.23.clone.1 | convolution fusion | flops 1610612736 | bytes 51642368 | tf_op jit(solution)/shard_map/while/body/eval_jaxpr/qgrd,kgd->grqk/dot_general | solution.py:265
  1108.1 83.3 %fusion.179 = f32[2,4,512,64]{2,3,1,0:T(8,128)} fusion(f32[2,512,4,3072]{3,1,2,0:T(8,128)} %fusion.177, f32[2,512,4,3072]{3,1,2,0:T(8,128)} %fusion.175, f32[2,4,512]{2,1,0:T(4,128)S(1)} %dynamic-slice_bitcast_fusion.2, pred[512,3072]{1,0:T(8,128)(4,1)} %compare_and_fusion.3, bf16[3072,2,64]{0,2,1:T(8,128)(2,1)} %get-tuple-element.999), kind=kOutput, calls=%fused_computation.17.clone.1 | convolution fusion | flops 1749031936 | bytes 104087552 | tf_op jit(solution)/shard_map/while/body/eval_jaxpr/grqk,kgd->qgrd/dot_general | solution.py:270
  1191.4 87.0 %fusion.178 = f32[2,64,3072,1]{2,1,3,0:T(8,128)} fusion(bf16[512,2,4,64]{0,3,2,1:T(8,128)(2,1)S(1)} %bitcast.268, f32[2,512,4,3072]{3,1,2,0:T(8,128)} %fusion.177, f32[2,512,4,3072]{3,1,2,0:T(8,128)} %fusion.175, f32[2,4,512]{2,1,0:T(4,128)S(1)} %dynamic-slice_bitcast_fusion.2, pred[512,3072]{1,0:T(8,128)(4,1)} %compare_and_fusion.3), kind=kOutput, calls=%fused_computation.18.clone.1 | convolution fusion | flops 1749031936 | bytes 104349696 | tf_op jit(solution)/shard_map/while/body/eval_jaxpr/grqk,qgrd->kgd/dot_general | solution.py:273
  1283.6 19.5 %dynamic_update_slice.49 = f32[2,512,512]{1,0,2:T(2,128)} dynamic-update-slice(f32[2,512,512]{1,0,2:T(2,128)} %get-tuple-element.981, f32[1,512,512]{1,0,2:T(1,128)S(1)} %copy.111, s32[]{:T(128)S(6)} %copy.142, s32[]{:T(128)} %constant.258.clone.1..sunk.2, s32[]{:T(128)} %constant.258.clone.1..sunk.2) | dynamic-update-slice | bytes 2097156 | tf_op jit(solution)/shard_map/while/body/jit(dynamic_update_index_in_dim)/dynamic_update_slice | solution.py:196
  1308.1 20.8 %fusion.175 = f32[2,512,4,3072]{3,1,2,0:T(8,128)} fusion(bf16[512,2,4,64]{0,3,2,1:T(8,128)(2,1)S(1)} %bitcast.267, bf16[3072,2,64]{0,2,1:T(8,128)(2,1)} %get-tuple-element.999), kind=kOutput, calls=%fused_computation.26.clone.1 | convolution fusion | flops 1610612736 | bytes 51642368 | tf_op jit(solution)/shard_map/while/body/eval_jaxpr/qgrd,kgd->grqk/dot_general | solution.py:165
  1328.9 22.3 %fusion.176 = f32[2,64,3072,1]{2,1,3,0:T(8,128)} fusion(bf16[512,2,4,64]{0,3,2,1:T(8,128)(2,1)S(1)} %bitcast.265, f32[2,512,4,3072]{3,1,2,0:T(8,128)} %fusion.175, f32[2,4,512]{2,1,0:T(4,128)S(1)} %dynamic-slice_bitcast_fusion.2, pred[512,3072]{1,0:T(8,128)(4,1)} %compare_and_fusion.3), kind=kOutput, calls=%fused_computation.15.clone.1 | convolution fusion | flops 1660944384 | bytes 54018048 | tf_op jit(solution)/shard_map/while/body/eval_jaxpr/grqk,qgrd->kgd/dot_general | solution.py:276
  1351.2 20.0 %fusion.177 = f32[2,512,4,3072]{3,1,2,0:T(8,128)} fusion(bf16[512,2,4,64]{0,3,2,1:T(8,128)(2,1)S(1)} %bitcast.266, bf16[3072,2,64]{0,2,1:T(8,128)(2,1)S(1)} %get-tuple-element.1002), kind=kOutput, calls=%fused_computation.23.clone.1 | convolution fusion | flops 1610612736 | bytes 51642368 | tf_op jit(solution)/shard_map/while/body/eval_jaxpr/qgrd,kgd->grqk/dot_general | solution.py:265
  1371.1 83.3 %fusion.179 = f32[2,4,512,64]{2,3,1,0:T(8,128)} fusion(f32[2,512,4,3072]{3,1,2,0:T(8,128)} %fusion.177, f32[2,512,4,3072]{3,1,2,0:T(8,128)} %fusion.175, f32[2,4,512]{2,1,0:T(4,128)S(1)} %dynamic-slice_bitcast_fusion.2, pred[512,3072]{1,0:T(8,128)(4,1)} %compare_and_fusion.3, bf16[3072,2,64]{0,2,1:T(8,128)(2,1)} %get-tuple-element.999), kind=kOutput, calls=%fused_computation.17.clone.1 | convolution fusion | flops 1749031936 | bytes 104087552 | tf_op jit(solution)/shard_map/while/body/eval_jaxpr/grqk,kgd->qgrd/dot_general | solution.py:270
  1454.5 87.0 %fusion.178 = f32[2,64,3072,1]{2,1,3,0:T(8,128)} fusion(bf16[512,2,4,64]{0,3,2,1:T(8,128)(2,1)S(1)} %bitcast.268, f32[2,512,4,3072]{3,1,2,0:T(8,128)} %fusion.177, f32[2,512,4,3072]{3,1,2,0:T(8,128)} %fusion.175, f32[2,4,512]{2,1,0:T(4,128)S(1)} %dynamic-slice_bitcast_fusion.2, pred[512,3072]{1,0:T(8,128)(4,1)} %compare_and_fusion.3), kind=kOutput, calls=%fused_computation.18.clone.1 | convolution fusion | flops 1749031936 | bytes 104349696 | tf_op jit(solution)/shard_map/while/body/eval_jaxpr/grqk,qgrd->kgd/dot_general | solution.py:273
  1541.5 4.7 bitcast_add_fusion.6
  1547.2 19.5 %dynamic_update_slice.49 = f32[2,512,512]{1,0,2:T(2,128)} dynamic-update-slice(f32[2,512,512]{1,0,2:T(2,128)} %get-tuple-element.981, f32[1,512,512]{1,0,2:T(1,128)S(1)} %copy.111, s32[]{:T(128)S(6)} %copy.142, s32[]{:T(128)} %constant.258.clone.1..sunk.2, s32[]{:T(128)} %constant.258.clone.1..sunk.2) | dynamic-update-slice | bytes 2097156 | tf_op jit(solution)/shard_map/while/body/jit(dynamic_update_index_in_dim)/dynamic_update_slice | solution.py:196
  1574.0 33.8 %while.64 = (s32[]{:T(128)}, f32[2,1024,128]{2,1,0:T(8,128)S(1)}, f32[3,2,1024,128]{3,2,0,1:T(8,128)}, s32[]{:T(128)}, s32[]{:T(128)}, /*index=5*/s32[]{:T(128)}, s32[]{:T(128)}) while((s32[]{:T(128)}, f32[2,1024,128]{2,1,0:T(8,128)S(1)}, f32[3,2,1024,128]{3,2,0,1:T(8,128)}, s32[]{:T(128)}, s32[]{:T(128)}, /*index=5*/s32[]{:T(128)}, ...), condition=%wide.region_19.20_spmd, body=%wide.region_18.19_spmd.sunk | while | flops 786438 | bytes 6291623 | solution.py:301
  1574.1 4.5 collective-permute-start.1
  1578.5 11.1 collective-permute-done.1
  1591.1 5.2 collective-permute-start.1
  1596.3 10.2 collective-permute-done.1
  1607.9 4.5 convolution_convert_fusion.6
  1613.0 4.5 convolution_convert_fusion.7
  1617.6 5.9 convolution_convert_fusion.4
  1636.9 5.2 fusion.57
  1645.5 22.3 %pmax.7 = f32[8]{0:T(128)S(1)} all-reduce(f32[8]{0:T(128)S(1)} %reshape.538), channel_id=1, replica_groups=mesh['fsdp'=8,'tp'=4] {'fsdp'}, use_global_device_ids=true, to_apply=%region_36.37 | all-reduce | flops 8 | bytes 64 | tf_op jit(solution)/shard_map/pmax | solution.py:226
  1670.1 6.2 all-reduce.3
  1685.1 6.0 all-reduce.1
  1691.2 17.2 all-reduce.5
  1711.1 28.9 %reduce-scatter.22.cloned.1.call-done = bf16[256,128]{1,0:T(8,128)(2,1)} async-done(((bf16[2048,128]{1,0:T(8,128)(2,1)}), bf16[256,128]{1,0:T(8,128)(2,1)}) %reduce-scatter.22.cloned.1.call-update) | async-done | bytes 65552 | tf_op jit(solution)/shard_map/reduce_scatter | solution.py:332
  1741.5 69.1 %reduce-scatter.26.cloned.1.call-done = bf16[512,256]{1,0:T(8,128)(2,1)} async-done(((bf16[512,2048]{1,0:T(8,128)(2,1)}), bf16[512,256]{1,0:T(8,128)(2,1)}) %reduce-scatter.26.cloned.1.call-update) | async-done | bytes 262160 | tf_op jit(solution)/shard_map/reduce_scatter | solution.py:338
  1812.4 68.5 %reduce-scatter.20.cloned.1.call-done = bf16[256,512]{1,0:T(8,128)(2,1)} async-done(((bf16[2048,512]{1,0:T(8,128)(2,1)}), bf16[256,512]{1,0:T(8,128)(2,1)}) %reduce-scatter.20.cloned.1.call-update) | async-done | bytes 262160 | tf_op jit(solution)/shard_map/reduce_scatter | solution.py:329
  1882.7 44.1 %reduce-scatter.18.cloned.1.call-done = bf16[256,2048]{1,0:T(8,128)(2,1)} async-done(((bf16[1024,2048]{1,0:T(8,128)(2,1)}), bf16[256,2048]{1,0:T(8,128)(2,1)}) %reduce-scatter.18.cloned.1.call-update) | async-done | bytes 1048592 | tf_op jit(solution)/shard_map/reduce_scatter | solution.py:317
  (294 shorter events, 115.2 us)
Async XLA Ops:
  7.2 6.3 copy-start.32
  7.2 6.3 copy-start.35
  7.2 6.5 copy-start.26
  7.2 39.5 %copy-start.16 = (bf16[256,128]{1,0:T(8,128)(2,1)S(1)}, bf16[256,128]{1,0:T(8,128)(2,1)}, u32[]{:S(2)}) copy-start(bf16[256,128]{1,0:T(8,128)(2,1)} %param.26) | copy-start | bytes 196612
  7.2 72.5 %all-gather.10.cloned.1.call-start = ((), (), s32[]{:S(2)}) async-start(), calls=%async_computation.11 | async-start | bytes 5242880 | tf_op jit(solution)/shard_map/all_gather | solution.py:133
  9.4 4.3 copy-start.29
  11.8 120.7 %all-gather.12.cloned.1.call-start = ((), (), s32[]{:S(2)}) async-start(), calls=%async_computation.12 | async-start | bytes 2359296 | tf_op jit(solution)/shard_map/all_gather | solution.py:122
  12.6 273.2 %all-gather.14.cloned.1.call-start = ((), (), s32[]{:S(2)}) async-start(), calls=%async_computation.13 | async-start | bytes 2359296 | tf_op jit(solution)/shard_map/all_gather | solution.py:125
  13.3 350.9 %reduce-scatter.12.cloned.1.call-start = ((), (), s32[]{:S(2)}) async-start(), calls=%async_computation.14 | async-start | bytes 10485760 | tf_op jit(solution)/shard_map/reduce_scatter | solution.py:202
  13.5 119.0 %copy-start.24 = (f32[2048]{0:T(1024)}, f32[2048]{0:T(1024)S(1)}, u32[]{:S(2)}) copy-start(f32[2048]{0:T(1024)S(1)} %convert_element_type.221) | copy-start | bytes 24580
  46.7 37.1 %copy-start.10 = (bf16[2048,128]{1,0:T(8,128)(2,1)}, bf16[2048,128]{1,0:T(8,128)(2,1)S(1)}, u32[]{:S(2)}) copy-start(bf16[2048,128]{1,0:T(8,128)(2,1)S(1)} %all_gather.36) | copy-start | bytes 1572868
  78.5 5.0 copy-start.12
  79.7 58.1 %copy-start.8 = (f32[1024,32]{0,1:T(8,128)}, f32[1024,32]{0,1:T(8,128)S(1)}, u32[]{:S(2)}) copy-start(f32[1024,32]{0,1:T(8,128)S(1)} %get-tuple-element.687) | copy-start | bytes 393220
  88.3 23.0 %collective-permute-start = (bf16[2,1024,128]{2,1,0:T(8,128)(2,1)}, bf16[2,1024,128]{2,1,0:T(8,128)(2,1)S(1)}, u32[]{:S(2)}, u32[]{:S(2)}) collective-permute-start(bf16[2,1024,128]{2,1,0:T(8,128)(2,1)} %get-tuple-element.917), channel_id=1, source_target_pairs={{0,4},{4,8},{8,12},{12,16},{16,20},{20,24},{24,28},{28,0},{1,5},{5... | collective-permute-start | bytes 1572872 | tf_op jit(solution)/shard_map/while/body/eval_jaxpr/ppermute | solution.py:20
  112.2 12.1 collective-permute-start
  192.7 19.4 %copy-start.41 = (bf16[2,512,512]{2,1,0:T(8,128)(2,1)S(1)}, bf16[2,512,512]{2,1,0:T(8,128)(2,1)}, u32[]{:S(2)}) copy-start(bf16[2,512,512]{2,1,0:T(8,128)(2,1)} %get-tuple-element.941) | copy-start | bytes 3145732 | tf_op jit(solution)/shard_map/while
  265.3 19.4 %copy-start.41 = (bf16[2,512,512]{2,1,0:T(8,128)(2,1)S(1)}, bf16[2,512,512]{2,1,0:T(8,128)(2,1)}, u32[]{:S(2)}) copy-start(bf16[2,512,512]{2,1,0:T(8,128)(2,1)} %get-tuple-element.941) | copy-start | bytes 3145732 | tf_op jit(solution)/shard_map/while
  285.7 7.6 copy-start.18
  285.7 7.6 copy-start.20
  285.7 7.6 copy-start.22
  285.7 7.6 copy-start.27
  285.8 7.6 copy-start.37
  293.3 70.8 %copy-start.2 = (bf16[256,2048]{1,0:T(8,128)(2,1)S(1)}, bf16[256,2048]{1,0:T(8,128)(2,1)}, u32[]{:S(2)}) copy-start(bf16[256,2048]{1,0:T(8,128)(2,1)} %param.21) | copy-start | bytes 3145732
  293.4 198.0 %all-gather.20.cloned.1.call-start = ((), (), s32[]{:S(2)}) async-start(), calls=%async_computation.17 | async-start | bytes 9437184 | tf_op jit(solution)/shard_map/all_gather | solution.py:127
  294.0 232.1 %all-gather.16.cloned.1.call-start = ((), (), s32[]{:S(2)}) async-start(), calls=%async_computation.15 | async-start | bytes 5242880 | tf_op jit(solution)/shard_map/all_gather | solution.py:211
  367.7 3.5 copy-start.33
  368.8 284.5 %all-gather.18.cloned.1.call-start = ((), (), s32[]{:S(2)}) async-start(), calls=%async_computation.16 | async-start | bytes 9437184 | tf_op jit(solution)/shard_map/all_gather | solution.py:126
  369.6 409.6 %all-gather.22.cloned.1.call-start = ((), (), s32[]{:S(2)}) async-start(), calls=%async_computation.18 | async-start | bytes 9437184 | tf_op jit(solution)/shard_map/all_gather | solution.py:128
  370.3 443.8 %all-gather.24.cloned.1.call-start = ((), (), s32[]{:S(2)}) async-start(), calls=%async_computation.20 | async-start | bytes 5242880 | tf_op jit(solution)/shard_map/all_gather | solution.py:234
  371.1 567.1 %reduce-scatter.16.cloned.1.call-start = ((), (), s32[]{:S(2)}) async-start(), calls=%async_computation.21 | async-start | bytes 10485760 | tf_op jit(solution)/shard_map/reduce_scatter | solution.py:246
  836.0 14.9 copy-start.39
  836.0 14.9 copy-start.46
  866.3 118.9 %reduce-scatter.14.cloned.1.call-start = ((), (), s32[]{:S(2)}) async-start(), calls=%async_computation.19 | async-start | bytes 5242880 | tf_op jit(solution)/shard_map/reduce_scatter | solution.py:219
  880.3 105.0 %copy-start.7 = (bf16[256,2048]{1,0:T(8,128)(2,1)S(1)}, bf16[256,2048]{1,0:T(8,128)(2,1)}, u32[]{:S(2)}) copy-start(bf16[256,2048]{1,0:T(8,128)(2,1)} %param.33) | copy-start | bytes 3145732
  880.3 152.9 %all-gather.26.cloned.1.call-start = ((), (), s32[]{:S(2)}) async-start(), calls=%async_computation.22 | async-start | bytes 5242880 | tf_op jit(solution)/shard_map/all_gather | solution.py:253
  990.0 686.3 %reduce-scatter.30.cloned.1.call-start = ((), (), s32[]{:S(2)}) async-start(), calls=%async_computation.29 | async-start | bytes 9437184 | tf_op jit(solution)/shard_map/reduce_scatter | solution.py:349
  1004.4 674.8 %reduce-scatter.28.cloned.1.call-start = ((), (), s32[]{:S(2)}) async-start(), calls=%async_computation.28 | async-start | bytes 9437184 | tf_op jit(solution)/shard_map/reduce_scatter | solution.py:346
  1018.5 663.6 %reduce-scatter.32.cloned.1.call-start = ((), (), s32[]{:S(2)}) async-start(), calls=%async_computation.30 | async-start | bytes 9437184 | tf_op jit(solution)/shard_map/reduce_scatter | solution.py:352
  1033.1 6.6 copy-start
  1033.1 6.6 copy-start.19
  1033.1 6.6 copy-start.21
  1033.1 6.6 copy-start.23
  1033.1 6.6 copy-start.28
  1033.1 676.4 %reduce-scatter.24.cloned.1.call-start = ((), (), s32[]{:S(2)}) async-start(), calls=%async_computation.26 | async-start | bytes 589824 | tf_op jit(solution)/shard_map/reduce_scatter | solution.py:335
  1278.4 4.2 copy-start.1
  1541.5 4.7 copy-start.1
  1574.0 33.8 %copy-start.25 = (f32[2048]{0:T(1024)S(1)}, f32[2048]{0:T(1024)}, u32[]{:S(2)}) copy-start(f32[2048]{0:T(1024)} %copy-done.24) | copy-start | bytes 24580
  1574.1 15.6 collective-permute-start.1
  1591.1 15.5 collective-permute-start.1
  1607.8 5.0 copy-start.9
  1607.9 5.0 copy-start.14
  1612.4 127.6 %reduce-scatter.22.cloned.1.call-start = ((), (), s32[]{:S(2)}) async-start(), calls=%async_computation.25 | async-start | bytes 589824 | tf_op jit(solution)/shard_map/reduce_scatter | solution.py:332
  1613.0 4.6 copy-start.43
  1617.5 193.1 %reduce-scatter.26.cloned.1.call-start = ((), (), s32[]{:S(2)}) async-start(), calls=%async_computation.27 | async-start | bytes 2359296 | tf_op jit(solution)/shard_map/reduce_scatter | solution.py:338
  1623.5 257.4 %reduce-scatter.20.cloned.1.call-start = ((), (), s32[]{:S(2)}) async-start(), calls=%async_computation.24 | async-start | bytes 2359296 | tf_op jit(solution)/shard_map/reduce_scatter | solution.py:329
  1628.9 4.0 copy-start.13
  1632.7 294.1 %reduce-scatter.18.cloned.1.call-start = ((), (), s32[]{:S(2)}) async-start(), calls=%async_computation.23 | async-start | bytes 5242880 | tf_op jit(solution)/shard_map/reduce_scatter | solution.py:317
  1642.1 26.2 %copy-start.17 = (bf16[256,128]{1,0:T(8,128)(2,1)S(1)}, bf16[256,128]{1,0:T(8,128)(2,1)}, u32[]{:S(2)}) copy-start(bf16[256,128]{1,0:T(8,128)(2,1)} %param.26) | copy-start | bytes 196612
  1642.2 26.9 %copy-start.15 = (bf16[256,512]{1,0:T(8,128)(2,1)S(1)}, bf16[256,512]{1,0:T(8,128)(2,1)}, u32[]{:S(2)}) copy-start(bf16[256,512]{1,0:T(8,128)(2,1)} %param.25) | copy-start | bytes 786436
  1642.2 27.7 %copy-start.31 = (f32[2048]{0:T(1024)S(1)}, f32[2048]{0:T(1024)}, u32[]{:S(2)}) copy-start(f32[2048]{0:T(1024)} %get-tuple-element.694) | copy-start | bytes 24580
  1679.2 247.6 %copy-start.3 = (bf16[256,2048]{1,0:T(8,128)(2,1)S(1)}, bf16[256,2048]{1,0:T(8,128)(2,1)}, u32[]{:S(2)}) copy-start(bf16[256,2048]{1,0:T(8,128)(2,1)} %param.21) | copy-start | bytes 3145732
  1682.0 246.4 %copy-start.5 = (f32[256,2048]{1,0:T(8,128)S(1)}, f32[256,2048]{1,0:T(8,128)}, u32[]{:S(2)}) copy-start(f32[256,2048]{1,0:T(8,128)} %get-tuple-element.652) | copy-start | bytes 6291460
  1682.0 246.4 %copy-start.30 = (f32[256]{0:T(256)S(1)}, f32[256]{0:T(256)}, u32[]{:S(2)}) copy-start(f32[256]{0:T(256)} %copy-done.29) | copy-start | bytes 3076
  1682.0 246.4 %copy-start.34 = (f32[256]{0:T(256)S(1)}, f32[256]{0:T(256)}, u32[]{:S(2)}) copy-start(f32[256]{0:T(256)} %get-tuple-element.688) | copy-start | bytes 3076
  (10 other events, 15.3 us)
Sparse Core Ops, SparseCore 0:
  11.9 37.1 all-gather.9
  51.3 55.5 all-gather.11
  108.9 56.2 all-gather.13
  293.5 70.6 reduce-scatter.11
  366.4 124.9 all-gather.19
  493.4 32.6 all-gather.15
  528.5 124.8 all-gather.17
  655.6 123.5 all-gather.21
  781.4 32.6 all-gather.23
  866.5 71.6 reduce-scatter.15
  940.7 44.4 reduce-scatter.13
  990.2 34.4 all-gather.25
  1028.7 148.9 reduce-scatter.29
  1181.3 147.9 reduce-scatter.27
  1333.2 148.3 reduce-scatter.31
  1612.5 62.8 reduce-scatter.23
  1678.9 61.0 reduce-scatter.21
  1743.4 67.1 reduce-scatter.25
  1814.1 66.7 reduce-scatter.19
  1883.2 43.4 reduce-scatter.17
where the time goes:
time: 1950 us; the launch traced here: 1940 us
  waiting for transfers between devices  856 us (44%)
  matrix products  740 us (38%)
  other arithmetic  120 us (6%)
  blocking collectives  117 us (6%)
  local copies, waits for them, and re-layouts  74.5 us (4%)
    dot_general x2, matrix products, backward_block(): jnp.einsum('grqk,qgrd->kgd', score_grad, query_heads, preferred_element_t...  174 us
    dot_general x2, matrix products, backward_block(): jnp.einsum('grqk,kgd->qgrd', score_grad, key_heads, preferred_element_typ...  167 us
    all_gather x1, waiting for transfers between devices, shards(): lax.all_gather(w_up, 'fsdp', axis=0, tiled=True)  120 us
    all_gather x1, waiting for transfers between devices, shards(): lax.all_gather(w_gate, 'fsdp', axis=0, tiled=True)  112 us
    all_gather x1, waiting for transfers between devices, shards(): lax.all_gather(w_down, 'fsdp', axis=1, tiled=True)  111 us
    dot_general x4, matrix products, score_block(): jnp.einsum('qgrd,kgd->grqk', query_heads, key_heads, preferred_element_ty...  84.7 us
    reduce_scatter x1, waiting for transfers between devices, shards(): lax.psum_scatter(jnp.dot(row_part, full_out, preferred_element_type=jnp.f...  70 us
    reduce_scatter x1, waiting for transfers between devices, shards(): lax.psum_scatter(grad_outproj.astype(jnp.bfloat16), 'fsdp', scatter_dimen...  69.1 us
  transfers between devices with their start and end apart: 24, of which 16 were waited for; matrix products, arithmetic and copies ran while one was open for 44% of the time, Pallas kernels for 0%

commit v1 on v0

v1 whole, which is shorter than its diff:
```python
import jax
import jax.numpy as jnp
import numpy as np
from jax import lax
from jax.experimental import pallas as pl
from jax.experimental.pallas import tpu as pltpu
from jax.sharding import Mesh
from jax.sharding import PartitionSpec as P

HD = 64
HALF = HD // 2
SLOT_LEN = 2048
LEAD = 512
CHUNK = 512
BLOCK = 256
HEADS = 4

EPSILON = 1e-05
THETA = 10000000.0
MULTIPLIER = 0.015625
RESIDUAL = 0.22
LEVEL_UNIT = 0.125
NEGATIVE = -1e30
GROUP = ("y", "x", "c")
EVERY = ("z", "y", "x", "c")
F32 = jnp.float32
BF16 = jnp.bfloat16


def swap(x, axis):
    return lax.ppermute(x, axis, [(0, 1), (1, 0)])


def along(x, by):
    peers = lax.axis_size("z")
    return lax.ppermute(x, "z", [(i, (i + by) % peers) for i in range(peers)])


def dot(left, right, left_dim, right_dim):
    return lax.dot_general(
        left, right, (((left_dim,), (right_dim,)), ((), ())), preferred_element_type=F32
    )


def half_of(x, which, axis):
    size = x.shape[axis] // 2
    return lax.dynamic_slice_in_dim(x, which * size, size, axis)


def ordered(own, other, rank, axis):
    return jnp.where(
        rank == 0,
        jnp.concatenate((own, other), axis=axis),
        jnp.concatenate((other, own), axis=axis),
    )


def gather_rows(v):
    half = v.shape[0] // 2
    a00, b00 = v[:half], v[half:]
    a01 = swap(a00, "x")
    b10 = swap(b00, "y")
    a1 = swap(jnp.concatenate((a00, a01)), "y")
    b1 = swap(jnp.concatenate((b00, b10)), "x")
    own = jnp.concatenate((v, a01, b1[:half], a1[:half], b10, a1[half:], b1[half:]))
    return jnp.concatenate((own, swap(own, "c")))


def scatter_rows(low, high):
    sent = swap(high().astype(BF16), "c")
    total = low() + sent.astype(F32)
    rows = total.shape[0] // 4
    cols = total.shape[1] // 2
    blocks = total.reshape(2, 2, rows, 2 * cols)
    left, right = blocks[..., :cols], blocks[..., cols:]
    left_x = swap(left[:, 1].astype(BF16), "x").astype(F32)
    right_y = swap(right[1].astype(BF16), "y").astype(F32)
    left_y = swap((left[1, 0] + left_x[1]).astype(BF16), "y").astype(F32)
    right_x = swap((right[0, 1] + right_y[1]).astype(BF16), "x").astype(F32)
    return jnp.concatenate(
        (left[0, 0] + left_x[0] + left_y, right[0, 0] + right_y[0] + right_x), axis=1
    )


def place_of(block, rank):
    j = jnp.bitwise_xor(block, rank)
    return jnp.bitwise_or(jnp.left_shift(jnp.bitwise_and(j, 1), 2), jnp.right_shift(j, 1))


def lanes_of(block, rank):
    return pl.ds(pl.multiple_of(place_of(block, rank) * BLOCK, BLOCK), BLOCK)


def rope_kernel(info, qkv, cos, sin, out):
    rank = info[0]

    @pl.loop(0, SLOT_LEN // BLOCK)
    def _(block):
        source = lanes_of(block, rank)
        target = pl.ds(pl.multiple_of(block * BLOCK, BLOCK), BLOCK)
        c, s = cos[:, target], sin[:, target]
        for head in range(HEADS + 1):
            first = qkv[pl.ds(head * HD, HALF), source]
            second = qkv[pl.ds(head * HD + HALF, HALF), source]
            scale = MULTIPLIER if head < HEADS else 1.0
            out[pl.ds(head * HD, HALF), target] = ((first * c - second * s).astype(BF16) * scale).astype(BF16)
            out[pl.ds(head * HD + HALF, HALF), target] = ((second * c + first * s).astype(BF16) * scale).astype(BF16)
        rest = (HEADS + 1) * HD
        out[pl.ds(rest, HD), target] = qkv[pl.ds(rest, HD), source].astype(BF16)


KEYS = SLOT_LEN + LEAD
K_AT = HEADS * HD
V_AT = K_AT + HD


def upright(x):
    return x.astype(F32).T.astype(BF16)


def causal():
    keys = lax.broadcasted_iota(jnp.int32, (CHUNK, CHUNK), 0)
    queries = lax.broadcasted_iota(jnp.int32, (CHUNK, CHUNK), 1)
    return keys <= queries


def key_range(step):
    last = step == SLOT_LEN // CHUNK - 1
    low = jnp.where(last, KEYS // CHUNK - 1, 0)
    high = jnp.where(last, KEYS // CHUNK, step + 2)
    return low, high


def chunk_of(i):
    return pl.ds(pl.multiple_of(i * CHUNK, CHUNK), CHUNK)


def head_rows(h):
    return pl.ds(pl.multiple_of(h * HD, HD), HD)


def attend_kernel(info, qkv, halo, heads_out, lse_out, peak_out, k_up, v_flat, scores):
    rank = info[0]
    k_up[pl.ds(0, LEAD), :] = upright(halo[pl.ds(0, HD), :])
    v_flat[:, pl.ds(0, LEAD)] = halo[pl.ds(HD, HD), :]
    v_flat[:, pl.ds(LEAD, SLOT_LEN)] = qkv[pl.ds(V_AT, HD), :]

    @pl.loop(0, SLOT_LEN // CHUNK)
    def _(i):
        k_up[pl.ds(pl.multiple_of(LEAD + i * CHUNK, CHUNK), CHUNK), :] = upright(
            qkv[pl.ds(K_AT, HD), chunk_of(i)]
        )

    peak_out[...] = jnp.full(peak_out.shape, NEGATIVE, F32)
    lse_out[...] = jnp.zeros(lse_out.shape, F32)

    @pl.loop(0, HEADS)
    def _(h):
        @pl.loop(0, SLOT_LEN // CHUNK)
        def _(step):
            low, high = key_range(step)
            query = qkv[head_rows(h), chunk_of(step)]

            def raw(kc):
                return jnp.dot(k_up[chunk_of(kc), :], query, preferred_element_type=F32)

            def first(kc, top):
                s = raw(kc)
                scores[chunk_of(kc - low), :] = s
                return jnp.maximum(top, jnp.max(s, axis=0, keepdims=True))

            s = jnp.where(causal(), raw(high - 1), NEGATIVE)
            scores[chunk_of(high - 1 - low), :] = s
            top = lax.fori_loop(low, high - 1, first, jnp.max(s, axis=0, keepdims=True))

            def second(kc, total):
                e = jnp.exp(scores[chunk_of(kc), :] - top)
                scores[chunk_of(kc), :] = e
                return total + jnp.sum(e, axis=0, keepdims=True)

            total = lax.fori_loop(0, high - low, second, jnp.zeros((1, CHUNK), F32))
            inverse = 1.0 / total

            def third(kc, mixed):
                probs = (scores[chunk_of(kc), :] * inverse).astype(BF16)
                return mixed + jnp.dot(
                    v_flat[:, chunk_of(kc + low)], probs, preferred_element_type=F32
                )

            mixed = lax.fori_loop(0, high - low, third, jnp.zeros((HD, CHUNK), F32))
            mixed = mixed.astype(BF16)
            for part in range(CHUNK // BLOCK):
                heads_out[head_rows(h), lanes_of(step * (CHUNK // BLOCK) + part, rank)] = mixed[
                    :, part * BLOCK : (part + 1) * BLOCK
                ]
            lse_out[pl.ds(h, 1), chunk_of(step)] = top + jnp.log(total)
            last = step == SLOT_LEN // CHUNK - 1
            start = jnp.where(last, 0, LEAD + step * CHUNK)
            alive = jnp.where(last, info[2], info[1])
            spots = lax.broadcasted_iota(jnp.int32, (1, CHUNK), 1) + start
            best = jnp.max(jnp.where(spots < alive, top, NEGATIVE), axis=1, keepdims=True)
            peak_out[pl.ds(h, 1), :] = jnp.maximum(peak_out[pl.ds(h, 1), :], best)


def attend_back_kernel(
    info, qkv, halo, upstream, lse, cos, sin, dq_out, dkv_out, halo_out,
    k_up, v_up, k_flat, probs_s, grads_s, dk_s, dv_s, up_abs,
):
    rank = info[0]
    k_up[pl.ds(0, LEAD), :] = upright(halo[pl.ds(0, HD), :])
    v_up[pl.ds(0, LEAD), :] = upright(halo[pl.ds(HD, HD), :])
    k_flat[:, pl.ds(0, LEAD)] = halo[pl.ds(0, HD), :]
    k_flat[:, pl.ds(LEAD, SLOT_LEN)] = qkv[pl.ds(K_AT, HD), :]

    @pl.loop(0, SLOT_LEN // CHUNK)
    def _(i):
        rows = pl.ds(pl.multiple_of(LEAD + i * CHUNK, CHUNK), CHUNK)
        k_up[rows, :] = upright(qkv[pl.ds(K_AT, HD), chunk_of(i)])
        v_up[rows, :] = upright(qkv[pl.ds(V_AT, HD), chunk_of(i)])

    @pl.loop(0, SLOT_LEN // BLOCK)
    def _(block):
        target = pl.ds(pl.multiple_of(block * BLOCK, BLOCK), BLOCK)
        up_abs[:, target] = upstream[:, lanes_of(block, rank)]

    dk_s[...] = jnp.zeros(dk_s.shape, F32)
    dv_s[...] = jnp.zeros(dv_s.shape, F32)

    @pl.loop(0, HEADS)
    def _(h):
        @pl.loop(0, SLOT_LEN // CHUNK)
        def _(step):
            low, high = key_range(step)
            here = chunk_of(step)
            query = qkv[head_rows(h), here]
            grad = up_abs[head_rows(h), here]
            query_up, grad_up = upright(query), upright(grad)
            logs = lse[pl.ds(h, 1), here]

            def one(kc, masked):
                s = jnp.dot(k_up[chunk_of(kc), :], query, preferred_element_type=F32)
                p = jnp.exp(s - logs)
                if masked:
                    p = jnp.where(causal(), p, 0.0)
                g = jnp.dot(v_up[chunk_of(kc), :], grad, preferred_element_type=F32)
                probs_s[chunk_of(kc - low), :] = p
                grads_s[chunk_of(kc - low), :] = g
                dv_s[chunk_of(kc), :] += jnp.dot(
                    p.astype(BF16), grad_up, preferred_element_type=F32
                )
                return jnp.sum(p * g, axis=0, keepdims=True)

            delta = one(high - 1, True)
            delta = lax.fori_loop(low, high - 1, lambda kc, d: d + one(kc, False), delta)

            def two(kc, dq):
                p, g = probs_s[chunk_of(kc - low), :], grads_s[chunk_of(kc - low), :]
                ds = (p * (g - delta)).astype(BF16)
                dk_s[chunk_of(kc), :] += jnp.dot(ds, query_up, preferred_element_type=F32)
                return dq + jnp.dot(k_flat[:, chunk_of(kc)], ds, preferred_element_type=F32)

            dq = lax.fori_loop(low, high, two, jnp.zeros((HD, CHUNK), F32)) * MULTIPLIER
            c, s = cos[:, here], sin[:, here]
            u1, u2 = dq[:HALF], dq[HALF:]
            t1, t2 = (u1 * c + u2 * s).astype(BF16), (u2 * c - u1 * s).astype(BF16)
            for part in range(CHUNK // BLOCK):
                there = lanes_of(step * (CHUNK // BLOCK) + part, rank)
                cut = slice(part * BLOCK, (part + 1) * BLOCK)
                dq_out[pl.ds(pl.multiple_of(h * HD, HD), HALF), there] = t1[:, cut]
                dq_out[pl.ds(pl.multiple_of(h * HD + HALF, HALF), HALF), there] = t2[:, cut]

    halo_out[pl.ds(0, HD), :] = dk_s[pl.ds(0, LEAD), :].T.astype(BF16)
    halo_out[pl.ds(HD, HD), :] = dv_s[pl.ds(0, LEAD), :].T.astype(BF16)

    @pl.loop(0, SLOT_LEN // CHUNK)
    def _(i):
        rows = pl.ds(pl.multiple_of(LEAD + i * CHUNK, CHUNK), CHUNK)
        dkv_out[pl.ds(0, HD), chunk_of(i)] = dk_s[rows, :].T
        dkv_out[pl.ds(HD, HD), chunk_of(i)] = dv_s[rows, :].T


def finish_kernel(info, dkv, halo, cos, sin, out):
    rank = info[0]
    owned = (SLOT_LEN - LEAD) // BLOCK
    for block in range(SLOT_LEN // BLOCK):
        source = pl.ds(block * BLOCK, BLOCK)
        target = lanes_of(block, rank)
        c, s = cos[:, source], sin[:, source]
        u1, u2 = dkv[pl.ds(0, HALF), source], dkv[pl.ds(HALF, HALF), source]
        rest = dkv[pl.ds(HD, HD), source]
        if block >= owned:
            part = pl.ds((block - owned) * BLOCK, BLOCK)
            u1 = u1 + halo[pl.ds(0, HALF), part].astype(F32)
            u2 = u2 + halo[pl.ds(HALF, HALF), part].astype(F32)
            rest = rest + halo[pl.ds(HD, HD), part].astype(F32)
        out[pl.ds(0, HALF), target] = (u1 * c + u2 * s).astype(BF16)
        out[pl.ds(HALF, HALF), target] = (u2 * c - u1 * s).astype(BF16)
        out[pl.ds(HD, HD), target] = rest.astype(BF16)


def call(kernel, info, args, outs, scratch, flops, name):
    moved = sum(a.size * a.dtype.itemsize for a in args)
    moved += sum(int(np.prod(s)) * np.dtype(d).itemsize for s, d in outs)
    spec = pl.BlockSpec(memory_space=pltpu.VMEM)
    return pl.pallas_call(
        kernel,
        out_shape=[jax.ShapeDtypeStruct(s, d) for s, d in outs],
        in_specs=[pl.BlockSpec(memory_space=pltpu.SMEM)] + [spec] * len(args),
        out_specs=[spec] * len(outs),
        scratch_shapes=[pltpu.VMEM(s, d) for s, d in scratch],
        compiler_params=pltpu.CompilerParams(vmem_limit_bytes=40 * 2**20),
        cost_estimate=pl.CostEstimate(flops=flops, bytes_accessed=moved, transcendentals=0),
        name=name,
    )(info, *args)


def norm_back(values, scale, upstream):
    mean_term = jnp.mean(values * upstream, axis=1, keepdims=True)
    return scale * upstream - values * (scale * scale * scale) * mean_term


def shards(
    layer_in, lengths, clip_level, attn_gain, w_query, w_key, w_value, w_out,
    mlp_gain, w_gate, w_up, w_down, cotangent,
):
    tok_rows, width = layer_in.shape
    z_rank, y_rank = lax.axis_index("z"), lax.axis_index("y")
    rank = (y_rank * 2 + lax.axis_index("x")) * 2 + lax.axis_index("c")
    slots = lengths.shape[0]
    next_slot = (z_rank + 1) % slots
    info = jnp.stack(
        (rank, lax.dynamic_index_in_dim(lengths, z_rank, keepdims=False),
         lax.dynamic_index_in_dim(lengths, next_slot, keepdims=False))
    ).astype(jnp.int32)
    inner = rank * tok_rows + jnp.arange(tok_rows, dtype=jnp.int32) + LEAD
    own_mask = jnp.where(inner < SLOT_LEN, inner < info[1], inner - SLOT_LEN < info[2])
    own_mask = own_mask.astype(F32)[:, None]
    spots = ((jnp.arange(SLOT_LEN, dtype=jnp.int32) + LEAD) % SLOT_LEN).astype(F32)
    freq = THETA ** (-(jnp.arange(HALF, dtype=F32) * 2.0 / HD))
    angles = spots[None, :] * freq[:, None]
    cos, sin = jnp.cos(angles), jnp.sin(angles)
    q_half = w_query.shape[1] // 2

    def heads_part(which):
        return jnp.concatenate(
            (half_of(w_query, which, 1), half_of(w_key, which, 1), half_of(w_value, which, 1)), 1
        )

    other_y = 1 - y_rank
    qkv_part = ordered(heads_part(y_rank), swap(heads_part(other_y), "y"), y_rank, 0)
    out_part = ordered(half_of(w_out, y_rank, 0), swap(half_of(w_out, other_y, 0), "y"), y_rank, 1)
    down_part = ordered(half_of(w_down, y_rank, 0), swap(half_of(w_down, other_y, 0), "y"), y_rank, 1)
    gate_part = ordered(half_of(w_gate, y_rank, 1), swap(half_of(w_gate, other_y, 1), "y"), y_rank, 0)
    up_part = ordered(half_of(w_up, y_rank, 1), swap(half_of(w_up, other_y, 1), "y"), y_rank, 0)
    full_qkv = lax.all_gather(qkv_part, "z", axis=0, tiled=True)
    full_out = lax.all_gather(out_part, "z", axis=1, tiled=True)
    full_down = lax.all_gather(down_part, "z", axis=1, tiled=True)
    full_gate = lax.all_gather(gate_part, "z", axis=0, tiled=True)
    full_up = lax.all_gather(up_part, "z", axis=0, tiled=True)

    layer_f = layer_in.astype(F32)
    scale_one = lax.rsqrt(jnp.mean(layer_f * layer_f, axis=1, keepdims=True) + EPSILON)
    normal_one = (layer_f * scale_one).astype(BF16)
    gain_one = attn_gain.astype(F32)
    acts_one = gather_rows((normal_one.astype(F32) * gain_one[None, :]).astype(BF16))
    grad_out = cotangent.astype(F32)
    down_rows = gather_rows((RESIDUAL * own_mask * grad_out).astype(BF16))

    rows = acts_one.shape[0]
    half_rows = rows // 2
    flat = dot(full_qkv, acts_one, 0, 1)
    (qkv,) = call(
        rope_kernel, info, (flat, cos, sin), [((flat.shape[0], rows), BF16)], [],
        4 * flat.size, "rope",
    )
    halo = along(qkv[K_AT:, SLOT_LEN - LEAD :], 1)
    work = 2 * HEADS * HD * 10 * CHUNK * CHUNK * 4
    heads, lse, peak = call(
        attend_kernel, info, (qkv, halo),
        [((HEADS * HD, rows), BF16), ((8, rows), F32), ((8, 128), F32)],
        [((KEYS, HD), BF16), ((HD, KEYS), BF16), ((SLOT_LEN, CHUNK), F32)],
        4 * work, "attend",
    )
    branch_one = scatter_rows(
        lambda: dot(heads[:, :half_rows], full_out, 0, 0),
        lambda: dot(heads[:, half_rows:], full_out, 0, 0),
    )
    resid = layer_f + RESIDUAL * own_mask * branch_one
    scale_two = lax.rsqrt(jnp.mean(resid * resid, axis=1, keepdims=True) + EPSILON)
    normal_two = (resid * scale_two).astype(BF16)
    gain_two = mlp_gain.astype(F32)
    acts_two = gather_rows((normal_two.astype(F32) * gain_two[None, :]).astype(BF16))

    hidden_grad = dot(down_rows, full_down, 1, 1)
    gate_proj = dot(acts_two, full_gate, 1, 0)
    up_proj = dot(acts_two, full_up, 1, 0)
    sigmoid_gate = jax.nn.sigmoid(gate_proj)
    hidden = (gate_proj * sigmoid_gate * up_proj).astype(BF16)
    gate_grad = (
        hidden_grad * up_proj * sigmoid_gate * (1.0 + gate_proj * (1.0 - sigmoid_gate))
    ).astype(BF16)
    up_grad = (hidden_grad * gate_proj * sigmoid_gate).astype(BF16)

    def reduced(grad, axis):
        return lax.psum_scatter(grad.astype(BF16), "z", scatter_dimension=axis, tiled=True)

    down_sum = reduced(dot(hidden, down_rows, 0, 0), 1)
    gate_sum = reduced(dot(acts_two, gate_grad, 0, 0), 0)
    up_sum = reduced(dot(acts_two, up_grad, 0, 0), 0)

    def acts_two_back(part):
        return dot(gate_grad[part], full_gate, 1, 1) + dot(up_grad[part], full_up, 1, 1)

    norm_two_grad = scatter_rows(
        lambda: acts_two_back(slice(None, half_rows)), lambda: acts_two_back(slice(half_rows, None))
    )
    gain_two_part = jnp.sum(normal_two.astype(F32) * norm_two_grad, axis=0)
    grad_resid = grad_out + norm_back(resid, scale_two, gain_two[None, :] * norm_two_grad)
    mixed_rows = gather_rows((RESIDUAL * own_mask * grad_resid).astype(BF16))
    branch_two = scatter_rows(
        lambda: dot(hidden[:half_rows], full_down, 1, 0),
        lambda: dot(hidden[half_rows:], full_down, 1, 0),
    )
    result = resid + RESIDUAL * own_mask * branch_two

    heads_grad = dot(full_out, mixed_rows, 1, 1).astype(BF16)
    dq, dkv, back = call(
        attend_back_kernel, info, (qkv, halo, heads_grad, lse, cos, sin),
        [((HEADS * HD, rows), BF16), ((2 * HD, rows), F32), ((2 * HD, LEAD), BF16)],
        [((KEYS, HD), BF16), ((KEYS, HD), BF16), ((HD, KEYS), BF16),
         ((SLOT_LEN, CHUNK), F32), ((SLOT_LEN, CHUNK), F32),
         ((KEYS, HD), F32), ((KEYS, HD), F32), ((HEADS * HD, SLOT_LEN), BF16)],
        10 * work, "attend_back",
    )
    (dkv_done,) = call(
        finish_kernel, info, (dkv, along(back, -1), cos, sin), [((2 * HD, rows), BF16)], [],
        4 * dkv.size, "finish",
    )
    dqkv = jnp.concatenate((dq, dkv_done))
    out_sum = reduced(dot(heads, mixed_rows, 1, 0), 1)
    qkv_sum = reduced(dot(acts_one, dqkv, 0, 1), 0)
    norm_one_grad = scatter_rows(
        lambda: dot(dqkv[:, :half_rows], full_qkv, 0, 1),
        lambda: dot(dqkv[:, half_rows:], full_qkv, 0, 1),
    )
    gain_one_part = jnp.sum(normal_one.astype(F32) * norm_one_grad, axis=0)
    grad_input = grad_resid + norm_back(layer_f, scale_one, gain_one[None, :] * norm_one_grad)

    def owned_rows(total):
        return half_of(total, y_rank, 0), swap(half_of(total, other_y, 0), "y")

    def owned_cols(total):
        return half_of(total, y_rank, 1), swap(half_of(total, other_y, 1), "y")

    down_grad = ordered(*owned_cols(down_sum), y_rank, 0).astype(F32)
    gate_w_grad = ordered(*owned_rows(gate_sum), y_rank, 1).astype(F32)
    up_w_grad = ordered(*owned_rows(up_sum), y_rank, 1).astype(F32)
    out_grad = ordered(*owned_cols(out_sum), y_rank, 0).astype(F32)
    own, other = owned_rows(qkv_sum)

    def columns(start, stop):
        return ordered(own[:, start:stop], other[:, start:stop], y_rank, 1).astype(F32)

    query_grad = columns(0, K_AT)
    key_grad = columns(K_AT, V_AT)
    value_grad = columns(V_AT, V_AT + HD)

    gains = jnp.stack((gain_one_part, gain_two_part))
    devices = lax.axis_size(EVERY)
    gains = lax.psum_scatter(
        gains.reshape(2, devices, -1).transpose(1, 0, 2), EVERY, scatter_dimension=0, tiled=True
    )[0]

    local = peak[:HEADS, 0]
    empty = jnp.full((HEADS,), NEGATIVE, F32)
    head_peak = lax.pmax(ordered(local, empty, y_rank, 0), ("z", "y"))
    level = clip_level[0].astype(F32) * LEVEL_UNIT
    factor = level / jnp.maximum(level, head_peak)
    query_clipped = w_query.astype(F32) * jnp.repeat(jnp.sqrt(factor), HD)[None, :]
    kv_factor = jnp.min(factor.reshape(-1, HEADS), axis=1)
    key_clipped = w_key.astype(F32) * jnp.repeat(jnp.sqrt(kv_factor), HD)[None, :]
    return (
        result.astype(BF16),
        grad_input.astype(BF16),
        gains[0],
        query_grad,
        key_grad,
        value_grad,
        out_grad,
        gains[1],
        gate_w_grad,
        up_w_grad,
        down_grad,
        query_clipped,
        key_clipped,
    )


def solution(mesh):
    fsdp, tp = mesh.shape["fsdp"], mesh.shape["tp"]
    fine = Mesh(mesh.devices.reshape(fsdp // 2, 2, tp // 2, 2), EVERY)
    rows, cols = ("z", "y"), ("x", "c")
    tokens, down, across = P(EVERY, None), P(rows, cols), P(cols, rows)
    in_specs = (
        tokens, P(), P(), P(), down, down, down, across, P(), down, down, across, tokens,
    )
    out_specs = (
        tokens, tokens, P(EVERY), down, down, down, across, P(EVERY), down, down, across,
        down, down,
    )
    return jax.shard_map(shards, mesh=fine, in_specs=in_specs, out_specs=out_specs, check_vma=False)
```

time: 1950 us -> 835 us (0.43)
  waiting for transfers between devices: 856 us -> 259 us
  matrix products: 740 us -> 186 us
  Pallas kernels: 0 us -> 70.6 us
  blocking collectives: 117 us -> 59.5 us
  starting transfers between devices: 12.7 us -> 69.9 us
  other arithmetic: 120 us -> 65.3 us
  local copies, waits for them, and re-layouts: 74.5 us -> 98.3 us
    dot_general x35 -> x20, matrix products: 740 us -> 186 us  [dot(): lax.dot_general(left, right, (((left_dim,), (right_dim,)), ((), ())), pre...]
    all_gather x9 -> x5, waiting for transfers between devices: 414 us -> 0.13 us  [the longest x1 0.13 us: shards(): full_gate = lax.all_gather(gate_part, 'z', axis=0, tiled=True)]
    reduce_scatter x11 -> x5, waiting for transfers between devices: 384 us -> 0.04 us  [reduced(): lax.psum_scatter(grad.astype(BF16), 'z', scatter_dimension=axis, tiled=True)]
    ppermute x4 -> x52, waiting for transfers between devices: 54.5 us -> 259 us  [the longest x50 245 us: swap(): return lax.ppermute(x, axis, [(0, 1), (1, 0)])]
    pallas_call x0 -> x4, Pallas kernels: none -> 70.6 us  [call(): pl.pallas_call(kernel, out_shape=[jax.ShapeDtypeStruct(s, d) for s, d in...]
    all_gather x2 -> x0, blocking collectives: 64.8 us -> none  [the longest x1 33.1 us: shards(): lax.all_gather(w_value, 'fsdp', axis=0, tiled=True)]
    reduce_max x3 -> x0, other arithmetic: 52.7 us -> none  [the longest x2 52.6 us: forward_block(): head_peak = jnp.max(jnp.where(counted, scores, NEGATIVE), axis=(2, 3))]
    unnamed x93 -> x155, local copies, waits for them, and re-layouts: 4.15 us -> 52.3 us
  transfers between devices with their start and end apart: 24 -> 62, of which waited for: 16 -> 29; matrix products, arithmetic and copies ran while one was open for 44% -> 37% of each run, Pallas kernels for 0% -> 9%
where the time goes in v1:
time: 835 us; the launch traced here: 825 us
  waiting for transfers between devices  259 us (31%)
  matrix products  186 us (22%)
  local copies, waits for them, and re-layouts  98.3 us (12%)
  Pallas kernels  70.6 us (8%)
  starting transfers between devices  69.9 us (8%)
  other arithmetic  65.3 us (8%)
  blocking collectives  59.5 us (7%)
  between operations  16.1 us (2%)
    ppermute x50, waiting for transfers between devices, swap(): return lax.ppermute(x, axis, [(0, 1), (1, 0)])  245 us
    dot_general x20, matrix products, dot(): lax.dot_general(left, right, (((left_dim,), (right_dim,)), ((), ())), pre...  186 us
    pallas_call x4, Pallas kernels, call(): pl.pallas_call(kernel, out_shape=[jax.ShapeDtypeStruct(s, d) for s, d in...  70.6 us
    unnamed x155, local copies, waits for them, and re-layouts  52.3 us
    ppermute x50, starting transfers between devices, swap(): return lax.ppermute(x, axis, [(0, 1), (1, 0)])  48.6 us
    unnamed x1, blocking collectives  37.2 us
    pmax x1, blocking collectives, shards(): head_peak = lax.pmax(ordered(local, empty, y_rank, 0), ('z', 'y'))  22.3 us
    concatenate x4, local copies, waits for them, and re-layouts, gather_rows(): return jnp.concatenate((own, swap(own, 'c')))  17.1 us
  transfers between devices with their start and end apart: 62, of which 29 were waited for; matrix products, arithmetic and copies ran while one was open for 37% of the time, Pallas kernels for 9%

profile of v1, /device:TPU:0, one launch (start us, length us, event | category | flops | bytes accessed | tf_op | source)
XLA Modules:
  0.0 824.8 jit_solution(15672030360169306125)
XLA Ops:
  10.4 3.0 collective-permute-start
  13.5 4.9 collective-permute-done
  30.2 9.5 %collective-permute-done.2 = bf16[128,2048]{1,0:T(8,128)(2,1)S(1)} collective-permute-done((bf16[128,2048]{1,0:T(8,128)(2,1)S(1)}, bf16[128,2048]{1,0:T(8,128)(2,1)S(1)}, u32[]{:S(2)}, u32[]{:S(2)}) %collective-permute-start.2) | collective-permute-done | bytes 524320 | tf_op jit(solution)/shard_map/ppermute | solution.py:31
  48.9 9.6 %collective-permute-done.20 = bf16[1024,256]{1,0:T(8,128)(2,1)S(1)} collective-permute-done((bf16[1024,256]{1,0:T(8,128)(2,1)S(1)}, bf16[1024,256]{1,0:T(8,128)(2,1)S(1)}, u32[]{:S(2)}, u32[]{:S(2)}) %collective-permute-start.20) | collective-permute-done | bytes 524320 | tf_op jit(solution)/shard_map/ppermute | solution.py:31
  60.9 3.0 collective-permute-done.3
  64.8 12.8 %collective-permute-done.4 = bf16[256,2048]{1,0:T(8,128)(2,1)} collective-permute-done((bf16[256,2048]{1,0:T(8,128)(2,1)}, bf16[256,2048]{1,0:T(8,128)(2,1)}, u32[]{:S(2)}, u32[]{:S(2)}) %collective-permute-start.4) | collective-permute-done | bytes 1048608 | tf_op jit(solution)/shard_map/ppermute | solution.py:31
  93.6 5.0 constant_dynamic-update-slice_fusion.3
  98.5 6.5 fusion.86.qkv
  109.2 7.6 collective-permute-done.6.halo
  116.8 28.7 %attend.1 = (bf16[256,2048]{1,0:T(8,128)(2,1)S(1)}, f32[8,2048]{1,0:T(8,128)S(1)}, f32[8,128]{1,0:T(8,128)S(1)}) custom-call(s32[3]{0:T(128)S(1)} %pad_add_fusion.info, bf16[384,2048]{1,0:T(8,128)(2,1)S(1)} %rope.1.qkv, bf16[128,512]{1,0:T(8,128)(2,1)S(1)} %collective-permute-done.6.halo), custom_call_target="tpu_custom_call" | custom-call | flops 21474836480 | bytes 2822144 | tf_op jit(solution)/shard_map/attend/pallas_call | solution.py:305
  145.5 4.9 convolution_convert_fusion.2
  158.7 10.5 %collective-permute-done.27 = bf16[128,2048]{1,0:T(8,128)(2,1)S(1)} collective-permute-done((bf16[128,2048]{1,0:T(8,128)(2,1)S(1)}, bf16[128,2048]{1,0:T(8,128)(2,1)S(1)}, u32[]{:S(2)}, u32[]{:S(2)}) %collective-permute-start.27) | collective-permute-done | bytes 524320 | tf_op jit(solution)/shard_map/ppermute | solution.py:31
  174.2 6.2 collective-permute-done.18
  182.0 12.4 %reduce-scatter.14.cloned.1.call-start = ((), (), s32[]{:S(2)}) async-start(), calls=%async_computation.14 | async-start | bytes 5242880 | tf_op jit(solution)/shard_map/reduce_scatter | solution.py:405
  196.6 4.0 convert_add_fusion.3
  205.3 20.0 %collective-permute-done.9 = bf16[2,256,1024]{2,1,0:T(8,128)(2,1)S(1)} collective-permute-done((bf16[2,256,1024]{2,1,0:T(8,128)(2,1)S(1)}, bf16[2,256,1024]{2,1,0:T(8,128)(2,1)S(1)}, u32[]{:S(2)}, u32[]{:S(2)}) %collective-permute-start.9) | collective-permute-done | bytes 1048608 | tf_op jit(solution)/shard_map/ppermute | solution.py:31
  228.7 9.8 %collective-permute-done.10 = bf16[256,1024]{1,0:T(8,128)(2,1)S(1)} collective-permute-done((bf16[256,1024]{1,0:T(8,128)(2,1)S(1)}, bf16[256,1024]{1,0:T(8,128)(2,1)S(1)}, u32[]{:S(2)}, u32[]{:S(2)}) %collective-permute-start.10) | collective-permute-done | bytes 524320 | tf_op jit(solution)/shard_map/ppermute | solution.py:31
  244.2 6.7 collective-permute-done.12
  259.7 5.1 collective-permute-done.14
  267.0 3.0 collective-permute-done.13
  274.2 15.7 %collective-permute-done.15 = bf16[256,2048]{1,0:T(8,128)(2,1)S(1)} collective-permute-done((bf16[256,2048]{1,0:T(8,128)(2,1)S(1)}, bf16[256,2048]{1,0:T(8,128)(2,1)S(1)}, u32[]{:S(2)}, u32[]{:S(2)}) %collective-permute-start.15) | collective-permute-done | bytes 1048608 | tf_op jit(solution)/shard_map/ppermute | solution.py:31
  294.4 2.5 constant_dynamic-update-slice_fusion.17
  296.9 14.7 %fusion.88 = f32[2048,1024]{1,0:T(8,128)} fusion(bf16[2048,2048]{1,0:T(8,128)(2,1)} %constant_dynamic-update-slice_fusion.17, bf16[1024,2048]{1,0:T(8,128)(2,1)} %all-gather.14.cloned.1.call-done), kind=kOutput, calls=%fused_computation.297 | convolution fusion | flops 8589934592 | bytes 20971520 | tf_op jit(solution)/shard_map/dot_general | solution.py:40
  314.9 4.8 constant_dynamic-update-slice_fusion.10
  319.7 14.5 %fusion.87 = f32[2048,1024]{1,0:T(8,128)} fusion(bf16[2048,2048]{1,0:T(8,128)(2,1)} %constant_dynamic-update-slice_fusion.10, bf16[2048,1024]{1,0:T(8,128)(2,1)} %all-gather.12.cloned.1.call-done), kind=kOutput, calls=%fused_computation.296 | convolution fusion | flops 8589934592 | bytes 20971520 | tf_op jit(solution)/shard_map/dot_general | solution.py:40
  334.3 22.2 %multiply_convert_fusion.1 = (bf16[2048,1024]{1,0:T(8,128)(2,1)}, bf16[2048,1024]{1,0:T(8,128)(2,1)}, bf16[2048,1024]{1,0:T(8,128)(2,1)}) fusion(f32[2048,1024]{1,0:T(8,128)} %fusion.88, f32[2048,1024]{1,0:T(8,128)} %fusion.87, bf16[2048,2048]{1,0:T(8,128)(2,1)} %constant_dynamic-update-slice_fusion.10, bf16[2048,1024]{1,0:T(8,128)(2,1)} %all-gather.10.cloned.1.call-done), kind=kOutput, calls=%fused_computation.8 | convolution fusion | flops 8623489024 | bytes 41943040 | tf_op jit(solution)/shard_map/dot_general | solution.py:40
  356.6 8.3 %convolution_convert_fusion.3 = bf16[1024,2048]{1,0:T(8,128)(2,1)} fusion(bf16[1024,2048]{1,0:T(8,128)(2,1)S(1)} %copy-done.48, bf16[2048,1024]{1,0:T(8,128)(2,1)} %get-tuple-element.43), kind=kOutput, calls=%fused_computation.21 | convolution fusion | flops 4297064448 | bytes 10485760 | tf_op jit(solution)/shard_map/dot_general | solution.py:40
  365.2 4.5 fusion.12
  369.8 7.9 add_convert_fusion
  377.8 12.8 %convolution_convert_fusion.1 = bf16[1024,2048]{1,0:T(8,128)(2,1)} fusion(bf16[2048,1024]{1,0:T(8,128)(2,1)S(1)} %copy-done.52, bf16[2048,2048]{1,0:T(8,128)(2,1)} %constant_dynamic-update-slice_fusion.17), kind=kOutput, calls=%fused_computation.19 | convolution fusion | flops 8592031744 | bytes 16777216 | tf_op jit(solution)/shard_map/dot_general | solution.py:40
  390.9 10.9 %fusion.15 = f32[1024,2048]{1,0:T(8,128)} fusion(bf16[2048,1024]{1,0:T(8,128)(2,1)} %all-gather.12.cloned.1.call-done, bf16[2048,1024]{1,0:T(8,128)(2,1)} %get-tuple-element.44), kind=kOutput, calls=%fused_computation.51 | convolution fusion | flops 4294967296 | bytes 14680064 | tf_op jit(solution)/shard_map/dot_general | solution.py:40
  401.8 6.3 convert_add_fusion.2
  411.1 11.2 %convert_add_fusion.1 = f32[1024,2048]{1,0:T(8,128)S(1)} fusion(bf16[1024,2048]{1,0:T(8,128)(2,1)} %collective-permute-done.31, f32[1024,2048]{1,0:T(8,128)} %fusion.15, bf16[2048,1024]{1,0:T(8,128)(2,1)} %all-gather.10.cloned.1.call-done, bf16[2048,1024]{1,0:T(8,128)(2,1)} %get-tuple-element.42), kind=kOutput, calls=%fused_computation.5 | convolution fusion | flops 4301258752 | bytes 27262976 | tf_op jit(solution)/shard_map/dot_general | solution.py:40
  426.9 8.8 %collective-permute-done.22 = bf16[2,256,1024]{2,1,0:T(8,128)(2,1)} collective-permute-done((bf16[2,256,1024]{2,1,0:T(8,128)(2,1)}, bf16[2,256,1024]{2,1,0:T(8,128)(2,1)}, u32[]{:S(2)}, u32[]{:S(2)}) %collective-permute-start.22) | collective-permute-done | bytes 1048608 | tf_op jit(solution)/shard_map/ppermute | solution.py:31
  439.1 18.4 %collective-permute-done.32 = bf16[2,256,1024]{2,1,0:T(8,128)(2,1)S(1)} collective-permute-done((bf16[2,256,1024]{2,1,0:T(8,128)(2,1)S(1)}, bf16[2,256,1024]{2,1,0:T(8,128)(2,1)S(1)}, u32[]{:S(2)}, u32[]{:S(2)}) %collective-permute-start.32) | collective-permute-done | bytes 1048608 | tf_op jit(solution)/shard_map/ppermute | solution.py:31
  459.6 13.5 %collective-permute-done.34 = bf16[2,256,1024]{2,1,0:T(8,128)(2,1)S(1)} collective-permute-done((bf16[2,256,1024]{2,1,0:T(8,128)(2,1)S(1)}, bf16[2,256,1024]{2,1,0:T(8,128)(2,1)S(1)}, u32[]{:S(2)}, u32[]{:S(2)}) %collective-permute-start.34) | collective-permute-done | bytes 1048608 | tf_op jit(solution)/shard_map/ppermute | solution.py:31
  473.4 11.0 %collective-permute-done.23 = bf16[256,1024]{1,0:T(8,128)(2,1)S(1)} collective-permute-done((bf16[256,1024]{1,0:T(8,128)(2,1)S(1)}, bf16[256,1024]{1,0:T(8,128)(2,1)S(1)}, u32[]{:S(2)}, u32[]{:S(2)}) %collective-permute-start.23) | collective-permute-done | bytes 524320 | tf_op jit(solution)/shard_map/ppermute | solution.py:31
  485.9 8.8 %collective-permute-done.33 = bf16[256,1024]{1,0:T(8,128)(2,1)S(1)} collective-permute-done((bf16[256,1024]{1,0:T(8,128)(2,1)S(1)}, bf16[256,1024]{1,0:T(8,128)(2,1)S(1)}, u32[]{:S(2)}, u32[]{:S(2)}) %collective-permute-start.33) | collective-permute-done | bytes 524320 | tf_op jit(solution)/shard_map/ppermute | solution.py:31
  494.7 2.6 fusion.37
  497.6 12.9 %convolution_convert_fusion.4 = bf16[2048,1024]{1,0:T(8,128)(2,1)} fusion(bf16[2048,2048]{1,0:T(8,128)(2,1)} %constant_dynamic-update-slice_fusion.10, bf16[2048,1024]{1,0:T(8,128)(2,1)S(1)} %copy-done.56), kind=kOutput, calls=%fused_computation.22 | convolution fusion | flops 8592031744 | bytes 16777216 | tf_op jit(solution)/shard_map/dot_general | solution.py:40
  522.0 10.2 %collective-permute-done.37 = bf16[128,2048]{1,0:T(8,128)(2,1)S(1)} collective-permute-done((bf16[128,2048]{1,0:T(8,128)(2,1)S(1)}, bf16[128,2048]{1,0:T(8,128)(2,1)S(1)}, u32[]{:S(2)}, u32[]{:S(2)}) %collective-permute-start.37) | collective-permute-done | bytes 524320 | tf_op jit(solution)/shard_map/ppermute | solution.py:31
  537.1 18.8 %collective-permute-done.38 = bf16[256,2048]{1,0:T(8,128)(2,1)S(1)} collective-permute-done((bf16[256,2048]{1,0:T(8,128)(2,1)S(1)}, bf16[256,2048]{1,0:T(8,128)(2,1)S(1)}, u32[]{:S(2)}, u32[]{:S(2)}) %collective-permute-start.38) | collective-permute-done | bytes 1048608 | tf_op jit(solution)/shard_map/ppermute | solution.py:31
  560.8 12.7 %convolution_convert_fusion.5 = bf16[2048,1024]{1,0:T(8,128)(2,1)} fusion(bf16[2048,2048]{1,0:T(8,128)(2,1)} %constant_dynamic-update-slice_fusion.10, bf16[2048,1024]{1,0:T(8,128)(2,1)S(1)} %copy-done.54), kind=kOutput, calls=%fused_computation.23 | convolution fusion | flops 8592031744 | bytes 16777216 | tf_op jit(solution)/shard_map/dot_general | solution.py:40
  579.5 4.9 constant_dynamic-update-slice_fusion.24
  584.4 5.8 convolution_convert_fusion.8.upstream
  590.2 40.3 %attend_back.1 = (bf16[256,2048]{1,0:T(8,128)(2,1)S(1)}, f32[128,2048]{1,0:T(8,128)S(1)}, bf16[128,512]{1,0:T(8,128)(2,1)S(1)}) custom-call(s32[3]{0:T(128)S(1)} %pad_add_fusion.info, bf16[384,2048]{1,0:T(8,128)(2,1)S(1)} %rope.1.qkv, bf16[128,512]{1,0:T(8,128)(2,1)S(1)} %collective-permute-done.6.halo, ...), custom_call_target="tpu_custom_call" | custom-call | flops 53687091200 | bytes 5570560 | tf_op jit(solution)/shard_map/attend_back/pallas_call | solution.py:305
  630.5 6.4 collective-permute-start.41
  636.9 6.6 collective-permute-done.41.halo
  644.2 4.3 convolution_convert_fusion
  648.6 6.8 convolution_convert_fusion.7
  656.3 22.3 %pmax.7 = f32[8]{0:T(128)S(1)} all-reduce(f32[8]{0:T(128)S(1)} %broadcast_select_fusion), channel_id=1, replica_groups=mesh['z'=4,'y'=2,'x'=2,'c'=2] {'z','y'}, use_global_device_ids=true, to_apply=%region_12.13 | all-reduce | flops 8 | bytes 64 | tf_op jit(solution)/shard_map/pmax | solution.py:476
  680.0 9.4 %convolution_convert_fusion.6 = bf16[2048,384]{1,0:T(8,128)(2,1)} fusion(bf16[2048,2048]{1,0:T(8,128)(2,1)} %constant_dynamic-update-slice_fusion.3, bf16[128,2048]{1,0:T(8,128)(2,1)S(1)} %finish.1, bf16[256,2048]{1,0:T(8,128)(2,1)S(1)} %copy-done.7), kind=kOutput, calls=%fused_computation.24 | convolution fusion | flops 3225157632 | bytes 11534336 | tf_op jit(solution)/shard_map/dot_general | solution.py:40
  695.6 5.1 convert_add_fusion
  700.7 3.3 copy-done.8
  708.3 2.9 fusion.56
  715.1 2.7 collective-permute-done.50
  717.8 2.9 fusion.55
  721.7 4.9 collective-permute-done.43
  732.0 2.8 fusion.54
  734.8 19.4 %collective-permute-done.48 = bf16[256,256]{1,0:T(8,128)(2,1)S(1)} collective-permute-done((bf16[256,256]{1,0:T(8,128)(2,1)S(1)}, bf16[256,256]{1,0:T(8,128)(2,1)S(1)}, u32[]{:S(2)}, u32[]{:S(2)}) %collective-permute-start.48) | collective-permute-done | bytes 131104 | tf_op jit(solution)/shard_map/ppermute | solution.py:31
  757.4 5.6 collective-permute-done.44
  769.1 5.1 collective-permute-done.46
  776.6 37.2 %all-reduce.2 = f32[32,2,64]{2,1,0:T(2,128)S(1)} all-reduce(f32[32,2,64]{2,1,0:T(2,128)S(1)} %maximum_bitcast_fusion), channel_id=2, replica_groups=mesh['z'=4,'y'=2,'x'=2,'c'=2] {'z','y','x','c'}, use_global_device_ids=true, to_apply=%region_6.7.clone | all-reduce | flops 4096 | bytes 32768
  814.4 3.5 fusion.10
  (365 shorter events, 179.1 us)
Async XLA Ops:
  7.2 91.4 %all-gather.6.cloned.1.call-start = ((), (), s32[]{:S(2)}) async-start(), calls=%async_computation.5 | async-start | bytes 1966080 | tf_op jit(solution)/shard_map/all_gather | solution.py:355
  10.4 7.9 collective-permute-start
  19.4 126.1 %all-gather.8.cloned.1.call-start = ((), (), s32[]{:S(2)}) async-start(), calls=%async_computation.6 | async-start | bytes 1310720 | tf_op jit(solution)/shard_map/all_gather | solution.py:356
  20.4 7.1 collective-permute-start.7
  27.2 12.5 %collective-permute-start.2 = (bf16[128,2048]{1,0:T(8,128)(2,1)S(1)}, bf16[128,2048]{1,0:T(8,128)(2,1)S(1)}, u32[]{:S(2)}, u32[]{:S(2)}) collective-permute-start(bf16[128,2048]{1,0:T(8,128)(2,1)S(1)} %get-tuple-element.80), channel_id=1, source_target_pairs={{0,4},{4,0},{1,5},{5,1},{2,6},{6,2},{3,7},{7,3},{8,12},{12,8},{9,1... | collective-permute-start | bytes 1572872 | tf_op jit(solution)/shard_map/ppermute | solution.py:31
  28.4 268.5 %all-gather.14.cloned.1.call-start = ((), (), s32[]{:S(2)}) async-start(), calls=%async_computation.9 | async-start | bytes 5242880 | tf_op jit(solution)/shard_map/all_gather | solution.py:357
  28.4 15.7 %collective-permute-start.1 = (bf16[128,2048]{1,0:T(8,128)(2,1)}, bf16[128,2048]{1,0:T(8,128)(2,1)S(1)}, u32[]{:S(2)}, u32[]{:S(2)}) collective-permute-start(bf16[128,2048]{1,0:T(8,128)(2,1)} %get-tuple-element.81), channel_id=1, source_target_pairs={{0,2},{2,0},{1,3},{3,1},{4,6},{6,4},{5,7},{7,5},{8,10},{10,8},{9,1... | collective-permute-start | bytes 1572872 | tf_op jit(solution)/shard_map/ppermute | solution.py:31
  40.8 23.1 %collective-permute-start.3 = (bf16[256,2048]{1,0:T(8,128)(2,1)}, bf16[256,2048]{1,0:T(8,128)(2,1)S(1)}, u32[]{:S(2)}, u32[]{:S(2)}) collective-permute-start(bf16[256,2048]{1,0:T(8,128)(2,1)} %pad_maximum_fusion.4), channel_id=1, source_target_pairs={{0,2},{2,0},{1,3},{3,1},{4,6},{6,4},{5,7},{7,5},{8,10},{10,8},{9,1... | collective-permute-start | bytes 3145736 | tf_op jit(solution)/shard_map/ppermute | solution.py:31
  43.6 14.9 %collective-permute-start.20 = (bf16[1024,256]{1,0:T(8,128)(2,1)S(1)}, bf16[1024,256]{1,0:T(8,128)(2,1)S(1)}, u32[]{:S(2)}, u32[]{:S(2)}) collective-permute-start(bf16[1024,256]{1,0:T(8,128)(2,1)S(1)} %get-tuple-element.77), channel_id=1, source_target_pairs={{0,4},{4,0},{1,5},{5,1},{2,6},{6,2},{3,7},{7,3},{8,12},{12,8},{9,1... | collective-permute-start | bytes 1572872 | tf_op jit(solution)/shard_map/ppermute | solution.py:31
  46.3 31.3 %collective-permute-start.4 = (bf16[256,2048]{1,0:T(8,128)(2,1)}, bf16[256,2048]{1,0:T(8,128)(2,1)}, u32[]{:S(2)}, u32[]{:S(2)}) collective-permute-start(bf16[256,2048]{1,0:T(8,128)(2,1)} %pad_maximum_fusion.5), channel_id=1, source_target_pairs={{0,4},{4,0},{1,5},{5,1},{2,6},{6,2},{3,7},{7,3},{8,12},{12,8},{9,1... | collective-permute-start | bytes 3145736 | tf_op jit(solution)/shard_map/ppermute | solution.py:31
  59.8 260.0 %all-gather.12.cloned.1.call-start = ((), (), s32[]{:S(2)}) async-start(), calls=%async_computation.8 | async-start | bytes 5242880 | tf_op jit(solution)/shard_map/all_gather | solution.py:359
  83.4 10.1 %collective-permute-start.5 = (bf16[1024,2048]{1,0:T(8,128)(2,1)}, bf16[1024,2048]{1,0:T(8,128)(2,1)}, u32[]{:S(2)}, u32[]{:S(2)}) collective-permute-start(bf16[1024,2048]{1,0:T(8,128)(2,1)} %get-tuple-element.78), channel_id=1, source_target_pairs={{0,1},{1,0},{2,3},{3,2},{4,5},{5,4},{6,7},{7,6},{8,9},{9,8},{10,11... | collective-permute-start | bytes 12582920 | tf_op jit(solution)/shard_map/ppermute | solution.py:31
  84.3 23.3 %collective-permute-start.19 = (bf16[256,1024]{1,0:T(8,128)(2,1)}, bf16[256,1024]{1,0:T(8,128)(2,1)S(1)}, u32[]{:S(2)}, u32[]{:S(2)}) collective-permute-start(bf16[256,1024]{1,0:T(8,128)(2,1)} %get-tuple-element.71), channel_id=1, source_target_pairs={{0,4},{4,0},{1,5},{5,1},{2,6},{6,2},{3,7},{7,3},{8,12},{12,8},{9,1... | collective-permute-start | bytes 1572872 | tf_op jit(solution)/shard_map/ppermute | solution.py:31
  106.0 10.8 %collective-permute-start.6 = (bf16[128,512]{1,0:T(8,128)(2,1)S(1)}, bf16[128,512]{1,0:T(8,128)(2,1)S(1)}, u32[]{:S(2)}, u32[]{:S(2)}) collective-permute-start(bf16[128,512]{1,0:T(8,128)(2,1)S(1)} %slice.384), channel_id=1, source_target_pairs={{0,8},{8,16},{16,24},{24,0},{1,9},{9,17},{17,25},{25,1},{2,10},{10... | collective-permute-start | bytes 393224 | tf_op jit(solution)/shard_map/ppermute | solution.py:36
  109.1 225.2 %all-gather.10.cloned.1.call-start = ((), (), s32[]{:S(2)}) async-start(), calls=%async_computation.7 | async-start | bytes 5242880 | tf_op jit(solution)/shard_map/all_gather | solution.py:358
  150.5 46.1 %collective-permute-start.8 = (bf16[1024,2048]{1,0:T(8,128)(2,1)}, bf16[1024,2048]{1,0:T(8,128)(2,1)}, u32[]{:S(2)}, u32[]{:S(2)}) collective-permute-start(bf16[1024,2048]{1,0:T(8,128)(2,1)} %convolution_convert_fusion.2), channel_id=1, source_target_pairs={{0,1},{1,0},{2,3},{3,2},{4,5},{5,4},{6,7},{7,6},{8,9},{9,8},{10,11... | collective-permute-start | bytes 12582920 | tf_op jit(solution)/shard_map/ppermute | solution.py:31
  151.9 99.4 %copy-start.38 = (f32[256]{0:T(256)}, f32[256]{0:T(256)S(1)}, u32[]{:S(2)}) copy-start(f32[256]{0:T(256)S(1)} %select_select_fusion) | copy-start | bytes 3076
  154.4 14.8 %collective-permute-start.27 = (bf16[128,2048]{1,0:T(8,128)(2,1)S(1)}, bf16[128,2048]{1,0:T(8,128)(2,1)S(1)}, u32[]{:S(2)}, u32[]{:S(2)}) collective-permute-start(bf16[128,2048]{1,0:T(8,128)(2,1)S(1)} %get-tuple-element.66), channel_id=1, source_target_pairs={{0,4},{4,0},{1,5},{5,1},{2,6},{6,2},{3,7},{7,3},{8,12},{12,8},{9,1... | collective-permute-start | bytes 1572872 | tf_op jit(solution)/shard_map/ppermute | solution.py:31
  156.0 15.2 %collective-permute-start.26 = (bf16[128,2048]{1,0:T(8,128)(2,1)S(1)}, bf16[128,2048]{1,0:T(8,128)(2,1)S(1)}, u32[]{:S(2)}, u32[]{:S(2)}) collective-permute-start(bf16[128,2048]{1,0:T(8,128)(2,1)S(1)} %get-tuple-element.67), channel_id=1, source_target_pairs={{0,2},{2,0},{1,3},{3,1},{4,6},{6,4},{5,7},{7,5},{8,10},{10,8},{9,1... | collective-permute-start | bytes 1572872 | tf_op jit(solution)/shard_map/ppermute | solution.py:31
  156.7 23.8 %collective-permute-start.18 = (bf16[256,1024]{1,0:T(8,128)(2,1)S(1)}, bf16[256,1024]{1,0:T(8,128)(2,1)S(1)}, u32[]{:S(2)}, u32[]{:S(2)}) collective-permute-start(bf16[256,1024]{1,0:T(8,128)(2,1)S(1)} %get-tuple-element.69), channel_id=1, source_target_pairs={{0,4},{4,0},{1,5},{5,1},{2,6},{6,2},{3,7},{7,3},{8,12},{12,8},{9,1... | collective-permute-start | bytes 1572872 | tf_op jit(solution)/shard_map/ppermute | solution.py:31
  158.7 93.7 %copy-start.36 = (f32[2048]{0:T(1024)}, f32[2048]{0:T(1024)S(1)}, u32[]{:S(2)}) copy-start(f32[2048]{0:T(1024)S(1)} %convert_element_type.267) | copy-start | bytes 24580
  170.3 31.5 %collective-permute-start.28 = (bf16[256,2048]{1,0:T(8,128)(2,1)}, bf16[256,2048]{1,0:T(8,128)(2,1)}, u32[]{:S(2)}, u32[]{:S(2)}) collective-permute-start(bf16[256,2048]{1,0:T(8,128)(2,1)} %pad_maximum_fusion.8), channel_id=1, source_target_pairs={{0,2},{2,0},{1,3},{3,1},{4,6},{6,4},{5,7},{7,5},{8,10},{10,8},{9,1... | collective-permute-start | bytes 3145736 | tf_op jit(solution)/shard_map/ppermute | solution.py:31
  173.0 31.2 %collective-permute-start.29 = (bf16[256,2048]{1,0:T(8,128)(2,1)}, bf16[256,2048]{1,0:T(8,128)(2,1)}, u32[]{:S(2)}, u32[]{:S(2)}) collective-permute-start(bf16[256,2048]{1,0:T(8,128)(2,1)} %pad_maximum_fusion.9), channel_id=1, source_target_pairs={{0,4},{4,0},{1,5},{5,1},{2,6},{6,2},{3,7},{7,3},{8,12},{12,8},{9,1... | collective-permute-start | bytes 3145736 | tf_op jit(solution)/shard_map/ppermute | solution.py:31
  182.0 508.2 %reduce-scatter.14.cloned.1.call-start = ((), (), s32[]{:S(2)}) async-start(), calls=%async_computation.14 | async-start | bytes 5242880 | tf_op jit(solution)/shard_map/reduce_scatter | solution.py:405
  200.7 24.6 %collective-permute-start.9 = (bf16[2,256,1024]{2,1,0:T(8,128)(2,1)S(1)}, bf16[2,256,1024]{2,1,0:T(8,128)(2,1)S(1)}, u32[]{:S(2)}, u32[]{:S(2)}) collective-permute-start(bf16[2,256,1024]{2,1,0:T(8,128)(2,1)S(1)} %slice_bitcast_fusion.38), channel_id=1, source_target_pairs={{0,2},{2,0},{1,3},{3,1},{4,6},{6,4},{5,7},{7,5},{8,10},{10,8},{9,1... | collective-permute-start | bytes 3145736 | tf_op jit(solution)/shard_map/ppermute | solution.py:31
  203.0 25.5 %collective-permute-start.11 = (bf16[2,256,1024]{2,1,0:T(8,128)(2,1)S(1)}, bf16[2,256,1024]{2,1,0:T(8,128)(2,1)S(1)}, u32[]{:S(2)}, u32[]{:S(2)}) collective-permute-start(bf16[2,256,1024]{2,1,0:T(8,128)(2,1)S(1)} %slice_bitcast_fusion.33), channel_id=1, source_target_pairs={{0,4},{4,0},{1,5},{5,1},{2,6},{6,2},{3,7},{7,3},{8,12},{12,8},{9,1... | collective-permute-start | bytes 3145736 | tf_op jit(solution)/shard_map/ppermute | solution.py:31
  225.7 12.8 %collective-permute-start.10 = (bf16[256,1024]{1,0:T(8,128)(2,1)S(1)}, bf16[256,1024]{1,0:T(8,128)(2,1)S(1)}, u32[]{:S(2)}, u32[]{:S(2)}) collective-permute-start(bf16[256,1024]{1,0:T(8,128)(2,1)S(1)} %fusion.51), channel_id=1, source_target_pairs={{0,4},{4,0},{1,5},{5,1},{2,6},{6,2},{3,7},{7,3},{8,12},{12,8},{9,1... | collective-permute-start | bytes 1572872 | tf_op jit(solution)/shard_map/ppermute | solution.py:31
  239.0 11.9 %collective-permute-start.12 = (bf16[256,1024]{1,0:T(8,128)(2,1)S(1)}, bf16[256,1024]{1,0:T(8,128)(2,1)S(1)}, u32[]{:S(2)}, u32[]{:S(2)}) collective-permute-start(bf16[256,1024]{1,0:T(8,128)(2,1)S(1)} %get-tuple-element.52), channel_id=1, source_target_pairs={{0,2},{2,0},{1,3},{3,1},{4,6},{6,4},{5,7},{7,5},{8,10},{10,8},{9,1... | collective-permute-start | bytes 1572872 | tf_op jit(solution)/shard_map/ppermute | solution.py:31
  242.3 52.1 %collective-permute-start.30 = (bf16[1024,2048]{1,0:T(8,128)(2,1)S(1)}, bf16[1024,2048]{1,0:T(8,128)(2,1)S(1)}, u32[]{:S(2)}, u32[]{:S(2)}) collective-permute-start(bf16[1024,2048]{1,0:T(8,128)(2,1)S(1)} %get-tuple-element.64), channel_id=1, source_target_pairs={{0,1},{1,0},{2,3},{3,2},{4,5},{5,4},{6,7},{7,6},{8,9},{9,8},{10,11... | collective-permute-start | bytes 12582920 | tf_op jit(solution)/shard_map/ppermute | solution.py:31
  253.7 11.1 %collective-permute-start.14 = (bf16[128,2048]{1,0:T(8,128)(2,1)S(1)}, bf16[128,2048]{1,0:T(8,128)(2,1)S(1)}, u32[]{:S(2)}, u32[]{:S(2)}) collective-permute-start(bf16[128,2048]{1,0:T(8,128)(2,1)S(1)} %get-tuple-element.74), channel_id=1, source_target_pairs={{0,4},{4,0},{1,5},{5,1},{2,6},{6,2},{3,7},{7,3},{8,12},{12,8},{9,1... | collective-permute-start | bytes 1572872 | tf_op jit(solution)/shard_map/ppermute | solution.py:31
  256.1 13.9 %collective-permute-start.13 = (bf16[128,2048]{1,0:T(8,128)(2,1)S(1)}, bf16[128,2048]{1,0:T(8,128)(2,1)S(1)}, u32[]{:S(2)}, u32[]{:S(2)}) collective-permute-start(bf16[128,2048]{1,0:T(8,128)(2,1)S(1)} %get-tuple-element.75), channel_id=1, source_target_pairs={{0,2},{2,0},{1,3},{3,1},{4,6},{6,4},{5,7},{7,5},{8,10},{10,8},{9,1... | collective-permute-start | bytes 1572872 | tf_op jit(solution)/shard_map/ppermute | solution.py:31
  264.9 25.0 %collective-permute-start.15 = (bf16[256,2048]{1,0:T(8,128)(2,1)S(1)}, bf16[256,2048]{1,0:T(8,128)(2,1)S(1)}, u32[]{:S(2)}, u32[]{:S(2)}) collective-permute-start(bf16[256,2048]{1,0:T(8,128)(2,1)S(1)} %pad_maximum_fusion.6), channel_id=1, source_target_pairs={{0,2},{2,0},{1,3},{3,1},{4,6},{6,4},{5,7},{7,5},{8,10},{10,8},{9,1... | collective-permute-start | bytes 3145736 | tf_op jit(solution)/shard_map/ppermute | solution.py:31
  270.1 20.7 %collective-permute-start.16 = (bf16[256,2048]{1,0:T(8,128)(2,1)S(1)}, bf16[256,2048]{1,0:T(8,128)(2,1)S(1)}, u32[]{:S(2)}, u32[]{:S(2)}) collective-permute-start(bf16[256,2048]{1,0:T(8,128)(2,1)S(1)} %pad_maximum_fusion.7), channel_id=1, source_target_pairs={{0,4},{4,0},{1,5},{5,1},{2,6},{6,2},{3,7},{7,3},{8,12},{12,8},{9,1... | collective-permute-start | bytes 3145736 | tf_op jit(solution)/shard_map/ppermute | solution.py:31
  294.4 20.5 %collective-permute-start.17 = (bf16[1024,2048]{1,0:T(8,128)(2,1)}, bf16[1024,2048]{1,0:T(8,128)(2,1)}, u32[]{:S(2)}, u32[]{:S(2)}) collective-permute-start(bf16[1024,2048]{1,0:T(8,128)(2,1)} %get-tuple-element.72), channel_id=1, source_target_pairs={{0,1},{1,0},{2,3},{3,2},{4,5},{5,4},{6,7},{7,6},{8,9},{9,8},{10,11... | collective-permute-start | bytes 12582920 | tf_op jit(solution)/shard_map/ppermute | solution.py:31
  364.8 37.0 %collective-permute-start.21 = (bf16[1024,2048]{1,0:T(8,128)(2,1)}, bf16[1024,2048]{1,0:T(8,128)(2,1)}, u32[]{:S(2)}, u32[]{:S(2)}) collective-permute-start(bf16[1024,2048]{1,0:T(8,128)(2,1)} %convolution_convert_fusion.3), channel_id=1, source_target_pairs={{0,1},{1,0},{2,3},{3,2},{4,5},{5,4},{6,7},{7,6},{8,9},{9,8},{10,11... | collective-permute-start | bytes 12582920 | tf_op jit(solution)/shard_map/ppermute | solution.py:31
  377.7 33.5 %collective-permute-start.31 = (bf16[1024,2048]{1,0:T(8,128)(2,1)}, bf16[1024,2048]{1,0:T(8,128)(2,1)}, u32[]{:S(2)}, u32[]{:S(2)}) collective-permute-start(bf16[1024,2048]{1,0:T(8,128)(2,1)} %add_convert_fusion), channel_id=1, source_target_pairs={{0,1},{1,0},{2,3},{3,2},{4,5},{5,4},{6,7},{7,6},{8,9},{9,8},{10,11... | collective-permute-start | bytes 12582920 | tf_op jit(solution)/shard_map/ppermute | solution.py:31
  390.6 301.0 %reduce-scatter.12.cloned.1.call-start = ((), (), s32[]{:S(2)}) async-start(), calls=%async_computation.13 | async-start | bytes 5242880 | tf_op jit(solution)/shard_map/reduce_scatter | solution.py:405
  409.4 26.3 %collective-permute-start.22 = (bf16[2,256,1024]{2,1,0:T(8,128)(2,1)}, bf16[2,256,1024]{2,1,0:T(8,128)(2,1)}, u32[]{:S(2)}, u32[]{:S(2)}) collective-permute-start(bf16[2,256,1024]{2,1,0:T(8,128)(2,1)} %slice_bitcast_fusion.28), channel_id=1, source_target_pairs={{0,2},{2,0},{1,3},{3,1},{4,6},{6,4},{5,7},{7,5},{8,10},{10,8},{9,1... | collective-permute-start | bytes 3145736 | tf_op jit(solution)/shard_map/ppermute | solution.py:31
  422.5 35.0 %collective-permute-start.32 = (bf16[2,256,1024]{2,1,0:T(8,128)(2,1)S(1)}, bf16[2,256,1024]{2,1,0:T(8,128)(2,1)S(1)}, u32[]{:S(2)}, u32[]{:S(2)}) collective-permute-start(bf16[2,256,1024]{2,1,0:T(8,128)(2,1)S(1)} %slice_bitcast_fusion.18), channel_id=1, source_target_pairs={{0,2},{2,0},{1,3},{3,1},{4,6},{6,4},{5,7},{7,5},{8,10},{10,8},{9,1... | collective-permute-start | bytes 3145736 | tf_op jit(solution)/shard_map/ppermute | solution.py:31
  424.6 34.7 %collective-permute-start.24 = (bf16[2,256,1024]{2,1,0:T(8,128)(2,1)S(1)}, bf16[2,256,1024]{2,1,0:T(8,128)(2,1)S(1)}, u32[]{:S(2)}, u32[]{:S(2)}) collective-permute-start(bf16[2,256,1024]{2,1,0:T(8,128)(2,1)S(1)} %slice_bitcast_fusion.23), channel_id=1, source_target_pairs={{0,4},{4,0},{1,5},{5,1},{2,6},{6,2},{3,7},{7,3},{8,12},{12,8},{9,1... | collective-permute-start | bytes 3145736 | tf_op jit(solution)/shard_map/ppermute | solution.py:31
  426.2 47.0 %collective-permute-start.34 = (bf16[2,256,1024]{2,1,0:T(8,128)(2,1)S(1)}, bf16[2,256,1024]{2,1,0:T(8,128)(2,1)S(1)}, u32[]{:S(2)}, u32[]{:S(2)}) collective-permute-start(bf16[2,256,1024]{2,1,0:T(8,128)(2,1)S(1)} %slice_bitcast_fusion.13), channel_id=1, source_target_pairs={{0,4},{4,0},{1,5},{5,1},{2,6},{6,2},{3,7},{7,3},{8,12},{12,8},{9,1... | collective-permute-start | bytes 3145736 | tf_op jit(solution)/shard_map/ppermute | solution.py:31
  437.3 47.0 %collective-permute-start.23 = (bf16[256,1024]{1,0:T(8,128)(2,1)S(1)}, bf16[256,1024]{1,0:T(8,128)(2,1)S(1)}, u32[]{:S(2)}, u32[]{:S(2)}) collective-permute-start(bf16[256,1024]{1,0:T(8,128)(2,1)S(1)} %fusion.43), channel_id=1, source_target_pairs={{0,4},{4,0},{1,5},{5,1},{2,6},{6,2},{3,7},{7,3},{8,12},{12,8},{9,1... | collective-permute-start | bytes 1572872 | tf_op jit(solution)/shard_map/ppermute | solution.py:31
  457.9 36.8 %collective-permute-start.33 = (bf16[256,1024]{1,0:T(8,128)(2,1)S(1)}, bf16[256,1024]{1,0:T(8,128)(2,1)S(1)}, u32[]{:S(2)}, u32[]{:S(2)}) collective-permute-start(bf16[256,1024]{1,0:T(8,128)(2,1)S(1)} %fusion.35), channel_id=1, source_target_pairs={{0,4},{4,0},{1,5},{5,1},{2,6},{6,2},{3,7},{7,3},{8,12},{12,8},{9,1... | collective-permute-start | bytes 1572872 | tf_op jit(solution)/shard_map/ppermute | solution.py:31
  485.8 24.9 %collective-permute-start.25 = (bf16[256,1024]{1,0:T(8,128)(2,1)S(1)}, bf16[256,1024]{1,0:T(8,128)(2,1)}, u32[]{:S(2)}, u32[]{:S(2)}) collective-permute-start(bf16[256,1024]{1,0:T(8,128)(2,1)S(1)} %get-tuple-element.50), channel_id=1, source_target_pairs={{0,2},{2,0},{1,3},{3,1},{4,6},{6,4},{5,7},{7,5},{8,10},{10,8},{9,1... | collective-permute-start | bytes 1572872 | tf_op jit(solution)/shard_map/ppermute | solution.py:31
  497.3 15.4 %collective-permute-start.35 = (bf16[256,1024]{1,0:T(8,128)(2,1)}, bf16[256,1024]{1,0:T(8,128)(2,1)}, u32[]{:S(2)}, u32[]{:S(2)}) collective-permute-start(bf16[256,1024]{1,0:T(8,128)(2,1)} %get-tuple-element.48), channel_id=1, source_target_pairs={{0,2},{2,0},{1,3},{3,1},{4,6},{6,4},{5,7},{7,5},{8,10},{10,8},{9,1... | collective-permute-start | bytes 1572872 | tf_op jit(solution)/shard_map/ppermute | solution.py:31
  510.6 195.6 %reduce-scatter.10.cloned.1.call-start = ((), (), s32[]{:S(2)}) async-start(), calls=%async_computation.12 | async-start | bytes 5242880 | tf_op jit(solution)/shard_map/reduce_scatter | solution.py:405
  519.2 13.1 %collective-permute-start.37 = (bf16[128,2048]{1,0:T(8,128)(2,1)S(1)}, bf16[128,2048]{1,0:T(8,128)(2,1)S(1)}, u32[]{:S(2)}, u32[]{:S(2)}) collective-permute-start(bf16[128,2048]{1,0:T(8,128)(2,1)S(1)} %get-tuple-element.62), channel_id=1, source_target_pairs={{0,4},{4,0},{1,5},{5,1},{2,6},{6,2},{3,7},{7,3},{8,12},{12,8},{9,1... | collective-permute-start | bytes 1572872 | tf_op jit(solution)/shard_map/ppermute | solution.py:31
  520.5 13.6 %collective-permute-start.36 = (bf16[128,2048]{1,0:T(8,128)(2,1)S(1)}, bf16[128,2048]{1,0:T(8,128)(2,1)S(1)}, u32[]{:S(2)}, u32[]{:S(2)}) collective-permute-start(bf16[128,2048]{1,0:T(8,128)(2,1)S(1)} %get-tuple-element.63), channel_id=1, source_target_pairs={{0,2},{2,0},{1,3},{3,1},{4,6},{6,4},{5,7},{7,5},{8,10},{10,8},{9,1... | collective-permute-start | bytes 1572872 | tf_op jit(solution)/shard_map/ppermute | solution.py:31
  532.3 23.5 %collective-permute-start.38 = (bf16[256,2048]{1,0:T(8,128)(2,1)S(1)}, bf16[256,2048]{1,0:T(8,128)(2,1)S(1)}, u32[]{:S(2)}, u32[]{:S(2)}) collective-permute-start(bf16[256,2048]{1,0:T(8,128)(2,1)S(1)} %pad_maximum_fusion.10), channel_id=1, source_target_pairs={{0,2},{2,0},{1,3},{3,1},{4,6},{6,4},{5,7},{7,5},{8,10},{10,8},{9,1... | collective-permute-start | bytes 3145736 | tf_op jit(solution)/shard_map/ppermute | solution.py:31
  534.1 23.1 %collective-permute-start.39 = (bf16[256,2048]{1,0:T(8,128)(2,1)S(1)}, bf16[256,2048]{1,0:T(8,128)(2,1)S(1)}, u32[]{:S(2)}, u32[]{:S(2)}) collective-permute-start(bf16[256,2048]{1,0:T(8,128)(2,1)S(1)} %pad_maximum_fusion.11), channel_id=1, source_target_pairs={{0,4},{4,0},{1,5},{5,1},{2,6},{6,2},{3,7},{7,3},{8,12},{12,8},{9,1... | collective-permute-start | bytes 3145736 | tf_op jit(solution)/shard_map/ppermute | solution.py:31
  560.8 18.6 %collective-permute-start.40 = (bf16[1024,2048]{1,0:T(8,128)(2,1)}, bf16[1024,2048]{1,0:T(8,128)(2,1)}, u32[]{:S(2)}, u32[]{:S(2)}) collective-permute-start(bf16[1024,2048]{1,0:T(8,128)(2,1)} %get-tuple-element.60), channel_id=1, source_target_pairs={{0,1},{1,0},{2,3},{3,2},{4,5},{5,4},{6,7},{7,6},{8,9},{9,8},{10,11... | collective-permute-start | bytes 12582920 | tf_op jit(solution)/shard_map/ppermute | solution.py:31
  573.5 147.1 %reduce-scatter.8.cloned.1.call-start = ((), (), s32[]{:S(2)}) async-start(), calls=%async_computation.11 | async-start | bytes 1310720 | tf_op jit(solution)/shard_map/reduce_scatter | solution.py:405
  630.5 13.0 %collective-permute-start.41 = (bf16[128,512]{1,0:T(8,128)(2,1)S(1)}, bf16[128,512]{1,0:T(8,128)(2,1)S(1)}, u32[]{:S(2)}, u32[]{:S(2)}) collective-permute-start(bf16[128,512]{1,0:T(8,128)(2,1)S(1)} %get-tuple-element.23), channel_id=1, source_target_pairs={{0,24},{8,0},{16,8},{24,16},{1,25},{9,1},{17,9},{25,17},{2,26},{10... | collective-permute-start | bytes 393224 | tf_op jit(solution)/shard_map/ppermute | solution.py:36
  648.6 47.1 %collective-permute-start.42 = (bf16[1024,2048]{1,0:T(8,128)(2,1)}, bf16[1024,2048]{1,0:T(8,128)(2,1)}, u32[]{:S(2)}, u32[]{:S(2)}) collective-permute-start(bf16[1024,2048]{1,0:T(8,128)(2,1)} %convolution_convert_fusion), channel_id=1, source_target_pairs={{0,1},{1,0},{2,3},{3,2},{4,5},{5,4},{6,7},{7,6},{8,9},{9,8},{10,11... | collective-permute-start | bytes 12582920 | tf_op jit(solution)/shard_map/ppermute | solution.py:31
  655.4 99.6 %reduce-scatter.6.cloned.1.call-start = ((), (), s32[]{:S(2)}) async-start(), calls=%async_computation.10 | async-start | bytes 1966080 | tf_op jit(solution)/shard_map/reduce_scatter | solution.py:405
  691.5 16.8 %collective-permute-start.51 = (bf16[1024,256]{1,0:T(8,128)(2,1)S(1)}, bf16[1024,256]{1,0:T(8,128)(2,1)}, u32[]{:S(2)}, u32[]{:S(2)}) collective-permute-start(bf16[1024,256]{1,0:T(8,128)(2,1)S(1)} %get-tuple-element.55), channel_id=1, source_target_pairs={{0,4},{4,0},{1,5},{5,1},{2,6},{6,2},{3,7},{7,3},{8,12},{12,8},{9,1... | collective-permute-start | bytes 1572872 | tf_op jit(solution)/shard_map/ppermute | solution.py:31
  693.7 24.1 %collective-permute-start.50 = (bf16[256,1024]{1,0:T(8,128)(2,1)}, bf16[256,1024]{1,0:T(8,128)(2,1)}, u32[]{:S(2)}, u32[]{:S(2)}) collective-permute-start(bf16[256,1024]{1,0:T(8,128)(2,1)} %get-tuple-element.57), channel_id=1, source_target_pairs={{0,4},{4,0},{1,5},{5,1},{2,6},{6,2},{3,7},{7,3},{8,12},{12,8},{9,1... | collective-permute-start | bytes 1572872 | tf_op jit(solution)/shard_map/ppermute | solution.py:31
  705.2 21.4 %collective-permute-start.43 = (bf16[2,256,1024]{2,1,0:T(8,128)(2,1)}, bf16[2,256,1024]{2,1,0:T(8,128)(2,1)}, u32[]{:S(2)}, u32[]{:S(2)}) collective-permute-start(bf16[2,256,1024]{2,1,0:T(8,128)(2,1)} %slice_bitcast_fusion.8), channel_id=1, source_target_pairs={{0,2},{2,0},{1,3},{3,1},{4,6},{6,4},{5,7},{7,5},{8,10},{10,8},{9,1... | collective-permute-start | bytes 3145736 | tf_op jit(solution)/shard_map/ppermute | solution.py:31
  708.3 23.7 %collective-permute-start.49 = (bf16[256,1024]{1,0:T(8,128)(2,1)}, bf16[256,1024]{1,0:T(8,128)(2,1)}, u32[]{:S(2)}, u32[]{:S(2)}) collective-permute-start(bf16[256,1024]{1,0:T(8,128)(2,1)} %get-tuple-element.59), channel_id=1, source_target_pairs={{0,4},{4,0},{1,5},{5,1},{2,6},{6,2},{3,7},{7,3},{8,12},{12,8},{9,1... | collective-permute-start | bytes 1572872 | tf_op jit(solution)/shard_map/ppermute | solution.py:31
  713.0 44.2 %collective-permute-start.45 = (bf16[2,256,1024]{2,1,0:T(8,128)(2,1)S(1)}, bf16[2,256,1024]{2,1,0:T(8,128)(2,1)S(1)}, u32[]{:S(2)}, u32[]{:S(2)}) collective-permute-start(bf16[2,256,1024]{2,1,0:T(8,128)(2,1)S(1)} %slice_bitcast_fusion.3), channel_id=1, source_target_pairs={{0,4},{4,0},{1,5},{5,1},{2,6},{6,2},{3,7},{7,3},{8,12},{12,8},{9,1... | collective-permute-start | bytes 3145736 | tf_op jit(solution)/shard_map/ppermute | solution.py:31
  721.7 32.5 %collective-permute-start.48 = (bf16[256,256]{1,0:T(8,128)(2,1)S(1)}, bf16[256,256]{1,0:T(8,128)(2,1)S(1)}, u32[]{:S(2)}, u32[]{:S(2)}) collective-permute-start(bf16[256,256]{1,0:T(8,128)(2,1)S(1)} %get-tuple-element.93), channel_id=1, source_target_pairs={{0,4},{4,0},{1,5},{5,1},{2,6},{6,2},{3,7},{7,3},{8,12},{12,8},{9,1... | collective-permute-start | bytes 393224 | tf_op jit(solution)/shard_map/ppermute | solution.py:31
  731.6 31.4 %collective-permute-start.44 = (bf16[256,1024]{1,0:T(8,128)(2,1)}, bf16[256,1024]{1,0:T(8,128)(2,1)S(1)}, u32[]{:S(2)}, u32[]{:S(2)}) collective-permute-start(bf16[256,1024]{1,0:T(8,128)(2,1)} %fusion.27), channel_id=1, source_target_pairs={{0,4},{4,0},{1,5},{5,1},{2,6},{6,2},{3,7},{7,3},{8,12},{12,8},{9,1... | collective-permute-start | bytes 1572872 | tf_op jit(solution)/shard_map/ppermute | solution.py:31
  756.2 11.1 %collective-permute-start.47 = (bf16[256,384]{1,0:T(8,128)(2,1)S(1)}, bf16[256,384]{1,0:T(8,128)(2,1)S(1)}, u32[]{:S(2)}, u32[]{:S(2)}) collective-permute-start(bf16[256,384]{1,0:T(8,128)(2,1)S(1)} %constant_dynamic-slice_fusion.9), channel_id=1, source_target_pairs={{0,4},{4,0},{1,5},{5,1},{2,6},{6,2},{3,7},{7,3},{8,12},{12,8},{9,1... | collective-permute-start | bytes 589832 | tf_op jit(solution)/shard_map/ppermute | solution.py:31
  765.0 9.2 %collective-permute-start.46 = (bf16[256,1024]{1,0:T(8,128)(2,1)S(1)}, bf16[256,1024]{1,0:T(8,128)(2,1)S(1)}, u32[]{:S(2)}, u32[]{:S(2)}) collective-permute-start(bf16[256,1024]{1,0:T(8,128)(2,1)S(1)} %get-tuple-element.46), channel_id=1, source_target_pairs={{0,2},{2,0},{1,3},{3,1},{4,6},{6,4},{5,7},{7,5},{8,10},{10,8},{9,1... | collective-permute-start | bytes 1572872 | tf_op jit(solution)/shard_map/ppermute | solution.py:31
  (55 other events, 797.2 us)
Sparse Core Ops, SparseCore 0:
  19.5 38.5 all-gather.5
  60.2 26.8 all-gather.7
  89.2 83.0 all-gather.13
  174.3 79.2 all-gather.11
  255.0 79.2 all-gather.9
  390.7 79.1 reduce-scatter.13
  510.7 79.0 reduce-scatter.11
  592.1 80.3 reduce-scatter.9
  675.4 27.6 reduce-scatter.7
  705.3 33.9 reduce-scatter.5

commit v2 on v1

--- a/solution.py
+++ b/solution.py
@@ -1,6 +1,5 @@
 import jax
 import jax.numpy as jnp
-import numpy as np
 from jax import lax
 from jax.experimental import pallas as pl
 from jax.experimental.pallas import tpu as pltpu
@@ -27,6 +26,10 @@
 BF16 = jnp.bfloat16
 
 
+def rounded(x):
+    return lax.reduce_precision(x, exponent_bits=8, mantissa_bits=7)
+
+
 def swap(x, axis):
     return lax.ppermute(x, axis, [(0, 1), (1, 0)])
 
@@ -55,31 +58,73 @@
     )
 
 
-def gather_rows(v):
+def after(x, *others):
+    return lax.optimization_barrier((x, *others))[0]
+
+
+def tie(*xs):
+    return lax.optimization_barrier(xs)
+
+
+def gather_one(v):
     half = v.shape[0] // 2
-    a00, b00 = v[:half], v[half:]
-    a01 = swap(a00, "x")
-    b10 = swap(b00, "y")
-    a1 = swap(jnp.concatenate((a00, a01)), "y")
-    b1 = swap(jnp.concatenate((b00, b10)), "x")
-    own = jnp.concatenate((v, a01, b1[:half], a1[:half], b10, a1[half:], b1[half:]))
-    return jnp.concatenate((own, swap(own, "c")))
-
-
-def scatter_rows(low, high):
-    sent = swap(high().astype(BF16), "c")
-    total = low() + sent.astype(F32)
-    rows = total.shape[0] // 4
-    cols = total.shape[1] // 2
+    return v, swap(v, "c"), swap(v[:half], "x"), swap(v[half:], "y")
+
+
+def gather_two(state):
+    v, near, a01, b10 = state
+    half = v.shape[0] // 2
+    a1 = swap(jnp.concatenate((v[:half], a01)), "y")
+    b1 = swap(jnp.concatenate((v[half:], b10)), "x")
+    second = swap(jnp.concatenate((a01, b10)), "c")
+    return v, near, a01, b10, second, a1, b1
+
+
+def gather_three(state):
+    v, near, a01, b10, second, a1, b1 = state
+    half = v.shape[0] // 2
+    third = swap(jnp.concatenate((a1, b1)), "c")
+
+    def block(own, one, two):
+        return (own, one[:half], two[2 * half : 3 * half], two[:half], one[half:],
+                two[half : 2 * half], two[3 * half :])
+
+    own = (v, a01, b1[:half], a1[:half], b10, a1[half:], b1[half:])
+    return jnp.concatenate(own + block(near, second, third))
+
+
+def fold_rows(low, high):
+    return low() + swap(high().astype(BF16), "c").astype(F32)
+
+
+def spread_one(total):
+    rows, cols = total.shape[0] // 4, total.shape[1] // 2
     blocks = total.reshape(2, 2, rows, 2 * cols)
     left, right = blocks[..., :cols], blocks[..., cols:]
-    left_x = swap(left[:, 1].astype(BF16), "x").astype(F32)
-    right_y = swap(right[1].astype(BF16), "y").astype(F32)
-    left_y = swap((left[1, 0] + left_x[1]).astype(BF16), "y").astype(F32)
-    right_x = swap((right[0, 1] + right_y[1]).astype(BF16), "x").astype(F32)
-    return jnp.concatenate(
-        (left[0, 0] + left_x[0] + left_y, right[0, 0] + right_y[0] + right_x), axis=1
-    )
+    send_x, send_y = left[:, 1].astype(BF16), right[1].astype(BF16)
+    return left[:, 0], right[0], swap(send_x, "x"), swap(send_y, "y"), (send_x, send_y)
+
+
+def spread_two(state):
+    left, right, left_x, right_y = state[:4]
+    left = left + left_x.astype(F32)
+    right = right + right_y.astype(F32)
+    send_y, send_x = left[1].astype(BF16), right[1].astype(BF16)
+    return left[0], right[0], swap(send_y, "y"), swap(send_x, "x"), (send_x, send_y)
+
+
+def spread_three(state):
+    left, right, left_y, right_x = state[:4]
+    return jnp.concatenate((left + left_y.astype(F32), right + right_x.astype(F32)), axis=1)
+
+
+def over_z(x, combine):
+    peers, step = lax.axis_size("z"), 1
+    assert peers & (peers - 1) == 0
+    while step < peers:
+        x = combine(x, along(x, step))
+        step *= 2
+    return x
 
 
 def place_of(block, rank):
@@ -298,9 +343,7 @@
         out[pl.ds(HD, HD), target] = rest.astype(BF16)
 
 
-def call(kernel, info, args, outs, scratch, flops, name):
-    moved = sum(a.size * a.dtype.itemsize for a in args)
-    moved += sum(int(np.prod(s)) * np.dtype(d).itemsize for s, d in outs)
+def call(kernel, info, args, outs, scratch, name):
     spec = pl.BlockSpec(memory_space=pltpu.VMEM)
     return pl.pallas_call(
         kernel,
@@ -309,7 +352,7 @@
         out_specs=[spec] * len(outs),
         scratch_shapes=[pltpu.VMEM(s, d) for s, d in scratch],
         compiler_params=pltpu.CompilerParams(vmem_limit_bytes=40 * 2**20),
-        cost_estimate=pl.CostEstimate(flops=flops, bytes_accessed=moved, transcendentals=0),
+        cost_estimate=pl.CostEstimate(flops=0, bytes_accessed=0, transcendentals=0),
         name=name,
     )(info, *args)
 
@@ -339,124 +382,185 @@
     freq = THETA ** (-(jnp.arange(HALF, dtype=F32) * 2.0 / HD))
     angles = spots[None, :] * freq[:, None]
     cos, sin = jnp.cos(angles), jnp.sin(angles)
-    q_half = w_query.shape[1] // 2
-
     def heads_part(which):
         return jnp.concatenate(
-            (half_of(w_query, which, 1), half_of(w_key, which, 1), half_of(w_value, which, 1)), 1
+            (half_of(w_query, which, 1), half_of(w_key, which, 1), half_of(w_value, which, 1),
+             half_of(w_out, which, 0).T), 1
         )
 
     other_y = 1 - y_rank
-    qkv_part = ordered(heads_part(y_rank), swap(heads_part(other_y), "y"), y_rank, 0)
-    out_part = ordered(half_of(w_out, y_rank, 0), swap(half_of(w_out, other_y, 0), "y"), y_rank, 1)
-    down_part = ordered(half_of(w_down, y_rank, 0), swap(half_of(w_down, other_y, 0), "y"), y_rank, 1)
-    gate_part = ordered(half_of(w_gate, y_rank, 1), swap(half_of(w_gate, other_y, 1), "y"), y_rank, 0)
-    up_part = ordered(half_of(w_up, y_rank, 1), swap(half_of(w_up, other_y, 1), "y"), y_rank, 0)
-    full_qkv = lax.all_gather(qkv_part, "z", axis=0, tiled=True)
-    full_out = lax.all_gather(out_part, "z", axis=1, tiled=True)
-    full_down = lax.all_gather(down_part, "z", axis=1, tiled=True)
-    full_gate = lax.all_gather(gate_part, "z", axis=0, tiled=True)
-    full_up = lax.all_gather(up_part, "z", axis=0, tiled=True)
+    heads_w = ordered(heads_part(y_rank), swap(heads_part(other_y), "y"), y_rank, 0)
+    full_heads = lax.all_gather(heads_w, "z", axis=0, tiled=True)
+    qkv_cols = V_AT + HD
 
     layer_f = layer_in.astype(F32)
     scale_one = lax.rsqrt(jnp.mean(layer_f * layer_f, axis=1, keepdims=True) + EPSILON)
-    normal_one = (layer_f * scale_one).astype(BF16)
+    normal_one = rounded(layer_f * scale_one)
     gain_one = attn_gain.astype(F32)
-    acts_one = gather_rows((normal_one.astype(F32) * gain_one[None, :]).astype(BF16))
+    acts = gather_one(after((normal_one * gain_one[None, :]).astype(BF16), heads_w))
+    acts = gather_two(acts)
+    gate_other = swap(after(half_of(w_gate, other_y, 1), acts[2], acts[3]), "y")
+    full_heads, *got = tie(full_heads, *acts[5:], gate_other)
+    gate_other = got[2]
+    full_qkv, full_out = full_heads[:, :qkv_cols], full_heads[:, qkv_cols:]
+    acts_one = gather_three((*acts[:5], *got[:2]))
+    gate_w = ordered(half_of(w_gate, y_rank, 1), gate_other, y_rank, 0)
+    full_gate = lax.all_gather(gate_w, "z", axis=0, tiled=True)
+    up_other = swap(after(half_of(w_up, other_y, 1), gate_w), "y")
+
     grad_out = cotangent.astype(F32)
-    down_rows = gather_rows((RESIDUAL * own_mask * grad_out).astype(BF16))
-
+    down_in = (RESIDUAL * own_mask * grad_out).astype(BF16)
+    back_rows = gather_one(after(down_in, gate_w))
     rows = acts_one.shape[0]
     half_rows = rows // 2
     flat = dot(full_qkv, acts_one, 0, 1)
     (qkv,) = call(
-        rope_kernel, info, (flat, cos, sin), [((flat.shape[0], rows), BF16)], [],
-        4 * flat.size, "rope",
+        rope_kernel, info, (flat, cos, sin), [((flat.shape[0], rows), BF16)], [], "rope"
     )
     halo = along(qkv[K_AT:, SLOT_LEN - LEAD :], 1)
-    work = 2 * HEADS * HD * 10 * CHUNK * CHUNK * 4
+    qkv, halo, up_other, *back_rows = tie(qkv, halo, up_other, *back_rows)
+    up_w = ordered(half_of(w_up, y_rank, 1), up_other, y_rank, 0)
+    full_up = lax.all_gather(up_w, "z", axis=0, tiled=True)
+    back_rows = gather_two(back_rows)
+    down_other = swap(after(half_of(w_down, other_y, 0), back_rows[2], back_rows[3]), "y")
     heads, lse, peak = call(
         attend_kernel, info, (qkv, halo),
         [((HEADS * HD, rows), BF16), ((8, rows), F32), ((8, 128), F32)],
         [((KEYS, HD), BF16), ((HD, KEYS), BF16), ((SLOT_LEN, CHUNK), F32)],
-        4 * work, "attend",
-    )
-    branch_one = scatter_rows(
-        lambda: dot(heads[:, :half_rows], full_out, 0, 0),
-        lambda: dot(heads[:, half_rows:], full_out, 0, 0),
-    )
+        "attend",
+    )
+    heads, down_other, up_w, *back_rows = tie(heads, down_other, up_w, *back_rows)
+    down_w = ordered(half_of(w_down, y_rank, 0), down_other, y_rank, 1)
+    full_down = lax.all_gather(down_w, "z", axis=1, tiled=True)
+
+    branch = fold_rows(
+        lambda: dot(heads[:, :half_rows], full_out, 0, 1),
+        lambda: dot(heads[:, half_rows:], full_out, 0, 1),
+    )
+    branch = spread_one(branch)
+    down_rows = gather_three((*back_rows[:5], *after((back_rows[5], back_rows[6]), branch[4])))
+    *got, down_rows, full_gate = tie(*branch[2:4], down_rows, full_gate)
+    branch = spread_two((*branch[:2], *got))
+    branch_one = spread_three(branch)
     resid = layer_f + RESIDUAL * own_mask * branch_one
     scale_two = lax.rsqrt(jnp.mean(resid * resid, axis=1, keepdims=True) + EPSILON)
-    normal_two = (resid * scale_two).astype(BF16)
+    normal_two = rounded(resid * scale_two)
     gain_two = mlp_gain.astype(F32)
-    acts_two = gather_rows((normal_two.astype(F32) * gain_two[None, :]).astype(BF16))
-
-    hidden_grad = dot(down_rows, full_down, 1, 1)
+    acts = gather_two(gather_one((normal_two * gain_two[None, :]).astype(BF16)))
+    acts_two = gather_three((*acts[:5], *after((acts[5], acts[6]), down_w)))
+    acts_two, full_up = tie(acts_two, full_up)
+
     gate_proj = dot(acts_two, full_gate, 1, 0)
     up_proj = dot(acts_two, full_up, 1, 0)
     sigmoid_gate = jax.nn.sigmoid(gate_proj)
     hidden = (gate_proj * sigmoid_gate * up_proj).astype(BF16)
+
+    def reduced(grad, axis):
+        return lax.psum_scatter(grad, "z", scatter_dimension=axis, tiled=True)
+
+    def traded(total, axis, *behind):
+        total = after(total, *behind)
+        return half_of(total, y_rank, axis), swap(half_of(total, other_y, axis), "y")
+
+    down_part = dot(hidden, down_rows, 0, 0).astype(BF16)
+    down_sum = reduced(down_part, 1)
+    own_peak = jnp.max(after(peak, down_part)[:HEADS], axis=1, keepdims=True)
+    own_peak = jnp.broadcast_to(own_peak, (HEADS, 128))
+    head_peak = over_z(ordered(own_peak, swap(own_peak, "y"), y_rank, 0), jnp.maximum)
+    down_rows, head_peak = tie(down_rows, head_peak)
+    head_peak = head_peak[:, 0]
+    hidden_grad = dot(down_rows, full_down, 1, 1)
     gate_grad = (
         hidden_grad * up_proj * sigmoid_gate * (1.0 + gate_proj * (1.0 - sigmoid_gate))
     ).astype(BF16)
     up_grad = (hidden_grad * gate_proj * sigmoid_gate).astype(BF16)
 
-    def reduced(grad, axis):
-        return lax.psum_scatter(grad.astype(BF16), "z", scatter_dimension=axis, tiled=True)
-
-    down_sum = reduced(dot(hidden, down_rows, 0, 0), 1)
-    gate_sum = reduced(dot(acts_two, gate_grad, 0, 0), 0)
-    up_sum = reduced(dot(acts_two, up_grad, 0, 0), 0)
-
     def acts_two_back(part):
         return dot(gate_grad[part], full_gate, 1, 1) + dot(up_grad[part], full_up, 1, 1)
 
-    norm_two_grad = scatter_rows(
-        lambda: acts_two_back(slice(None, half_rows)), lambda: acts_two_back(slice(half_rows, None))
-    )
-    gain_two_part = jnp.sum(normal_two.astype(F32) * norm_two_grad, axis=0)
+    norm_two = spread_one(
+        fold_rows(
+            lambda: acts_two_back(slice(None, half_rows)),
+            lambda: acts_two_back(slice(half_rows, None)),
+        )
+    )
+    held = after(acts_two, *norm_two[4])
+    gate_part = dot(held, gate_grad, 0, 0).astype(BF16)
+    up_part = dot(held, up_grad, 0, 0).astype(BF16)
+    gate_sum, up_sum = reduced(gate_part, 0), reduced(up_part, 0)
+    got = tie(*norm_two[2:4], gate_part, up_part)[:2]
+    norm_two = spread_two((*norm_two[:2], *got))
+    held = after(hidden, *norm_two[4])
+    high_part = dot(held[half_rows:], full_down, 1, 0).astype(BF16)
+    got = tie(*norm_two[2:4], high_part)[:2]
+    norm_two_grad = spread_three((*norm_two[:2], *got))
     grad_resid = grad_out + norm_back(resid, scale_two, gain_two[None, :] * norm_two_grad)
-    mixed_rows = gather_rows((RESIDUAL * own_mask * grad_resid).astype(BF16))
-    branch_two = scatter_rows(
-        lambda: dot(hidden[:half_rows], full_down, 1, 0),
-        lambda: dot(hidden[half_rows:], full_down, 1, 0),
-    )
-    result = resid + RESIDUAL * own_mask * branch_two
-
-    heads_grad = dot(full_out, mixed_rows, 1, 1).astype(BF16)
+    mixed = gather_one((RESIDUAL * own_mask * grad_resid).astype(BF16))
+    held = after(hidden, mixed[0])
+    folded = fold_rows(lambda: dot(held[:half_rows], full_down, 1, 0), lambda: high_part)
+    gain_two_part = jnp.sum(normal_two * norm_two_grad, axis=0)
+    got = tie(*mixed[2:4], folded, gain_two_part)
+    folded, gain_two_part = got[2:]
+    mixed = gather_two((*mixed[:2], *got[:2]))
+    mixed_rows = gather_three(mixed)
+    mixed_rows, down_sum, gate_sum = tie(mixed_rows, down_sum, gate_sum)
+    second = spread_one(after(folded, mixed[5], mixed[6]))
+    down_own, down_other = traded(down_sum, 1)
+    gate_own, gate_other = traded(gate_sum, 0)
+
+    heads_grad = dot(full_out, mixed_rows, 0, 1).astype(BF16)
     dq, dkv, back = call(
         attend_back_kernel, info, (qkv, halo, heads_grad, lse, cos, sin),
         [((HEADS * HD, rows), BF16), ((2 * HD, rows), F32), ((2 * HD, LEAD), BF16)],
         [((KEYS, HD), BF16), ((KEYS, HD), BF16), ((HD, KEYS), BF16),
          ((SLOT_LEN, CHUNK), F32), ((SLOT_LEN, CHUNK), F32),
          ((KEYS, HD), F32), ((KEYS, HD), F32), ((HEADS * HD, SLOT_LEN), BF16)],
-        10 * work, "attend_back",
-    )
+        "attend_back",
+    )
+    back, down_other, gate_other, *got = tie(back, down_other, gate_other, *second[2:4])
+    back_sent = along(back, -1)
+    second = spread_two((*second[:2], *got))
+    out_part = dot(after(mixed_rows, back), heads, 0, 1).astype(BF16)
+    out_sum = reduced(out_part, 0)
+    dkv, back_sent, out_part, up_sum = tie(dkv, back_sent, out_part, up_sum)
+    up_own, up_other = traded(up_sum, 0)
     (dkv_done,) = call(
-        finish_kernel, info, (dkv, along(back, -1), cos, sin), [((2 * HD, rows), BF16)], [],
-        4 * dkv.size, "finish",
+        finish_kernel, info, (dkv, back_sent, cos, sin), [((2 * HD, rows), BF16)], [], "finish"
     )
     dqkv = jnp.concatenate((dq, dkv_done))
-    out_sum = reduced(dot(heads, mixed_rows, 1, 0), 1)
-    qkv_sum = reduced(dot(acts_one, dqkv, 0, 1), 0)
-    norm_one_grad = scatter_rows(
+    folded = fold_rows(
         lambda: dot(dqkv[:, :half_rows], full_qkv, 0, 1),
         lambda: dot(dqkv[:, half_rows:], full_qkv, 0, 1),
     )
-    gain_one_part = jnp.sum(normal_one.astype(F32) * norm_one_grad, axis=0)
+    folded, up_other, *got = tie(folded, up_other, *second[2:4])
+    branch_two = spread_three((*second[:2], *got))
+    result = resid + RESIDUAL * own_mask * branch_two
+
+    norm_one = spread_one(folded)
+    part = dot(after(acts_one, *norm_one[4]), dqkv, 0, 1)
+    gain_one_part = jnp.sum(part * full_qkv.astype(F32), axis=1) / gain_one
+    qkv_part = part.astype(BF16)
+    qkv_sum = reduced(qkv_part, 0)
+    *got, gain_one_part = tie(*norm_one[2:4], gain_one_part, qkv_part)[:3]
+    norm_one = spread_two((*norm_one[:2], *got))
+    norm_one_grad = spread_three(norm_one)
     grad_input = grad_resid + norm_back(layer_f, scale_one, gain_one[None, :] * norm_one_grad)
-
-    def owned_rows(total):
-        return half_of(total, y_rank, 0), swap(half_of(total, other_y, 0), "y")
-
-    def owned_cols(total):
-        return half_of(total, y_rank, 1), swap(half_of(total, other_y, 1), "y")
-
-    down_grad = ordered(*owned_cols(down_sum), y_rank, 0).astype(F32)
-    gate_w_grad = ordered(*owned_rows(gate_sum), y_rank, 1).astype(F32)
-    up_w_grad = ordered(*owned_rows(up_sum), y_rank, 1).astype(F32)
-    out_grad = ordered(*owned_cols(out_sum), y_rank, 0).astype(F32)
-    own, other = owned_rows(qkv_sum)
+    gain_one_part = after(gain_one_part, norm_one_grad)
+    out_own, out_other = traded(out_sum, 0, norm_one_grad)
+    own, other = traded(qkv_sum, 0, norm_one_grad)
+
+    gains = jnp.stack((gain_one_part, gain_two_part))
+    gains = gains.reshape(2, lax.axis_size("z"), 2, 2, 2, -1)
+    for dim, axis in ((4, "c"), (3, "x"), (2, "y")):
+        at = lax.axis_index(axis)
+        other_at = lax.dynamic_index_in_dim(gains, 1 - at, dim, keepdims=False)
+        gains = lax.dynamic_index_in_dim(gains, at, dim, keepdims=False) + swap(other_at, axis)
+    gains = lax.dynamic_index_in_dim(over_z(gains, jnp.add), z_rank, 1, keepdims=False)
+
+    down_grad = ordered(down_own, down_other, y_rank, 0).astype(F32)
+    gate_w_grad = ordered(gate_own, gate_other, y_rank, 1).astype(F32)
+    up_w_grad = ordered(up_own, up_other, y_rank, 1).astype(F32)
+    out_grad = ordered(out_own.T, out_other.T, y_rank, 0).astype(F32)
 
     def columns(start, stop):
         return ordered(own[:, start:stop], other[:, start:stop], y_rank, 1).astype(F32)
@@ -465,15 +569,6 @@
     key_grad = columns(K_AT, V_AT)
     value_grad = columns(V_AT, V_AT + HD)
 
-    gains = jnp.stack((gain_one_part, gain_two_part))
-    devices = lax.axis_size(EVERY)
-    gains = lax.psum_scatter(
-        gains.reshape(2, devices, -1).transpose(1, 0, 2), EVERY, scatter_dimension=0, tiled=True
-    )[0]
-
-    local = peak[:HEADS, 0]
-    empty = jnp.full((HEADS,), NEGATIVE, F32)
-    head_peak = lax.pmax(ordered(local, empty, y_rank, 0), ("z", "y"))
     level = clip_level[0].astype(F32) * LEVEL_UNIT
     factor = level / jnp.maximum(level, head_peak)
     query_clipped = w_query.astype(F32) * jnp.repeat(jnp.sqrt(factor), HD)[None, :]

time: 835 us -> 739 us (0.89)
  waiting for transfers between devices: 259 us -> 195 us
  blocking collectives: 59.5 us -> 0 us
  other arithmetic: 65.3 us -> 88.8 us
  local copies, waits for them, and re-layouts: 98.3 us -> 108 us
    ppermute x50 -> x61, waiting for transfers between devices: 245 us -> 176 us  [swap(): return lax.ppermute(x, axis, [(0, 1), (1, 0)])]
    unnamed x1 -> x0, blocking collectives: 37.2 us -> none
    unnamed x155 -> x203, local copies, waits for them, and re-layouts: 52.3 us -> 77.9 us
    pmax x1 -> x0, blocking collectives: 22.3 us -> none  [shards(): head_peak = lax.pmax(ordered(local, empty, y_rank, 0), ('z', 'y'))]
    add x8 -> x18, other arithmetic: 12.1 us -> 31.8 us  [the longest x1 13.6 us: fold_rows(): return low() + swap(high().astype(BF16), 'c').astype(F32)]
    concatenate x8 -> x4, local copies, waits for them, and re-layouts: 22.4 us -> 3.36 us  [gather_three(): return jnp.concatenate(own + block(near, second, third))]
    reduce_scatter x5, starting transfers between devices: 13.2 us -> 1.19 us  [reduced(): return lax.psum_scatter(grad, 'z', scatter_dimension=axis, tiled=True)]
    all_gather x5 -> x4, starting transfers between devices: 0.2 us -> 11.8 us  [the longest x1 11.7 us: shards(): full_down = lax.all_gather(down_w, 'z', axis=1, tiled=True)]
  transfers between devices with their start and end apart: 62 -> 76, of which waited for: 29 -> 35; matrix products, arithmetic and copies ran while one was open for 37% -> 49% of each run, Pallas kernels for 9% -> 10%
where the time goes in v2:
time: 739 us; the launch traced here: 734 us
  waiting for transfers between devices  195 us (26%)
  matrix products  181 us (24%)
  local copies, waits for them, and re-layouts  108 us (15%)
  other arithmetic  88.8 us (12%)
  starting transfers between devices  74.3 us (10%)
  Pallas kernels  70.8 us (10%)
  between operations  16 us (2%)
    dot_general x20, matrix products, dot(): lax.dot_general(left, right, (((left_dim,), (right_dim,)), ((), ())), pre...  181 us
    ppermute x61, waiting for transfers between devices, swap(): return lax.ppermute(x, axis, [(0, 1), (1, 0)])  176 us
    unnamed x203, local copies, waits for them, and re-layouts  77.9 us
    pallas_call x4, Pallas kernels, call(): pl.pallas_call(kernel, out_shape=[jax.ShapeDtypeStruct(s, d) for s, d in...  70.8 us
    ppermute x61, starting transfers between devices, swap(): return lax.ppermute(x, axis, [(0, 1), (1, 0)])  52.8 us
    ppermute x6, waiting for transfers between devices, along(): return lax.ppermute(x, 'z', [(i, (i + by) % peers) for i in range(peers)])  19.1 us
  transfers between devices with their start and end apart: 76, of which 35 were waited for; matrix products, arithmetic and copies ran while one was open for 49% of the time, Pallas kernels for 10%

profile of v2, /device:TPU:0, one launch (start us, length us, event | category | flops | bytes accessed | tf_op | source)
XLA Modules:
  0.0 734.4 jit_solution(15081485785544276794)
XLA Ops:
  10.0 3.0 collective-permute-start
  13.3 7.4 %collective-permute-done = bf16[256,640]{0,1:T(8,128)(2,1)S(1)} collective-permute-done((bf16[256,640]{0,1:T(8,128)(2,1)S(1)}, bf16[256,640]{0,1:T(8,128)(2,1)S(1)}, u32[]{:S(2)}, u32[]{:S(2)}) %collective-permute-start) | collective-permute-done | bytes 327712 | tf_op jit(solution)/shard_map/ppermute | solution.py:34
  24.7 2.3 constant_dynamic-slice_fusion.18
  34.2 9.5 %collective-permute-done.3 = bf16[128,2048]{1,0:T(8,128)(2,1)S(1)} collective-permute-done((bf16[128,2048]{1,0:T(8,128)(2,1)S(1)}, bf16[128,2048]{1,0:T(8,128)(2,1)S(1)}, u32[]{:S(2)}, u32[]{:S(2)}) %collective-permute-start.3) | collective-permute-done | bytes 524320 | tf_op jit(solution)/shard_map/ppermute | solution.py:34
  52.1 2.3 constant_dynamic-update-slice_fusion.3
  55.8 24.5 %collective-permute-done.5 = bf16[256,1024]{1,0:T(8,128)(2,1)S(1)} collective-permute-done((bf16[256,1024]{1,0:T(8,128)(2,1)S(1)}, bf16[256,1024]{1,0:T(8,128)(2,1)S(1)}, u32[]{:S(2)}, u32[]{:S(2)}) %collective-permute-start.5) | collective-permute-done | bytes 524320 | tf_op jit(solution)/shard_map/ppermute | solution.py:34
  81.0 3.0 maximum_select_fusion
  97.2 2.3 constant_dynamic-update-slice_fusion
  108.3 5.9 fusion.46.qkv
  116.9 8.8 %collective-permute-done.9.halo = bf16[128,512]{1,0:T(8,128)(2,1)S(1)} collective-permute-done((bf16[128,512]{1,0:T(8,128)(2,1)S(1)}, bf16[128,512]{1,0:T(8,128)(2,1)S(1)}, u32[]{:S(2)}, u32[]{:S(2)}) %collective-permute-start.9) | collective-permute-done | bytes 131104 | tf_op jit(solution)/shard_map/ppermute | solution.py:39
  131.3 28.6 %attend.1 = (bf16[256,2048]{1,0:T(8,128)(2,1)S(1)}, f32[8,2048]{1,0:T(8,128)S(1)}, f32[8,128]{1,0:T(8,128)S(1)}) custom-call(s32[3]{0:T(128)S(1)} %pad_add_fusion.info, bf16[384,2048]{1,0:T(8,128)(2,1)S(1)} %rope.1.qkv, bf16[128,512]{1,0:T(8,128)(2,1)S(1)} %collective-permute-done.9.halo), custom_call_target="tpu_custom_call" | custom-call | tf_op jit(solution)/shard_map/attend/pallas_call | solution.py:348
  161.4 3.9 collective-permute-done.14
  165.4 4.5 convolution_convert_fusion.2
  169.9 11.7 %all-gather.11.cloned.1.call-start = ((), (), s32[]{:S(2)}) async-start(), calls=%async_computation.8 | async-start | bytes 5242880 | tf_op jit(solution)/shard_map/all_gather | solution.py:434
  181.6 2.3 constant_dynamic-update-slice_fusion.7
  185.8 3.8 convert_add_fusion.3
  190.3 2.7 copy-done.8
  216.1 5.0 collective-permute-done.19
  222.3 3.2 fusion.24
  227.3 11.5 %collective-permute-done.23 = bf16[256,1024]{1,0:T(8,128)(2,1)S(1)} collective-permute-done((bf16[256,1024]{1,0:T(8,128)(2,1)S(1)}, bf16[256,1024]{1,0:T(8,128)(2,1)S(1)}, u32[]{:S(2)}, u32[]{:S(2)}) %collective-permute-start.23) | collective-permute-done | bytes 524320 | tf_op jit(solution)/shard_map/ppermute | solution.py:34
  245.1 10.1 %collective-permute-done.26 = bf16[128,2048]{1,0:T(8,128)(2,1)S(1)} collective-permute-done((bf16[128,2048]{1,0:T(8,128)(2,1)S(1)}, bf16[128,2048]{1,0:T(8,128)(2,1)S(1)}, u32[]{:S(2)}, u32[]{:S(2)}) %collective-permute-start.26) | collective-permute-done | bytes 524320 | tf_op jit(solution)/shard_map/ppermute | solution.py:34
  260.0 2.4 maximum_select_fusion.2
  265.0 14.9 %collective-permute-done.25 = bf16[256,2048]{1,0:T(8,128)(2,1)S(1)} collective-permute-done((bf16[256,2048]{1,0:T(8,128)(2,1)}, bf16[256,2048]{1,0:T(8,128)(2,1)S(1)}, u32[]{:S(2)}, u32[]{:S(2)}) %collective-permute-start.25) | collective-permute-done | bytes 1048608 | tf_op jit(solution)/shard_map/ppermute | solution.py:34
  295.2 14.7 %fusion.89 = f32[2048,1024]{1,0:T(8,128)} fusion(bf16[2048,2048]{1,0:T(8,128)(2,1)} %slice_dynamic-update-slice_fusion.10, bf16[2048,1024]{1,0:T(8,128)(2,1)} %all-gather.7.cloned.1.call-done), kind=kOutput, calls=%fused_computation.298 | convolution fusion | flops 8589934592 | bytes 20971520 | tf_op jit(solution)/shard_map/dot_general | solution.py:43
  310.0 14.7 %multiply_convert_fusion.2 = (bf16[2048,1024]{1,0:T(8,128)(2,1)}, f32[2048,1024]{1,0:T(8,128)}) fusion(f32[2048,1024]{1,0:T(8,128)} %fusion.89, bf16[2048,2048]{1,0:T(8,128)(2,1)S(1)} %copy-done.49, bf16[2048,1024]{1,0:T(8,128)(2,1)} %all-gather.9.cloned.1.call-done), kind=kOutput, calls=%fused_computation.6 | convolution fusion | flops 8602517504 | bytes 33554432 | tf_op jit(solution)/shard_map/dot_general | solution.py:43
  324.7 12.4 %convolution_convert_fusion.1 = bf16[1024,2048]{1,0:T(8,128)(2,1)} fusion(bf16[2048,1024]{1,0:T(8,128)(2,1)} %get-tuple-element.137, bf16[2048,2048]{1,0:T(8,128)(2,1)S(1)} %bitcast.161), kind=kOutput, calls=%fused_computation.15 | convolution fusion | flops 8592031744 | bytes 16777216 | tf_op jit(solution)/shard_map/dot_general | solution.py:43
  337.9 3.1 collective-permute-done.31
  341.7 5.1 collective-permute-done.32
  346.8 3.5 collective-permute-start.33
  352.5 22.9 %multiply_convert_fusion.1 = (bf16[2048,1024]{1,0:T(8,128)(2,1)}, bf16[2048,1024]{1,0:T(8,128)(2,1)}) fusion(f32[2048,1024]{1,0:T(8,128)} %fusion.89, f32[2048,1024]{1,0:T(8,128)} %get-tuple-element.337, bf16[2048,2048]{1,0:T(8,128)(2,1)} %slice_dynamic-update-slice_fusion.16, bf16[1024,2048]{1,0:T(8,128)(2,1)} %all-gather.11.cloned.1.call-done), kind=kOutput, calls=%fused_computation.5 | convolution fusion | flops 8617197568 | bytes 37748736 | tf_op jit(solution)/shard_map/dot_general | solution.py:43
  375.4 8.6 %fusion.16 = f32[1024,2048]{1,0:T(8,128)} fusion(bf16[2048,1024]{1,0:T(8,128)(2,1)S(1)} %copy-done.64, bf16[2048,1024]{1,0:T(8,128)(2,1)} %get-tuple-element.261), kind=kOutput, calls=%fused_computation.50 | convolution fusion | flops 4294967296 | bytes 14680064 | tf_op jit(solution)/shard_map/dot_general | solution.py:43
  384.0 7.7 %add_convert_fusion = bf16[1024,2048]{1,0:T(8,128)(2,1)S(1)} fusion(f32[1024,2048]{1,0:T(8,128)} %fusion.16, bf16[2048,1024]{1,0:T(8,128)(2,1)S(1)} %copy-done.63, bf16[2048,1024]{1,0:T(8,128)(2,1)} %get-tuple-element.260), kind=kOutput, calls=%fused_computation.3 | convolution fusion | flops 4299161600 | bytes 18874368 | tf_op jit(solution)/shard_map/dot_general | solution.py:43
  391.8 8.5 %fusion.21 = f32[1024,2048]{1,0:T(8,128)} fusion(bf16[2048,1024]{1,0:T(8,128)(2,1)S(1)} %copy-done.63, bf16[2048,1024]{1,0:T(8,128)(2,1)} %get-tuple-element.260), kind=kOutput, calls=%fused_computation.55 | convolution fusion | flops 4294967296 | bytes 14680064 | tf_op jit(solution)/shard_map/dot_general | solution.py:43
  400.4 7.0 fusion.19
  407.4 13.6 %convert_add_fusion.2 = f32[1024,2048]{1,0:T(8,128)} fusion(bf16[1024,2048]{1,0:T(8,128)(2,1)} %collective-permute-done.34, f32[1024,2048]{1,0:T(8,128)} %fusion.21, f32[1024,2048]{1,0:T(8,128)} %fusion.19), kind=kLoop, calls=%fused_computation.2 | loop fusion | flops 6291456 | bytes 29360128 | tf_op jit(solution)/shard_map/add | solution.py:97
  421.0 4.2 convert.43
  429.5 12.9 %convolution_convert_fusion.5 = bf16[2048,1024]{1,0:T(8,128)(2,1)} fusion(bf16[2048,2048]{1,0:T(8,128)(2,1)} %slice_dynamic-update-slice_fusion.10, bf16[2048,1024]{1,0:T(8,128)(2,1)S(1)} %copy-done.68), kind=kOutput, calls=%fused_computation.19 | convolution fusion | flops 8592031744 | bytes 16777216 | tf_op jit(solution)/shard_map/dot_general | solution.py:43
  442.6 14.2 %convolution_convert_fusion.4 = bf16[2048,1024]{1,0:T(8,128)(2,1)} fusion(bf16[2048,2048]{1,0:T(8,128)(2,1)} %slice_dynamic-update-slice_fusion.10, bf16[2048,1024]{1,0:T(8,128)(2,1)} %get-tuple-element.261), kind=kOutput, calls=%fused_computation.18 | convolution fusion | flops 8592031744 | bytes 16777216 | tf_op jit(solution)/shard_map/dot_general | solution.py:43
  456.8 3.1 fusion.15
  461.5 4.7 convolution_convert_fusion.3
  468.3 12.4 %collective-permute-done.38 = bf16[256,1024]{1,0:T(8,128)(2,1)S(1)} collective-permute-done((bf16[256,1024]{1,0:T(8,128)(2,1)S(1)}, bf16[256,1024]{1,0:T(8,128)(2,1)S(1)}, u32[]{:S(2)}, u32[]{:S(2)}) %collective-permute-start.38) | collective-permute-done | bytes 524320 | tf_op jit(solution)/shard_map/ppermute | solution.py:34
  483.5 2.4 constant_dynamic-update-slice_fusion.15
  487.4 6.8 convert_add_fusion.1
  494.2 5.1 collective-permute-done.40
  506.5 18.5 %collective-permute-done.42 = bf16[256,2048]{1,0:T(8,128)(2,1)S(1)} collective-permute-done((bf16[256,2048]{1,0:T(8,128)(2,1)}, bf16[256,2048]{1,0:T(8,128)(2,1)S(1)}, u32[]{:S(2)}, u32[]{:S(2)}) %collective-permute-start.42) | collective-permute-done | bytes 1048608 | tf_op jit(solution)/shard_map/ppermute | solution.py:34
  527.8 4.2 convert.46
  551.9 2.1 constant_dynamic-slice_fusion.4
  554.7 6.2 convolution_convert_fusion.7.upstream
  561.0 40.5 %attend_back.1 = (bf16[256,2048]{1,0:T(8,128)(2,1)S(1)}, f32[128,2048]{1,0:T(8,128)S(1)}, bf16[128,512]{1,0:T(8,128)(2,1)S(1)}) custom-call(s32[3]{0:T(128)S(1)} %copy-done.7, bf16[384,2048]{1,0:T(8,128)(2,1)S(1)} %copy-done.1, bf16[128,512]{1,0:T(8,128)(2,1)S(1)} %copy-done.5, bf16[256,2048]{1,0:T(8,128)(2,1)S(1)} %convolution_convert_fusion.7.upstream, ...), custom_call_target="tpu_custom_call" | custom-call | tf_op jit(solution)/shard_map/attend_back/pallas_call | solution.py:348
  601.5 2.5 collective-permute-start.51
  604.0 6.9 convolution_convert_fusion.6
  611.6 5.8 convolution_convert_fusion
  620.7 3.5 fusion.13
  631.3 4.7 convert_add_fusion
  636.0 2.8 collective-permute-done.55
  640.6 10.5 %collective-permute-done.53 = bf16[256,1024]{1,0:T(8,128)(2,1)S(1)} collective-permute-done((bf16[256,1024]{1,0:T(8,128)(2,1)S(1)}, bf16[256,1024]{1,0:T(8,128)(2,1)S(1)}, u32[]{:S(2)}, u32[]{:S(2)}) %collective-permute-start.53) | collective-permute-done | bytes 524320 | tf_op jit(solution)/shard_map/ppermute | solution.py:34
  656.0 8.2 %fusion.80 = (bf16[2048,384]{0,1:T(8,128)(2,1)}, f32[2048]{0:T(1024)S(1)}) fusion(bf16[2048,640]{0,1:T(8,128)(2,1)S(1)} %copy-done.20, bf16[2048,2048]{1,0:T(8,128)(2,1)} %slice_dynamic-update-slice_fusion.20, bf16[128,2048]{1,0:T(8,128)(2,1)S(1)} %finish.1, bf16[256,2048]{1,0:T(8,128)(2,1)S(1)} %get-tuple-element.148), kind=kOutput, calls=%fused_computation.289 | convolution fusion | flops 3227514880 | bytes 13115392 | tf_op jit(solution)/shard_map/dot_general | solution.py:43
  667.3 10.5 %collective-permute-done.56 = bf16[2,256,1024]{2,1,0:T(8,128)(2,1)} collective-permute-done((bf16[2,256,1024]{2,1,0:T(8,128)(2,1)}, bf16[2,256,1024]{2,1,0:T(8,128)(2,1)}, u32[]{:S(2)}, u32[]{:S(2)}) %collective-permute-start.56) | collective-permute-done | bytes 1048608 | tf_op jit(solution)/shard_map/ppermute | solution.py:34
  679.3 3.5 fusion.11
  686.9 8.2 %collective-permute-done.59 = bf16[256,1024]{1,0:T(8,128)(2,1)S(1)} collective-permute-done((bf16[256,1024]{1,0:T(8,128)(2,1)S(1)}, bf16[256,1024]{1,0:T(8,128)(2,1)S(1)}, u32[]{:S(2)}, u32[]{:S(2)}) %collective-permute-start.59) | collective-permute-done | bytes 524320 | tf_op jit(solution)/shard_map/ppermute | solution.py:34
  704.4 2.3 collective-permute-done.62
  709.1 3.1 collective-permute-done.63
  712.2 3.4 fusion.8
  722.3 2.7 collective-permute-done.65
  (452 shorter events, 206.4 us)
Async XLA Ops:
  7.2 73.8 %all-gather.5.cloned.1.call-start = ((), (), s32[]{:S(2)}) async-start(), calls=%async_computation.5 | async-start | bytes 3276800 | tf_op jit(solution)/shard_map/all_gather | solution.py:393
  10.0 10.7 %collective-permute-start = (bf16[256,640]{0,1:T(8,128)(2,1)S(1)}, bf16[256,640]{0,1:T(8,128)(2,1)S(1)}, u32[]{:S(2)}, u32[]{:S(2)}) collective-permute-start(bf16[256,640]{0,1:T(8,128)(2,1)S(1)} %pad_maximum_fusion.20), channel_id=1, source_target_pairs={{0,4},{4,0},{1,5},{5,1},{2,6},{6,2},{3,7},{7,3},{8,12},{12,8},{9,1... | collective-permute-start | bytes 983048 | tf_op jit(solution)/shard_map/ppermute | solution.py:34
  21.8 194.3 %all-gather.7.cloned.1.call-start = ((), (), s32[]{:S(2)}) async-start(), calls=%async_computation.6 | async-start | bytes 5242880 | tf_op jit(solution)/shard_map/all_gather | solution.py:408
  30.6 13.1 %collective-permute-start.3 = (bf16[128,2048]{1,0:T(8,128)(2,1)S(1)}, bf16[128,2048]{1,0:T(8,128)(2,1)S(1)}, u32[]{:S(2)}, u32[]{:S(2)}) collective-permute-start(bf16[128,2048]{1,0:T(8,128)(2,1)S(1)} %get-tuple-element.292), channel_id=1, source_target_pairs={{0,4},{4,0},{1,5},{5,1},{2,6},{6,2},{3,7},{7,3},{8,12},{12,8},{9,1... | collective-permute-start | bytes 1572872 | tf_op jit(solution)/shard_map/ppermute | solution.py:34
  32.4 12.4 %collective-permute-start.1 = (bf16[128,2048]{1,0:T(8,128)(2,1)S(1)}, bf16[128,2048]{1,0:T(8,128)(2,1)S(1)}, u32[]{:S(2)}, u32[]{:S(2)}) collective-permute-start(bf16[128,2048]{1,0:T(8,128)(2,1)S(1)} %get-tuple-element.293), channel_id=1, source_target_pairs={{0,2},{2,0},{1,3},{3,1},{4,6},{6,4},{5,7},{7,5},{8,10},{10,8},{9,1... | collective-permute-start | bytes 1572872 | tf_op jit(solution)/shard_map/ppermute | solution.py:34
  46.2 34.1 %collective-permute-start.2 = (bf16[256,2048]{1,0:T(8,128)(2,1)S(1)}, bf16[256,2048]{1,0:T(8,128)(2,1)}, u32[]{:S(2)}, u32[]{:S(2)}) collective-permute-start(bf16[256,2048]{1,0:T(8,128)(2,1)S(1)} %get-tuple-element.304), channel_id=1, source_target_pairs={{0,4},{4,0},{1,5},{5,1},{2,6},{6,2},{3,7},{7,3},{8,12},{12,8},{9,1... | collective-permute-start | bytes 3145736 | tf_op jit(solution)/shard_map/ppermute | solution.py:34
  46.8 34.3 %collective-permute-start.4 = (bf16[256,2048]{1,0:T(8,128)(2,1)S(1)}, bf16[256,2048]{1,0:T(8,128)(2,1)}, u32[]{:S(2)}, u32[]{:S(2)}) collective-permute-start(bf16[256,2048]{1,0:T(8,128)(2,1)S(1)} %get-tuple-element.305), channel_id=1, source_target_pairs={{0,2},{2,0},{1,3},{3,1},{4,6},{6,4},{5,7},{7,5},{8,10},{10,8},{9,1... | collective-permute-start | bytes 3145736 | tf_op jit(solution)/shard_map/ppermute | solution.py:34
  49.1 31.1 %collective-permute-start.5 = (bf16[256,1024]{1,0:T(8,128)(2,1)S(1)}, bf16[256,1024]{1,0:T(8,128)(2,1)S(1)}, u32[]{:S(2)}, u32[]{:S(2)}) collective-permute-start(bf16[256,1024]{1,0:T(8,128)(2,1)S(1)} %get-tuple-element.93), channel_id=1, source_target_pairs={{0,4},{4,0},{1,5},{5,1},{2,6},{6,2},{3,7},{7,3},{8,12},{12,8},{9,1... | collective-permute-start | bytes 1572872 | tf_op jit(solution)/shard_map/ppermute | solution.py:34
  52.1 43.9 %collective-permute-start.6 = (bf16[256,2048]{1,0:T(8,128)(2,1)}, bf16[256,2048]{1,0:T(8,128)(2,1)}, u32[]{:S(2)}, u32[]{:S(2)}) collective-permute-start(bf16[256,2048]{1,0:T(8,128)(2,1)} %fusion.4), channel_id=1, source_target_pairs={{0,1},{1,0},{2,3},{3,2},{4,5},{5,4},{6,7},{7,6},{8,9},{9,8},{10,11... | collective-permute-start | bytes 3145736 | tf_op jit(solution)/shard_map/ppermute | solution.py:34
  54.4 45.1 %collective-permute-start.7 = (bf16[256,2048]{1,0:T(8,128)(2,1)}, bf16[256,2048]{1,0:T(8,128)(2,1)}, u32[]{:S(2)}, u32[]{:S(2)}) collective-permute-start(bf16[256,2048]{1,0:T(8,128)(2,1)} %get-tuple-element.303), channel_id=1, source_target_pairs={{0,1},{1,0},{2,3},{3,2},{4,5},{5,4},{6,7},{7,6},{8,9},{9,8},{10,11... | collective-permute-start | bytes 3145736 | tf_op jit(solution)/shard_map/ppermute | solution.py:34
  84.0 211.2 %all-gather.9.cloned.1.call-start = ((), (), s32[]{:S(2)}) async-start(), calls=%async_computation.7 | async-start | bytes 5242880 | tf_op jit(solution)/shard_map/all_gather | solution.py:423
  84.1 32.7 %collective-permute-start.10 = (bf16[256,1024]{1,0:T(8,128)(2,1)}, bf16[256,1024]{1,0:T(8,128)(2,1)S(1)}, u32[]{:S(2)}, u32[]{:S(2)}) collective-permute-start(bf16[256,1024]{1,0:T(8,128)(2,1)} %get-tuple-element.98), channel_id=1, source_target_pairs={{0,4},{4,0},{1,5},{5,1},{2,6},{6,2},{3,7},{7,3},{8,12},{12,8},{9,1... | collective-permute-start | bytes 1572872 | tf_op jit(solution)/shard_map/ppermute | solution.py:34
  85.1 31.8 %collective-permute-start.11 = (bf16[256,2048]{1,0:T(8,128)(2,1)S(1)}, bf16[256,2048]{1,0:T(8,128)(2,1)S(1)}, u32[]{:S(2)}, u32[]{:S(2)}) collective-permute-start(bf16[256,2048]{1,0:T(8,128)(2,1)S(1)} %fusion), channel_id=1, source_target_pairs={{0,1},{1,0},{2,3},{3,2},{4,5},{5,4},{6,7},{7,6},{8,9},{9,8},{10,11... | collective-permute-start | bytes 3145736 | tf_op jit(solution)/shard_map/ppermute | solution.py:34
  86.9 16.1 %collective-permute-start.8 = (bf16[512,2048]{1,0:T(8,128)(2,1)S(1)}, bf16[512,2048]{1,0:T(8,128)(2,1)S(1)}, u32[]{:S(2)}, u32[]{:S(2)}) collective-permute-start(bf16[512,2048]{1,0:T(8,128)(2,1)S(1)} %pad_maximum_fusion.1), channel_id=1, source_target_pairs={{0,1},{1,0},{2,3},{3,2},{4,5},{5,4},{6,7},{7,6},{8,9},{9,8},{10,11... | collective-permute-start | bytes 6291464 | tf_op jit(solution)/shard_map/ppermute | solution.py:34
  96.1 20.8 %collective-permute-start.13 = (bf16[128,2048]{1,0:T(8,128)(2,1)S(1)}, bf16[128,2048]{1,0:T(8,128)(2,1)S(1)}, u32[]{:S(2)}, u32[]{:S(2)}) collective-permute-start(bf16[128,2048]{1,0:T(8,128)(2,1)S(1)} %get-tuple-element.288), channel_id=1, source_target_pairs={{0,4},{4,0},{1,5},{5,1},{2,6},{6,2},{3,7},{7,3},{8,12},{12,8},{9,1... | collective-permute-start | bytes 1572872 | tf_op jit(solution)/shard_map/ppermute | solution.py:34
  99.5 17.3 %collective-permute-start.12 = (bf16[128,2048]{1,0:T(8,128)(2,1)S(1)}, bf16[128,2048]{1,0:T(8,128)(2,1)S(1)}, u32[]{:S(2)}, u32[]{:S(2)}) collective-permute-start(bf16[128,2048]{1,0:T(8,128)(2,1)S(1)} %get-tuple-element.289), channel_id=1, source_target_pairs={{0,2},{2,0},{1,3},{3,1},{4,6},{6,4},{5,7},{7,5},{8,10},{10,8},{9,1... | collective-permute-start | bytes 1572872 | tf_op jit(solution)/shard_map/ppermute | solution.py:34
  115.2 10.5 %collective-permute-start.9 = (bf16[128,512]{1,0:T(8,128)(2,1)S(1)}, bf16[128,512]{1,0:T(8,128)(2,1)S(1)}, u32[]{:S(2)}, u32[]{:S(2)}) collective-permute-start(bf16[128,512]{1,0:T(8,128)(2,1)S(1)} %slice.474), channel_id=1, source_target_pairs={{0,8},{8,16},{16,24},{24,0},{1,9},{9,17},{17,25},{25,1},{2,10},{10... | collective-permute-start | bytes 393224 | tf_op jit(solution)/shard_map/ppermute | solution.py:39
  127.7 37.7 %collective-permute-start.17 = (bf16[256,2048]{1,0:T(8,128)(2,1)}, bf16[256,2048]{1,0:T(8,128)(2,1)}, u32[]{:S(2)}, u32[]{:S(2)}) collective-permute-start(bf16[256,2048]{1,0:T(8,128)(2,1)} %get-tuple-element.300), channel_id=1, source_target_pairs={{0,2},{2,0},{1,3},{3,1},{4,6},{6,4},{5,7},{7,5},{8,10},{10,8},{9,1... | collective-permute-start | bytes 3145736 | tf_op jit(solution)/shard_map/ppermute | solution.py:34
  128.2 37.1 %collective-permute-start.15 = (bf16[256,2048]{1,0:T(8,128)(2,1)}, bf16[256,2048]{1,0:T(8,128)(2,1)}, u32[]{:S(2)}, u32[]{:S(2)}) collective-permute-start(bf16[256,2048]{1,0:T(8,128)(2,1)} %get-tuple-element.301), channel_id=1, source_target_pairs={{0,1},{1,0},{2,3},{3,2},{4,5},{5,4},{6,7},{7,6},{8,9},{9,8},{10,11... | collective-permute-start | bytes 3145736 | tf_op jit(solution)/shard_map/ppermute | solution.py:34
  128.2 37.1 %collective-permute-start.16 = (bf16[256,2048]{1,0:T(8,128)(2,1)}, bf16[256,2048]{1,0:T(8,128)(2,1)}, u32[]{:S(2)}, u32[]{:S(2)}) collective-permute-start(bf16[256,2048]{1,0:T(8,128)(2,1)} %get-tuple-element.302), channel_id=1, source_target_pairs={{0,4},{4,0},{1,5},{5,1},{2,6},{6,2},{3,7},{7,3},{8,12},{12,8},{9,1... | collective-permute-start | bytes 3145736 | tf_op jit(solution)/shard_map/ppermute | solution.py:34
  130.2 35.2 %collective-permute-start.14 = (bf16[1024,256]{1,0:T(8,128)(2,1)}, bf16[1024,256]{1,0:T(8,128)(2,1)}, u32[]{:S(2)}, u32[]{:S(2)}) collective-permute-start(bf16[1024,256]{1,0:T(8,128)(2,1)} %get-tuple-element.105), channel_id=1, source_target_pairs={{0,4},{4,0},{1,5},{5,1},{2,6},{6,2},{3,7},{7,3},{8,12},{12,8},{9,1... | collective-permute-start | bytes 1572872 | tf_op jit(solution)/shard_map/ppermute | solution.py:34
  169.9 15.9 %collective-permute-start.18 = (bf16[1024,2048]{1,0:T(8,128)(2,1)}, bf16[1024,2048]{1,0:T(8,128)(2,1)}, u32[]{:S(2)}, u32[]{:S(2)}) collective-permute-start(bf16[1024,2048]{1,0:T(8,128)(2,1)} %convolution_convert_fusion.2), channel_id=1, source_target_pairs={{0,1},{1,0},{2,3},{3,2},{4,5},{5,4},{6,7},{7,6},{8,9},{9,8},{10,11... | collective-permute-start | bytes 12582920 | tf_op jit(solution)/shard_map/ppermute | solution.py:34
  169.9 182.6 %all-gather.11.cloned.1.call-start = ((), (), s32[]{:S(2)}) async-start(), calls=%async_computation.8 | async-start | bytes 5242880 | tf_op jit(solution)/shard_map/all_gather | solution.py:434
  195.2 25.8 %collective-permute-start.19 = (bf16[2,256,1024]{2,1,0:T(8,128)(2,1)}, bf16[2,256,1024]{2,1,0:T(8,128)(2,1)S(1)}, u32[]{:S(2)}, u32[]{:S(2)}) collective-permute-start(bf16[2,256,1024]{2,1,0:T(8,128)(2,1)} %slice_bitcast_fusion.23), channel_id=1, source_target_pairs={{0,2},{2,0},{1,3},{3,1},{4,6},{6,4},{5,7},{7,5},{8,10},{10,8},{9,1... | collective-permute-start | bytes 3145736 | tf_op jit(solution)/shard_map/ppermute | solution.py:34
  196.7 25.6 %collective-permute-start.20 = (bf16[2,256,1024]{2,1,0:T(8,128)(2,1)}, bf16[2,256,1024]{2,1,0:T(8,128)(2,1)}, u32[]{:S(2)}, u32[]{:S(2)}) collective-permute-start(bf16[2,256,1024]{2,1,0:T(8,128)(2,1)} %slice_bitcast_fusion.22), channel_id=1, source_target_pairs={{0,4},{4,0},{1,5},{5,1},{2,6},{6,2},{3,7},{7,3},{8,12},{12,8},{9,1... | collective-permute-start | bytes 3145736 | tf_op jit(solution)/shard_map/ppermute | solution.py:34
  199.4 11.5 %collective-permute-start.21 = (bf16[512,2048]{1,0:T(8,128)(2,1)S(1)}, bf16[512,2048]{1,0:T(8,128)(2,1)S(1)}, u32[]{:S(2)}, u32[]{:S(2)}) collective-permute-start(bf16[512,2048]{1,0:T(8,128)(2,1)S(1)} %pad_maximum_fusion.2), channel_id=1, source_target_pairs={{0,1},{1,0},{2,3},{3,2},{4,5},{5,4},{6,7},{7,6},{8,9},{9,8},{10,11... | collective-permute-start | bytes 6291464 | tf_op jit(solution)/shard_map/ppermute | solution.py:34
  225.6 13.3 %collective-permute-start.23 = (bf16[256,1024]{1,0:T(8,128)(2,1)S(1)}, bf16[256,1024]{1,0:T(8,128)(2,1)S(1)}, u32[]{:S(2)}, u32[]{:S(2)}) collective-permute-start(bf16[256,1024]{1,0:T(8,128)(2,1)S(1)} %fusion.56), channel_id=1, source_target_pairs={{0,2},{2,0},{1,3},{3,1},{4,6},{6,4},{5,7},{7,5},{8,10},{10,8},{9,1... | collective-permute-start | bytes 1572872 | tf_op jit(solution)/shard_map/ppermute | solution.py:34
  226.4 13.1 %collective-permute-start.22 = (bf16[256,1024]{1,0:T(8,128)(2,1)S(1)}, bf16[256,1024]{1,0:T(8,128)(2,1)S(1)}, u32[]{:S(2)}, u32[]{:S(2)}) collective-permute-start(bf16[256,1024]{1,0:T(8,128)(2,1)S(1)} %fusion.55), channel_id=1, source_target_pairs={{0,4},{4,0},{1,5},{5,1},{2,6},{6,2},{3,7},{7,3},{8,12},{12,8},{9,1... | collective-permute-start | bytes 1572872 | tf_op jit(solution)/shard_map/ppermute | solution.py:34
  242.9 12.3 %collective-permute-start.26 = (bf16[128,2048]{1,0:T(8,128)(2,1)S(1)}, bf16[128,2048]{1,0:T(8,128)(2,1)S(1)}, u32[]{:S(2)}, u32[]{:S(2)}) collective-permute-start(bf16[128,2048]{1,0:T(8,128)(2,1)S(1)} %get-tuple-element.282), channel_id=1, source_target_pairs={{0,4},{4,0},{1,5},{5,1},{2,6},{6,2},{3,7},{7,3},{8,12},{12,8},{9,1... | collective-permute-start | bytes 1572872 | tf_op jit(solution)/shard_map/ppermute | solution.py:34
  243.7 11.8 %collective-permute-start.24 = (bf16[128,2048]{1,0:T(8,128)(2,1)S(1)}, bf16[128,2048]{1,0:T(8,128)(2,1)S(1)}, u32[]{:S(2)}, u32[]{:S(2)}) collective-permute-start(bf16[128,2048]{1,0:T(8,128)(2,1)S(1)} %get-tuple-element.283), channel_id=1, source_target_pairs={{0,2},{2,0},{1,3},{3,1},{4,6},{6,4},{5,7},{7,5},{8,10},{10,8},{9,1... | collective-permute-start | bytes 1572872 | tf_op jit(solution)/shard_map/ppermute | solution.py:34
  257.3 22.5 %collective-permute-start.25 = (bf16[256,2048]{1,0:T(8,128)(2,1)}, bf16[256,2048]{1,0:T(8,128)(2,1)S(1)}, u32[]{:S(2)}, u32[]{:S(2)}) collective-permute-start(bf16[256,2048]{1,0:T(8,128)(2,1)} %get-tuple-element.298), channel_id=1, source_target_pairs={{0,4},{4,0},{1,5},{5,1},{2,6},{6,2},{3,7},{7,3},{8,12},{12,8},{9,1... | collective-permute-start | bytes 3145736 | tf_op jit(solution)/shard_map/ppermute | solution.py:34
  258.8 22.4 %collective-permute-start.27 = (bf16[256,2048]{1,0:T(8,128)(2,1)}, bf16[256,2048]{1,0:T(8,128)(2,1)}, u32[]{:S(2)}, u32[]{:S(2)}) collective-permute-start(bf16[256,2048]{1,0:T(8,128)(2,1)} %get-tuple-element.299), channel_id=1, source_target_pairs={{0,2},{2,0},{1,3},{3,1},{4,6},{6,4},{5,7},{7,5},{8,10},{10,8},{9,1... | collective-permute-start | bytes 3145736 | tf_op jit(solution)/shard_map/ppermute | solution.py:34
  262.5 286.1 %reduce-scatter.6.cloned.1.call-start = ((), (), s32[]{:S(2)}) async-start(), calls=%async_computation.9 | async-start | bytes 5242880 | tf_op jit(solution)/shard_map/reduce_scatter | solution.py:459
  262.5 26.5 %collective-permute-start.28 = (bf16[256,2048]{1,0:T(8,128)(2,1)S(1)}, bf16[256,2048]{1,0:T(8,128)(2,1)S(1)}, u32[]{:S(2)}, u32[]{:S(2)}) collective-permute-start(bf16[256,2048]{1,0:T(8,128)(2,1)S(1)} %get-tuple-element.257), channel_id=1, source_target_pairs={{0,1},{1,0},{2,3},{3,2},{4,5},{5,4},{6,7},{7,6},{8,9},{9,8},{10,11... | collective-permute-start | bytes 3145736 | tf_op jit(solution)/shard_map/ppermute | solution.py:34
  262.6 27.5 %collective-permute-start.29 = (bf16[256,2048]{1,0:T(8,128)(2,1)}, bf16[256,2048]{1,0:T(8,128)(2,1)S(1)}, u32[]{:S(2)}, u32[]{:S(2)}) collective-permute-start(bf16[256,2048]{1,0:T(8,128)(2,1)} %get-tuple-element.297), channel_id=1, source_target_pairs={{0,1},{1,0},{2,3},{3,2},{4,5},{5,4},{6,7},{7,6},{8,9},{9,8},{10,11... | collective-permute-start | bytes 3145736 | tf_op jit(solution)/shard_map/ppermute | solution.py:34
  350.4 198.1 %reduce-scatter.8.cloned.1.call-start = ((), (), s32[]{:S(2)}) async-start(), calls=%async_computation.10 | async-start | bytes 5242880 | tf_op jit(solution)/shard_map/reduce_scatter | solution.py:459
  391.7 15.6 %collective-permute-start.34 = (bf16[1024,2048]{1,0:T(8,128)(2,1)S(1)}, bf16[1024,2048]{1,0:T(8,128)(2,1)}, u32[]{:S(2)}, u32[]{:S(2)}) collective-permute-start(bf16[1024,2048]{1,0:T(8,128)(2,1)S(1)} %add_convert_fusion), channel_id=1, source_target_pairs={{0,1},{1,0},{2,3},{3,2},{4,5},{5,4},{6,7},{7,6},{8,9},{9,8},{10,11... | collective-permute-start | bytes 12582920 | tf_op jit(solution)/shard_map/ppermute | solution.py:34
  426.3 30.5 %collective-permute-start.35 = (bf16[2,256,1024]{2,1,0:T(8,128)(2,1)}, bf16[2,256,1024]{2,1,0:T(8,128)(2,1)S(1)}, u32[]{:S(2)}, u32[]{:S(2)}) collective-permute-start(bf16[2,256,1024]{2,1,0:T(8,128)(2,1)} %slice_bitcast_fusion.19), channel_id=1, source_target_pairs={{0,2},{2,0},{1,3},{3,1},{4,6},{6,4},{5,7},{7,5},{8,10},{10,8},{9,1... | collective-permute-start | bytes 3145736 | tf_op jit(solution)/shard_map/ppermute | solution.py:34
  428.1 28.7 %collective-permute-start.36 = (bf16[2,256,1024]{2,1,0:T(8,128)(2,1)}, bf16[2,256,1024]{2,1,0:T(8,128)(2,1)S(1)}, u32[]{:S(2)}, u32[]{:S(2)}) collective-permute-start(bf16[2,256,1024]{2,1,0:T(8,128)(2,1)} %slice_bitcast_fusion.18), channel_id=1, source_target_pairs={{0,4},{4,0},{1,5},{5,1},{2,6},{6,2},{3,7},{7,3},{8,12},{12,8},{9,1... | collective-permute-start | bytes 3145736 | tf_op jit(solution)/shard_map/ppermute | solution.py:34
  442.5 168.4 %reduce-scatter.10.cloned.1.call-start = ((), (), s32[]{:S(2)}) async-start(), calls=%async_computation.11 | async-start | bytes 5242880 | tf_op jit(solution)/shard_map/reduce_scatter | solution.py:459
  466.3 21.0 %collective-permute-start.41 = (bf16[1024,2048]{1,0:T(8,128)(2,1)S(1)}, bf16[1024,2048]{1,0:T(8,128)(2,1)S(1)}, u32[]{:S(2)}, u32[]{:S(2)}) collective-permute-start(bf16[1024,2048]{1,0:T(8,128)(2,1)S(1)} %convolution_convert_fusion.3), channel_id=1, source_target_pairs={{0,1},{1,0},{2,3},{3,2},{4,5},{5,4},{6,7},{7,6},{8,9},{9,8},{10,11... | collective-permute-start | bytes 12582920 | tf_op jit(solution)/shard_map/ppermute | solution.py:34
  466.4 14.3 %collective-permute-start.38 = (bf16[256,1024]{1,0:T(8,128)(2,1)S(1)}, bf16[256,1024]{1,0:T(8,128)(2,1)S(1)}, u32[]{:S(2)}, u32[]{:S(2)}) collective-permute-start(bf16[256,1024]{1,0:T(8,128)(2,1)S(1)} %fusion.58), channel_id=1, source_target_pairs={{0,2},{2,0},{1,3},{3,1},{4,6},{6,4},{5,7},{7,5},{8,10},{10,8},{9,1... | collective-permute-start | bytes 1572872 | tf_op jit(solution)/shard_map/ppermute | solution.py:34
  467.8 14.0 %collective-permute-start.37 = (bf16[256,1024]{1,0:T(8,128)(2,1)S(1)}, bf16[256,1024]{1,0:T(8,128)(2,1)S(1)}, u32[]{:S(2)}, u32[]{:S(2)}) collective-permute-start(bf16[256,1024]{1,0:T(8,128)(2,1)S(1)} %fusion.57), channel_id=1, source_target_pairs={{0,4},{4,0},{1,5},{5,1},{2,6},{6,2},{3,7},{7,3},{8,12},{12,8},{9,1... | collective-permute-start | bytes 1572872 | tf_op jit(solution)/shard_map/ppermute | solution.py:34
  485.9 13.3 %collective-permute-start.40 = (bf16[128,2048]{1,0:T(8,128)(2,1)S(1)}, bf16[128,2048]{1,0:T(8,128)(2,1)S(1)}, u32[]{:S(2)}, u32[]{:S(2)}) collective-permute-start(bf16[128,2048]{1,0:T(8,128)(2,1)S(1)} %get-tuple-element.278), channel_id=1, source_target_pairs={{0,4},{4,0},{1,5},{5,1},{2,6},{6,2},{3,7},{7,3},{8,12},{12,8},{9,1... | collective-permute-start | bytes 1572872 | tf_op jit(solution)/shard_map/ppermute | solution.py:34
  486.6 13.0 %collective-permute-start.39 = (bf16[128,2048]{1,0:T(8,128)(2,1)S(1)}, bf16[128,2048]{1,0:T(8,128)(2,1)S(1)}, u32[]{:S(2)}, u32[]{:S(2)}) collective-permute-start(bf16[128,2048]{1,0:T(8,128)(2,1)S(1)} %get-tuple-element.279), channel_id=1, source_target_pairs={{0,2},{2,0},{1,3},{3,1},{4,6},{6,4},{5,7},{7,5},{8,10},{10,8},{9,1... | collective-permute-start | bytes 1572872 | tf_op jit(solution)/shard_map/ppermute | solution.py:34
  501.4 23.6 %collective-permute-start.42 = (bf16[256,2048]{1,0:T(8,128)(2,1)}, bf16[256,2048]{1,0:T(8,128)(2,1)S(1)}, u32[]{:S(2)}, u32[]{:S(2)}) collective-permute-start(bf16[256,2048]{1,0:T(8,128)(2,1)} %get-tuple-element.295), channel_id=1, source_target_pairs={{0,4},{4,0},{1,5},{5,1},{2,6},{6,2},{3,7},{7,3},{8,12},{12,8},{9,1... | collective-permute-start | bytes 3145736 | tf_op jit(solution)/shard_map/ppermute | solution.py:34
  502.8 23.4 %collective-permute-start.43 = (bf16[256,2048]{1,0:T(8,128)(2,1)}, bf16[256,2048]{1,0:T(8,128)(2,1)}, u32[]{:S(2)}, u32[]{:S(2)}) collective-permute-start(bf16[256,2048]{1,0:T(8,128)(2,1)} %get-tuple-element.296), channel_id=1, source_target_pairs={{0,2},{2,0},{1,3},{3,1},{4,6},{6,4},{5,7},{7,5},{8,10},{10,8},{9,1... | collective-permute-start | bytes 3145736 | tf_op jit(solution)/shard_map/ppermute | solution.py:34
  503.6 200.8 %reduce-scatter.14.cloned.1.call-start = ((), (), s32[]{:S(2)}) async-start(), calls=%async_computation.13 | async-start | bytes 1310720 | tf_op jit(solution)/shard_map/reduce_scatter | solution.py:459
  504.1 38.3 %collective-permute-start.44 = (bf16[256,2048]{1,0:T(8,128)(2,1)S(1)}, bf16[256,2048]{1,0:T(8,128)(2,1)S(1)}, u32[]{:S(2)}, u32[]{:S(2)}) collective-permute-start(bf16[256,2048]{1,0:T(8,128)(2,1)S(1)} %get-tuple-element.254), channel_id=1, source_target_pairs={{0,1},{1,0},{2,3},{3,2},{4,5},{5,4},{6,7},{7,6},{8,9},{9,8},{10,11... | collective-permute-start | bytes 3145736 | tf_op jit(solution)/shard_map/ppermute | solution.py:34
  504.2 39.3 %collective-permute-start.45 = (bf16[256,2048]{1,0:T(8,128)(2,1)}, bf16[256,2048]{1,0:T(8,128)(2,1)S(1)}, u32[]{:S(2)}, u32[]{:S(2)}) collective-permute-start(bf16[256,2048]{1,0:T(8,128)(2,1)} %get-tuple-element.294), channel_id=1, source_target_pairs={{0,1},{1,0},{2,3},{3,2},{4,5},{5,4},{6,7},{7,6},{8,9},{9,8},{10,11... | collective-permute-start | bytes 3145736 | tf_op jit(solution)/shard_map/ppermute | solution.py:34
  527.7 16.6 %collective-permute-start.46 = (bf16[512,2048]{1,0:T(8,128)(2,1)S(1)}, bf16[512,2048]{1,0:T(8,128)(2,1)S(1)}, u32[]{:S(2)}, u32[]{:S(2)}) collective-permute-start(bf16[512,2048]{1,0:T(8,128)(2,1)S(1)} %pad_maximum_fusion.5), channel_id=1, source_target_pairs={{0,1},{1,0},{2,3},{3,2},{4,5},{5,4},{6,7},{7,6},{8,9},{9,8},{10,11... | collective-permute-start | bytes 6291464 | tf_op jit(solution)/shard_map/ppermute | solution.py:34
  537.8 63.7 %collective-permute-start.49 = (bf16[2,256,1024]{2,1,0:T(8,128)(2,1)}, bf16[2,256,1024]{2,1,0:T(8,128)(2,1)}, u32[]{:S(2)}, u32[]{:S(2)}) collective-permute-start(bf16[2,256,1024]{2,1,0:T(8,128)(2,1)} %slice_bitcast_fusion.15), channel_id=1, source_target_pairs={{0,2},{2,0},{1,3},{3,1},{4,6},{6,4},{5,7},{7,5},{8,10},{10,8},{9,1... | collective-permute-start | bytes 3145736 | tf_op jit(solution)/shard_map/ppermute | solution.py:34
  539.0 62.5 %collective-permute-start.50 = (bf16[2,256,1024]{2,1,0:T(8,128)(2,1)}, bf16[2,256,1024]{2,1,0:T(8,128)(2,1)}, u32[]{:S(2)}, u32[]{:S(2)}) collective-permute-start(bf16[2,256,1024]{2,1,0:T(8,128)(2,1)} %slice_bitcast_fusion.14), channel_id=1, source_target_pairs={{0,4},{4,0},{1,5},{5,1},{2,6},{6,2},{3,7},{7,3},{8,12},{12,8},{9,1... | collective-permute-start | bytes 3145736 | tf_op jit(solution)/shard_map/ppermute | solution.py:34
  550.6 50.9 %collective-permute-start.47 = (bf16[1024,256]{1,0:T(8,128)(2,1)S(1)}, bf16[1024,256]{1,0:T(8,128)(2,1)S(1)}, u32[]{:S(2)}, u32[]{:S(2)}) collective-permute-start(bf16[1024,256]{1,0:T(8,128)(2,1)S(1)} %get-tuple-element.273), channel_id=1, source_target_pairs={{0,4},{4,0},{1,5},{5,1},{2,6},{6,2},{3,7},{7,3},{8,12},{12,8},{9,1... | collective-permute-start | bytes 1572872 | tf_op jit(solution)/shard_map/ppermute | solution.py:34
  554.0 47.5 %collective-permute-start.48 = (bf16[256,1024]{1,0:T(8,128)(2,1)S(1)}, bf16[256,1024]{1,0:T(8,128)(2,1)S(1)}, u32[]{:S(2)}, u32[]{:S(2)}) collective-permute-start(bf16[256,1024]{1,0:T(8,128)(2,1)S(1)} %get-tuple-element.277), channel_id=1, source_target_pairs={{0,4},{4,0},{1,5},{5,1},{2,6},{6,2},{3,7},{7,3},{8,12},{12,8},{9,1... | collective-permute-start | bytes 1572872 | tf_op jit(solution)/shard_map/ppermute | solution.py:34
  617.4 13.9 %collective-permute-start.52 = (bf16[1024,2048]{1,0:T(8,128)(2,1)}, bf16[1024,2048]{1,0:T(8,128)(2,1)}, u32[]{:S(2)}, u32[]{:S(2)}) collective-permute-start(bf16[1024,2048]{1,0:T(8,128)(2,1)} %convolution_convert_fusion), channel_id=1, source_target_pairs={{0,1},{1,0},{2,3},{3,2},{4,5},{5,4},{6,7},{7,6},{8,9},{9,8},{10,11... | collective-permute-start | bytes 12582920 | tf_op jit(solution)/shard_map/ppermute | solution.py:34
  620.4 97.9 %reduce-scatter.12.cloned.1.call-start = ((), (), s32[]{:S(2)}) async-start(), calls=%async_computation.12 | async-start | bytes 1966080 | tf_op jit(solution)/shard_map/reduce_scatter | solution.py:459
  624.4 14.4 %collective-permute-start.55 = (bf16[256,1024]{1,0:T(8,128)(2,1)S(1)}, bf16[256,1024]{1,0:T(8,128)(2,1)S(1)}, u32[]{:S(2)}, u32[]{:S(2)}) collective-permute-start(bf16[256,1024]{1,0:T(8,128)(2,1)S(1)} %fusion.60), channel_id=1, source_target_pairs={{0,2},{2,0},{1,3},{3,1},{4,6},{6,4},{5,7},{7,5},{8,10},{10,8},{9,1... | collective-permute-start | bytes 1572872 | tf_op jit(solution)/shard_map/ppermute | solution.py:34
  625.8 14.8 %collective-permute-start.54 = (bf16[256,1024]{1,0:T(8,128)(2,1)S(1)}, bf16[256,1024]{1,0:T(8,128)(2,1)S(1)}, u32[]{:S(2)}, u32[]{:S(2)}) collective-permute-start(bf16[256,1024]{1,0:T(8,128)(2,1)S(1)} %fusion.59), channel_id=1, source_target_pairs={{0,4},{4,0},{1,5},{5,1},{2,6},{6,2},{3,7},{7,3},{8,12},{12,8},{9,1... | collective-permute-start | bytes 1572872 | tf_op jit(solution)/shard_map/ppermute | solution.py:34
  630.5 20.7 %collective-permute-start.53 = (bf16[256,1024]{1,0:T(8,128)(2,1)S(1)}, bf16[256,1024]{1,0:T(8,128)(2,1)S(1)}, u32[]{:S(2)}, u32[]{:S(2)}) collective-permute-start(bf16[256,1024]{1,0:T(8,128)(2,1)S(1)} %get-tuple-element.275), channel_id=1, source_target_pairs={{0,4},{4,0},{1,5},{5,1},{2,6},{6,2},{3,7},{7,3},{8,12},{12,8},{9,1... | collective-permute-start | bytes 1572872 | tf_op jit(solution)/shard_map/ppermute | solution.py:34
  653.0 24.8 %collective-permute-start.56 = (bf16[2,256,1024]{2,1,0:T(8,128)(2,1)}, bf16[2,256,1024]{2,1,0:T(8,128)(2,1)}, u32[]{:S(2)}, u32[]{:S(2)}) collective-permute-start(bf16[2,256,1024]{2,1,0:T(8,128)(2,1)} %slice_bitcast_fusion.11), channel_id=1, source_target_pairs={{0,2},{2,0},{1,3},{3,1},{4,6},{6,4},{5,7},{7,5},{8,10},{10,8},{9,1... | collective-permute-start | bytes 3145736 | tf_op jit(solution)/shard_map/ppermute | solution.py:34
  654.8 24.5 %collective-permute-start.57 = (bf16[2,256,1024]{2,1,0:T(8,128)(2,1)}, bf16[2,256,1024]{2,1,0:T(8,128)(2,1)}, u32[]{:S(2)}, u32[]{:S(2)}) collective-permute-start(bf16[2,256,1024]{2,1,0:T(8,128)(2,1)} %slice_bitcast_fusion.10), channel_id=1, source_target_pairs={{0,4},{4,0},{1,5},{5,1},{2,6},{6,2},{3,7},{7,3},{8,12},{12,8},{9,1... | collective-permute-start | bytes 3145736 | tf_op jit(solution)/shard_map/ppermute | solution.py:34
  683.0 12.1 %collective-permute-start.59 = (bf16[256,1024]{1,0:T(8,128)(2,1)S(1)}, bf16[256,1024]{1,0:T(8,128)(2,1)S(1)}, u32[]{:S(2)}, u32[]{:S(2)}) collective-permute-start(bf16[256,1024]{1,0:T(8,128)(2,1)S(1)} %fusion.62), channel_id=1, source_target_pairs={{0,2},{2,0},{1,3},{3,1},{4,6},{6,4},{5,7},{7,5},{8,10},{10,8},{9,1... | collective-permute-start | bytes 1572872 | tf_op jit(solution)/shard_map/ppermute | solution.py:34
  684.4 11.8 %collective-permute-start.58 = (bf16[256,1024]{1,0:T(8,128)(2,1)S(1)}, bf16[256,1024]{1,0:T(8,128)(2,1)S(1)}, u32[]{:S(2)}, u32[]{:S(2)}) collective-permute-start(bf16[256,1024]{1,0:T(8,128)(2,1)S(1)} %fusion.61), channel_id=1, source_target_pairs={{0,4},{4,0},{1,5},{5,1},{2,6},{6,2},{3,7},{7,3},{8,12},{12,8},{9,1... | collective-permute-start | bytes 1572872 | tf_op jit(solution)/shard_map/ppermute | solution.py:34
  (83 other events, 1236.8 us)
Sparse Core Ops, SparseCore 0:
  21.9 56.2 all-gather.4
  84.2 83.8 all-gather.6
  170.0 83.8 all-gather.8
  262.6 83.2 all-gather.10
  350.5 74.2 reduce-scatter.5
  442.6 76.1 reduce-scatter.7
  521.1 77.2 reduce-scatter.9
  620.5 25.8 reduce-scatter.13
  664.4 33.6 reduce-scatter.11

commit v3 on v2

--- a/solution.py
+++ b/solution.py
@@ -1,3 +1,5 @@
+import functools
+
 import jax
 import jax.numpy as jnp
 from jax import lax
@@ -24,6 +26,7 @@
 EVERY = ("z", "y", "x", "c")
 F32 = jnp.float32
 BF16 = jnp.bfloat16
+FREE = pl.CostEstimate(flops=0, bytes_accessed=0, transcendentals=0)
 
 
 def rounded(x):
@@ -67,42 +70,159 @@
 
 
 def gather_one(v):
-    half = v.shape[0] // 2
-    return v, swap(v, "c"), swap(v[:half], "x"), swap(v[half:], "y")
+    half = v.shape[1] // 2
+    return v, swap(v, "c"), swap(v[:, :half], "x"), swap(v[:, half:], "y")
 
 
 def gather_two(state):
     v, near, a01, b10 = state
-    half = v.shape[0] // 2
-    a1 = swap(jnp.concatenate((v[:half], a01)), "y")
-    b1 = swap(jnp.concatenate((v[half:], b10)), "x")
+    half = v.shape[1] // 2
+    a1 = swap(jnp.concatenate((v[:, :half], a01)), "y")
+    b1 = swap(jnp.concatenate((v[:, half:], b10)), "x")
     second = swap(jnp.concatenate((a01, b10)), "c")
     return v, near, a01, b10, second, a1, b1
 
 
 def gather_three(state):
-    v, near, a01, b10, second, a1, b1 = state
-    half = v.shape[0] // 2
-    third = swap(jnp.concatenate((a1, b1)), "c")
-
-    def block(own, one, two):
-        return (own, one[:half], two[2 * half : 3 * half], two[:half], one[half:],
-                two[half : 2 * half], two[3 * half :])
-
-    own = (v, a01, b1[:half], a1[:half], b10, a1[half:], b1[half:])
-    return jnp.concatenate(own + block(near, second, third))
-
-
-def fold_rows(low, high):
-    return low() + swap(high().astype(BF16), "c").astype(F32)
-
-
-def spread_one(total):
-    rows, cols = total.shape[0] // 4, total.shape[1] // 2
-    blocks = total.reshape(2, 2, rows, 2 * cols)
-    left, right = blocks[..., :cols], blocks[..., cols:]
-    send_x, send_y = left[:, 1].astype(BF16), right[1].astype(BF16)
-    return left[:, 0], right[0], swap(send_x, "x"), swap(send_y, "y"), (send_x, send_y)
+    size, half = state[0].shape[0], state[0].shape[1] // 2
+    state = (state[0], *tie(*state[1:]))
+    third = swap(jnp.concatenate(state[5:]), "c")
+    spots = (
+        (0, 0, size, 0, 0), (1, 0, size, 4 * size, 0), (2, 0, size, size, 0),
+        (3, 0, size, 2 * size, half), (4, 0, size, 5 * size, 0),
+        (4, size, size, 6 * size, half), (5, 0, 2 * size, 2 * size, 0),
+        (6, 0, size, size, half), (6, size, size, 3 * size, half),
+        (7, 0, 2 * size, 6 * size, 0), (7, 2 * size, size, 5 * size, half),
+        (7, 3 * size, size, 7 * size, half),
+    )
+    return place((*state, third), spots, 8 * size)
+
+
+def place_kernel(spots, *refs):
+    pieces, (out, sems) = refs[:-2], refs[-2:]
+    copies = []
+    for at, (piece, start, size, row, col) in enumerate(spots):
+        source = pieces[piece]
+        copies.append(
+            pltpu.make_async_copy(
+                source.at[pl.ds(start, size), :],
+                out.at[pl.ds(row, size), pl.ds(col, source.shape[1])],
+                sems.at[at],
+            )
+        )
+    for copy in copies:
+        copy.start()
+    for copy in copies:
+        copy.wait()
+
+
+def place(pieces, spots, count):
+    return pl.pallas_call(
+        functools.partial(place_kernel, spots),
+        out_shape=jax.ShapeDtypeStruct((count, pieces[0].shape[1]), BF16),
+        in_specs=[pl.BlockSpec(memory_space=pltpu.VMEM)] * len(pieces),
+        out_specs=pl.BlockSpec(memory_space=pltpu.HBM),
+        scratch_shapes=[pltpu.SemaphoreType.DMA((len(spots),))],
+        compiler_params=pltpu.CompilerParams(vmem_limit_bytes=60 * 2**20),
+        cost_estimate=FREE,
+        name="place",
+    )(*pieces)
+
+
+def product_kernel(terms, keep, *refs):
+    count = len(terms)
+    step = pl.program_id(0)
+    flipped = sum(term[0] == 0 for term in terms)
+    scratch = refs[len(refs) - flipped :]
+    total, used = None, 0
+    for at, (left_dim, right_dim, cut) in enumerate(terms):
+        left, right = refs[2 * at], refs[2 * at + 1]
+        if left_dim == 0:
+            store = scratch[used]
+            used += 1
+
+            @pl.when(step == 0)
+            def _(left=left, store=store):
+                store[...] = upright(left[...])
+
+            left = store
+        block = right[...] if cut is None else right[:, cut[0] : cut[1]]
+        one = dot(left[...], block, 1, right_dim)
+        total = one if total is None else total + one
+    if not keep:
+        refs[2 * count][...] = total.astype(BF16)
+        return
+    came, left_out, right_out, x_out, y_out = refs[2 * count : 2 * count + 5]
+    total = total + came[...].astype(F32)
+    blocks = total.reshape(2, 2, total.shape[0] // 4, total.shape[1])
+    half = pl.num_programs(0) // 2
+
+    @pl.when(step < half)
+    def _():
+        left_out[...] = blocks[:, 0]
+        x_out[...] = blocks[:, 1].astype(BF16)
+
+    @pl.when(step >= half)
+    def _():
+        right_out[...] = blocks[0]
+        y_out[...] = blocks[1].astype(BF16)
+
+
+def product(terms, part, came=None):
+    tile = 512
+    args, specs, kinds, scratch = [], [], [], []
+    for left, right, left_dim, right_dim, cut, *block in terms:
+        rows = left.shape[1 - left_dim] // 2
+        depth = left.shape[left_dim]
+        if left_dim == 1:
+            specs.append(pl.BlockSpec((rows, depth), lambda n: (part, 0)))
+        else:
+            specs.append(pl.BlockSpec((depth, rows), lambda n: (0, part)))
+            scratch.append(pltpu.VMEM((rows, depth), BF16))
+        if right_dim == 1:
+            width = right.shape[0]
+            if block:
+                specs.append(pl.BlockSpec((tile, depth), lambda n, at=block[0]: (n, at)))
+            else:
+                specs.append(pl.BlockSpec((tile, right.shape[1]), lambda n: (n, 0)))
+        else:
+            width = right.shape[1]
+            specs.append(pl.BlockSpec((right.shape[0], tile), lambda n: (0, n)))
+        args += [left, right]
+        kinds.append((left_dim, right_dim, cut))
+    if came is None:
+        out_shape = jax.ShapeDtypeStruct((rows, width), BF16)
+        out_specs = pl.BlockSpec((rows, tile), lambda n: (0, n))
+    else:
+        args.append(came)
+        specs.append(pl.BlockSpec((rows, tile), lambda n: (0, n)))
+        half = width // tile // 2
+        shape = (2, rows // 4, width // 2)
+        out_shape = [jax.ShapeDtypeStruct(shape, d) for d in (F32, F32, BF16, BF16)]
+        first = pl.BlockSpec((2, rows // 4, tile), lambda n: (0, 0, jnp.minimum(n, half - 1)))
+        last = pl.BlockSpec((2, rows // 4, tile), lambda n: (0, 0, jnp.maximum(n - half, 0)))
+        out_specs = [first, last, first, last]
+    return pl.pallas_call(
+        functools.partial(product_kernel, kinds, came is not None),
+        out_shape=out_shape,
+        grid=(width // tile,),
+        in_specs=specs,
+        out_specs=out_specs,
+        scratch_shapes=scratch,
+        compiler_params=pltpu.CompilerParams(vmem_limit_bytes=56 * 2**20),
+        cost_estimate=pl.CostEstimate(
+            flops=2 * sum(t[0].size for t in terms) // 2 * width,
+            bytes_accessed=2 * sum(t[0].size for t in terms) + 2 * rows * width,
+            transcendentals=0,
+        ),
+        name="product",
+    )(*args)
+
+
+def spread_one(terms, came=None):
+    came = swap(product(terms, 1), "c") if came is None else came
+    left, right, send_x, send_y = product(terms, 0, came)
+    return left, right, swap(send_x, "x"), swap(send_y, "y"), (send_x, send_y)
 
 
 def spread_two(state):
@@ -352,9 +472,86 @@
         out_specs=[spec] * len(outs),
         scratch_shapes=[pltpu.VMEM(s, d) for s, d in scratch],
         compiler_params=pltpu.CompilerParams(vmem_limit_bytes=40 * 2**20),
-        cost_estimate=pl.CostEstimate(flops=0, bytes_accessed=0, transcendentals=0),
+        cost_estimate=FREE,
         name=name,
     )(info, *args)
+
+
+def hidden_kernel(rows, gate_w, up_w, gate_out, up_out, hidden_out):
+    gate, up = dot(rows[...], gate_w[...], 1, 0), dot(rows[...], up_w[...], 1, 0)
+    gate_out[...], up_out[...] = gate, up
+    hidden_out[...] = (gate * jax.nn.sigmoid(gate) * up).astype(BF16)
+
+
+def hidden_back_kernel(rows, weights, gates, ups, gate_out, up_out):
+    grad = dot(rows[...], weights[...], 1, 1)
+    gate = gates[...]
+    sig = jax.nn.sigmoid(gate)
+    gate_out[...] = (grad * ups[...] * sig * (1.0 + gate * (1.0 - sig))).astype(BF16)
+    up_out[...] = (grad * gate * sig).astype(BF16)
+
+
+def ffn_call(kernel, rows, weights, width, kinds, held, name):
+    high, wide = min(512, rows.shape[0]), min(512, width)
+    depth, steps = rows.shape[1], width // wide
+    tile = pl.BlockSpec((high, wide), lambda n, m: (m, n))
+    if held:
+        specs = [pl.BlockSpec((wide, depth), lambda n, m: (n, 0))]
+    else:
+        specs = [pl.BlockSpec((depth, wide), lambda n, m: (0, n)),
+                 pl.BlockSpec((depth, wide), lambda n, m: (0, n + steps))]
+    return pl.pallas_call(
+        kernel,
+        out_shape=[jax.ShapeDtypeStruct((rows.shape[0], width), kind) for kind in kinds],
+        grid=(steps, rows.shape[0] // high),
+        in_specs=[pl.BlockSpec((high, depth), lambda n, m: (m, 0))] + specs + [tile] * len(held),
+        out_specs=[tile] * len(kinds),
+        compiler_params=pltpu.CompilerParams(vmem_limit_bytes=56 * 2**20),
+        cost_estimate=FREE,
+        name=name,
+    )(rows, *([weights] * len(specs)), *held)
+
+
+def outer_kernel(right_dim, left, right, out):
+    out[...] = dot(left[...], right[...], 0, right_dim).astype(BF16)
+
+
+def outer_gain_kernel(right_dim, cut, left, right, weights, out, gain):
+    total = dot(left[...], right[...], 0, right_dim)
+    out[...] = total.astype(BF16)
+    scaled = total * weights[:, cut[0] : cut[1]].astype(F32)
+    gain[...] = jnp.broadcast_to(jnp.sum(scaled, axis=1, keepdims=True), gain.shape)
+
+
+def outer(left, right, right_dim, weights=None, cut=None):
+    depth, high = left.shape
+    wide = right.shape[1 - right_dim]
+    rows, cols = min(512, high), min(1024, wide)
+    right_block = (depth, cols) if right_dim == 0 else (cols, depth)
+    right_map = (lambda n, m: (0, n)) if right_dim == 0 else (lambda n, m: (n, 0))
+    specs = [pl.BlockSpec((depth, rows), lambda n, m: (0, m)), pl.BlockSpec(right_block, right_map)]
+    outs = [jax.ShapeDtypeStruct((high, wide), BF16)]
+    out_specs = [pl.BlockSpec((rows, cols), lambda n, m: (m, n))]
+    args, kernel = (left, right), functools.partial(outer_kernel, right_dim)
+    if weights is not None:
+        args, kernel = (left, right, weights), functools.partial(outer_gain_kernel, right_dim, cut)
+        specs.append(pl.BlockSpec((rows, weights.shape[1]), lambda n, m: (m, 0)))
+        outs.append(jax.ShapeDtypeStruct((high, 128), F32))
+        out_specs.append(pl.BlockSpec((rows, 128), lambda n, m: (m, 0)))
+    return pl.pallas_call(
+        kernel,
+        out_shape=outs,
+        grid=(wide // cols, high // rows),
+        in_specs=specs,
+        out_specs=out_specs,
+        compiler_params=pltpu.CompilerParams(vmem_limit_bytes=56 * 2**20),
+        cost_estimate=pl.CostEstimate(
+            flops=2 * depth * high * wide,
+            bytes_accessed=2 * (depth * (high + wide) + high * wide),
+            transcendentals=0,
+        ),
+        name="outer",
+    )(*args)
 
 
 def norm_back(values, scale, upstream):
@@ -384,76 +581,78 @@
     cos, sin = jnp.cos(angles), jnp.sin(angles)
     def heads_part(which):
         return jnp.concatenate(
-            (half_of(w_query, which, 1), half_of(w_key, which, 1), half_of(w_value, which, 1),
-             half_of(w_out, which, 0).T), 1
+            (half_of(w_out, which, 0).T, half_of(w_query, which, 1), half_of(w_key, which, 1),
+             half_of(w_value, which, 1)), 1
         )
+
+    def ffn_part(which):
+        return jnp.concatenate((half_of(w_gate, which, 1), half_of(w_up, which, 1)), 1)
 
     other_y = 1 - y_rank
     heads_w = ordered(heads_part(y_rank), swap(heads_part(other_y), "y"), y_rank, 0)
     full_heads = lax.all_gather(heads_w, "z", axis=0, tiled=True)
-    qkv_cols = V_AT + HD
-
+    out_cols = HEADS * HD
+    heads_cut = (out_cols, full_heads.shape[1])
+
+    ffn_other = swap(after(ffn_part(other_y), heads_w), "y")
+    ffn_w = ordered(ffn_part(y_rank), ffn_other, y_rank, 0)
     layer_f = layer_in.astype(F32)
     scale_one = lax.rsqrt(jnp.mean(layer_f * layer_f, axis=1, keepdims=True) + EPSILON)
     normal_one = rounded(layer_f * scale_one)
     gain_one = attn_gain.astype(F32)
     acts = gather_one(after((normal_one * gain_one[None, :]).astype(BF16), heads_w))
     acts = gather_two(acts)
-    gate_other = swap(after(half_of(w_gate, other_y, 1), acts[2], acts[3]), "y")
-    full_heads, *got = tie(full_heads, *acts[5:], gate_other)
-    gate_other = got[2]
-    full_qkv, full_out = full_heads[:, :qkv_cols], full_heads[:, qkv_cols:]
-    acts_one = gather_three((*acts[:5], *got[:2]))
-    gate_w = ordered(half_of(w_gate, y_rank, 1), gate_other, y_rank, 0)
-    full_gate = lax.all_gather(gate_w, "z", axis=0, tiled=True)
-    up_other = swap(after(half_of(w_up, other_y, 1), gate_w), "y")
+    full_heads, ffn_w, *acts = tie(full_heads, ffn_w, *acts)
+    full_out, full_qkv = full_heads[:, :out_cols], full_heads[:, out_cols:]
+    acts_one = gather_three(acts)
+    full_ffn = lax.all_gather(ffn_w, "z", axis=0, tiled=True)
 
     grad_out = cotangent.astype(F32)
     down_in = (RESIDUAL * own_mask * grad_out).astype(BF16)
-    back_rows = gather_one(after(down_in, gate_w))
+    back_rows = gather_one(after(down_in, ffn_other))
     rows = acts_one.shape[0]
-    half_rows = rows // 2
     flat = dot(full_qkv, acts_one, 0, 1)
     (qkv,) = call(
         rope_kernel, info, (flat, cos, sin), [((flat.shape[0], rows), BF16)], [], "rope"
     )
     halo = along(qkv[K_AT:, SLOT_LEN - LEAD :], 1)
-    qkv, halo, up_other, *back_rows = tie(qkv, halo, up_other, *back_rows)
-    up_w = ordered(half_of(w_up, y_rank, 1), up_other, y_rank, 0)
-    full_up = lax.all_gather(up_w, "z", axis=0, tiled=True)
+    qkv, halo, *back_rows = tie(qkv, halo, *back_rows)
+    down_other = swap(after(half_of(w_down, other_y, 0), back_rows[2], back_rows[3]), "y")
     back_rows = gather_two(back_rows)
-    down_other = swap(after(half_of(w_down, other_y, 0), back_rows[2], back_rows[3]), "y")
     heads, lse, peak = call(
         attend_kernel, info, (qkv, halo),
         [((HEADS * HD, rows), BF16), ((8, rows), F32), ((8, 128), F32)],
         [((KEYS, HD), BF16), ((HD, KEYS), BF16), ((SLOT_LEN, CHUNK), F32)],
         "attend",
     )
-    heads, down_other, up_w, *back_rows = tie(heads, down_other, up_w, *back_rows)
+    heads, down_other, *back_rows = tie(heads, down_other, *back_rows)
     down_w = ordered(half_of(w_down, y_rank, 0), down_other, y_rank, 1)
+
+    terms = [(heads, full_heads, 0, 1, (0, out_cols))]
+    own_peak = peak[:HEADS]
+    came, other_peak = tie(swap(product(terms, 1), "c"), swap(own_peak, "y"))
+    branch = spread_one(terms, came)
+    head_peak = after(ordered(own_peak, other_peak, y_rank, 0), *branch[4])
+    head_peak = over_z(head_peak, jnp.maximum)
+    down_rows = gather_three((*back_rows[:5], *after(back_rows[5:], *branch[4])))
+    *got, down_rows, down_w, head_peak = tie(*branch[2:4], down_rows, down_w, head_peak)
+    head_peak = head_peak[:, 0]
+    branch = spread_two((*branch[:2], *got))
     full_down = lax.all_gather(down_w, "z", axis=1, tiled=True)
-
-    branch = fold_rows(
-        lambda: dot(heads[:, :half_rows], full_out, 0, 1),
-        lambda: dot(heads[:, half_rows:], full_out, 0, 1),
-    )
-    branch = spread_one(branch)
-    down_rows = gather_three((*back_rows[:5], *after((back_rows[5], back_rows[6]), branch[4])))
-    *got, down_rows, full_gate = tie(*branch[2:4], down_rows, full_gate)
-    branch = spread_two((*branch[:2], *got))
     branch_one = spread_three(branch)
     resid = layer_f + RESIDUAL * own_mask * branch_one
     scale_two = lax.rsqrt(jnp.mean(resid * resid, axis=1, keepdims=True) + EPSILON)
     normal_two = rounded(resid * scale_two)
     gain_two = mlp_gain.astype(F32)
-    acts = gather_two(gather_one((normal_two * gain_two[None, :]).astype(BF16)))
-    acts_two = gather_three((*acts[:5], *after((acts[5], acts[6]), down_w)))
-    acts_two, full_up = tie(acts_two, full_up)
-
-    gate_proj = dot(acts_two, full_gate, 1, 0)
-    up_proj = dot(acts_two, full_up, 1, 0)
-    sigmoid_gate = jax.nn.sigmoid(gate_proj)
-    hidden = (gate_proj * sigmoid_gate * up_proj).astype(BF16)
+    acts = gather_one((normal_two * gain_two[None, :]).astype(BF16))
+    full_ffn, *acts = tie(full_ffn, *acts)
+    acts = gather_two(acts)
+    acts_two = gather_three(acts)
+
+    width = full_ffn.shape[1] // 2
+    gate_proj, up_proj, hidden = ffn_call(
+        hidden_kernel, acts_two, full_ffn, width, (F32, F32, BF16), (), "hidden"
+    )
 
     def reduced(grad, axis):
         return lax.psum_scatter(grad, "z", scatter_dimension=axis, tiled=True)
@@ -462,51 +661,36 @@
         total = after(total, *behind)
         return half_of(total, y_rank, axis), swap(half_of(total, other_y, axis), "y")
 
-    down_part = dot(hidden, down_rows, 0, 0).astype(BF16)
+    (down_part,) = outer(hidden, down_rows, 0)
     down_sum = reduced(down_part, 1)
-    own_peak = jnp.max(after(peak, down_part)[:HEADS], axis=1, keepdims=True)
-    own_peak = jnp.broadcast_to(own_peak, (HEADS, 128))
-    head_peak = over_z(ordered(own_peak, swap(own_peak, "y"), y_rank, 0), jnp.maximum)
-    down_rows, head_peak = tie(down_rows, head_peak)
-    head_peak = head_peak[:, 0]
-    hidden_grad = dot(down_rows, full_down, 1, 1)
-    gate_grad = (
-        hidden_grad * up_proj * sigmoid_gate * (1.0 + gate_proj * (1.0 - sigmoid_gate))
-    ).astype(BF16)
-    up_grad = (hidden_grad * gate_proj * sigmoid_gate).astype(BF16)
-
-    def acts_two_back(part):
-        return dot(gate_grad[part], full_gate, 1, 1) + dot(up_grad[part], full_up, 1, 1)
-
+    down_rows = after(down_rows, down_part)
+    gate_grad, up_grad = ffn_call(
+        hidden_back_kernel, down_rows, full_down, width, (BF16, BF16), (gate_proj, up_proj),
+        "hidden_back",
+    )
     norm_two = spread_one(
-        fold_rows(
-            lambda: acts_two_back(slice(None, half_rows)),
-            lambda: acts_two_back(slice(half_rows, None)),
-        )
-    )
-    held = after(acts_two, *norm_two[4])
-    gate_part = dot(held, gate_grad, 0, 0).astype(BF16)
-    up_part = dot(held, up_grad, 0, 0).astype(BF16)
-    gate_sum, up_sum = reduced(gate_part, 0), reduced(up_part, 0)
-    got = tie(*norm_two[2:4], gate_part, up_part)[:2]
+        [(gate_grad, full_ffn, 1, 1, None, 0), (up_grad, full_ffn, 1, 1, None, 1)]
+    )
+    held = after(acts_two, swap(norm_two[4][0][0, :8, :128], "c"))
+    ffn_parts = [outer(held, grad, 0)[0] for grad in (gate_grad, up_grad)]
+    one_sum, two_sum = [reduced(part, 0) for part in ffn_parts]
+    got = tie(*norm_two[2:4], *ffn_parts)[:2]
     norm_two = spread_two((*norm_two[:2], *got))
     held = after(hidden, *norm_two[4])
-    high_part = dot(held[half_rows:], full_down, 1, 0).astype(BF16)
+    high_part = product([(held, full_down, 1, 0, None)], 1)
     got = tie(*norm_two[2:4], high_part)[:2]
     norm_two_grad = spread_three((*norm_two[:2], *got))
     grad_resid = grad_out + norm_back(resid, scale_two, gain_two[None, :] * norm_two_grad)
     mixed = gather_one((RESIDUAL * own_mask * grad_resid).astype(BF16))
-    held = after(hidden, mixed[0])
-    folded = fold_rows(lambda: dot(held[:half_rows], full_down, 1, 0), lambda: high_part)
+    low_part = product([(after(hidden, mixed[0]), full_down, 1, 0, None)], 0, swap(high_part, "c"))
     gain_two_part = jnp.sum(normal_two * norm_two_grad, axis=0)
-    got = tie(*mixed[2:4], folded, gain_two_part)
-    folded, gain_two_part = got[2:]
-    mixed = gather_two((*mixed[:2], *got[:2]))
+    *got, gain_two_part = tie(*mixed[2:4], gain_two_part, *low_part)[:3]
+    mixed = gather_two((*mixed[:2], *got))
+    send_x, send_y = after(low_part[2:], *mixed[1:])
+    second = (*low_part[:2], swap(send_x, "x"), swap(send_y, "y"))
     mixed_rows = gather_three(mixed)
-    mixed_rows, down_sum, gate_sum = tie(mixed_rows, down_sum, gate_sum)
-    second = spread_one(after(folded, mixed[5], mixed[6]))
+    mixed_rows, down_sum = tie(mixed_rows, down_sum)
     down_own, down_other = traded(down_sum, 1)
-    gate_own, gate_other = traded(gate_sum, 0)
 
     heads_grad = dot(full_out, mixed_rows, 0, 1).astype(BF16)
     dq, dkv, back = call(
@@ -517,33 +701,32 @@
          ((KEYS, HD), F32), ((KEYS, HD), F32), ((HEADS * HD, SLOT_LEN), BF16)],
         "attend_back",
     )
-    back, down_other, gate_other, *got = tie(back, down_other, gate_other, *second[2:4])
+    back, down_other, *got = tie(back, down_other, *second[2:4])
     back_sent = along(back, -1)
     second = spread_two((*second[:2], *got))
-    out_part = dot(after(mixed_rows, back), heads, 0, 1).astype(BF16)
+    (out_part,) = outer(after(mixed_rows, back), heads, 1)
     out_sum = reduced(out_part, 0)
-    dkv, back_sent, out_part, up_sum = tie(dkv, back_sent, out_part, up_sum)
-    up_own, up_other = traded(up_sum, 0)
+    dkv, back_sent, out_part, one_sum = tie(dkv, back_sent, out_part, one_sum)
+    one_own, one_other = traded(one_sum, 0)
     (dkv_done,) = call(
         finish_kernel, info, (dkv, back_sent, cos, sin), [((2 * HD, rows), BF16)], [], "finish"
     )
     dqkv = jnp.concatenate((dq, dkv_done))
-    folded = fold_rows(
-        lambda: dot(dqkv[:, :half_rows], full_qkv, 0, 1),
-        lambda: dot(dqkv[:, half_rows:], full_qkv, 0, 1),
-    )
-    folded, up_other, *got = tie(folded, up_other, *second[2:4])
+    terms = [(dqkv, full_heads, 0, 1, heads_cut)]
+    came = swap(product(terms, 1), "c")
+    came, out_sum, two_sum, one_other, *got = tie(came, out_sum, two_sum, one_other, *second[2:4])
     branch_two = spread_three((*second[:2], *got))
     result = resid + RESIDUAL * own_mask * branch_two
 
-    norm_one = spread_one(folded)
-    part = dot(after(acts_one, *norm_one[4]), dqkv, 0, 1)
-    gain_one_part = jnp.sum(part * full_qkv.astype(F32), axis=1) / gain_one
-    qkv_part = part.astype(BF16)
+    norm_one = spread_one(terms, came)
+    qkv_part, sums = outer(after(acts_one, *norm_one[4]), dqkv, 1, full_heads, heads_cut)
+    gain_one_part = sums[:, 0] / gain_one
     qkv_sum = reduced(qkv_part, 0)
     *got, gain_one_part = tie(*norm_one[2:4], gain_one_part, qkv_part)[:3]
     norm_one = spread_two((*norm_one[:2], *got))
+    two_own, two_other = traded(two_sum, 0, *norm_one[4])
     norm_one_grad = spread_three(norm_one)
+    norm_one_grad, qkv_sum = tie(norm_one_grad, qkv_sum)
     grad_input = grad_resid + norm_back(layer_f, scale_one, gain_one[None, :] * norm_one_grad)
     gain_one_part = after(gain_one_part, norm_one_grad)
     out_own, out_other = traded(out_sum, 0, norm_one_grad)
@@ -558,8 +741,8 @@
     gains = lax.dynamic_index_in_dim(over_z(gains, jnp.add), z_rank, 1, keepdims=False)
 
     down_grad = ordered(down_own, down_other, y_rank, 0).astype(F32)
-    gate_w_grad = ordered(gate_own, gate_other, y_rank, 1).astype(F32)
-    up_w_grad = ordered(up_own, up_other, y_rank, 1).astype(F32)
+    gate_w_grad = ordered(one_own, one_other, y_rank, 1).astype(F32)
+    up_w_grad = ordered(two_own, two_other, y_rank, 1).astype(F32)
     out_grad = ordered(out_own.T, out_other.T, y_rank, 0).astype(F32)
 
     def columns(start, stop):

time: 739 us -> 722 us (0.977)
  Pallas kernels: 70.8 us -> 279 us
  matrix products: 181 us -> 12.2 us
  local copies, waits for them, and re-layouts: 108 us -> 34.9 us
  waiting for transfers between devices: 195 us -> 238 us
  other arithmetic: 88.8 us -> 71.2 us
  starting transfers between devices: 74.3 us -> 61.2 us
    pallas_call x0 -> x19, Pallas kernels: none -> 208 us  [the longest x8 76.7 us: product(): pl.pallas_call(functools.partial(product_kernel, kinds, came is not None)...]
    dot_general x20 -> x2, matrix products: 181 us -> 12.2 us  [dot(): lax.dot_general(left, right, (((left_dim,), (right_dim,)), ((), ())), pre...]
    unnamed x203 -> x132, local copies, waits for them, and re-layouts: 77.9 us -> 11.6 us
    ppermute x61 -> x60, waiting for transfers between devices: 176 us -> 212 us  [swap(): return lax.ppermute(x, axis, [(0, 1), (1, 0)])]
    all_gather x1, starting transfers between devices: 11.7 us -> 0.04 us  [shards(): full_down = lax.all_gather(down_w, 'z', axis=1, tiled=True)]
    another operation x4 -> x0, other arithmetic: 9.7 us -> none
    add x1 -> x4, other arithmetic: 13.6 us -> 4.13 us  [spread_two(): right = right + right_y.astype(F32)]
    convert_element_type x8 -> x0, local copies, waits for them, and re-layouts: 8.53 us -> none  [spread_one(): send_x, send_y = (left[:, 1].astype(BF16), right[1].astype(BF16))]
  transfers between devices with their start and end apart: 76 -> 74, of which waited for: 35 -> 44; matrix products, arithmetic and copies ran while one was open for 49% -> 13% of each run, Pallas kernels for 10% -> 38%
where the time goes in v3:
time: 722 us; the launch traced here: 713 us
  Pallas kernels  279 us (39%)
  waiting for transfers between devices  238 us (33%)
  other arithmetic  71.2 us (10%)
  starting transfers between devices  61.2 us (8%)
  local copies, waits for them, and re-layouts  34.9 us (5%)
  between operations  16.4 us (2%)
  matrix products  12.2 us (2%)
    ppermute x60, waiting for transfers between devices, swap(): return lax.ppermute(x, axis, [(0, 1), (1, 0)])  212 us
    pallas_call x8, Pallas kernels, product(): pl.pallas_call(functools.partial(product_kernel, kinds, came is not None)...  76.7 us
    pallas_call x4, Pallas kernels, call(): pl.pallas_call(kernel, out_shape=[jax.ShapeDtypeStruct(s, d) for s, d in...  70.7 us
    pallas_call x5, Pallas kernels, outer(): pl.pallas_call(kernel, out_shape=outs, grid=(wide // cols, high // rows),...  56.6 us
    ppermute x60, starting transfers between devices, swap(): return lax.ppermute(x, axis, [(0, 1), (1, 0)])  49.7 us
    pallas_call x2, Pallas kernels, ffn_call(): pl.pallas_call(kernel, out_shape=[jax.ShapeDtypeStruct((rows.shape[0], wi...  46.2 us
    pallas_call x4, Pallas kernels, place(): pl.pallas_call(functools.partial(place_kernel, spots), out_shape=jax.Shap...  28.6 us
    ppermute x6, waiting for transfers between devices, along(): return lax.ppermute(x, 'z', [(i, (i + by) % peers) for i in range(peers)])  25.7 us
  transfers between devices with their start and end apart: 74, of which 44 were waited for; matrix products, arithmetic and copies ran while one was open for 13% of the time, Pallas kernels for 38%

profile of v3, /device:TPU:0, one launch (start us, length us, event | category | flops | bytes accessed | tf_op | source)
XLA Modules:
  0.0 712.7 jit_solution(8011357691146659356)
XLA Ops:
  9.8 3.0 collective-permute-start
  12.9 7.6 %collective-permute-done = bf16[256,640]{1,0:T(8,128)(2,1)S(1)} collective-permute-done((bf16[256,640]{1,0:T(8,128)(2,1)S(1)}, bf16[256,640]{1,0:T(8,128)(2,1)S(1)}, u32[]{:S(2)}, u32[]{:S(2)}) %collective-permute-start) | collective-permute-done | bytes 327712 | tf_op jit(solution)/shard_map/ppermute | solution.py:37
  27.3 9.0 %collective-permute-done.3.refs_2_ = bf16[256,1024]{1,0:T(8,128)(2,1)S(1)} collective-permute-done((bf16[256,1024]{1,0:T(8,128)(2,1)S(1)}, bf16[256,1024]{1,0:T(8,128)(2,1)S(1)}, u32[]{:S(2)}, u32[]{:S(2)}) %collective-permute-start.3) | collective-permute-done | bytes 524320 | tf_op jit(solution)/shard_map/ppermute | solution.py:37
  36.3 3.5 collective-permute-done.4.refs_3_
  43.7 18.5 %collective-permute-done.1 = bf16[256,2048]{1,0:T(8,128)(2,1)S(1)} collective-permute-done((bf16[256,2048]{1,0:T(8,128)(2,1)S(1)}, bf16[256,2048]{1,0:T(8,128)(2,1)S(1)}, u32[]{:S(2)}, u32[]{:S(2)}) %collective-permute-start.1) | collective-permute-done | bytes 1048608 | tf_op jit(solution)/shard_map/ppermute | solution.py:37
  62.2 9.1 %maximum_select_fusion = bf16[512,2048]{1,0:T(8,128)(2,1)} fusion(bf16[256,2048]{1,0:T(8,128)(2,1)S(1)} %collective-permute-done.1, bf16[256,1024]{1,0:T(8,128)(2,1)S(1)} %get-tuple-element.363, bf16[256,1024]{1,0:T(8,128)(2,1)S(1)} %get-tuple-element.412, pred[]{:T(512)S(6)} %eq.6), kind=kLoop, calls=%fused_computation.18 | loop fusion | flops 13631488 | bytes 4194305 | tf_op jit(solution)/shard_map/jit(_where)/select_n | solution.py:57
  71.3 11.0 %collective-permute-done.6.refs_5_ = bf16[512,1024]{1,0:T(8,128)(2,1)S(1)} collective-permute-done((bf16[512,1024]{1,0:T(8,128)(2,1)}, bf16[512,1024]{1,0:T(8,128)(2,1)S(1)}, u32[]{:S(2)}, u32[]{:S(2)}) %collective-permute-start.6) | collective-permute-done | bytes 1048608 | tf_op jit(solution)/shard_map/ppermute | solution.py:37
  90.9 2.4 fusion.49
  95.2 7.7 %place.4.left = bf16[2048,2048]{1,0:T(8,128)(2,1)} custom-call(bf16[256,2048]{1,0:T(8,128)(2,1)} %copy-done.12, bf16[256,2048]{1,0:T(8,128)(2,1)} %collective-permute-done.2.refs_1_, bf16[256,1024]{1,0:T(8,128)(2,1)} %copy-done.28, bf16[256,1024]{1,0:T(8,128)(2,1)} %copy-done.29, bf16[512,1024]{1,0:T(8,128)(2,1)} %collective-permute-done.5.refs_4_, ...), custom_call_target="tpu_custom_call" | custom-call | tf_op jit(solution)/shard_map/place/pallas_call | solution.py:120
  103.0 6.0 fusion.12.qkv
  110.0 2.1 collective-permute-start.9
  112.1 9.1 %collective-permute-done.9.halo = bf16[128,512]{1,0:T(8,128)(2,1)S(1)} collective-permute-done((bf16[128,512]{1,0:T(8,128)(2,1)S(1)}, bf16[128,512]{1,0:T(8,128)(2,1)S(1)}, u32[]{:S(2)}, u32[]{:S(2)}) %collective-permute-start.9) | collective-permute-done | bytes 131104 | tf_op jit(solution)/shard_map/ppermute | solution.py:42
  127.9 28.7 %attend.1 = (bf16[256,2048]{1,0:T(8,128)(2,1)S(1)}, f32[8,2048]{1,0:T(8,128)S(1)}, f32[8,128]{1,0:T(8,128)S(1)}) custom-call(s32[3]{0:T(128)S(1)} %pad_add_fusion.info, bf16[384,2048]{1,0:T(8,128)(2,1)S(1)} %rope.1.qkv, bf16[128,512]{1,0:T(8,128)(2,1)S(1)} %collective-permute-done.9.halo), custom_call_target="tpu_custom_call" | custom-call | tf_op jit(solution)/shard_map/attend/pallas_call | solution.py:468
  157.6 3.4 collective-permute-done.13
  161.0 6.5 product.8
  168.7 2.4 collective-permute-done.18
  171.2 3.8 collective-permute-done.17.refs_2_
  175.0 7.4 %product.9 = (f32[2,256,1024]{2,1,0:T(8,128)}, f32[2,256,1024]{2,1,0:T(8,128)}, bf16[2,256,1024]{2,1,0:T(8,128)(2,1)}, bf16[2,256,1024]{2,1,0:T(8,128)(2,1)}) custom-call(bf16[256,2048]{1,0:T(8,128)(2,1)} %copy-done, bf16[2048,640]{1,0:T(8,128)(2,1)} %all-gather.4.cloned.1.call-done.refs_1_.weights, bf16[1024,2048]{1,0:T(8,128)(2,1)} %collective-permute-done.17.refs_2_), custom_call_target="tpu_custom_call" | custom-call | flops 1073741824 | bytes 5242880 | tf_op jit(solution)/shard_map/product/pallas_call | solution.py:205
  186.7 8.9 %collective-permute-done.22 = f32[8,128]{1,0:T(8,128)S(1)} collective-permute-done((f32[8,128]{1,0:T(8,128)S(1)}, f32[8,128]{1,0:T(8,128)S(1)}, u32[]{:S(2)}, u32[]{:S(2)}) %collective-permute-start.22) | collective-permute-done | bytes 4128 | tf_op jit(solution)/shard_map/ppermute | solution.py:42
  195.6 2.2 collective-permute-start.23
  200.2 7.0 place.5.right.rows
  207.2 2.5 collective-permute-done.19
  210.9 2.3 convert_add_fusion.9
  217.8 9.8 %collective-permute-done.24 = bf16[256,1024]{1,0:T(8,128)(2,1)} collective-permute-done((bf16[256,1024]{1,0:T(8,128)(2,1)}, bf16[256,1024]{1,0:T(8,128)(2,1)}, u32[]{:S(2)}, u32[]{:S(2)}) %collective-permute-start.24) | collective-permute-done | bytes 524320 | tf_op jit(solution)/shard_map/ppermute | solution.py:37
  235.3 12.1 %collective-permute-done.27.refs_2_ = bf16[256,1024]{1,0:T(8,128)(2,1)} collective-permute-done((bf16[256,1024]{1,0:T(8,128)(2,1)S(1)}, bf16[256,1024]{1,0:T(8,128)(2,1)}, u32[]{:S(2)}, u32[]{:S(2)}) %collective-permute-start.27) | collective-permute-done | bytes 524320 | tf_op jit(solution)/shard_map/ppermute | solution.py:37
  252.4 22.9 %collective-permute-done.30.refs_5_ = bf16[512,1024]{1,0:T(8,128)(2,1)S(1)} collective-permute-done((bf16[512,1024]{1,0:T(8,128)(2,1)S(1)}, bf16[512,1024]{1,0:T(8,128)(2,1)S(1)}, u32[]{:S(2)}, u32[]{:S(2)}) %collective-permute-start.30) | collective-permute-done | bytes 1048608 | tf_op jit(solution)/shard_map/ppermute | solution.py:37
  277.1 4.3 collective-permute-done.32.refs_7_
  281.4 6.9 place.6.rows.left
  288.3 25.1 %hidden.1 = (f32[2048,1024]{1,0:T(8,128)}, f32[2048,1024]{1,0:T(8,128)}, bf16[2048,1024]{1,0:T(8,128)(2,1)}) custom-call(bf16[2048,2048]{1,0:T(8,128)(2,1)} %place.6.rows.left, bf16[2048,2048]{1,0:T(8,128)(2,1)} %all-gather.6.cloned.1.call-done.gate_w.up_w.refs_1_.refs_3_, bf16[2048,2048]{1,0:T(8,128)(2,1)} %all-gather.6.cloned.1.call-done.gate_w.up_w.refs_1_.refs_3_), custom_call_target="tpu_custom_call" | custom-call | tf_op jit(solution)/shard_map/hidden/pallas_call | solution.py:503
  313.4 14.1 %outer.5 = bf16[1024,2048]{1,0:T(8,128)(2,1)} custom-call(bf16[2048,1024]{1,0:T(8,128)(2,1)} %get-tuple-element.228.left.refs_0_, bf16[2048,2048]{1,0:T(8,128)(2,1)} %place.5.right.rows), custom_call_target="tpu_custom_call" | custom-call | flops 8589934592 | bytes 16777216 | tf_op jit(solution)/shard_map/outer/pallas_call | solution.py:541
  327.8 21.2 %hidden_back.1 = (bf16[2048,1024]{1,0:T(8,128)(2,1)}, bf16[2048,1024]{1,0:T(8,128)(2,1)}) custom-call(bf16[2048,2048]{1,0:T(8,128)(2,1)} %place.5.right.rows, bf16[1024,2048]{1,0:T(8,128)(2,1)} %all-gather.8.cloned.1.call-done.weights.refs_1_, f32[2048,1024]{1,0:T(8,128)} %get-tuple-element.215.gates, f32[2048,1024]{1,0:T(8,128)} %get-tuple-element.216.ups), custom_call_target="tpu_custom_call" | custom-call | tf_op jit(solution)/shard_map/hidden_back/pallas_call | solution.py:503
  349.0 13.5 %product.10 = bf16[1024,2048]{1,0:T(8,128)(2,1)} custom-call(bf16[2048,1024]{1,0:T(8,128)(2,1)} %get-tuple-element.217.refs_0_.right, bf16[2048,2048]{1,0:T(8,128)(2,1)} %all-gather.6.cloned.1.call-done.gate_w.up_w.refs_1_.refs_3_, bf16[2048,1024]{1,0:T(8,128)(2,1)} %get-tuple-element.218.refs_2_.right, ...), custom_call_target="tpu_custom_call" | custom-call | flops 8589934592 | bytes 12582912 | tf_op jit(solution)/shard_map/product/pallas_call | solution.py:205
  362.6 13.3 %outer.6 = bf16[2048,1024]{1,0:T(8,128)(2,1)} custom-call(bf16[2048,2048]{1,0:T(8,128)(2,1)} %place.6.rows.left, bf16[2048,1024]{1,0:T(8,128)(2,1)} %get-tuple-element.217.refs_0_.right), custom_call_target="tpu_custom_call" | custom-call | flops 8589934592 | bytes 16777216 | tf_op jit(solution)/shard_map/outer/pallas_call | solution.py:541
  376.0 15.8 %product.11 = (f32[2,256,1024]{2,1,0:T(8,128)}, f32[2,256,1024]{2,1,0:T(8,128)}, bf16[2,256,1024]{2,1,0:T(8,128)(2,1)}, bf16[2,256,1024]{2,1,0:T(8,128)(2,1)}) custom-call(bf16[2048,1024]{1,0:T(8,128)(2,1)} %get-tuple-element.217.refs_0_.right, bf16[2048,2048]{1,0:T(8,128)(2,1)} %all-gather.6.cloned.1.call-done.gate_w.up_w.refs_1_.refs_3_, ...), custom_call_target="tpu_custom_call" | custom-call | flops 8589934592 | bytes 12582912 | tf_op jit(solution)/shard_map/product/pallas_call | solution.py:205
  394.1 13.3 %outer.7 = bf16[2048,1024]{1,0:T(8,128)(2,1)} custom-call(bf16[2048,2048]{1,0:T(8,128)(2,1)} %place.6.rows.left, bf16[2048,1024]{1,0:T(8,128)(2,1)} %get-tuple-element.218.refs_2_.right), custom_call_target="tpu_custom_call" | custom-call | flops 8589934592 | bytes 16777216 | tf_op jit(solution)/shard_map/outer/pallas_call | solution.py:541
  407.4 10.1 %collective-permute-done.34 = bf16[2,256,1024]{2,1,0:T(8,128)(2,1)} collective-permute-done((bf16[2,256,1024]{2,1,0:T(8,128)(2,1)}, bf16[2,256,1024]{2,1,0:T(8,128)(2,1)}, u32[]{:S(2)}, u32[]{:S(2)}) %collective-permute-start.34) | collective-permute-done | bytes 1048608 | tf_op jit(solution)/shard_map/ppermute | solution.py:37
  418.5 2.3 convert_add_fusion.7
  424.9 8.4 %product.12 = bf16[1024,2048]{1,0:T(8,128)(2,1)} custom-call(bf16[2048,1024]{1,0:T(8,128)(2,1)} %get-tuple-element.228.left.refs_0_, bf16[1024,2048]{1,0:T(8,128)(2,1)} %all-gather.8.cloned.1.call-done.weights.refs_1_), custom_call_target="tpu_custom_call" | custom-call | flops 4294967296 | bytes 8388608 | tf_op jit(solution)/shard_map/product/pallas_call | solution.py:205
  435.8 12.1 %collective-permute-done.36 = bf16[256,1024]{1,0:T(8,128)(2,1)S(1)} collective-permute-done((bf16[256,1024]{1,0:T(8,128)(2,1)}, bf16[256,1024]{1,0:T(8,128)(2,1)S(1)}, u32[]{:S(2)}, u32[]{:S(2)}) %collective-permute-start.36) | collective-permute-done | bytes 524320 | tf_op jit(solution)/shard_map/ppermute | solution.py:37
  452.9 2.1 multiply_convert_fusion
  457.0 10.4 %product.13 = (f32[2,256,1024]{2,1,0:T(8,128)}, f32[2,256,1024]{2,1,0:T(8,128)}, bf16[2,256,1024]{2,1,0:T(8,128)(2,1)}, bf16[2,256,1024]{2,1,0:T(8,128)(2,1)}) custom-call(bf16[2048,1024]{1,0:T(8,128)(2,1)} %get-tuple-element.228.left.refs_0_, bf16[1024,2048]{1,0:T(8,128)(2,1)} %all-gather.8.cloned.1.call-done.weights.refs_1_, ...), custom_call_target="tpu_custom_call" | custom-call | flops 4294967296 | bytes 8388608 | tf_op jit(solution)/shard_map/product/pallas_call | solution.py:205
  472.6 22.9 %collective-permute-done.43.refs_5_ = bf16[512,1024]{1,0:T(8,128)(2,1)S(1)} collective-permute-done((bf16[512,1024]{1,0:T(8,128)(2,1)S(1)}, bf16[512,1024]{1,0:T(8,128)(2,1)S(1)}, u32[]{:S(2)}, u32[]{:S(2)}) %collective-permute-start.43) | collective-permute-done | bytes 1048608 | tf_op jit(solution)/shard_map/ppermute | solution.py:37
  499.3 2.0 collective-permute-done.45.refs_7_
  501.4 6.9 place.7.left
  508.3 2.1 constant_dynamic-slice_fusion.2
  511.6 6.1 convolution_convert_fusion.upstream
  517.8 40.4 %attend_back.1 = (bf16[256,2048]{1,0:T(8,128)(2,1)S(1)}, f32[128,2048]{1,0:T(8,128)S(1)}, bf16[128,512]{1,0:T(8,128)(2,1)S(1)}) custom-call(s32[3]{0:T(128)S(1)} %pad_add_fusion.info, bf16[384,2048]{1,0:T(8,128)(2,1)S(1)} %rope.1.qkv, bf16[128,512]{1,0:T(8,128)(2,1)S(1)} %collective-permute-done.9.halo, ...), custom_call_target="tpu_custom_call" | custom-call | tf_op jit(solution)/shard_map/attend_back/pallas_call | solution.py:468
  560.0 6.2 collective-permute-start.49
  566.1 6.7 outer.8
  574.8 6.5 product.14
  594.8 2.8 fusion.24
  597.5 3.1 collective-permute-done.52
  600.6 3.1 collective-permute-done.53
  603.7 7.8 %collective-permute-done.51 = bf16[256,1024]{1,0:T(8,128)(2,1)} collective-permute-done((bf16[256,1024]{1,0:T(8,128)(2,1)}, bf16[256,1024]{1,0:T(8,128)(2,1)}, u32[]{:S(2)}, u32[]{:S(2)}) %collective-permute-start.51) | collective-permute-done | bytes 524320 | tf_op jit(solution)/shard_map/ppermute | solution.py:37
  611.4 8.3 %product.15 = (f32[2,256,1024]{2,1,0:T(8,128)}, f32[2,256,1024]{2,1,0:T(8,128)}, bf16[2,256,1024]{2,1,0:T(8,128)(2,1)}, bf16[2,256,1024]{2,1,0:T(8,128)(2,1)}) custom-call(bf16[384,2048]{1,0:T(8,128)(2,1)} %pad_maximum_fusion.6.refs_0_.right, bf16[2048,640]{1,0:T(8,128)(2,1)} %all-gather.4.cloned.1.call-done.refs_1_.weights, ...), custom_call_target="tpu_custom_call" | custom-call | flops 1610612736 | bytes 5767168 | tf_op jit(solution)/shard_map/product/pallas_call | solution.py:205
  622.5 9.1 %outer.9 = (bf16[2048,384]{1,0:T(8,128)(2,1)}, f32[2048,128]{1,0:T(8,128)}) custom-call(bf16[2048,2048]{1,0:T(8,128)(2,1)} %place.4.left, bf16[384,2048]{1,0:T(8,128)(2,1)} %pad_maximum_fusion.6.refs_0_.right, bf16[2048,640]{1,0:T(8,128)(2,1)} %all-gather.4.cloned.1.call-done.refs_1_.weights), custom_call_target="tpu_custom_call" | custom-call | flops 3221225472 | bytes 11534336 | tf_op jit(solution)/shard_map/outer/pallas_call | solution.py:541
  636.3 8.6 %collective-permute-done.54 = bf16[2,256,1024]{2,1,0:T(8,128)(2,1)} collective-permute-done((bf16[2,256,1024]{2,1,0:T(8,128)(2,1)}, bf16[2,256,1024]{2,1,0:T(8,128)(2,1)}, u32[]{:S(2)}, u32[]{:S(2)}) %collective-permute-start.54) | collective-permute-done | bytes 1048608 | tf_op jit(solution)/shard_map/ppermute | solution.py:37
  651.6 2.9 fusion.22
  655.3 7.4 %collective-permute-done.56 = bf16[256,1024]{1,0:T(8,128)(2,1)S(1)} collective-permute-done((bf16[256,1024]{1,0:T(8,128)(2,1)S(1)}, bf16[256,1024]{1,0:T(8,128)(2,1)S(1)}, u32[]{:S(2)}, u32[]{:S(2)}) %collective-permute-start.56) | collective-permute-done | bytes 524320 | tf_op jit(solution)/shard_map/ppermute | solution.py:37
  663.4 8.0 %collective-permute-done.65 = bf16[256,1024]{1,0:T(8,128)(2,1)S(1)} collective-permute-done((bf16[256,1024]{1,0:T(8,128)(2,1)S(1)}, bf16[256,1024]{1,0:T(8,128)(2,1)S(1)}, u32[]{:S(2)}, u32[]{:S(2)}) %collective-permute-start.65) | collective-permute-done | bytes 524320 | tf_op jit(solution)/shard_map/ppermute | solution.py:37
  684.1 5.4 collective-permute-done.60
  689.5 3.2 fusion.8
  692.7 2.2 collective-permute-done.61
  695.0 4.4 collective-permute-done.62
  (365 shorter events, 138.4 us)
Async XLA Ops:
  7.2 75.2 %all-gather.4.cloned.1.call-start = ((), (), s32[]{:S(2)}) async-start(), calls=%async_computation.5 | async-start | bytes 3276800 | tf_op jit(solution)/shard_map/all_gather | solution.py:593
  9.8 10.7 %collective-permute-start = (bf16[256,640]{1,0:T(8,128)(2,1)S(1)}, bf16[256,640]{1,0:T(8,128)(2,1)S(1)}, u32[]{:S(2)}, u32[]{:S(2)}) collective-permute-start(bf16[256,640]{1,0:T(8,128)(2,1)S(1)} %pad_maximum_fusion.20), channel_id=1, source_target_pairs={{0,4},{4,0},{1,5},{5,1},{2,6},{6,2},{3,7},{7,3},{8,12},{12,8},{9,1... | collective-permute-start | bytes 983048 | tf_op jit(solution)/shard_map/ppermute | solution.py:37
  21.7 226.1 %all-gather.6.cloned.1.call-start = ((), (), s32[]{:S(2)}) async-start(), calls=%async_computation.6 | async-start | bytes 10485760 | tf_op jit(solution)/shard_map/all_gather | solution.py:608
  23.1 13.1 %collective-permute-start.3 = (bf16[256,1024]{1,0:T(8,128)(2,1)S(1)}, bf16[256,1024]{1,0:T(8,128)(2,1)S(1)}, u32[]{:S(2)}, u32[]{:S(2)}) collective-permute-start(bf16[256,1024]{1,0:T(8,128)(2,1)S(1)} %get-tuple-element.360), channel_id=1, source_target_pairs={{0,2},{2,0},{1,3},{3,1},{4,6},{6,4},{5,7},{7,5},{8,10},{10,8},{9,1... | collective-permute-start | bytes 1572872 | tf_op jit(solution)/shard_map/ppermute | solution.py:37
  24.9 14.9 %collective-permute-start.4 = (bf16[256,1024]{1,0:T(8,128)(2,1)S(1)}, bf16[256,1024]{1,0:T(8,128)(2,1)S(1)}, u32[]{:S(2)}, u32[]{:S(2)}) collective-permute-start(bf16[256,1024]{1,0:T(8,128)(2,1)S(1)} %get-tuple-element.359), channel_id=1, source_target_pairs={{0,4},{4,0},{1,5},{5,1},{2,6},{6,2},{3,7},{7,3},{8,12},{12,8},{9,1... | collective-permute-start | bytes 1572872 | tf_op jit(solution)/shard_map/ppermute | solution.py:37
  26.7 35.5 %collective-permute-start.1 = (bf16[256,2048]{1,0:T(8,128)(2,1)S(1)}, bf16[256,2048]{1,0:T(8,128)(2,1)S(1)}, u32[]{:S(2)}, u32[]{:S(2)}) collective-permute-start(bf16[256,2048]{1,0:T(8,128)(2,1)S(1)} %pad_maximum_fusion.15), channel_id=1, source_target_pairs={{0,4},{4,0},{1,5},{5,1},{2,6},{6,2},{3,7},{7,3},{8,12},{12,8},{9,1... | collective-permute-start | bytes 3145736 | tf_op jit(solution)/shard_map/ppermute | solution.py:37
  27.3 44.0 %collective-permute-start.2 = (bf16[256,2048]{1,0:T(8,128)(2,1)S(1)}, bf16[256,2048]{1,0:T(8,128)(2,1)}, u32[]{:S(2)}, u32[]{:S(2)}) collective-permute-start(bf16[256,2048]{1,0:T(8,128)(2,1)S(1)} %fusion.4.refs_0_), channel_id=1, source_target_pairs={{0,1},{1,0},{2,3},{3,2},{4,5},{5,4},{6,7},{7,6},{8,9},{9,8},{10,11... | collective-permute-start | bytes 3145736 | tf_op jit(solution)/shard_map/ppermute | solution.py:37
  41.6 29.7 %collective-permute-start.5 = (bf16[512,1024]{1,0:T(8,128)(2,1)}, bf16[512,1024]{1,0:T(8,128)(2,1)}, u32[]{:S(2)}, u32[]{:S(2)}) collective-permute-start(bf16[512,1024]{1,0:T(8,128)(2,1)} %get-tuple-element.375), channel_id=1, source_target_pairs={{0,1},{1,0},{2,3},{3,2},{4,5},{5,4},{6,7},{7,6},{8,9},{9,8},{10,11... | collective-permute-start | bytes 3145736 | tf_op jit(solution)/shard_map/ppermute | solution.py:37
  41.6 40.7 %collective-permute-start.6 = (bf16[512,1024]{1,0:T(8,128)(2,1)}, bf16[512,1024]{1,0:T(8,128)(2,1)S(1)}, u32[]{:S(2)}, u32[]{:S(2)}) collective-permute-start(bf16[512,1024]{1,0:T(8,128)(2,1)} %get-tuple-element.376), channel_id=1, source_target_pairs={{0,4},{4,0},{1,5},{5,1},{2,6},{6,2},{3,7},{7,3},{8,12},{12,8},{9,1... | collective-permute-start | bytes 3145736 | tf_op jit(solution)/shard_map/ppermute | solution.py:37
  43.2 39.2 %collective-permute-start.7 = (bf16[512,1024]{1,0:T(8,128)(2,1)}, bf16[512,1024]{1,0:T(8,128)(2,1)S(1)}, u32[]{:S(2)}, u32[]{:S(2)}) collective-permute-start(bf16[512,1024]{1,0:T(8,128)(2,1)} %get-tuple-element.374), channel_id=1, source_target_pairs={{0,2},{2,0},{1,3},{3,1},{4,6},{6,4},{5,7},{7,5},{8,10},{10,8},{9,1... | collective-permute-start | bytes 3145736 | tf_op jit(solution)/shard_map/ppermute | solution.py:37
  84.8 10.4 %collective-permute-start.8 = (bf16[1024,1024]{1,0:T(8,128)(2,1)}, bf16[1024,1024]{1,0:T(8,128)(2,1)}, u32[]{:S(2)}, u32[]{:S(2)}) collective-permute-start(bf16[1024,1024]{1,0:T(8,128)(2,1)} %pad_maximum_fusion), channel_id=1, source_target_pairs={{0,1},{1,0},{2,3},{3,2},{4,5},{5,4},{6,7},{7,6},{8,9},{9,8},{10,11... | collective-permute-start | bytes 6291464 | tf_op jit(solution)/shard_map/ppermute | solution.py:37
  84.8 243.0 %all-gather.8.cloned.1.call-start = ((), (), s32[]{:S(2)}) async-start(), calls=%async_computation.7 | async-start | bytes 5242880 | tf_op jit(solution)/shard_map/all_gather | solution.py:641
  90.9 21.2 %collective-permute-start.10 = (bf16[256,2048]{1,0:T(8,128)(2,1)}, bf16[256,2048]{1,0:T(8,128)(2,1)}, u32[]{:S(2)}, u32[]{:S(2)}) collective-permute-start(bf16[256,2048]{1,0:T(8,128)(2,1)} %fusion.refs_0_), channel_id=1, source_target_pairs={{0,1},{1,0},{2,3},{3,2},{4,5},{5,4},{6,7},{7,6},{8,9},{9,8},{10,11... | collective-permute-start | bytes 3145736 | tf_op jit(solution)/shard_map/ppermute | solution.py:37
  93.3 18.8 %collective-permute-start.11 = (bf16[256,1024]{1,0:T(8,128)(2,1)}, bf16[256,1024]{1,0:T(8,128)(2,1)S(1)}, u32[]{:S(2)}, u32[]{:S(2)}) collective-permute-start(bf16[256,1024]{1,0:T(8,128)(2,1)} %get-tuple-element.358), channel_id=1, source_target_pairs={{0,2},{2,0},{1,3},{3,1},{4,6},{6,4},{5,7},{7,5},{8,10},{10,8},{9,1... | collective-permute-start | bytes 1572872 | tf_op jit(solution)/shard_map/ppermute | solution.py:37
  93.8 18.3 %collective-permute-start.12 = (bf16[256,1024]{1,0:T(8,128)(2,1)}, bf16[256,1024]{1,0:T(8,128)(2,1)}, u32[]{:S(2)}, u32[]{:S(2)}) collective-permute-start(bf16[256,1024]{1,0:T(8,128)(2,1)} %get-tuple-element.357), channel_id=1, source_target_pairs={{0,4},{4,0},{1,5},{5,1},{2,6},{6,2},{3,7},{7,3},{8,12},{12,8},{9,1... | collective-permute-start | bytes 1572872 | tf_op jit(solution)/shard_map/ppermute | solution.py:37
  110.0 11.2 %collective-permute-start.9 = (bf16[128,512]{1,0:T(8,128)(2,1)S(1)}, bf16[128,512]{1,0:T(8,128)(2,1)S(1)}, u32[]{:S(2)}, u32[]{:S(2)}) collective-permute-start(bf16[128,512]{1,0:T(8,128)(2,1)S(1)} %slice.183), channel_id=1, source_target_pairs={{0,8},{8,16},{16,24},{24,0},{1,9},{9,17},{17,25},{25,1},{2,10},{10... | collective-permute-start | bytes 393224 | tf_op jit(solution)/shard_map/ppermute | solution.py:42
  124.1 36.9 %collective-permute-start.14 = (bf16[512,1024]{1,0:T(8,128)(2,1)S(1)}, bf16[512,1024]{1,0:T(8,128)(2,1)S(1)}, u32[]{:S(2)}, u32[]{:S(2)}) collective-permute-start(bf16[512,1024]{1,0:T(8,128)(2,1)S(1)} %get-tuple-element.372), channel_id=1, source_target_pairs={{0,1},{1,0},{2,3},{3,2},{4,5},{5,4},{6,7},{7,6},{8,9},{9,8},{10,11... | collective-permute-start | bytes 3145736 | tf_op jit(solution)/shard_map/ppermute | solution.py:37
  124.1 36.8 %collective-permute-start.15 = (bf16[512,1024]{1,0:T(8,128)(2,1)S(1)}, bf16[512,1024]{1,0:T(8,128)(2,1)S(1)}, u32[]{:S(2)}, u32[]{:S(2)}) collective-permute-start(bf16[512,1024]{1,0:T(8,128)(2,1)S(1)} %get-tuple-element.373), channel_id=1, source_target_pairs={{0,4},{4,0},{1,5},{5,1},{2,6},{6,2},{3,7},{7,3},{8,12},{12,8},{9,1... | collective-permute-start | bytes 3145736 | tf_op jit(solution)/shard_map/ppermute | solution.py:37
  125.3 35.6 %collective-permute-start.16 = (bf16[512,1024]{1,0:T(8,128)(2,1)S(1)}, bf16[512,1024]{1,0:T(8,128)(2,1)S(1)}, u32[]{:S(2)}, u32[]{:S(2)}) collective-permute-start(bf16[512,1024]{1,0:T(8,128)(2,1)S(1)} %get-tuple-element.371), channel_id=1, source_target_pairs={{0,2},{2,0},{1,3},{3,1},{4,6},{6,4},{5,7},{7,5},{8,10},{10,8},{9,1... | collective-permute-start | bytes 3145736 | tf_op jit(solution)/shard_map/ppermute | solution.py:37
  126.9 34.0 %collective-permute-start.13 = (bf16[1024,256]{1,0:T(8,128)(2,1)S(1)}, bf16[1024,256]{1,0:T(8,128)(2,1)S(1)}, u32[]{:S(2)}, u32[]{:S(2)}) collective-permute-start(bf16[1024,256]{1,0:T(8,128)(2,1)S(1)} %get-tuple-element.169), channel_id=1, source_target_pairs={{0,4},{4,0},{1,5},{5,1},{2,6},{6,2},{3,7},{7,3},{8,12},{12,8},{9,1... | collective-permute-start | bytes 1572872 | tf_op jit(solution)/shard_map/ppermute | solution.py:37
  167.5 7.5 %collective-permute-start.17 = (bf16[1024,2048]{1,0:T(8,128)(2,1)}, bf16[1024,2048]{1,0:T(8,128)(2,1)}, u32[]{:S(2)}, u32[]{:S(2)}) collective-permute-start(bf16[1024,2048]{1,0:T(8,128)(2,1)} %product.8), channel_id=1, source_target_pairs={{0,1},{1,0},{2,3},{3,2},{4,5},{5,4},{6,7},{7,6},{8,9},{9,8},{10,11... | collective-permute-start | bytes 12582920 | tf_op jit(solution)/shard_map/ppermute | solution.py:37
  183.9 16.3 %collective-permute-start.21 = (bf16[1024,1024]{1,0:T(8,128)(2,1)}, bf16[1024,1024]{1,0:T(8,128)(2,1)}, u32[]{:S(2)}, u32[]{:S(2)}) collective-permute-start(bf16[1024,1024]{1,0:T(8,128)(2,1)} %pad_maximum_fusion.1), channel_id=1, source_target_pairs={{0,1},{1,0},{2,3},{3,2},{4,5},{5,4},{6,7},{7,6},{8,9},{9,8},{10,11... | collective-permute-start | bytes 6291464 | tf_op jit(solution)/shard_map/ppermute | solution.py:37
  184.0 25.8 %collective-permute-start.19 = (bf16[2,256,1024]{2,1,0:T(8,128)(2,1)}, bf16[2,256,1024]{2,1,0:T(8,128)(2,1)}, u32[]{:S(2)}, u32[]{:S(2)}) collective-permute-start(bf16[2,256,1024]{2,1,0:T(8,128)(2,1)} %get-tuple-element.176), channel_id=1, source_target_pairs={{0,2},{2,0},{1,3},{3,1},{4,6},{6,4},{5,7},{7,5},{8,10},{10,8},{9,1... | collective-permute-start | bytes 3145736 | tf_op jit(solution)/shard_map/ppermute | solution.py:37
  185.6 25.4 %collective-permute-start.20 = (bf16[2,256,1024]{2,1,0:T(8,128)(2,1)}, bf16[2,256,1024]{2,1,0:T(8,128)(2,1)S(1)}, u32[]{:S(2)}, u32[]{:S(2)}) collective-permute-start(bf16[2,256,1024]{2,1,0:T(8,128)(2,1)} %get-tuple-element.177), channel_id=1, source_target_pairs={{0,4},{4,0},{1,5},{5,1},{2,6},{6,2},{3,7},{7,3},{8,12},{12,8},{9,1... | collective-permute-start | bytes 3145736 | tf_op jit(solution)/shard_map/ppermute | solution.py:37
  186.7 8.9 %collective-permute-start.22 = (f32[8,128]{1,0:T(8,128)S(1)}, f32[8,128]{1,0:T(8,128)S(1)}, u32[]{:S(2)}, u32[]{:S(2)}) collective-permute-start(f32[8,128]{1,0:T(8,128)S(1)} %maximum_select_fusion.10), channel_id=1, source_target_pairs={{0,8},{8,16},{16,24},{24,0},{1,9},{9,17},{17,25},{25,1},{2,10},{10... | collective-permute-start | bytes 12296 | tf_op jit(solution)/shard_map/ppermute | solution.py:42
  214.2 13.5 %collective-permute-start.24 = (bf16[256,1024]{1,0:T(8,128)(2,1)}, bf16[256,1024]{1,0:T(8,128)(2,1)}, u32[]{:S(2)}, u32[]{:S(2)}) collective-permute-start(bf16[256,1024]{1,0:T(8,128)(2,1)} %fusion.26), channel_id=1, source_target_pairs={{0,4},{4,0},{1,5},{5,1},{2,6},{6,2},{3,7},{7,3},{8,12},{12,8},{9,1... | collective-permute-start | bytes 1572872 | tf_op jit(solution)/shard_map/ppermute | solution.py:37
  217.2 13.2 %collective-permute-start.25 = (bf16[256,1024]{1,0:T(8,128)(2,1)}, bf16[256,1024]{1,0:T(8,128)(2,1)}, u32[]{:S(2)}, u32[]{:S(2)}) collective-permute-start(bf16[256,1024]{1,0:T(8,128)(2,1)} %fusion.27), channel_id=1, source_target_pairs={{0,2},{2,0},{1,3},{3,1},{4,6},{6,4},{5,7},{7,5},{8,10},{10,8},{9,1... | collective-permute-start | bytes 1572872 | tf_op jit(solution)/shard_map/ppermute | solution.py:37
  217.8 290.5 %reduce-scatter.6.cloned.1.call-start = ((), (), s32[]{:S(2)}) async-start(), calls=%async_computation.8 | async-start | bytes 5242880 | tf_op jit(solution)/shard_map/reduce_scatter | solution.py:658
  232.8 15.0 %collective-permute-start.26 = (bf16[256,2048]{1,0:T(8,128)(2,1)S(1)}, bf16[256,2048]{1,0:T(8,128)(2,1)}, u32[]{:S(2)}, u32[]{:S(2)}) collective-permute-start(bf16[256,2048]{1,0:T(8,128)(2,1)S(1)} %multiply_convert_fusion.1.refs_0_), channel_id=1, source_target_pairs={{0,1},{1,0},{2,3},{3,2},{4,5},{5,4},{6,7},{7,6},{8,9},{9,8},{10,11... | collective-permute-start | bytes 3145736 | tf_op jit(solution)/shard_map/ppermute | solution.py:37
  233.7 13.7 %collective-permute-start.27 = (bf16[256,1024]{1,0:T(8,128)(2,1)S(1)}, bf16[256,1024]{1,0:T(8,128)(2,1)}, u32[]{:S(2)}, u32[]{:S(2)}) collective-permute-start(bf16[256,1024]{1,0:T(8,128)(2,1)S(1)} %get-tuple-element.352), channel_id=1, source_target_pairs={{0,2},{2,0},{1,3},{3,1},{4,6},{6,4},{5,7},{7,5},{8,10},{10,8},{9,1... | collective-permute-start | bytes 1572872 | tf_op jit(solution)/shard_map/ppermute | solution.py:37
  234.3 13.4 %collective-permute-start.28 = (bf16[256,1024]{1,0:T(8,128)(2,1)S(1)}, bf16[256,1024]{1,0:T(8,128)(2,1)}, u32[]{:S(2)}, u32[]{:S(2)}) collective-permute-start(bf16[256,1024]{1,0:T(8,128)(2,1)S(1)} %get-tuple-element.351), channel_id=1, source_target_pairs={{0,4},{4,0},{1,5},{5,1},{2,6},{6,2},{3,7},{7,3},{8,12},{12,8},{9,1... | collective-permute-start | bytes 1572872 | tf_op jit(solution)/shard_map/ppermute | solution.py:37
  249.8 25.6 %collective-permute-start.30 = (bf16[512,1024]{1,0:T(8,128)(2,1)S(1)}, bf16[512,1024]{1,0:T(8,128)(2,1)S(1)}, u32[]{:S(2)}, u32[]{:S(2)}) collective-permute-start(bf16[512,1024]{1,0:T(8,128)(2,1)S(1)} %get-tuple-element.370), channel_id=1, source_target_pairs={{0,4},{4,0},{1,5},{5,1},{2,6},{6,2},{3,7},{7,3},{8,12},{12,8},{9,1... | collective-permute-start | bytes 3145736 | tf_op jit(solution)/shard_map/ppermute | solution.py:37
  250.9 25.2 %collective-permute-start.31 = (bf16[512,1024]{1,0:T(8,128)(2,1)S(1)}, bf16[512,1024]{1,0:T(8,128)(2,1)S(1)}, u32[]{:S(2)}, u32[]{:S(2)}) collective-permute-start(bf16[512,1024]{1,0:T(8,128)(2,1)S(1)} %get-tuple-element.368), channel_id=1, source_target_pairs={{0,2},{2,0},{1,3},{3,1},{4,6},{6,4},{5,7},{7,5},{8,10},{10,8},{9,1... | collective-permute-start | bytes 3145736 | tf_op jit(solution)/shard_map/ppermute | solution.py:37
  327.6 245.3 %reduce-scatter.8.cloned.1.call-start = ((), (), s32[]{:S(2)}) async-start(), calls=%async_computation.9 | async-start | bytes 5242880 | tf_op jit(solution)/shard_map/reduce_scatter | solution.py:658
  362.5 13.5 %collective-permute-start.33 = (bf16[1024,2048]{1,0:T(8,128)(2,1)}, bf16[1024,2048]{1,0:T(8,128)(2,1)}, u32[]{:S(2)}, u32[]{:S(2)}) collective-permute-start(bf16[1024,2048]{1,0:T(8,128)(2,1)} %product.10), channel_id=1, source_target_pairs={{0,1},{1,0},{2,3},{3,2},{4,5},{5,4},{6,7},{7,6},{8,9},{9,8},{10,11... | collective-permute-start | bytes 12582920 | tf_op jit(solution)/shard_map/ppermute | solution.py:37
  375.9 221.6 %reduce-scatter.12.cloned.1.call-start = ((), (), s32[]{:S(2)}) async-start(), calls=%async_computation.11 | async-start | bytes 5242880 | tf_op jit(solution)/shard_map/reduce_scatter | solution.py:658
  391.7 25.8 %collective-permute-start.34 = (bf16[2,256,1024]{2,1,0:T(8,128)(2,1)}, bf16[2,256,1024]{2,1,0:T(8,128)(2,1)}, u32[]{:S(2)}, u32[]{:S(2)}) collective-permute-start(bf16[2,256,1024]{2,1,0:T(8,128)(2,1)} %get-tuple-element.220), channel_id=1, source_target_pairs={{0,2},{2,0},{1,3},{3,1},{4,6},{6,4},{5,7},{7,5},{8,10},{10,8},{9,1... | collective-permute-start | bytes 3145736 | tf_op jit(solution)/shard_map/ppermute | solution.py:37
  393.2 25.4 %collective-permute-start.35 = (bf16[2,256,1024]{2,1,0:T(8,128)(2,1)}, bf16[2,256,1024]{2,1,0:T(8,128)(2,1)S(1)}, u32[]{:S(2)}, u32[]{:S(2)}) collective-permute-start(bf16[2,256,1024]{2,1,0:T(8,128)(2,1)} %get-tuple-element.221), channel_id=1, source_target_pairs={{0,4},{4,0},{1,5},{5,1},{2,6},{6,2},{3,7},{7,3},{8,12},{12,8},{9,1... | collective-permute-start | bytes 3145736 | tf_op jit(solution)/shard_map/ppermute | solution.py:37
  433.3 23.6 %collective-permute-start.38 = (bf16[1024,2048]{1,0:T(8,128)(2,1)}, bf16[1024,2048]{1,0:T(8,128)(2,1)}, u32[]{:S(2)}, u32[]{:S(2)}) collective-permute-start(bf16[1024,2048]{1,0:T(8,128)(2,1)} %product.12), channel_id=1, source_target_pairs={{0,1},{1,0},{2,3},{3,2},{4,5},{5,4},{6,7},{7,6},{8,9},{9,8},{10,11... | collective-permute-start | bytes 12582920 | tf_op jit(solution)/shard_map/ppermute | solution.py:37
  433.3 14.5 %collective-permute-start.36 = (bf16[256,1024]{1,0:T(8,128)(2,1)}, bf16[256,1024]{1,0:T(8,128)(2,1)S(1)}, u32[]{:S(2)}, u32[]{:S(2)}) collective-permute-start(bf16[256,1024]{1,0:T(8,128)(2,1)} %fusion.28), channel_id=1, source_target_pairs={{0,4},{4,0},{1,5},{5,1},{2,6},{6,2},{3,7},{7,3},{8,12},{12,8},{9,1... | collective-permute-start | bytes 1572872 | tf_op jit(solution)/shard_map/ppermute | solution.py:37
  434.5 14.3 %collective-permute-start.37 = (bf16[256,1024]{1,0:T(8,128)(2,1)}, bf16[256,1024]{1,0:T(8,128)(2,1)S(1)}, u32[]{:S(2)}, u32[]{:S(2)}) collective-permute-start(bf16[256,1024]{1,0:T(8,128)(2,1)} %fusion.29), channel_id=1, source_target_pairs={{0,2},{2,0},{1,3},{3,1},{4,6},{6,4},{5,7},{7,5},{8,10},{10,8},{9,1... | collective-permute-start | bytes 1572872 | tf_op jit(solution)/shard_map/ppermute | solution.py:37
  435.5 175.9 %reduce-scatter.10.cloned.1.call-start = ((), (), s32[]{:S(2)}) async-start(), calls=%async_computation.10 | async-start | bytes 1310720 | tf_op jit(solution)/shard_map/reduce_scatter | solution.py:658
  455.1 13.4 %collective-permute-start.40 = (bf16[256,1024]{1,0:T(8,128)(2,1)S(1)}, bf16[256,1024]{1,0:T(8,128)(2,1)S(1)}, u32[]{:S(2)}, u32[]{:S(2)}) collective-permute-start(bf16[256,1024]{1,0:T(8,128)(2,1)S(1)} %get-tuple-element.348), channel_id=1, source_target_pairs={{0,2},{2,0},{1,3},{3,1},{4,6},{6,4},{5,7},{7,5},{8,10},{10,8},{9,1... | collective-permute-start | bytes 1572872 | tf_op jit(solution)/shard_map/ppermute | solution.py:37
  456.1 13.1 %collective-permute-start.41 = (bf16[256,1024]{1,0:T(8,128)(2,1)S(1)}, bf16[256,1024]{1,0:T(8,128)(2,1)S(1)}, u32[]{:S(2)}, u32[]{:S(2)}) collective-permute-start(bf16[256,1024]{1,0:T(8,128)(2,1)S(1)} %get-tuple-element.347), channel_id=1, source_target_pairs={{0,4},{4,0},{1,5},{5,1},{2,6},{6,2},{3,7},{7,3},{8,12},{12,8},{9,1... | collective-permute-start | bytes 1572872 | tf_op jit(solution)/shard_map/ppermute | solution.py:37
  456.9 15.0 %collective-permute-start.39 = (bf16[256,2048]{1,0:T(8,128)(2,1)S(1)}, bf16[256,2048]{1,0:T(8,128)(2,1)S(1)}, u32[]{:S(2)}, u32[]{:S(2)}) collective-permute-start(bf16[256,2048]{1,0:T(8,128)(2,1)S(1)} %get-tuple-element.337.refs_0_), channel_id=1, source_target_pairs={{0,1},{1,0},{2,3},{3,2},{4,5},{5,4},{6,7},{7,6},{8,9},{9,8},{10,11... | collective-permute-start | bytes 3145736 | tf_op jit(solution)/shard_map/ppermute | solution.py:37
  470.0 25.6 %collective-permute-start.43 = (bf16[512,1024]{1,0:T(8,128)(2,1)S(1)}, bf16[512,1024]{1,0:T(8,128)(2,1)S(1)}, u32[]{:S(2)}, u32[]{:S(2)}) collective-permute-start(bf16[512,1024]{1,0:T(8,128)(2,1)S(1)} %get-tuple-element.367), channel_id=1, source_target_pairs={{0,4},{4,0},{1,5},{5,1},{2,6},{6,2},{3,7},{7,3},{8,12},{12,8},{9,1... | collective-permute-start | bytes 3145736 | tf_op jit(solution)/shard_map/ppermute | solution.py:37
  470.8 25.3 %collective-permute-start.44 = (bf16[512,1024]{1,0:T(8,128)(2,1)S(1)}, bf16[512,1024]{1,0:T(8,128)(2,1)S(1)}, u32[]{:S(2)}, u32[]{:S(2)}) collective-permute-start(bf16[512,1024]{1,0:T(8,128)(2,1)S(1)} %get-tuple-element.365), channel_id=1, source_target_pairs={{0,2},{2,0},{1,3},{3,1},{4,6},{6,4},{5,7},{7,5},{8,10},{10,8},{9,1... | collective-permute-start | bytes 3145736 | tf_op jit(solution)/shard_map/ppermute | solution.py:37
  497.1 62.1 %collective-permute-start.47 = (bf16[2,256,1024]{2,1,0:T(8,128)(2,1)}, bf16[2,256,1024]{2,1,0:T(8,128)(2,1)}, u32[]{:S(2)}, u32[]{:S(2)}) collective-permute-start(bf16[2,256,1024]{2,1,0:T(8,128)(2,1)} %get-tuple-element.245), channel_id=1, source_target_pairs={{0,2},{2,0},{1,3},{3,1},{4,6},{6,4},{5,7},{7,5},{8,10},{10,8},{9,1... | collective-permute-start | bytes 3145736 | tf_op jit(solution)/shard_map/ppermute | solution.py:37
  498.2 61.0 %collective-permute-start.48 = (bf16[2,256,1024]{2,1,0:T(8,128)(2,1)}, bf16[2,256,1024]{2,1,0:T(8,128)(2,1)}, u32[]{:S(2)}, u32[]{:S(2)}) collective-permute-start(bf16[2,256,1024]{2,1,0:T(8,128)(2,1)} %get-tuple-element.246), channel_id=1, source_target_pairs={{0,4},{4,0},{1,5},{5,1},{2,6},{6,2},{3,7},{7,3},{8,12},{12,8},{9,1... | collective-permute-start | bytes 3145736 | tf_op jit(solution)/shard_map/ppermute | solution.py:37
  510.4 48.7 %collective-permute-start.46 = (bf16[1024,256]{1,0:T(8,128)(2,1)S(1)}, bf16[1024,256]{1,0:T(8,128)(2,1)S(1)}, u32[]{:S(2)}, u32[]{:S(2)}) collective-permute-start(bf16[1024,256]{1,0:T(8,128)(2,1)S(1)} %get-tuple-element.342), channel_id=1, source_target_pairs={{0,4},{4,0},{1,5},{5,1},{2,6},{6,2},{3,7},{7,3},{8,12},{12,8},{9,1... | collective-permute-start | bytes 1572872 | tf_op jit(solution)/shard_map/ppermute | solution.py:37
  560.0 12.9 %collective-permute-start.49 = (bf16[128,512]{1,0:T(8,128)(2,1)S(1)}, bf16[128,512]{1,0:T(8,128)(2,1)S(1)}, u32[]{:S(2)}, u32[]{:S(2)}) collective-permute-start(bf16[128,512]{1,0:T(8,128)(2,1)S(1)} %get-tuple-element.250), channel_id=1, source_target_pairs={{0,24},{8,0},{16,8},{24,16},{1,25},{9,1},{17,9},{25,17},{2,26},{10... | collective-permute-start | bytes 393224 | tf_op jit(solution)/shard_map/ppermute | solution.py:42
  581.3 30.1 %collective-permute-start.50 = (bf16[1024,2048]{1,0:T(8,128)(2,1)}, bf16[1024,2048]{1,0:T(8,128)(2,1)}, u32[]{:S(2)}, u32[]{:S(2)}) collective-permute-start(bf16[1024,2048]{1,0:T(8,128)(2,1)} %product.14), channel_id=1, source_target_pairs={{0,1},{1,0},{2,3},{3,2},{4,5},{5,4},{6,7},{7,6},{8,9},{9,8},{10,11... | collective-permute-start | bytes 12582920 | tf_op jit(solution)/shard_map/ppermute | solution.py:37
  582.6 90.6 %reduce-scatter.14.cloned.1.call-start = ((), (), s32[]{:S(2)}) async-start(), calls=%async_computation.12 | async-start | bytes 1966080 | tf_op jit(solution)/shard_map/reduce_scatter | solution.py:658
  585.5 15.1 %collective-permute-start.52 = (bf16[256,1024]{1,0:T(8,128)(2,1)}, bf16[256,1024]{1,0:T(8,128)(2,1)}, u32[]{:S(2)}, u32[]{:S(2)}) collective-permute-start(bf16[256,1024]{1,0:T(8,128)(2,1)} %fusion.30), channel_id=1, source_target_pairs={{0,4},{4,0},{1,5},{5,1},{2,6},{6,2},{3,7},{7,3},{8,12},{12,8},{9,1... | collective-permute-start | bytes 1572872 | tf_op jit(solution)/shard_map/ppermute | solution.py:37
  589.3 14.4 %collective-permute-start.53 = (bf16[256,1024]{1,0:T(8,128)(2,1)}, bf16[256,1024]{1,0:T(8,128)(2,1)}, u32[]{:S(2)}, u32[]{:S(2)}) collective-permute-start(bf16[256,1024]{1,0:T(8,128)(2,1)} %fusion.31), channel_id=1, source_target_pairs={{0,2},{2,0},{1,3},{3,1},{4,6},{6,4},{5,7},{7,5},{8,10},{10,8},{9,1... | collective-permute-start | bytes 1572872 | tf_op jit(solution)/shard_map/ppermute | solution.py:37
  591.6 19.8 %collective-permute-start.51 = (bf16[256,1024]{1,0:T(8,128)(2,1)}, bf16[256,1024]{1,0:T(8,128)(2,1)}, u32[]{:S(2)}, u32[]{:S(2)}) collective-permute-start(bf16[256,1024]{1,0:T(8,128)(2,1)} %get-tuple-element.346), channel_id=1, source_target_pairs={{0,4},{4,0},{1,5},{5,1},{2,6},{6,2},{3,7},{7,3},{8,12},{12,8},{9,1... | collective-permute-start | bytes 1572872 | tf_op jit(solution)/shard_map/ppermute | solution.py:37
  619.8 25.1 %collective-permute-start.54 = (bf16[2,256,1024]{2,1,0:T(8,128)(2,1)}, bf16[2,256,1024]{2,1,0:T(8,128)(2,1)}, u32[]{:S(2)}, u32[]{:S(2)}) collective-permute-start(bf16[2,256,1024]{2,1,0:T(8,128)(2,1)} %get-tuple-element.260), channel_id=1, source_target_pairs={{0,2},{2,0},{1,3},{3,1},{4,6},{6,4},{5,7},{7,5},{8,10},{10,8},{9,1... | collective-permute-start | bytes 3145736 | tf_op jit(solution)/shard_map/ppermute | solution.py:37
  621.2 24.8 %collective-permute-start.55 = (bf16[2,256,1024]{2,1,0:T(8,128)(2,1)}, bf16[2,256,1024]{2,1,0:T(8,128)(2,1)}, u32[]{:S(2)}, u32[]{:S(2)}) collective-permute-start(bf16[2,256,1024]{2,1,0:T(8,128)(2,1)} %get-tuple-element.261), channel_id=1, source_target_pairs={{0,4},{4,0},{1,5},{5,1},{2,6},{6,2},{3,7},{7,3},{8,12},{12,8},{9,1... | collective-permute-start | bytes 3145736 | tf_op jit(solution)/shard_map/ppermute | solution.py:37
  647.8 14.9 %collective-permute-start.56 = (bf16[256,1024]{1,0:T(8,128)(2,1)S(1)}, bf16[256,1024]{1,0:T(8,128)(2,1)S(1)}, u32[]{:S(2)}, u32[]{:S(2)}) collective-permute-start(bf16[256,1024]{1,0:T(8,128)(2,1)S(1)} %fusion.32), channel_id=1, source_target_pairs={{0,4},{4,0},{1,5},{5,1},{2,6},{6,2},{3,7},{7,3},{8,12},{12,8},{9,1... | collective-permute-start | bytes 1572872 | tf_op jit(solution)/shard_map/ppermute | solution.py:37
  651.0 12.1 %collective-permute-start.57 = (bf16[256,1024]{1,0:T(8,128)(2,1)S(1)}, bf16[256,1024]{1,0:T(8,128)(2,1)S(1)}, u32[]{:S(2)}, u32[]{:S(2)}) collective-permute-start(bf16[256,1024]{1,0:T(8,128)(2,1)S(1)} %fusion.33), channel_id=1, source_target_pairs={{0,2},{2,0},{1,3},{3,1},{4,6},{6,4},{5,7},{7,5},{8,10},{10,8},{9,1... | collective-permute-start | bytes 1572872 | tf_op jit(solution)/shard_map/ppermute | solution.py:37
  654.5 16.9 %collective-permute-start.65 = (bf16[256,1024]{1,0:T(8,128)(2,1)S(1)}, bf16[256,1024]{1,0:T(8,128)(2,1)S(1)}, u32[]{:S(2)}, u32[]{:S(2)}) collective-permute-start(bf16[256,1024]{1,0:T(8,128)(2,1)S(1)} %get-tuple-element.344), channel_id=1, source_target_pairs={{0,4},{4,0},{1,5},{5,1},{2,6},{6,2},{3,7},{7,3},{8,12},{12,8},{9,1... | collective-permute-start | bytes 1572872 | tf_op jit(solution)/shard_map/ppermute | solution.py:37
  679.6 20.3 %collective-permute-start.64 = (bf16[256,256]{1,0:T(8,128)(2,1)}, bf16[256,256]{1,0:T(8,128)(2,1)S(1)}, u32[]{:S(2)}, u32[]{:S(2)}) collective-permute-start(bf16[256,256]{1,0:T(8,128)(2,1)} %get-tuple-element.380), channel_id=1, source_target_pairs={{0,4},{4,0},{1,5},{5,1},{2,6},{6,2},{3,7},{7,3},{8,12},{12,8},{9,1... | collective-permute-start | bytes 393224 | tf_op jit(solution)/shard_map/ppermute | solution.py:37
  680.9 20.1 %collective-permute-start.63 = (bf16[256,384]{1,0:T(8,128)(2,1)}, bf16[256,384]{1,0:T(8,128)(2,1)}, u32[]{:S(2)}, u32[]{:S(2)}) collective-permute-start(bf16[256,384]{1,0:T(8,128)(2,1)} %constant_dynamic-slice_fusion.7), channel_id=1, source_target_pairs={{0,4},{4,0},{1,5},{5,1},{2,6},{6,2},{3,7},{7,3},{8,12},{12,8},{9,1... | collective-permute-start | bytes 589832 | tf_op jit(solution)/shard_map/ppermute | solution.py:37
  682.0 7.5 %collective-permute-start.60 = (f32[2,4,64]{2,1,0:T(4,128)S(1)}, f32[2,4,64]{2,1,0:T(4,128)S(1)}, u32[]{:S(2)}, u32[]{:S(2)}) collective-permute-start(f32[2,4,64]{2,1,0:T(4,128)S(1)} %bitcast.77), channel_id=1, source_target_pairs={{0,4},{4,0},{1,5},{5,1},{2,6},{6,2},{3,7},{7,3},{8,12},{12,8},{9,1... | collective-permute-start | bytes 6152 | tf_op jit(solution)/shard_map/ppermute | solution.py:37
  (74 other events, 443.7 us)
Sparse Core Ops, SparseCore 0:
  21.8 56.2 all-gather.3
  85.0 153.0 all-gather.5
  239.7 78.9 all-gather.7
  327.7 80.9 reduce-scatter.5
  411.0 77.2 reduce-scatter.7
  490.4 78.2 reduce-scatter.11
  582.7 25.2 reduce-scatter.9
  631.8 31.8 reduce-scatter.13

commit v4 on v3

--- a/solution.py
+++ b/solution.py
@@ -69,9 +69,10 @@
     return lax.optimization_barrier(xs)
 
 
-def gather_one(v):
+def gather_one(v, halves=None):
     half = v.shape[1] // 2
-    return v, swap(v, "c"), swap(v[:, :half], "x"), swap(v[:, half:], "y")
+    halves = (v[:, :half], v[:, half:]) if halves is None else halves
+    return v, swap(v, "c"), swap(halves[0], "x"), swap(halves[1], "y")
 
 
 def gather_two(state):
@@ -210,32 +211,114 @@
         out_specs=out_specs,
         scratch_shapes=scratch,
         compiler_params=pltpu.CompilerParams(vmem_limit_bytes=56 * 2**20),
-        cost_estimate=pl.CostEstimate(
-            flops=2 * sum(t[0].size for t in terms) // 2 * width,
-            bytes_accessed=2 * sum(t[0].size for t in terms) + 2 * rows * width,
-            transcendentals=0,
-        ),
+        cost_estimate=FREE,
         name="product",
     )(*args)
 
 
-def spread_one(terms, came=None):
+def spread_one(terms, came=None, *later):
     came = swap(product(terms, 1), "c") if came is None else came
     left, right, send_x, send_y = product(terms, 0, came)
-    return left, right, swap(send_x, "x"), swap(send_y, "y"), (send_x, send_y)
-
-
-def spread_two(state):
-    left, right, left_x, right_y = state[:4]
-    left = left + left_x.astype(F32)
-    right = right + right_y.astype(F32)
-    send_y, send_x = left[1].astype(BF16), right[1].astype(BF16)
-    return left[0], right[0], swap(send_y, "y"), swap(send_x, "x"), (send_x, send_y)
+    if later:
+        send_x, send_y, *later = tie(send_x, send_y, *later)
+    return left, right, swap(send_x, "x"), swap(send_y, "y"), *later
+
+
+def fold_kernel(left, right, left_x, right_y, left_out, right_out, y_out, x_out):
+    total = left[...] + left_x[...].astype(F32)
+    left_out[...], y_out[...] = total[0], total[1].astype(BF16)
+    total = right[...] + right_y[...].astype(F32)
+    right_out[...], x_out[...] = total[0], total[1].astype(BF16)
+
+
+def fold(*parts):
+    rows, cols = parts[0].shape[1:]
+    size = rows // 4
+    return pl.pallas_call(
+        fold_kernel,
+        out_shape=[jax.ShapeDtypeStruct((rows, cols), d) for d in (F32, F32, BF16, BF16)],
+        grid=(4,),
+        in_specs=[pl.BlockSpec((2, size, cols), lambda i: (0, i, 0))] * 4,
+        out_specs=[pl.BlockSpec((size, cols), lambda i: (i, 0))] * 4,
+        cost_estimate=FREE,
+        name="fold",
+    )(*parts)
+
+
+def spread_two(state, *extra):
+    left, right, send_y, send_x = fold(*state[:4])
+    if extra:
+        send_y, send_x, *extra = tie(send_y, send_x, *extra)
+    return left, right, swap(send_y, "y"), swap(send_x, "x"), *extra
 
 
 def spread_three(state):
     left, right, left_y, right_x = state[:4]
     return jnp.concatenate((left + left_y.astype(F32), right + right_x.astype(F32)), axis=1)
+
+
+def joined(left, right, left_y, right_x):
+    return jnp.concatenate(
+        (left[...] + left_y[...].astype(F32), right[...] + right_x[...].astype(F32)), axis=1
+    )
+
+
+def store_halves(value, out, left_out, right_out):
+    half = value.shape[1] // 2
+    out[...], left_out[...], right_out[...] = value, value[:, :half], value[:, half:]
+
+
+def residual_kernel(*refs):
+    values, mask, gain = (ref[...] for ref in refs[4:7])
+    resid_out, scale_out = refs[7:9]
+    resid = values.astype(F32) + RESIDUAL * mask * joined(*refs[:4])
+    scale = lax.rsqrt(jnp.mean(resid * resid, axis=1, keepdims=True) + EPSILON)
+    resid_out[...], scale_out[...] = resid, scale
+    normal = (resid * scale).astype(BF16).astype(F32)
+    store_halves((normal * gain).astype(BF16), *refs[9:12])
+
+
+def residual_back_kernel(*refs):
+    base, values, scale, gain, mask = (ref[...] for ref in refs[4:9])
+    sums, grad_out = refs[9:11]
+    upstream = joined(*refs[:4])
+    normal = (values * scale).astype(BF16).astype(F32)
+
+    @pl.when(pl.program_id(0) == 0)
+    def _():
+        sums[...] = jnp.zeros(sums.shape, F32)
+
+    share = normal * upstream
+    sums[...] += jnp.sum(share.reshape(-1, 8, share.shape[1]), axis=0)
+    grad = base.astype(F32) + norm_back(values, scale, gain * upstream)
+    grad_out[...] = grad
+    store_halves((RESIDUAL * mask * grad).astype(BF16), *refs[11:14])
+
+
+def input_back_kernel(*refs):
+    base, values, scale, gain = (ref[...] for ref in refs[4:8])
+    grad = base + norm_back(values.astype(F32), scale, gain * joined(*refs[:4]))
+    refs[8][...] = grad.astype(BF16)
+
+
+def row_call(kernel, args, outs, name):
+    rows = args[0].shape[0]
+    size = rows // 4
+
+    def spec(shape):
+        if shape[0] == rows:
+            return pl.BlockSpec((size, shape[1]), lambda i: (i, 0))
+        return pl.BlockSpec(shape, lambda i: (0, 0))
+
+    return pl.pallas_call(
+        kernel,
+        out_shape=[jax.ShapeDtypeStruct(shape, kind) for shape, kind in outs],
+        grid=(4,),
+        in_specs=[spec(arg.shape) for arg in args],
+        out_specs=[spec(shape) for shape, _ in outs],
+        cost_estimate=FREE,
+        name=name,
+    )(*args)
 
 
 def over_z(x, combine):
@@ -545,11 +628,7 @@
         in_specs=specs,
         out_specs=out_specs,
         compiler_params=pltpu.CompilerParams(vmem_limit_bytes=56 * 2**20),
-        cost_estimate=pl.CostEstimate(
-            flops=2 * depth * high * wide,
-            bytes_accessed=2 * (depth * (high + wide) + high * wide),
-            transcendentals=0,
-        ),
+        cost_estimate=FREE,
         name="outer",
     )(*args)
 
@@ -594,8 +673,8 @@
     out_cols = HEADS * HD
     heads_cut = (out_cols, full_heads.shape[1])
 
-    ffn_other = swap(after(ffn_part(other_y), heads_w), "y")
-    ffn_w = ordered(ffn_part(y_rank), ffn_other, y_rank, 0)
+    ffn_own, ffn_sent = tie(ffn_part(y_rank), ffn_part(other_y))
+    ffn_w = ordered(ffn_own, swap(ffn_sent, "y"), y_rank, 0)
     layer_f = layer_in.astype(F32)
     scale_one = lax.rsqrt(jnp.mean(layer_f * layer_f, axis=1, keepdims=True) + EPSILON)
     normal_one = rounded(layer_f * scale_one)
@@ -609,7 +688,7 @@
 
     grad_out = cotangent.astype(F32)
     down_in = (RESIDUAL * own_mask * grad_out).astype(BF16)
-    back_rows = gather_one(after(down_in, ffn_other))
+    back_rows = gather_one(down_in)
     rows = acts_one.shape[0]
     flat = dot(full_qkv, acts_one, 0, 1)
     (qkv,) = call(
@@ -632,26 +711,27 @@
     own_peak = peak[:HEADS]
     came, other_peak = tie(swap(product(terms, 1), "c"), swap(own_peak, "y"))
     branch = spread_one(terms, came)
-    head_peak = after(ordered(own_peak, other_peak, y_rank, 0), *branch[4])
-    head_peak = over_z(head_peak, jnp.maximum)
-    down_rows = gather_three((*back_rows[:5], *after(back_rows[5:], *branch[4])))
+    head_peak = over_z(ordered(own_peak, other_peak, y_rank, 0), jnp.maximum)
+    down_rows = gather_three(back_rows)
     *got, down_rows, down_w, head_peak = tie(*branch[2:4], down_rows, down_w, head_peak)
     head_peak = head_peak[:, 0]
     branch = spread_two((*branch[:2], *got))
     full_down = lax.all_gather(down_w, "z", axis=1, tiled=True)
-    branch_one = spread_three(branch)
-    resid = layer_f + RESIDUAL * own_mask * branch_one
-    scale_two = lax.rsqrt(jnp.mean(resid * resid, axis=1, keepdims=True) + EPSILON)
-    normal_two = rounded(resid * scale_two)
     gain_two = mlp_gain.astype(F32)
-    acts = gather_one((normal_two * gain_two[None, :]).astype(BF16))
+    narrow = (tok_rows, width // 2)
+    resid, scale_two, *acts = row_call(
+        residual_kernel, (*branch[:4], layer_in, own_mask, gain_two[None, :]),
+        [((tok_rows, width), F32), ((tok_rows, 1), F32), ((tok_rows, width), BF16),
+         (narrow, BF16), (narrow, BF16)], "residual",
+    )
+    acts = gather_one(acts[0], acts[1:])
     full_ffn, *acts = tie(full_ffn, *acts)
     acts = gather_two(acts)
     acts_two = gather_three(acts)
 
-    width = full_ffn.shape[1] // 2
+    hid = full_ffn.shape[1] // 2
     gate_proj, up_proj, hidden = ffn_call(
-        hidden_kernel, acts_two, full_ffn, width, (F32, F32, BF16), (), "hidden"
+        hidden_kernel, acts_two, full_ffn, hid, (F32, F32, BF16), (), "hidden"
     )
 
     def reduced(grad, axis):
@@ -665,32 +745,34 @@
     down_sum = reduced(down_part, 1)
     down_rows = after(down_rows, down_part)
     gate_grad, up_grad = ffn_call(
-        hidden_back_kernel, down_rows, full_down, width, (BF16, BF16), (gate_proj, up_proj),
+        hidden_back_kernel, down_rows, full_down, hid, (BF16, BF16), (gate_proj, up_proj),
         "hidden_back",
     )
-    norm_two = spread_one(
-        [(gate_grad, full_ffn, 1, 1, None, 0), (up_grad, full_ffn, 1, 1, None, 1)]
-    )
-    held = after(acts_two, swap(norm_two[4][0][0, :8, :128], "c"))
-    ffn_parts = [outer(held, grad, 0)[0] for grad in (gate_grad, up_grad)]
+    terms = [(gate_grad, full_ffn, 1, 1, None, 0), (up_grad, full_ffn, 1, 1, None, 1)]
+    *norm_two, acts_two = spread_one(terms, None, acts_two)
+    ffn_parts = [outer(acts_two, grad, 0)[0] for grad in (gate_grad, up_grad)]
+    *got, ffn_parts[0], ffn_parts[1] = tie(*norm_two[2:4], *ffn_parts)
     one_sum, two_sum = [reduced(part, 0) for part in ffn_parts]
-    got = tie(*norm_two[2:4], *ffn_parts)[:2]
     norm_two = spread_two((*norm_two[:2], *got))
-    held = after(hidden, *norm_two[4])
-    high_part = product([(held, full_down, 1, 0, None)], 1)
-    got = tie(*norm_two[2:4], high_part)[:2]
-    norm_two_grad = spread_three((*norm_two[:2], *got))
-    grad_resid = grad_out + norm_back(resid, scale_two, gain_two[None, :] * norm_two_grad)
-    mixed = gather_one((RESIDUAL * own_mask * grad_resid).astype(BF16))
-    low_part = product([(after(hidden, mixed[0]), full_down, 1, 0, None)], 0, swap(high_part, "c"))
-    gain_two_part = jnp.sum(normal_two * norm_two_grad, axis=0)
-    *got, gain_two_part = tie(*mixed[2:4], gain_two_part, *low_part)[:3]
+    gain_two_part, grad_resid, *mixed = row_call(
+        residual_back_kernel,
+        (*norm_two[:4], cotangent, resid, scale_two, gain_two[None, :], own_mask),
+        [((8, width), F32), ((tok_rows, width), F32), ((tok_rows, width), BF16), (narrow, BF16),
+         (narrow, BF16)], "residual_back",
+    )
+    mixed_in, hidden = tie(mixed[0], hidden)
+    mixed = gather_one(mixed_in, mixed[1:])
+    terms = [(hidden, full_down, 1, 0, None)]
+    *got, high_part = tie(*mixed[2:4], product(terms, 1))
     mixed = gather_two((*mixed[:2], *got))
-    send_x, send_y = after(low_part[2:], *mixed[1:])
-    second = (*low_part[:2], swap(send_x, "x"), swap(send_y, "y"))
+    low_part = product(terms, 0, swap(high_part, "c"))
+    a1, b1, *low_part = tie(*mixed[5:], *low_part)
+    mixed = (*mixed[:5], a1, b1)
+    second = (*low_part[:2], swap(low_part[2], "x"), swap(low_part[3], "y"))
     mixed_rows = gather_three(mixed)
-    mixed_rows, down_sum = tie(mixed_rows, down_sum)
+    mixed_rows, down_sum, one_sum = tie(mixed_rows, down_sum, one_sum)
     down_own, down_other = traded(down_sum, 1)
+    one_own, one_other = traded(one_sum, 0)
 
     heads_grad = dot(full_out, mixed_rows, 0, 1).astype(BF16)
     dq, dkv, back = call(
@@ -701,44 +783,50 @@
          ((KEYS, HD), F32), ((KEYS, HD), F32), ((HEADS * HD, SLOT_LEN), BF16)],
         "attend_back",
     )
-    back, down_other, *got = tie(back, down_other, *second[2:4])
+    back, down_other, one_other, *got = tie(back, down_other, one_other, *second[2:4])
     back_sent = along(back, -1)
-    second = spread_two((*second[:2], *got))
-    (out_part,) = outer(after(mixed_rows, back), heads, 1)
+    left, right, *sent = fold(*second[:2], *got)
+    (out_part,) = outer(mixed_rows, heads, 1)
+    dkv, back_sent, out_part, *sent = tie(dkv, back_sent, out_part, *sent)
     out_sum = reduced(out_part, 0)
-    dkv, back_sent, out_part, one_sum = tie(dkv, back_sent, out_part, one_sum)
-    one_own, one_other = traded(one_sum, 0)
+    second = left, right, swap(sent[0], "y"), swap(sent[1], "x")
     (dkv_done,) = call(
         finish_kernel, info, (dkv, back_sent, cos, sin), [((2 * HD, rows), BF16)], [], "finish"
     )
     dqkv = jnp.concatenate((dq, dkv_done))
     terms = [(dqkv, full_heads, 0, 1, heads_cut)]
-    came = swap(product(terms, 1), "c")
-    came, out_sum, two_sum, one_other, *got = tie(came, out_sum, two_sum, one_other, *second[2:4])
+    high_part, acts_one, two_sum = tie(product(terms, 1), acts_one, two_sum)
+    two_own, two_sent = half_of(two_sum, y_rank, 0), half_of(two_sum, other_y, 0)
+    qkv_part, sums = outer(acts_one, dqkv, 1, full_heads, heads_cut)
+    came, qkv_part, sums, *got = tie(swap(high_part, "c"), qkv_part, sums, *second[2:4])
     branch_two = spread_three((*second[:2], *got))
     result = resid + RESIDUAL * own_mask * branch_two
-
     norm_one = spread_one(terms, came)
-    qkv_part, sums = outer(after(acts_one, *norm_one[4]), dqkv, 1, full_heads, heads_cut)
-    gain_one_part = sums[:, 0] / gain_one
     qkv_sum = reduced(qkv_part, 0)
-    *got, gain_one_part = tie(*norm_one[2:4], gain_one_part, qkv_part)[:3]
-    norm_one = spread_two((*norm_one[:2], *got))
-    two_own, two_other = traded(two_sum, 0, *norm_one[4])
-    norm_one_grad = spread_three(norm_one)
-    norm_one_grad, qkv_sum = tie(norm_one_grad, qkv_sum)
-    grad_input = grad_resid + norm_back(layer_f, scale_one, gain_one[None, :] * norm_one_grad)
-    gain_one_part = after(gain_one_part, norm_one_grad)
-    out_own, out_other = traded(out_sum, 0, norm_one_grad)
-    own, other = traded(qkv_sum, 0, norm_one_grad)
-
-    gains = jnp.stack((gain_one_part, gain_two_part))
-    gains = gains.reshape(2, lax.axis_size("z"), 2, 2, 2, -1)
-    for dim, axis in ((4, "c"), (3, "x"), (2, "y")):
+    gains = jnp.stack((sums[:, 0] / gain_one, jnp.sum(gain_two_part, axis=0)))
+    gains = over_z(gains, jnp.add).reshape(2, lax.axis_size("z"), 2, 2, 2, -1)
+
+    def halved(gains, dim, axis):
         at = lax.axis_index(axis)
-        other_at = lax.dynamic_index_in_dim(gains, 1 - at, dim, keepdims=False)
-        gains = lax.dynamic_index_in_dim(gains, at, dim, keepdims=False) + swap(other_at, axis)
-    gains = lax.dynamic_index_in_dim(over_z(gains, jnp.add), z_rank, 1, keepdims=False)
+        return (lax.dynamic_index_in_dim(gains, at, dim, keepdims=False),
+                lax.dynamic_index_in_dim(gains, 1 - at, dim, keepdims=False))
+
+    kept, sent = halved(gains, 4, "c")
+    kept, sent = halved(kept + swap(sent, "c"), 3, "x")
+    *got, out_sum = tie(*norm_one[2:4], out_sum)
+    out_own, out_sent = half_of(out_sum, y_rank, 0), half_of(out_sum, other_y, 0)
+    norm_one = spread_two((*norm_one[:2], *got), sent, out_sent, two_sent)
+    sent, out_sent, two_sent = norm_one[4:]
+    kept, sent = halved(kept + swap(sent, "x"), 2, "y")
+    gains = kept + swap(sent, "y")
+    two_other, out_other = swap(two_sent, "y"), swap(out_sent, "y")
+    *norm_one, qkv_sum = tie(*norm_one[:4], qkv_sum)
+    own, other = traded(qkv_sum, 0)
+    (grad_input,) = row_call(
+        input_back_kernel, (*norm_one, grad_resid, layer_in, scale_one, gain_one[None, :]),
+        [((tok_rows, width), BF16)], "input_back",
+    )
+    gains = lax.dynamic_index_in_dim(gains, z_rank, 1, keepdims=False)
 
     down_grad = ordered(down_own, down_other, y_rank, 0).astype(F32)
     gate_w_grad = ordered(one_own, one_other, y_rank, 1).astype(F32)
@@ -759,7 +847,7 @@
     key_clipped = w_key.astype(F32) * jnp.repeat(jnp.sqrt(kv_factor), HD)[None, :]
     return (
         result.astype(BF16),
-        grad_input.astype(BF16),
+        grad_input,
         gains[0],
         query_grad,
         key_grad,

time: 722 us -> 696 us (0.964)
  Pallas kernels: 279 us -> 314 us
  other arithmetic: 71.2 us -> 38 us
  waiting for transfers between devices: 238 us -> 211 us
    pallas_call x0 -> x7, Pallas kernels: none -> 35.8 us  [the longest x4 19.6 us: fold(): pl.pallas_call(fold_kernel, out_shape=[jax.ShapeDtypeStruct((rows, cols),...]
    ppermute x60, waiting for transfers between devices: 212 us -> 192 us  [swap(): return lax.ppermute(x, axis, [(0, 1), (1, 0)])]
    add x11 -> x3, other arithmetic: 12.1 us -> 0.02 us  [the longest x1 0.01 us: shards(): kept, sent = halved(kept + swap(sent, 'c'), 3, 'x')]
  transfers between devices with their start and end apart: 74 -> 74, of which waited for: 44 -> 38; matrix products, arithmetic and copies ran while one was open for 13% -> 9% of each run, Pallas kernels for 38% -> 46%
where the time goes in v4:
time: 696 us; the launch traced here: 686 us
  Pallas kernels  314 us (45%)
  waiting for transfers between devices  211 us (30%)
  starting transfers between devices  63.3 us (9%)
  other arithmetic  38 us (5%)
  local copies, waits for them, and re-layouts  30.3 us (4%)
  between operations  16 us (2%)
  matrix products  12.8 us (2%)
    ppermute x60, waiting for transfers between devices, swap(): return lax.ppermute(x, axis, [(0, 1), (1, 0)])  192 us
    pallas_call x8, Pallas kernels, product(): pl.pallas_call(functools.partial(product_kernel, kinds, came is not None)...  76.7 us
    pallas_call x4, Pallas kernels, call(): pl.pallas_call(kernel, out_shape=[jax.ShapeDtypeStruct(s, d) for s, d in...  70.8 us
    pallas_call x5, Pallas kernels, outer(): pl.pallas_call(kernel, out_shape=outs, grid=(wide // cols, high // rows),...  56.9 us
    ppermute x60, starting transfers between devices, swap(): return lax.ppermute(x, axis, [(0, 1), (1, 0)])  48.3 us
    pallas_call x2, Pallas kernels, ffn_call(): pl.pallas_call(kernel, out_shape=[jax.ShapeDtypeStruct((rows.shape[0], wi...  46 us
    pallas_call x4, Pallas kernels, place(): pl.pallas_call(functools.partial(place_kernel, spots), out_shape=jax.Shap...  28.4 us
    pallas_call x4, Pallas kernels, fold(): pl.pallas_call(fold_kernel, out_shape=[jax.ShapeDtypeStruct((rows, cols),...  19.6 us
  transfers between devices with their start and end apart: 74, of which 38 were waited for; matrix products, arithmetic and copies ran while one was open for 9% of the time, Pallas kernels for 46%

profile of v4, /device:TPU:0, one launch (start us, length us, event | category | flops | bytes accessed | tf_op | source)
XLA Modules:
  0.0 686.1 jit_solution(8662560844832727371)
XLA Ops:
  9.8 3.0 collective-permute-start
  13.0 7.6 %collective-permute-done = bf16[256,640]{1,0:T(8,128)(2,1)S(1)} collective-permute-done((bf16[256,640]{1,0:T(8,128)(2,1)S(1)}, bf16[256,640]{1,0:T(8,128)(2,1)S(1)}, u32[]{:S(2)}, u32[]{:S(2)}) %collective-permute-start) | collective-permute-done | bytes 327712 | tf_op jit(solution)/shard_map/ppermute | solution.py:37
  27.9 9.1 %collective-permute-done.3.refs_2_ = bf16[256,1024]{1,0:T(8,128)(2,1)S(1)} collective-permute-done((bf16[256,1024]{1,0:T(8,128)(2,1)S(1)}, bf16[256,1024]{1,0:T(8,128)(2,1)S(1)}, u32[]{:S(2)}, u32[]{:S(2)}) %collective-permute-start.3) | collective-permute-done | bytes 524320 | tf_op jit(solution)/shard_map/ppermute | solution.py:37
  37.1 3.5 collective-permute-done.4.refs_3_
  44.5 18.5 %collective-permute-done.1 = bf16[256,2048]{1,0:T(8,128)(2,1)S(1)} collective-permute-done((bf16[256,2048]{1,0:T(8,128)(2,1)S(1)}, bf16[256,2048]{1,0:T(8,128)(2,1)S(1)}, u32[]{:S(2)}, u32[]{:S(2)}) %collective-permute-start.1) | collective-permute-done | bytes 1048608 | tf_op jit(solution)/shard_map/ppermute | solution.py:37
  63.0 2.4 maximum_select_fusion
  65.4 17.7 %collective-permute-done.6.refs_5_ = bf16[512,1024]{1,0:T(8,128)(2,1)S(1)} collective-permute-done((bf16[512,1024]{1,0:T(8,128)(2,1)}, bf16[512,1024]{1,0:T(8,128)(2,1)S(1)}, u32[]{:S(2)}, u32[]{:S(2)}) %collective-permute-start.6) | collective-permute-done | bytes 1048608 | tf_op jit(solution)/shard_map/ppermute | solution.py:37
  88.7 2.3 fusion.32
  95.4 7.5 %place.4.left = bf16[2048,2048]{1,0:T(8,128)(2,1)} custom-call(bf16[256,2048]{1,0:T(8,128)(2,1)} %copy-done.5, bf16[256,2048]{1,0:T(8,128)(2,1)} %collective-permute-done.2.refs_1_, bf16[256,1024]{1,0:T(8,128)(2,1)} %copy-done.17, bf16[256,1024]{1,0:T(8,128)(2,1)} %copy-done.18, bf16[512,1024]{1,0:T(8,128)(2,1)} %collective-permute-done.5.refs_4_, ...), custom_call_target="tpu_custom_call" | custom-call | tf_op jit(solution)/shard_map/place/pallas_call | solution.py:121
  102.9 6.1 fusion.6.qkv
  111.7 8.9 %collective-permute-done.9.halo = bf16[128,512]{1,0:T(8,128)(2,1)S(1)} collective-permute-done((bf16[128,512]{1,0:T(8,128)(2,1)S(1)}, bf16[128,512]{1,0:T(8,128)(2,1)S(1)}, u32[]{:S(2)}, u32[]{:S(2)}) %collective-permute-start.9) | collective-permute-done | bytes 131104 | tf_op jit(solution)/shard_map/ppermute | solution.py:42
  127.4 28.7 %attend.1 = (bf16[256,2048]{1,0:T(8,128)(2,1)S(1)}, f32[8,2048]{1,0:T(8,128)S(1)}, f32[8,128]{1,0:T(8,128)S(1)}) custom-call(s32[3]{0:T(128)S(1)} %pad_add_fusion.info, bf16[384,2048]{1,0:T(8,128)(2,1)S(1)} %rope.1.qkv, bf16[128,512]{1,0:T(8,128)(2,1)S(1)} %collective-permute-done.9.halo), custom_call_target="tpu_custom_call" | custom-call | tf_op jit(solution)/shard_map/attend/pallas_call | solution.py:551
  157.0 3.4 collective-permute-done.13
  160.4 6.6 product.8
  169.9 2.7 collective-permute-done.18
  172.6 1.9 collective-permute-done.17.refs_2_
  174.5 7.4 %product.9 = (f32[2,256,1024]{2,1,0:T(8,128)}, f32[2,256,1024]{2,1,0:T(8,128)}, bf16[2,256,1024]{2,1,0:T(8,128)(2,1)}, bf16[2,256,1024]{2,1,0:T(8,128)(2,1)}) custom-call(bf16[256,2048]{1,0:T(8,128)(2,1)} %copy-done, bf16[2048,640]{1,0:T(8,128)(2,1)} %all-gather.4.cloned.1.call-done.refs_1_.weights, bf16[1024,2048]{1,0:T(8,128)(2,1)} %collective-permute-done.17.refs_2_), custom_call_target="tpu_custom_call" | custom-call | tf_op jit(solution)/shard_map/product/pallas_call | solution.py:206
  184.5 8.4 %collective-permute-done.22 = f32[8,128]{1,0:T(8,128)S(1)} collective-permute-done((f32[8,128]{1,0:T(8,128)S(1)}, f32[8,128]{1,0:T(8,128)S(1)}, u32[]{:S(2)}, u32[]{:S(2)}) %collective-permute-start.22) | collective-permute-done | bytes 4128 | tf_op jit(solution)/shard_map/ppermute | solution.py:42
  192.9 3.1 collective-permute-start.23
  197.2 7.0 %place.5.right.rows = bf16[2048,2048]{1,0:T(8,128)(2,1)} custom-call(bf16[256,2048]{1,0:T(8,128)(2,1)} %multiply_convert_fusion.refs_0_, bf16[256,2048]{1,0:T(8,128)(2,1)} %collective-permute-done.10.refs_1_, bf16[256,1024]{1,0:T(8,128)(2,1)} %copy-done.19, bf16[256,1024]{1,0:T(8,128)(2,1)} %collective-permute-done.12.refs_3_, bf16[512,1024]{1,0:T(8,128)(2,1)} %copy-done.27, ...), custom_call_target="tpu_custom_call" | custom-call | tf_op jit(solution)/shard_map/place/pallas_call | solution.py:121
  204.3 3.0 collective-permute-done.19.left_x
  208.7 4.8 fold.4
  216.0 2.0 fusion.18.refs_5_.refs_8_
  218.0 8.6 %collective-permute-done.24.refs_2_ = bf16[256,1024]{1,0:T(8,128)(2,1)S(1)} collective-permute-done((bf16[256,1024]{1,0:T(8,128)(2,1)}, bf16[256,1024]{1,0:T(8,128)(2,1)S(1)}, u32[]{:S(2)}, u32[]{:S(2)}) %collective-permute-start.24) | collective-permute-done | bytes 524320 | tf_op jit(solution)/shard_map/ppermute | solution.py:37
  227.9 5.0 residual.1
  235.7 11.8 %collective-permute-done.27.refs_2_ = bf16[256,1024]{1,0:T(8,128)(2,1)S(1)} collective-permute-done((bf16[256,1024]{1,0:T(8,128)(2,1)}, bf16[256,1024]{1,0:T(8,128)(2,1)S(1)}, u32[]{:S(2)}, u32[]{:S(2)}) %collective-permute-start.27) | collective-permute-done | bytes 524320 | tf_op jit(solution)/shard_map/ppermute | solution.py:37
  253.3 22.9 %collective-permute-done.30.refs_5_ = bf16[512,1024]{1,0:T(8,128)(2,1)S(1)} collective-permute-done((bf16[512,1024]{1,0:T(8,128)(2,1)S(1)}, bf16[512,1024]{1,0:T(8,128)(2,1)S(1)}, u32[]{:S(2)}, u32[]{:S(2)}) %collective-permute-start.30) | collective-permute-done | bytes 1048608 | tf_op jit(solution)/shard_map/ppermute | solution.py:37
  278.3 4.3 collective-permute-done.32.refs_7_
  282.5 7.0 %place.6.rows.left = bf16[2048,2048]{1,0:T(8,128)(2,1)} custom-call(bf16[256,2048]{1,0:T(8,128)(2,1)} %get-tuple-element.244.refs_0_, bf16[256,2048]{1,0:T(8,128)(2,1)} %collective-permute-done.26.refs_1_, bf16[256,1024]{1,0:T(8,128)(2,1)} %copy-done.21, bf16[256,1024]{1,0:T(8,128)(2,1)} %copy-done.22, bf16[512,1024]{1,0:T(8,128)(2,1)} %copy-done.28, ...), custom_call_target="tpu_custom_call" | custom-call | tf_op jit(solution)/shard_map/place/pallas_call | solution.py:121
  289.5 25.2 %hidden.1 = (f32[2048,1024]{1,0:T(8,128)}, f32[2048,1024]{1,0:T(8,128)}, bf16[2048,1024]{1,0:T(8,128)(2,1)}) custom-call(bf16[2048,2048]{1,0:T(8,128)(2,1)} %place.6.rows.left, bf16[2048,2048]{1,0:T(8,128)(2,1)} %all-gather.6.cloned.1.call-done.gate_w.up_w.refs_1_.refs_3_, bf16[2048,2048]{1,0:T(8,128)(2,1)} %all-gather.6.cloned.1.call-done.gate_w.up_w.refs_1_.refs_3_), custom_call_target="tpu_custom_call" | custom-call | tf_op jit(solution)/shard_map/hidden/pallas_call | solution.py:586
  314.7 14.2 %outer.5 = bf16[1024,2048]{1,0:T(8,128)(2,1)} custom-call(bf16[2048,1024]{1,0:T(8,128)(2,1)} %get-tuple-element.280.left.refs_0_, bf16[2048,2048]{1,0:T(8,128)(2,1)} %place.5.right.rows), custom_call_target="tpu_custom_call" | custom-call | tf_op jit(solution)/shard_map/outer/pallas_call | solution.py:624
  329.0 20.8 %hidden_back.1 = (bf16[2048,1024]{1,0:T(8,128)(2,1)}, bf16[2048,1024]{1,0:T(8,128)(2,1)}) custom-call(bf16[2048,2048]{1,0:T(8,128)(2,1)} %place.5.right.rows, bf16[1024,2048]{1,0:T(8,128)(2,1)} %all-gather.8.cloned.1.call-done.weights.refs_1_, f32[2048,1024]{1,0:T(8,128)} %get-tuple-element.258.gates, f32[2048,1024]{1,0:T(8,128)} %get-tuple-element.259.ups), custom_call_target="tpu_custom_call" | custom-call | tf_op jit(solution)/shard_map/hidden_back/pallas_call | solution.py:586
  349.8 13.4 %product.10 = bf16[1024,2048]{1,0:T(8,128)(2,1)} custom-call(bf16[2048,1024]{1,0:T(8,128)(2,1)} %get-tuple-element.260.refs_0_.right, bf16[2048,2048]{1,0:T(8,128)(2,1)} %all-gather.6.cloned.1.call-done.gate_w.up_w.refs_1_.refs_3_, bf16[2048,1024]{1,0:T(8,128)(2,1)} %get-tuple-element.261.refs_2_.right, ...), custom_call_target="tpu_custom_call" | custom-call | tf_op jit(solution)/shard_map/product/pallas_call | solution.py:206
  363.5 7.1 %collective-permute-done.33.refs_4_ = bf16[1024,2048]{1,0:T(8,128)(2,1)S(1)} collective-permute-done((bf16[1024,2048]{1,0:T(8,128)(2,1)}, bf16[1024,2048]{1,0:T(8,128)(2,1)S(1)}, u32[]{:S(2)}, u32[]{:S(2)}) %collective-permute-start.33) | collective-permute-done | bytes 4194336 | tf_op jit(solution)/shard_map/ppermute | solution.py:37
  370.6 2.0 copy-done.8
  372.6 15.6 %product.11 = (f32[2,256,1024]{2,1,0:T(8,128)}, f32[2,256,1024]{2,1,0:T(8,128)}, bf16[2,256,1024]{2,1,0:T(8,128)(2,1)}, bf16[2,256,1024]{2,1,0:T(8,128)(2,1)}) custom-call(bf16[2048,1024]{1,0:T(8,128)(2,1)} %get-tuple-element.260.refs_0_.right, bf16[2048,2048]{1,0:T(8,128)(2,1)} %all-gather.6.cloned.1.call-done.gate_w.up_w.refs_1_.refs_3_, ...), custom_call_target="tpu_custom_call" | custom-call | tf_op jit(solution)/shard_map/product/pallas_call | solution.py:206
  390.0 13.4 %outer.7 = bf16[2048,1024]{1,0:T(8,128)(2,1)} custom-call(bf16[2048,2048]{1,0:T(8,128)(2,1)} %place.6.rows.left, bf16[2048,1024]{1,0:T(8,128)(2,1)} %get-tuple-element.261.refs_2_.right), custom_call_target="tpu_custom_call" | custom-call | tf_op jit(solution)/shard_map/outer/pallas_call | solution.py:624
  403.4 13.3 %outer.6 = bf16[2048,1024]{1,0:T(8,128)(2,1)} custom-call(bf16[2048,2048]{1,0:T(8,128)(2,1)} %place.6.rows.left, bf16[2048,1024]{1,0:T(8,128)(2,1)} %get-tuple-element.260.refs_0_.right), custom_call_target="tpu_custom_call" | custom-call | tf_op jit(solution)/shard_map/outer/pallas_call | solution.py:624
  417.7 4.8 fold.5
  425.0 11.2 %collective-permute-done.36.refs_2_ = bf16[256,1024]{1,0:T(8,128)(2,1)S(1)} collective-permute-done((bf16[256,1024]{1,0:T(8,128)(2,1)}, bf16[256,1024]{1,0:T(8,128)(2,1)S(1)}, u32[]{:S(2)}, u32[]{:S(2)}) %collective-permute-start.36) | collective-permute-done | bytes 524320 | tf_op jit(solution)/shard_map/ppermute | solution.py:37
  437.9 6.2 residual_back.1
  446.4 8.5 %product.12 = bf16[1024,2048]{1,0:T(8,128)(2,1)} custom-call(bf16[2048,1024]{1,0:T(8,128)(2,1)} %get-tuple-element.280.left.refs_0_, bf16[1024,2048]{1,0:T(8,128)(2,1)} %all-gather.8.cloned.1.call-done.weights.refs_1_), custom_call_target="tpu_custom_call" | custom-call | tf_op jit(solution)/shard_map/product/pallas_call | solution.py:206
  457.8 2.8 pad_maximum_fusion.11
  462.7 2.4 collective-permute-done.42.refs_2_
  465.1 2.1 copy-done.7
  467.2 10.2 %product.13 = (f32[2,256,1024]{2,1,0:T(8,128)}, f32[2,256,1024]{2,1,0:T(8,128)}, bf16[2,256,1024]{2,1,0:T(8,128)(2,1)}, bf16[2,256,1024]{2,1,0:T(8,128)(2,1)}) custom-call(bf16[2048,1024]{1,0:T(8,128)(2,1)} %get-tuple-element.280.left.refs_0_, bf16[1024,2048]{1,0:T(8,128)(2,1)} %all-gather.8.cloned.1.call-done.weights.refs_1_, bf16[1024,2048]{1,0:T(8,128)(2,1)} %copy-done.7), custom_call_target="tpu_custom_call" | custom-call | tf_op jit(solution)/shard_map/product/pallas_call | solution.py:206
  477.4 9.1 %collective-permute-done.40.refs_5_ = bf16[512,1024]{1,0:T(8,128)(2,1)} collective-permute-done((bf16[512,1024]{1,0:T(8,128)(2,1)}, bf16[512,1024]{1,0:T(8,128)(2,1)}, u32[]{:S(2)}, u32[]{:S(2)}) %collective-permute-start.40) | collective-permute-done | bytes 1048608 | tf_op jit(solution)/shard_map/ppermute | solution.py:37
  490.9 2.4 collective-permute-done.45.refs_7_
  493.3 6.9 %place.7.left = bf16[2048,2048]{1,0:T(8,128)(2,1)} custom-call(bf16[256,2048]{1,0:T(8,128)(2,1)} %get-tuple-element.277.refs_0_, bf16[256,2048]{1,0:T(8,128)(2,1)} %collective-permute-done.43.refs_1_, bf16[256,1024]{1,0:T(8,128)(2,1)} %copy-done.20, bf16[256,1024]{1,0:T(8,128)(2,1)} %collective-permute-done.39.refs_3_, ...), custom_call_target="tpu_custom_call" | custom-call | tf_op jit(solution)/shard_map/place/pallas_call | solution.py:121
  500.3 2.2 constant_dynamic-slice_fusion.2
  505.4 6.7 convolution_convert_fusion.upstream
  512.1 40.4 %attend_back.1 = (bf16[256,2048]{1,0:T(8,128)(2,1)S(1)}, f32[128,2048]{1,0:T(8,128)S(1)}, bf16[128,512]{1,0:T(8,128)(2,1)S(1)}) custom-call(s32[3]{0:T(128)S(1)} %pad_add_fusion.info, bf16[384,2048]{1,0:T(8,128)(2,1)S(1)} %rope.1.qkv, bf16[128,512]{1,0:T(8,128)(2,1)S(1)} %collective-permute-done.9.halo, ...), custom_call_target="tpu_custom_call" | custom-call | tf_op jit(solution)/shard_map/attend_back/pallas_call | solution.py:551
  554.5 6.2 collective-permute-start.50
  560.7 6.7 outer.8
  567.4 5.0 fold.6
  574.4 6.5 product.14
  588.1 9.3 %outer.9 = (bf16[2048,384]{1,0:T(8,128)(2,1)}, f32[2048,128]{1,0:T(8,128)}) custom-call(bf16[2048,2048]{1,0:T(8,128)(2,1)} %place.4.left, bf16[384,2048]{1,0:T(8,128)(2,1)} %pad_maximum_fusion.4.refs_0_.right, bf16[2048,640]{1,0:T(8,128)(2,1)} %all-gather.4.cloned.1.call-done.refs_1_.weights), custom_call_target="tpu_custom_call" | custom-call | tf_op jit(solution)/shard_map/outer/pallas_call | solution.py:624
  602.5 8.5 %product.15 = (f32[2,256,1024]{2,1,0:T(8,128)}, f32[2,256,1024]{2,1,0:T(8,128)}, bf16[2,256,1024]{2,1,0:T(8,128)(2,1)}, bf16[2,256,1024]{2,1,0:T(8,128)(2,1)}) custom-call(bf16[384,2048]{1,0:T(8,128)(2,1)} %pad_maximum_fusion.4.refs_0_.right, bf16[2048,640]{1,0:T(8,128)(2,1)} %all-gather.4.cloned.1.call-done.refs_1_.weights, ...), custom_call_target="tpu_custom_call" | custom-call | tf_op jit(solution)/shard_map/product/pallas_call | solution.py:206
  619.3 16.8 %collective-permute-done.54.left_x = bf16[2,256,1024]{2,1,0:T(8,128)(2,1)} collective-permute-done((bf16[2,256,1024]{2,1,0:T(8,128)(2,1)}, bf16[2,256,1024]{2,1,0:T(8,128)(2,1)}, u32[]{:S(2)}, u32[]{:S(2)}) %collective-permute-start.54) | collective-permute-done | bytes 1048608 | tf_op jit(solution)/shard_map/ppermute | solution.py:37
  636.5 5.0 fold.7
  650.5 7.8 %collective-permute-done.62 = f32[2,4,64]{2,1,0:T(4,128)S(1)} collective-permute-done((f32[2,4,64]{2,1,0:T(4,128)S(1)}, f32[2,4,64]{2,1,0:T(4,128)S(1)}, u32[]{:S(2)}, u32[]{:S(2)}) %collective-permute-start.62) | collective-permute-done | bytes 2080 | tf_op jit(solution)/shard_map/ppermute | solution.py:37
  658.8 2.3 collective-permute-done.64
  663.9 5.6 collective-permute-done.59.refs_2_
  671.4 5.0 input_back.1
  (329 shorter events, 119.5 us)
Async XLA Ops:
  7.2 76.0 %all-gather.4.cloned.1.call-start = ((), (), s32[]{:S(2)}) async-start(), calls=%async_computation.5 | async-start | bytes 3276800 | tf_op jit(solution)/shard_map/all_gather | solution.py:672
  9.8 10.7 %collective-permute-start = (bf16[256,640]{1,0:T(8,128)(2,1)S(1)}, bf16[256,640]{1,0:T(8,128)(2,1)S(1)}, u32[]{:S(2)}, u32[]{:S(2)}) collective-permute-start(bf16[256,640]{1,0:T(8,128)(2,1)S(1)} %pad_maximum_fusion.19), channel_id=1, source_target_pairs={{0,4},{4,0},{1,5},{5,1},{2,6},{6,2},{3,7},{7,3},{8,12},{12,8},{9,1... | collective-permute-start | bytes 983048 | tf_op jit(solution)/shard_map/ppermute | solution.py:37
  21.8 226.9 %all-gather.6.cloned.1.call-start = ((), (), s32[]{:S(2)}) async-start(), calls=%async_computation.6 | async-start | bytes 10485760 | tf_op jit(solution)/shard_map/all_gather | solution.py:687
  23.9 13.2 %collective-permute-start.3 = (bf16[256,1024]{1,0:T(8,128)(2,1)S(1)}, bf16[256,1024]{1,0:T(8,128)(2,1)S(1)}, u32[]{:S(2)}, u32[]{:S(2)}) collective-permute-start(bf16[256,1024]{1,0:T(8,128)(2,1)S(1)} %get-tuple-element.428), channel_id=1, source_target_pairs={{0,2},{2,0},{1,3},{3,1},{4,6},{6,4},{5,7},{7,5},{8,10},{10,8},{9,1... | collective-permute-start | bytes 1572872 | tf_op jit(solution)/shard_map/ppermute | solution.py:37
  25.7 14.9 %collective-permute-start.4 = (bf16[256,1024]{1,0:T(8,128)(2,1)S(1)}, bf16[256,1024]{1,0:T(8,128)(2,1)S(1)}, u32[]{:S(2)}, u32[]{:S(2)}) collective-permute-start(bf16[256,1024]{1,0:T(8,128)(2,1)S(1)} %get-tuple-element.427), channel_id=1, source_target_pairs={{0,4},{4,0},{1,5},{5,1},{2,6},{6,2},{3,7},{7,3},{8,12},{12,8},{9,1... | collective-permute-start | bytes 1572872 | tf_op jit(solution)/shard_map/ppermute | solution.py:37
  27.3 35.7 %collective-permute-start.1 = (bf16[256,2048]{1,0:T(8,128)(2,1)S(1)}, bf16[256,2048]{1,0:T(8,128)(2,1)S(1)}, u32[]{:S(2)}, u32[]{:S(2)}) collective-permute-start(bf16[256,2048]{1,0:T(8,128)(2,1)S(1)} %pad_maximum_fusion.14), channel_id=1, source_target_pairs={{0,4},{4,0},{1,5},{5,1},{2,6},{6,2},{3,7},{7,3},{8,12},{12,8},{9,1... | collective-permute-start | bytes 3145736 | tf_op jit(solution)/shard_map/ppermute | solution.py:37
  27.9 37.5 %collective-permute-start.2 = (bf16[256,2048]{1,0:T(8,128)(2,1)S(1)}, bf16[256,2048]{1,0:T(8,128)(2,1)}, u32[]{:S(2)}, u32[]{:S(2)}) collective-permute-start(bf16[256,2048]{1,0:T(8,128)(2,1)S(1)} %fusion.3.refs_0_), channel_id=1, source_target_pairs={{0,1},{1,0},{2,3},{3,2},{4,5},{5,4},{6,7},{7,6},{8,9},{9,8},{10,11... | collective-permute-start | bytes 3145736 | tf_op jit(solution)/shard_map/ppermute | solution.py:37
  42.4 23.0 %collective-permute-start.5 = (bf16[512,1024]{1,0:T(8,128)(2,1)}, bf16[512,1024]{1,0:T(8,128)(2,1)}, u32[]{:S(2)}, u32[]{:S(2)}) collective-permute-start(bf16[512,1024]{1,0:T(8,128)(2,1)} %get-tuple-element.443), channel_id=1, source_target_pairs={{0,1},{1,0},{2,3},{3,2},{4,5},{5,4},{6,7},{7,6},{8,9},{9,8},{10,11... | collective-permute-start | bytes 3145736 | tf_op jit(solution)/shard_map/ppermute | solution.py:37
  42.4 40.7 %collective-permute-start.6 = (bf16[512,1024]{1,0:T(8,128)(2,1)}, bf16[512,1024]{1,0:T(8,128)(2,1)S(1)}, u32[]{:S(2)}, u32[]{:S(2)}) collective-permute-start(bf16[512,1024]{1,0:T(8,128)(2,1)} %get-tuple-element.444), channel_id=1, source_target_pairs={{0,4},{4,0},{1,5},{5,1},{2,6},{6,2},{3,7},{7,3},{8,12},{12,8},{9,1... | collective-permute-start | bytes 3145736 | tf_op jit(solution)/shard_map/ppermute | solution.py:37
  44.0 39.2 %collective-permute-start.7 = (bf16[512,1024]{1,0:T(8,128)(2,1)}, bf16[512,1024]{1,0:T(8,128)(2,1)S(1)}, u32[]{:S(2)}, u32[]{:S(2)}) collective-permute-start(bf16[512,1024]{1,0:T(8,128)(2,1)} %get-tuple-element.442), channel_id=1, source_target_pairs={{0,2},{2,0},{1,3},{3,1},{4,6},{6,4},{5,7},{7,5},{8,10},{10,8},{9,1... | collective-permute-start | bytes 3145736 | tf_op jit(solution)/shard_map/ppermute | solution.py:37
  83.2 245.8 %all-gather.8.cloned.1.call-start = ((), (), s32[]{:S(2)}) async-start(), calls=%async_computation.7 | async-start | bytes 5242880 | tf_op jit(solution)/shard_map/all_gather | solution.py:719
  85.1 10.3 %collective-permute-start.8 = (bf16[1024,1024]{1,0:T(8,128)(2,1)}, bf16[1024,1024]{1,0:T(8,128)(2,1)}, u32[]{:S(2)}, u32[]{:S(2)}) collective-permute-start(bf16[1024,1024]{1,0:T(8,128)(2,1)} %pad_maximum_fusion), channel_id=1, source_target_pairs={{0,1},{1,0},{2,3},{3,2},{4,5},{5,4},{6,7},{7,6},{8,9},{9,8},{10,11... | collective-permute-start | bytes 6291464 | tf_op jit(solution)/shard_map/ppermute | solution.py:37
  88.2 23.5 %collective-permute-start.10 = (bf16[256,2048]{1,0:T(8,128)(2,1)}, bf16[256,2048]{1,0:T(8,128)(2,1)}, u32[]{:S(2)}, u32[]{:S(2)}) collective-permute-start(bf16[256,2048]{1,0:T(8,128)(2,1)} %multiply_convert_fusion.refs_0_), channel_id=1, source_target_pairs={{0,1},{1,0},{2,3},{3,2},{4,5},{5,4},{6,7},{7,6},{8,9},{9,8},{10,11... | collective-permute-start | bytes 3145736 | tf_op jit(solution)/shard_map/ppermute | solution.py:37
  91.0 20.7 %collective-permute-start.11 = (bf16[256,1024]{1,0:T(8,128)(2,1)}, bf16[256,1024]{1,0:T(8,128)(2,1)S(1)}, u32[]{:S(2)}, u32[]{:S(2)}) collective-permute-start(bf16[256,1024]{1,0:T(8,128)(2,1)} %get-tuple-element.426), channel_id=1, source_target_pairs={{0,2},{2,0},{1,3},{3,1},{4,6},{6,4},{5,7},{7,5},{8,10},{10,8},{9,1... | collective-permute-start | bytes 1572872 | tf_op jit(solution)/shard_map/ppermute | solution.py:37
  91.6 20.1 %collective-permute-start.12 = (bf16[256,1024]{1,0:T(8,128)(2,1)}, bf16[256,1024]{1,0:T(8,128)(2,1)}, u32[]{:S(2)}, u32[]{:S(2)}) collective-permute-start(bf16[256,1024]{1,0:T(8,128)(2,1)} %get-tuple-element.425), channel_id=1, source_target_pairs={{0,4},{4,0},{1,5},{5,1},{2,6},{6,2},{3,7},{7,3},{8,12},{12,8},{9,1... | collective-permute-start | bytes 1572872 | tf_op jit(solution)/shard_map/ppermute | solution.py:37
  110.0 10.6 %collective-permute-start.9 = (bf16[128,512]{1,0:T(8,128)(2,1)S(1)}, bf16[128,512]{1,0:T(8,128)(2,1)S(1)}, u32[]{:S(2)}, u32[]{:S(2)}) collective-permute-start(bf16[128,512]{1,0:T(8,128)(2,1)S(1)} %slice.100), channel_id=1, source_target_pairs={{0,8},{8,16},{16,24},{24,0},{1,9},{9,17},{17,25},{25,1},{2,10},{10... | collective-permute-start | bytes 393224 | tf_op jit(solution)/shard_map/ppermute | solution.py:42
  123.5 36.9 %collective-permute-start.14 = (bf16[512,1024]{1,0:T(8,128)(2,1)S(1)}, bf16[512,1024]{1,0:T(8,128)(2,1)S(1)}, u32[]{:S(2)}, u32[]{:S(2)}) collective-permute-start(bf16[512,1024]{1,0:T(8,128)(2,1)S(1)} %get-tuple-element.440), channel_id=1, source_target_pairs={{0,1},{1,0},{2,3},{3,2},{4,5},{5,4},{6,7},{7,6},{8,9},{9,8},{10,11... | collective-permute-start | bytes 3145736 | tf_op jit(solution)/shard_map/ppermute | solution.py:37
  123.6 36.8 %collective-permute-start.15 = (bf16[512,1024]{1,0:T(8,128)(2,1)S(1)}, bf16[512,1024]{1,0:T(8,128)(2,1)S(1)}, u32[]{:S(2)}, u32[]{:S(2)}) collective-permute-start(bf16[512,1024]{1,0:T(8,128)(2,1)S(1)} %get-tuple-element.441), channel_id=1, source_target_pairs={{0,4},{4,0},{1,5},{5,1},{2,6},{6,2},{3,7},{7,3},{8,12},{12,8},{9,1... | collective-permute-start | bytes 3145736 | tf_op jit(solution)/shard_map/ppermute | solution.py:37
  124.5 35.9 %collective-permute-start.16 = (bf16[512,1024]{1,0:T(8,128)(2,1)S(1)}, bf16[512,1024]{1,0:T(8,128)(2,1)S(1)}, u32[]{:S(2)}, u32[]{:S(2)}) collective-permute-start(bf16[512,1024]{1,0:T(8,128)(2,1)S(1)} %get-tuple-element.439), channel_id=1, source_target_pairs={{0,2},{2,0},{1,3},{3,1},{4,6},{6,4},{5,7},{7,5},{8,10},{10,8},{9,1... | collective-permute-start | bytes 3145736 | tf_op jit(solution)/shard_map/ppermute | solution.py:37
  126.0 34.4 %collective-permute-start.13 = (bf16[1024,256]{1,0:T(8,128)(2,1)S(1)}, bf16[1024,256]{1,0:T(8,128)(2,1)S(1)}, u32[]{:S(2)}, u32[]{:S(2)}) collective-permute-start(bf16[1024,256]{1,0:T(8,128)(2,1)S(1)} %get-tuple-element.207), channel_id=1, source_target_pairs={{0,4},{4,0},{1,5},{5,1},{2,6},{6,2},{3,7},{7,3},{8,12},{12,8},{9,1... | collective-permute-start | bytes 1572872 | tf_op jit(solution)/shard_map/ppermute | solution.py:37
  167.0 7.5 %collective-permute-start.17 = (bf16[1024,2048]{1,0:T(8,128)(2,1)}, bf16[1024,2048]{1,0:T(8,128)(2,1)}, u32[]{:S(2)}, u32[]{:S(2)}) collective-permute-start(bf16[1024,2048]{1,0:T(8,128)(2,1)} %product.8), channel_id=1, source_target_pairs={{0,1},{1,0},{2,3},{3,2},{4,5},{5,4},{6,7},{7,6},{8,9},{9,8},{10,11... | collective-permute-start | bytes 12582920 | tf_op jit(solution)/shard_map/ppermute | solution.py:37
  168.5 28.7 %collective-permute-start.21 = (bf16[1024,1024]{1,0:T(8,128)(2,1)}, bf16[1024,1024]{1,0:T(8,128)(2,1)}, u32[]{:S(2)}, u32[]{:S(2)}) collective-permute-start(bf16[1024,1024]{1,0:T(8,128)(2,1)} %pad_maximum_fusion.1), channel_id=1, source_target_pairs={{0,1},{1,0},{2,3},{3,2},{4,5},{5,4},{6,7},{7,6},{8,9},{9,8},{10,11... | collective-permute-start | bytes 6291464 | tf_op jit(solution)/shard_map/ppermute | solution.py:37
  181.9 25.4 %collective-permute-start.19 = (bf16[2,256,1024]{2,1,0:T(8,128)(2,1)}, bf16[2,256,1024]{2,1,0:T(8,128)(2,1)S(1)}, u32[]{:S(2)}, u32[]{:S(2)}) collective-permute-start(bf16[2,256,1024]{2,1,0:T(8,128)(2,1)} %get-tuple-element.215), channel_id=1, source_target_pairs={{0,2},{2,0},{1,3},{3,1},{4,6},{6,4},{5,7},{7,5},{8,10},{10,8},{9,1... | collective-permute-start | bytes 3145736 | tf_op jit(solution)/shard_map/ppermute | solution.py:37
  183.4 25.2 %collective-permute-start.20 = (bf16[2,256,1024]{2,1,0:T(8,128)(2,1)}, bf16[2,256,1024]{2,1,0:T(8,128)(2,1)}, u32[]{:S(2)}, u32[]{:S(2)}) collective-permute-start(bf16[2,256,1024]{2,1,0:T(8,128)(2,1)} %get-tuple-element.216), channel_id=1, source_target_pairs={{0,4},{4,0},{1,5},{5,1},{2,6},{6,2},{3,7},{7,3},{8,12},{12,8},{9,1... | collective-permute-start | bytes 3145736 | tf_op jit(solution)/shard_map/ppermute | solution.py:37
  184.2 8.8 %collective-permute-start.22 = (f32[8,128]{1,0:T(8,128)S(1)}, f32[8,128]{1,0:T(8,128)S(1)}, u32[]{:S(2)}, u32[]{:S(2)}) collective-permute-start(f32[8,128]{1,0:T(8,128)S(1)} %maximum_select_fusion.10), channel_id=1, source_target_pairs={{0,8},{8,16},{16,24},{24,0},{1,9},{9,17},{17,25},{25,1},{2,10},{10... | collective-permute-start | bytes 12296 | tf_op jit(solution)/shard_map/ppermute | solution.py:42
  192.9 11.4 %collective-permute-start.23 = (f32[8,128]{1,0:T(8,128)S(1)}, f32[8,128]{1,0:T(8,128)S(1)}, u32[]{:S(2)}, u32[]{:S(2)}) collective-permute-start(f32[8,128]{1,0:T(8,128)S(1)} %max.17), channel_id=1, source_target_pairs={{0,16},{8,24},{16,0},{24,8},{1,17},{9,25},{17,1},{25,9},{2,18},{10... | collective-permute-start | bytes 12296 | tf_op jit(solution)/shard_map/ppermute | solution.py:42
  208.7 291.6 %reduce-scatter.6.cloned.1.call-start = ((), (), s32[]{:S(2)}) async-start(), calls=%async_computation.8 | async-start | bytes 5242880 | tf_op jit(solution)/shard_map/reduce_scatter | solution.py:738
  213.6 13.0 %collective-permute-start.24 = (bf16[256,1024]{1,0:T(8,128)(2,1)}, bf16[256,1024]{1,0:T(8,128)(2,1)S(1)}, u32[]{:S(2)}, u32[]{:S(2)}) collective-permute-start(bf16[256,1024]{1,0:T(8,128)(2,1)} %get-tuple-element.236), channel_id=1, source_target_pairs={{0,4},{4,0},{1,5},{5,1},{2,6},{6,2},{3,7},{7,3},{8,12},{12,8},{9,1... | collective-permute-start | bytes 1572872 | tf_op jit(solution)/shard_map/ppermute | solution.py:37
  214.3 12.8 %collective-permute-start.25 = (bf16[256,1024]{1,0:T(8,128)(2,1)}, bf16[256,1024]{1,0:T(8,128)(2,1)S(1)}, u32[]{:S(2)}, u32[]{:S(2)}) collective-permute-start(bf16[256,1024]{1,0:T(8,128)(2,1)} %get-tuple-element.237), channel_id=1, source_target_pairs={{0,2},{2,0},{1,3},{3,1},{4,6},{6,4},{5,7},{7,5},{8,10},{10,8},{9,1... | collective-permute-start | bytes 1572872 | tf_op jit(solution)/shard_map/ppermute | solution.py:37
  232.9 15.8 %collective-permute-start.26 = (bf16[256,2048]{1,0:T(8,128)(2,1)}, bf16[256,2048]{1,0:T(8,128)(2,1)}, u32[]{:S(2)}, u32[]{:S(2)}) collective-permute-start(bf16[256,2048]{1,0:T(8,128)(2,1)} %get-tuple-element.244.refs_0_), channel_id=1, source_target_pairs={{0,1},{1,0},{2,3},{3,2},{4,5},{5,4},{6,7},{7,6},{8,9},{9,8},{10,11... | collective-permute-start | bytes 3145736 | tf_op jit(solution)/shard_map/ppermute | solution.py:37
  232.9 14.5 %collective-permute-start.27 = (bf16[256,1024]{1,0:T(8,128)(2,1)}, bf16[256,1024]{1,0:T(8,128)(2,1)S(1)}, u32[]{:S(2)}, u32[]{:S(2)}) collective-permute-start(bf16[256,1024]{1,0:T(8,128)(2,1)} %get-tuple-element.242), channel_id=1, source_target_pairs={{0,2},{2,0},{1,3},{3,1},{4,6},{6,4},{5,7},{7,5},{8,10},{10,8},{9,1... | collective-permute-start | bytes 1572872 | tf_op jit(solution)/shard_map/ppermute | solution.py:37
  234.5 14.2 %collective-permute-start.28 = (bf16[256,1024]{1,0:T(8,128)(2,1)}, bf16[256,1024]{1,0:T(8,128)(2,1)S(1)}, u32[]{:S(2)}, u32[]{:S(2)}) collective-permute-start(bf16[256,1024]{1,0:T(8,128)(2,1)} %get-tuple-element.243), channel_id=1, source_target_pairs={{0,4},{4,0},{1,5},{5,1},{2,6},{6,2},{3,7},{7,3},{8,12},{12,8},{9,1... | collective-permute-start | bytes 1572872 | tf_op jit(solution)/shard_map/ppermute | solution.py:37
  250.7 25.6 %collective-permute-start.30 = (bf16[512,1024]{1,0:T(8,128)(2,1)S(1)}, bf16[512,1024]{1,0:T(8,128)(2,1)S(1)}, u32[]{:S(2)}, u32[]{:S(2)}) collective-permute-start(bf16[512,1024]{1,0:T(8,128)(2,1)S(1)} %get-tuple-element.438), channel_id=1, source_target_pairs={{0,4},{4,0},{1,5},{5,1},{2,6},{6,2},{3,7},{7,3},{8,12},{12,8},{9,1... | collective-permute-start | bytes 3145736 | tf_op jit(solution)/shard_map/ppermute | solution.py:37
  252.0 25.2 %collective-permute-start.31 = (bf16[512,1024]{1,0:T(8,128)(2,1)S(1)}, bf16[512,1024]{1,0:T(8,128)(2,1)S(1)}, u32[]{:S(2)}, u32[]{:S(2)}) collective-permute-start(bf16[512,1024]{1,0:T(8,128)(2,1)S(1)} %get-tuple-element.436), channel_id=1, source_target_pairs={{0,2},{2,0},{1,3},{3,1},{4,6},{6,4},{5,7},{7,5},{8,10},{10,8},{9,1... | collective-permute-start | bytes 3145736 | tf_op jit(solution)/shard_map/ppermute | solution.py:37
  328.9 171.4 %reduce-scatter.8.cloned.1.call-start = ((), (), s32[]{:S(2)}) async-start(), calls=%async_computation.9 | async-start | bytes 5242880 | tf_op jit(solution)/shard_map/reduce_scatter | solution.py:738
  388.2 28.5 %collective-permute-start.34 = (bf16[2,256,1024]{2,1,0:T(8,128)(2,1)}, bf16[2,256,1024]{2,1,0:T(8,128)(2,1)S(1)}, u32[]{:S(2)}, u32[]{:S(2)}) collective-permute-start(bf16[2,256,1024]{2,1,0:T(8,128)(2,1)} %get-tuple-element.266), channel_id=1, source_target_pairs={{0,2},{2,0},{1,3},{3,1},{4,6},{6,4},{5,7},{7,5},{8,10},{10,8},{9,1... | collective-permute-start | bytes 3145736 | tf_op jit(solution)/shard_map/ppermute | solution.py:37
  389.2 27.5 %collective-permute-start.35 = (bf16[2,256,1024]{2,1,0:T(8,128)(2,1)}, bf16[2,256,1024]{2,1,0:T(8,128)(2,1)}, u32[]{:S(2)}, u32[]{:S(2)}) collective-permute-start(bf16[2,256,1024]{2,1,0:T(8,128)(2,1)} %get-tuple-element.267), channel_id=1, source_target_pairs={{0,4},{4,0},{1,5},{5,1},{2,6},{6,2},{3,7},{7,3},{8,12},{12,8},{9,1... | collective-permute-start | bytes 3145736 | tf_op jit(solution)/shard_map/ppermute | solution.py:37
  417.7 163.2 %reduce-scatter.10.cloned.1.call-start = ((), (), s32[]{:S(2)}) async-start(), calls=%async_computation.10 | async-start | bytes 5242880 | tf_op jit(solution)/shard_map/reduce_scatter | solution.py:738
  422.5 13.7 %collective-permute-start.36 = (bf16[256,1024]{1,0:T(8,128)(2,1)}, bf16[256,1024]{1,0:T(8,128)(2,1)S(1)}, u32[]{:S(2)}, u32[]{:S(2)}) collective-permute-start(bf16[256,1024]{1,0:T(8,128)(2,1)} %get-tuple-element.273), channel_id=1, source_target_pairs={{0,4},{4,0},{1,5},{5,1},{2,6},{6,2},{3,7},{7,3},{8,12},{12,8},{9,1... | collective-permute-start | bytes 1572872 | tf_op jit(solution)/shard_map/ppermute | solution.py:37
  423.8 13.3 %collective-permute-start.37 = (bf16[256,1024]{1,0:T(8,128)(2,1)}, bf16[256,1024]{1,0:T(8,128)(2,1)S(1)}, u32[]{:S(2)}, u32[]{:S(2)}) collective-permute-start(bf16[256,1024]{1,0:T(8,128)(2,1)} %get-tuple-element.274), channel_id=1, source_target_pairs={{0,2},{2,0},{1,3},{3,1},{4,6},{6,4},{5,7},{7,5},{8,10},{10,8},{9,1... | collective-permute-start | bytes 1572872 | tf_op jit(solution)/shard_map/ppermute | solution.py:37
  424.8 194.6 %reduce-scatter.12.cloned.1.call-start = ((), (), s32[]{:S(2)}) async-start(), calls=%async_computation.11 | async-start | bytes 1310720 | tf_op jit(solution)/shard_map/reduce_scatter | solution.py:738
  444.1 12.5 %collective-permute-start.38 = (bf16[256,1024]{1,0:T(8,128)(2,1)}, bf16[256,1024]{1,0:T(8,128)(2,1)S(1)}, u32[]{:S(2)}, u32[]{:S(2)}) collective-permute-start(bf16[256,1024]{1,0:T(8,128)(2,1)} %get-tuple-element.278), channel_id=1, source_target_pairs={{0,2},{2,0},{1,3},{3,1},{4,6},{6,4},{5,7},{7,5},{8,10},{10,8},{9,1... | collective-permute-start | bytes 1572872 | tf_op jit(solution)/shard_map/ppermute | solution.py:37
  445.3 12.4 %collective-permute-start.39 = (bf16[256,1024]{1,0:T(8,128)(2,1)}, bf16[256,1024]{1,0:T(8,128)(2,1)}, u32[]{:S(2)}, u32[]{:S(2)}) collective-permute-start(bf16[256,1024]{1,0:T(8,128)(2,1)} %get-tuple-element.279), channel_id=1, source_target_pairs={{0,4},{4,0},{1,5},{5,1},{2,6},{6,2},{3,7},{7,3},{8,12},{12,8},{9,1... | collective-permute-start | bytes 1572872 | tf_op jit(solution)/shard_map/ppermute | solution.py:37
  460.6 25.9 %collective-permute-start.40 = (bf16[512,1024]{1,0:T(8,128)(2,1)}, bf16[512,1024]{1,0:T(8,128)(2,1)}, u32[]{:S(2)}, u32[]{:S(2)}) collective-permute-start(bf16[512,1024]{1,0:T(8,128)(2,1)} %get-tuple-element.434), channel_id=1, source_target_pairs={{0,4},{4,0},{1,5},{5,1},{2,6},{6,2},{3,7},{7,3},{8,12},{12,8},{9,1... | collective-permute-start | bytes 3145736 | tf_op jit(solution)/shard_map/ppermute | solution.py:37
  461.6 25.6 %collective-permute-start.41 = (bf16[512,1024]{1,0:T(8,128)(2,1)}, bf16[512,1024]{1,0:T(8,128)(2,1)}, u32[]{:S(2)}, u32[]{:S(2)}) collective-permute-start(bf16[512,1024]{1,0:T(8,128)(2,1)} %get-tuple-element.435), channel_id=1, source_target_pairs={{0,2},{2,0},{1,3},{3,1},{4,6},{6,4},{5,7},{7,5},{8,10},{10,8},{9,1... | collective-permute-start | bytes 3145736 | tf_op jit(solution)/shard_map/ppermute | solution.py:37
  462.2 25.1 %collective-permute-start.43 = (bf16[256,2048]{1,0:T(8,128)(2,1)S(1)}, bf16[256,2048]{1,0:T(8,128)(2,1)}, u32[]{:S(2)}, u32[]{:S(2)}) collective-permute-start(bf16[256,2048]{1,0:T(8,128)(2,1)S(1)} %copy-done.9), channel_id=1, source_target_pairs={{0,1},{1,0},{2,3},{3,2},{4,5},{5,4},{6,7},{7,6},{8,9},{9,8},{10,11... | collective-permute-start | bytes 3145736 | tf_op jit(solution)/shard_map/ppermute | solution.py:37
  462.2 25.1 %collective-permute-start.44 = (bf16[512,1024]{1,0:T(8,128)(2,1)}, bf16[512,1024]{1,0:T(8,128)(2,1)}, u32[]{:S(2)}, u32[]{:S(2)}) collective-permute-start(bf16[512,1024]{1,0:T(8,128)(2,1)} %get-tuple-element.433), channel_id=1, source_target_pairs={{0,1},{1,0},{2,3},{3,2},{4,5},{5,4},{6,7},{7,6},{8,9},{9,8},{10,11... | collective-permute-start | bytes 3145736 | tf_op jit(solution)/shard_map/ppermute | solution.py:37
  489.1 64.4 %collective-permute-start.48 = (bf16[2,256,1024]{2,1,0:T(8,128)(2,1)}, bf16[2,256,1024]{2,1,0:T(8,128)(2,1)}, u32[]{:S(2)}, u32[]{:S(2)}) collective-permute-start(bf16[2,256,1024]{2,1,0:T(8,128)(2,1)} %get-tuple-element.304), channel_id=1, source_target_pairs={{0,2},{2,0},{1,3},{3,1},{4,6},{6,4},{5,7},{7,5},{8,10},{10,8},{9,1... | collective-permute-start | bytes 3145736 | tf_op jit(solution)/shard_map/ppermute | solution.py:37
  489.7 63.8 %collective-permute-start.49 = (bf16[2,256,1024]{2,1,0:T(8,128)(2,1)}, bf16[2,256,1024]{2,1,0:T(8,128)(2,1)}, u32[]{:S(2)}, u32[]{:S(2)}) collective-permute-start(bf16[2,256,1024]{2,1,0:T(8,128)(2,1)} %get-tuple-element.305), channel_id=1, source_target_pairs={{0,4},{4,0},{1,5},{5,1},{2,6},{6,2},{3,7},{7,3},{8,12},{12,8},{9,1... | collective-permute-start | bytes 3145736 | tf_op jit(solution)/shard_map/ppermute | solution.py:37
  502.5 51.0 %collective-permute-start.46 = (bf16[1024,256]{1,0:T(8,128)(2,1)S(1)}, bf16[1024,256]{1,0:T(8,128)(2,1)S(1)}, u32[]{:S(2)}, u32[]{:S(2)}) collective-permute-start(bf16[1024,256]{1,0:T(8,128)(2,1)S(1)} %get-tuple-element.412), channel_id=1, source_target_pairs={{0,4},{4,0},{1,5},{5,1},{2,6},{6,2},{3,7},{7,3},{8,12},{12,8},{9,1... | collective-permute-start | bytes 1572872 | tf_op jit(solution)/shard_map/ppermute | solution.py:37
  504.3 49.1 %collective-permute-start.47 = (bf16[256,1024]{1,0:T(8,128)(2,1)S(1)}, bf16[256,1024]{1,0:T(8,128)(2,1)S(1)}, u32[]{:S(2)}, u32[]{:S(2)}) collective-permute-start(bf16[256,1024]{1,0:T(8,128)(2,1)S(1)} %get-tuple-element.416), channel_id=1, source_target_pairs={{0,4},{4,0},{1,5},{5,1},{2,6},{6,2},{3,7},{7,3},{8,12},{12,8},{9,1... | collective-permute-start | bytes 1572872 | tf_op jit(solution)/shard_map/ppermute | solution.py:37
  554.5 18.0 %collective-permute-start.50 = (bf16[128,512]{1,0:T(8,128)(2,1)S(1)}, bf16[128,512]{1,0:T(8,128)(2,1)S(1)}, u32[]{:S(2)}, u32[]{:S(2)}) collective-permute-start(bf16[128,512]{1,0:T(8,128)(2,1)S(1)} %get-tuple-element.311), channel_id=1, source_target_pairs={{0,24},{8,0},{16,8},{24,16},{1,25},{9,1},{17,9},{25,17},{2,26},{10... | collective-permute-start | bytes 393224 | tf_op jit(solution)/shard_map/ppermute | solution.py:42
  580.9 17.2 %collective-permute-start.51 = (bf16[1024,2048]{1,0:T(8,128)(2,1)}, bf16[1024,2048]{1,0:T(8,128)(2,1)}, u32[]{:S(2)}, u32[]{:S(2)}) collective-permute-start(bf16[1024,2048]{1,0:T(8,128)(2,1)} %product.14), channel_id=1, source_target_pairs={{0,1},{1,0},{2,3},{3,2},{4,5},{5,4},{6,7},{7,6},{8,9},{9,8},{10,11... | collective-permute-start | bytes 12582920 | tf_op jit(solution)/shard_map/ppermute | solution.py:37
  581.0 88.5 %reduce-scatter.14.cloned.1.call-start = ((), (), s32[]{:S(2)}) async-start(), calls=%async_computation.12 | async-start | bytes 1966080 | tf_op jit(solution)/shard_map/reduce_scatter | solution.py:738
  583.3 14.5 %collective-permute-start.52 = (bf16[256,1024]{1,0:T(8,128)(2,1)}, bf16[256,1024]{1,0:T(8,128)(2,1)S(1)}, u32[]{:S(2)}, u32[]{:S(2)}) collective-permute-start(bf16[256,1024]{1,0:T(8,128)(2,1)} %get-tuple-element.321), channel_id=1, source_target_pairs={{0,4},{4,0},{1,5},{5,1},{2,6},{6,2},{3,7},{7,3},{8,12},{12,8},{9,1... | collective-permute-start | bytes 1572872 | tf_op jit(solution)/shard_map/ppermute | solution.py:37
  584.0 14.0 %collective-permute-start.53 = (bf16[256,1024]{1,0:T(8,128)(2,1)S(1)}, bf16[256,1024]{1,0:T(8,128)(2,1)S(1)}, u32[]{:S(2)}, u32[]{:S(2)}) collective-permute-start(bf16[256,1024]{1,0:T(8,128)(2,1)S(1)} %copy-done.56), channel_id=1, source_target_pairs={{0,2},{2,0},{1,3},{3,1},{4,6},{6,4},{5,7},{7,5},{8,10},{10,8},{9,1... | collective-permute-start | bytes 1572872 | tf_op jit(solution)/shard_map/ppermute | solution.py:37
  599.7 13.2 %collective-permute-start.56 = (f32[2,2048]{1,0:T(2,128)S(1)}, f32[2,2048]{1,0:T(2,128)S(1)}, u32[]{:S(2)}, u32[]{:S(2)}) collective-permute-start(f32[2,2048]{1,0:T(2,128)S(1)} %pad_maximum_fusion.20), channel_id=1, source_target_pairs={{0,8},{8,16},{16,24},{24,0},{1,9},{9,17},{17,25},{25,1},{2,10},{10... | collective-permute-start | bytes 49160 | tf_op jit(solution)/shard_map/ppermute | solution.py:42
  611.0 25.1 %collective-permute-start.54 = (bf16[2,256,1024]{2,1,0:T(8,128)(2,1)}, bf16[2,256,1024]{2,1,0:T(8,128)(2,1)}, u32[]{:S(2)}, u32[]{:S(2)}) collective-permute-start(bf16[2,256,1024]{2,1,0:T(8,128)(2,1)} %get-tuple-element.329), channel_id=1, source_target_pairs={{0,2},{2,0},{1,3},{3,1},{4,6},{6,4},{5,7},{7,5},{8,10},{10,8},{9,1... | collective-permute-start | bytes 3145736 | tf_op jit(solution)/shard_map/ppermute | solution.py:37
  612.2 24.3 %collective-permute-start.55 = (bf16[2,256,1024]{2,1,0:T(8,128)(2,1)}, bf16[2,256,1024]{2,1,0:T(8,128)(2,1)}, u32[]{:S(2)}, u32[]{:S(2)}) collective-permute-start(bf16[2,256,1024]{2,1,0:T(8,128)(2,1)} %get-tuple-element.330), channel_id=1, source_target_pairs={{0,4},{4,0},{1,5},{5,1},{2,6},{6,2},{3,7},{7,3},{8,12},{12,8},{9,1... | collective-permute-start | bytes 3145736 | tf_op jit(solution)/shard_map/ppermute | solution.py:37
  643.1 19.2 %collective-permute-start.65 = (bf16[256,1024]{1,0:T(8,128)(2,1)}, bf16[256,1024]{1,0:T(8,128)(2,1)S(1)}, u32[]{:S(2)}, u32[]{:S(2)}) collective-permute-start(bf16[256,1024]{1,0:T(8,128)(2,1)} %get-tuple-element.354), channel_id=1, source_target_pairs={{0,4},{4,0},{1,5},{5,1},{2,6},{6,2},{3,7},{7,3},{8,12},{12,8},{9,1... | collective-permute-start | bytes 1572872 | tf_op jit(solution)/shard_map/ppermute | solution.py:37
  645.3 13.0 %collective-permute-start.62 = (f32[2,4,64]{2,1,0:T(4,128)S(1)}, f32[2,4,64]{2,1,0:T(4,128)S(1)}, u32[]{:S(2)}, u32[]{:S(2)}) collective-permute-start(f32[2,4,64]{2,1,0:T(4,128)S(1)} %bitcast.44), channel_id=1, source_target_pairs={{0,4},{4,0},{1,5},{5,1},{2,6},{6,2},{3,7},{7,3},{8,12},{12,8},{9,1... | collective-permute-start | bytes 6152 | tf_op jit(solution)/shard_map/ppermute | solution.py:37
  647.6 13.5 %collective-permute-start.64 = (bf16[256,256]{1,0:T(8,128)(2,1)S(1)}, bf16[256,256]{1,0:T(8,128)(2,1)S(1)}, u32[]{:S(2)}, u32[]{:S(2)}) collective-permute-start(bf16[256,256]{1,0:T(8,128)(2,1)S(1)} %get-tuple-element.352), channel_id=1, source_target_pairs={{0,4},{4,0},{1,5},{5,1},{2,6},{6,2},{3,7},{7,3},{8,12},{12,8},{9,1... | collective-permute-start | bytes 393224 | tf_op jit(solution)/shard_map/ppermute | solution.py:37
  648.7 20.9 %collective-permute-start.59 = (bf16[256,1024]{1,0:T(8,128)(2,1)}, bf16[256,1024]{1,0:T(8,128)(2,1)S(1)}, u32[]{:S(2)}, u32[]{:S(2)}) collective-permute-start(bf16[256,1024]{1,0:T(8,128)(2,1)} %get-tuple-element.342), channel_id=1, source_target_pairs={{0,4},{4,0},{1,5},{5,1},{2,6},{6,2},{3,7},{7,3},{8,12},{12,8},{9,1... | collective-permute-start | bytes 1572872 | tf_op jit(solution)/shard_map/ppermute | solution.py:37
  649.6 19.9 %collective-permute-start.60 = (bf16[256,1024]{1,0:T(8,128)(2,1)S(1)}, bf16[256,1024]{1,0:T(8,128)(2,1)S(1)}, u32[]{:S(2)}, u32[]{:S(2)}) collective-permute-start(bf16[256,1024]{1,0:T(8,128)(2,1)S(1)} %copy-done.57), channel_id=1, source_target_pairs={{0,2},{2,0},{1,3},{3,1},{4,6},{6,4},{5,7},{7,5},{8,10},{10,8},{9,1... | collective-permute-start | bytes 1572872 | tf_op jit(solution)/shard_map/ppermute | solution.py:37
  (68 other events, 351.4 us)
Sparse Core Ops, SparseCore 0:
  21.9 56.2 all-gather.3
  83.3 152.9 all-gather.5
  237.9 78.8 all-gather.7
  329.0 79.3 reduce-scatter.5
  416.9 80.4 reduce-scatter.7
  499.5 80.0 reduce-scatter.9
  582.0 27.9 reduce-scatter.11
  613.0 34.8 reduce-scatter.13

commit v5 on v4

--- a/solution.py
+++ b/solution.py
@@ -99,31 +99,41 @@
     return place((*state, third), spots, 8 * size)
 
 
-def place_kernel(spots, *refs):
-    pieces, (out, sems) = refs[:-2], refs[-2:]
+def place_kernel(spots, count, *refs):
+    pieces, out, held = refs[:count], refs[count], refs[count + 1 : 2 * count + 1]
+    load_sems, sems = refs[-2:]
+    loads = [
+        pltpu.make_async_copy(piece, here, load_sems.at[i])
+        for i, (piece, here) in enumerate(zip(pieces, held, strict=True))
+    ]
+    for load in loads:
+        load.start()
     copies = []
-    for at, (piece, start, size, row, col) in enumerate(spots):
-        source = pieces[piece]
-        copies.append(
-            pltpu.make_async_copy(
-                source.at[pl.ds(start, size), :],
-                out.at[pl.ds(row, size), pl.ds(col, source.shape[1])],
-                sems.at[at],
-            )
-        )
-    for copy in copies:
-        copy.start()
+    for i, load in enumerate(loads):
+        load.wait()
+        for at, (piece, start, size, row, col) in enumerate(spots):
+            if piece == i:
+                source = held[piece]
+                copy = pltpu.make_async_copy(
+                    source.at[pl.ds(start, size), :],
+                    out.at[pl.ds(row, size), pl.ds(col, source.shape[1])],
+                    sems.at[at],
+                )
+                copy.start()
+                copies.append(copy)
     for copy in copies:
         copy.wait()
 
 
 def place(pieces, spots, count):
+    number = len(pieces)
     return pl.pallas_call(
-        functools.partial(place_kernel, spots),
+        functools.partial(place_kernel, spots, number),
         out_shape=jax.ShapeDtypeStruct((count, pieces[0].shape[1]), BF16),
-        in_specs=[pl.BlockSpec(memory_space=pltpu.VMEM)] * len(pieces),
+        in_specs=[pl.BlockSpec(memory_space=pl.ANY)] * number,
         out_specs=pl.BlockSpec(memory_space=pltpu.HBM),
-        scratch_shapes=[pltpu.SemaphoreType.DMA((len(spots),))],
+        scratch_shapes=[pltpu.VMEM(piece.shape, BF16) for piece in pieces]
+        + [pltpu.SemaphoreType.DMA((number,)), pltpu.SemaphoreType.DMA((len(spots),))],
         compiler_params=pltpu.CompilerParams(vmem_limit_bytes=60 * 2**20),
         cost_estimate=FREE,
         name="place",
@@ -233,11 +243,11 @@
 
 def fold(*parts):
     rows, cols = parts[0].shape[1:]
-    size = rows // 4
+    size = rows // 2
     return pl.pallas_call(
         fold_kernel,
         out_shape=[jax.ShapeDtypeStruct((rows, cols), d) for d in (F32, F32, BF16, BF16)],
-        grid=(4,),
+        grid=(2,),
         in_specs=[pl.BlockSpec((2, size, cols), lambda i: (0, i, 0))] * 4,
         out_specs=[pl.BlockSpec((size, cols), lambda i: (i, 0))] * 4,
         cost_estimate=FREE,
@@ -357,6 +367,7 @@
         out[pl.ds(rest, HD), target] = qkv[pl.ds(rest, HD), source].astype(BF16)
 
 
+TOGETHER = 4
 KEYS = SLOT_LEN + LEAD
 K_AT = HEADS * HD
 V_AT = K_AT + HD
@@ -402,52 +413,69 @@
     peak_out[...] = jnp.full(peak_out.shape, NEGATIVE, F32)
     lse_out[...] = jnp.zeros(lse_out.shape, F32)
 
-    @pl.loop(0, HEADS)
-    def _(h):
+    @pl.loop(0, HEADS // TOGETHER)
+    def _(group):
         @pl.loop(0, SLOT_LEN // CHUNK)
         def _(step):
             low, high = key_range(step)
-            query = qkv[head_rows(h), chunk_of(step)]
-
-            def raw(kc):
-                return jnp.dot(k_up[chunk_of(kc), :], query, preferred_element_type=F32)
-
-            def first(kc, top):
-                s = raw(kc)
-                scores[chunk_of(kc - low), :] = s
-                return jnp.maximum(top, jnp.max(s, axis=0, keepdims=True))
-
-            s = jnp.where(causal(), raw(high - 1), NEGATIVE)
-            scores[chunk_of(high - 1 - low), :] = s
-            top = lax.fori_loop(low, high - 1, first, jnp.max(s, axis=0, keepdims=True))
-
-            def second(kc, total):
-                e = jnp.exp(scores[chunk_of(kc), :] - top)
-                scores[chunk_of(kc), :] = e
-                return total + jnp.sum(e, axis=0, keepdims=True)
-
-            total = lax.fori_loop(0, high - low, second, jnp.zeros((1, CHUNK), F32))
-            inverse = 1.0 / total
+            heads = [group * TOGETHER + i for i in range(TOGETHER)]
+            query = [qkv[head_rows(h), chunk_of(step)] for h in heads]
+
+            def raw(kc, i):
+                return jnp.dot(k_up[chunk_of(kc), :], query[i], preferred_element_type=F32)
+
+            def first(kc, tops):
+                outs = []
+                for i in range(TOGETHER):
+                    s = raw(kc, i)
+                    scores[i, chunk_of(kc - low)] = s
+                    outs.append(jnp.maximum(tops[i], jnp.max(s, axis=0, keepdims=True)))
+                return tuple(outs)
+
+            tops = []
+            for i in range(TOGETHER):
+                s = jnp.where(causal(), raw(high - 1, i), NEGATIVE)
+                scores[i, chunk_of(high - 1 - low)] = s
+                tops.append(jnp.max(s, axis=0, keepdims=True))
+            tops = lax.fori_loop(low, high - 1, first, tuple(tops))
+
+            def second(kc, totals):
+                outs = []
+                for i in range(TOGETHER):
+                    e = jnp.exp(scores[i, chunk_of(kc)] - tops[i])
+                    scores[i, chunk_of(kc)] = e
+                    outs.append(totals[i] + jnp.sum(e, axis=0, keepdims=True))
+                return tuple(outs)
+
+            totals = lax.fori_loop(0, high - low, second, (jnp.zeros((1, CHUNK), F32),) * TOGETHER)
+            inverses = [1.0 / total for total in totals]
 
             def third(kc, mixed):
-                probs = (scores[chunk_of(kc), :] * inverse).astype(BF16)
-                return mixed + jnp.dot(
-                    v_flat[:, chunk_of(kc + low)], probs, preferred_element_type=F32
-                )
-
-            mixed = lax.fori_loop(0, high - low, third, jnp.zeros((HD, CHUNK), F32))
-            mixed = mixed.astype(BF16)
-            for part in range(CHUNK // BLOCK):
-                heads_out[head_rows(h), lanes_of(step * (CHUNK // BLOCK) + part, rank)] = mixed[
-                    :, part * BLOCK : (part + 1) * BLOCK
-                ]
-            lse_out[pl.ds(h, 1), chunk_of(step)] = top + jnp.log(total)
+                outs = []
+                for i in range(TOGETHER):
+                    probs = (scores[i, chunk_of(kc)] * inverses[i]).astype(BF16)
+                    more = jnp.dot(
+                        v_flat[:, chunk_of(kc + low)], probs, preferred_element_type=F32
+                    )
+                    outs.append(mixed[i] + more)
+                return tuple(outs)
+
+            mixed_all = lax.fori_loop(
+                0, high - low, third, (jnp.zeros((HD, CHUNK), F32),) * TOGETHER
+            )
             last = step == SLOT_LEN // CHUNK - 1
             start = jnp.where(last, 0, LEAD + step * CHUNK)
             alive = jnp.where(last, info[2], info[1])
             spots = lax.broadcasted_iota(jnp.int32, (1, CHUNK), 1) + start
-            best = jnp.max(jnp.where(spots < alive, top, NEGATIVE), axis=1, keepdims=True)
-            peak_out[pl.ds(h, 1), :] = jnp.maximum(peak_out[pl.ds(h, 1), :], best)
+            for i, h in enumerate(heads):
+                mixed = mixed_all[i].astype(BF16)
+                for part in range(CHUNK // BLOCK):
+                    there = lanes_of(step * (CHUNK // BLOCK) + part, rank)
+                    heads_out[head_rows(h), there] = mixed[:, part * BLOCK : (part + 1) * BLOCK]
+                lse_out[pl.ds(h, 1), chunk_of(step)] = tops[i] + jnp.log(totals[i])
+                best = jnp.where(spots < alive, tops[i], NEGATIVE)
+                best = jnp.max(best, axis=1, keepdims=True)
+                peak_out[pl.ds(h, 1), :] = jnp.maximum(peak_out[pl.ds(h, 1), :], best)
 
 
 def attend_back_kernel(
@@ -474,48 +502,68 @@
     dk_s[...] = jnp.zeros(dk_s.shape, F32)
     dv_s[...] = jnp.zeros(dv_s.shape, F32)
 
-    @pl.loop(0, HEADS)
-    def _(h):
+    @pl.loop(0, HEADS // TOGETHER)
+    def _(group):
         @pl.loop(0, SLOT_LEN // CHUNK)
         def _(step):
             low, high = key_range(step)
             here = chunk_of(step)
-            query = qkv[head_rows(h), here]
-            grad = up_abs[head_rows(h), here]
-            query_up, grad_up = upright(query), upright(grad)
-            logs = lse[pl.ds(h, 1), here]
+            heads = [group * TOGETHER + i for i in range(TOGETHER)]
+            query = [qkv[head_rows(h), here] for h in heads]
+            grad = [up_abs[head_rows(h), here] for h in heads]
+            query_up, grad_up = [upright(x) for x in query], [upright(x) for x in grad]
+            logs = [lse[pl.ds(h, 1), here] for h in heads]
+
+            def spot(i, kc):
+                return i, chunk_of(kc - low)
 
             def one(kc, masked):
-                s = jnp.dot(k_up[chunk_of(kc), :], query, preferred_element_type=F32)
-                p = jnp.exp(s - logs)
-                if masked:
-                    p = jnp.where(causal(), p, 0.0)
-                g = jnp.dot(v_up[chunk_of(kc), :], grad, preferred_element_type=F32)
-                probs_s[chunk_of(kc - low), :] = p
-                grads_s[chunk_of(kc - low), :] = g
-                dv_s[chunk_of(kc), :] += jnp.dot(
-                    p.astype(BF16), grad_up, preferred_element_type=F32
-                )
-                return jnp.sum(p * g, axis=0, keepdims=True)
-
-            delta = one(high - 1, True)
-            delta = lax.fori_loop(low, high - 1, lambda kc, d: d + one(kc, False), delta)
-
-            def two(kc, dq):
-                p, g = probs_s[chunk_of(kc - low), :], grads_s[chunk_of(kc - low), :]
-                ds = (p * (g - delta)).astype(BF16)
-                dk_s[chunk_of(kc), :] += jnp.dot(ds, query_up, preferred_element_type=F32)
-                return dq + jnp.dot(k_flat[:, chunk_of(kc)], ds, preferred_element_type=F32)
-
-            dq = lax.fori_loop(low, high, two, jnp.zeros((HD, CHUNK), F32)) * MULTIPLIER
+                deltas, added = [], None
+                for i in range(TOGETHER):
+                    s = jnp.dot(k_up[chunk_of(kc), :], query[i], preferred_element_type=F32)
+                    p = jnp.exp(s - logs[i])
+                    if masked:
+                        p = jnp.where(causal(), p, 0.0)
+                    g = jnp.dot(v_up[chunk_of(kc), :], grad[i], preferred_element_type=F32)
+                    probs_s[spot(i, kc)] = p
+                    grads_s[spot(i, kc)] = g
+                    more = jnp.dot(p.astype(BF16), grad_up[i], preferred_element_type=F32)
+                    added = more if added is None else added + more
+                    deltas.append(jnp.sum(p * g, axis=0, keepdims=True))
+                dv_s[chunk_of(kc), :] += added
+                return tuple(deltas)
+
+            def both(kc, deltas):
+                return tuple(d + e for d, e in zip(deltas, one(kc, False), strict=True))
+
+            deltas = lax.fori_loop(low, high - 1, both, one(high - 1, True))
+
+            def two(kc, dqs):
+                outs, added = [], None
+                for i in range(TOGETHER):
+                    p, g = probs_s[spot(i, kc)], grads_s[spot(i, kc)]
+                    ds = (p * (g - deltas[i])).astype(BF16)
+                    more = jnp.dot(ds, query_up[i], preferred_element_type=F32)
+                    added = more if added is None else added + more
+                    outs.append(
+                        dqs[i] + jnp.dot(k_flat[:, chunk_of(kc)], ds, preferred_element_type=F32)
+                    )
+                dk_s[chunk_of(kc), :] += added
+                return tuple(outs)
+
+            zero = jnp.zeros((HD, CHUNK), F32)
+            dqs = lax.fori_loop(low, high, two, (zero,) * TOGETHER)
             c, s = cos[:, here], sin[:, here]
-            u1, u2 = dq[:HALF], dq[HALF:]
-            t1, t2 = (u1 * c + u2 * s).astype(BF16), (u2 * c - u1 * s).astype(BF16)
-            for part in range(CHUNK // BLOCK):
-                there = lanes_of(step * (CHUNK // BLOCK) + part, rank)
-                cut = slice(part * BLOCK, (part + 1) * BLOCK)
-                dq_out[pl.ds(pl.multiple_of(h * HD, HD), HALF), there] = t1[:, cut]
-                dq_out[pl.ds(pl.multiple_of(h * HD + HALF, HALF), HALF), there] = t2[:, cut]
+            for i in range(TOGETHER):
+                dq = dqs[i] * MULTIPLIER
+                u1, u2 = dq[:HALF], dq[HALF:]
+                t1, t2 = (u1 * c + u2 * s).astype(BF16), (u2 * c - u1 * s).astype(BF16)
+                at = heads[i] * HD
+                for part in range(CHUNK // BLOCK):
+                    there = lanes_of(step * (CHUNK // BLOCK) + part, rank)
+                    cut = slice(part * BLOCK, (part + 1) * BLOCK)
+                    dq_out[pl.ds(pl.multiple_of(at, HD), HALF), there] = t1[:, cut]
+                    dq_out[pl.ds(pl.multiple_of(at + HALF, HALF), HALF), there] = t2[:, cut]
 
     halo_out[pl.ds(0, HD), :] = dk_s[pl.ds(0, LEAD), :].T.astype(BF16)
     halo_out[pl.ds(HD, HD), :] = dv_s[pl.ds(0, LEAD), :].T.astype(BF16)
@@ -546,7 +594,7 @@
         out[pl.ds(HD, HD), target] = rest.astype(BF16)
 
 
-def call(kernel, info, args, outs, scratch, name):
+def call(kernel, info, args, outs, scratch, name, limit=40):
     spec = pl.BlockSpec(memory_space=pltpu.VMEM)
     return pl.pallas_call(
         kernel,
@@ -554,7 +602,7 @@
         in_specs=[pl.BlockSpec(memory_space=pltpu.SMEM)] + [spec] * len(args),
         out_specs=[spec] * len(outs),
         scratch_shapes=[pltpu.VMEM(s, d) for s, d in scratch],
-        compiler_params=pltpu.CompilerParams(vmem_limit_bytes=40 * 2**20),
+        compiler_params=pltpu.CompilerParams(vmem_limit_bytes=limit * 2**20),
         cost_estimate=FREE,
         name=name,
     )(info, *args)
@@ -575,7 +623,7 @@
 
 
 def ffn_call(kernel, rows, weights, width, kinds, held, name):
-    high, wide = min(512, rows.shape[0]), min(512, width)
+    high, wide = min(256 if held else 512, rows.shape[0]), min(1024, width)
     depth, steps = rows.shape[1], width // wide
     tile = pl.BlockSpec((high, wide), lambda n, m: (m, n))
     if held:
@@ -701,15 +749,15 @@
     heads, lse, peak = call(
         attend_kernel, info, (qkv, halo),
         [((HEADS * HD, rows), BF16), ((8, rows), F32), ((8, 128), F32)],
-        [((KEYS, HD), BF16), ((HD, KEYS), BF16), ((SLOT_LEN, CHUNK), F32)],
+        [((KEYS, HD), BF16), ((HD, KEYS), BF16), ((TOGETHER, SLOT_LEN, CHUNK), F32)],
         "attend",
     )
-    heads, down_other, *back_rows = tie(heads, down_other, *back_rows)
+    heads, *back_rows = tie(heads, *back_rows)
+
+    terms = [(heads, full_heads, 0, 1, (0, out_cols))]
+    high_part, own_peak, down_other = tie(product(terms, 1), peak[:HEADS], down_other)
+    came, other_peak = tie(swap(high_part, "c"), swap(own_peak, "y"))
     down_w = ordered(half_of(w_down, y_rank, 0), down_other, y_rank, 1)
-
-    terms = [(heads, full_heads, 0, 1, (0, out_cols))]
-    own_peak = peak[:HEADS]
-    came, other_peak = tie(swap(product(terms, 1), "c"), swap(own_peak, "y"))
     branch = spread_one(terms, came)
     head_peak = over_z(ordered(own_peak, other_peak, y_rank, 0), jnp.maximum)
     down_rows = gather_three(back_rows)
@@ -779,9 +827,9 @@
         attend_back_kernel, info, (qkv, halo, heads_grad, lse, cos, sin),
         [((HEADS * HD, rows), BF16), ((2 * HD, rows), F32), ((2 * HD, LEAD), BF16)],
         [((KEYS, HD), BF16), ((KEYS, HD), BF16), ((HD, KEYS), BF16),
-         ((SLOT_LEN, CHUNK), F32), ((SLOT_LEN, CHUNK), F32),
+         ((TOGETHER, SLOT_LEN, CHUNK), F32), ((TOGETHER, SLOT_LEN, CHUNK), F32),
          ((KEYS, HD), F32), ((KEYS, HD), F32), ((HEADS * HD, SLOT_LEN), BF16)],
-        "attend_back",
+        "attend_back", 60,
     )
     back, down_other, one_other, *got = tie(back, down_other, one_other, *second[2:4])
     back_sent = along(back, -1)
@@ -795,38 +843,41 @@
     )
     dqkv = jnp.concatenate((dq, dkv_done))
     terms = [(dqkv, full_heads, 0, 1, heads_cut)]
-    high_part, acts_one, two_sum = tie(product(terms, 1), acts_one, two_sum)
-    two_own, two_sent = half_of(two_sum, y_rank, 0), half_of(two_sum, other_y, 0)
+    high_part, acts_one = tie(product(terms, 1), acts_one)
     qkv_part, sums = outer(acts_one, dqkv, 1, full_heads, heads_cut)
-    came, qkv_part, sums, *got = tie(swap(high_part, "c"), qkv_part, sums, *second[2:4])
+    came, qkv_part, sums, two_sum, *got = tie(
+        swap(high_part, "c"), qkv_part, sums, two_sum, *second[2:4]
+    )
+    two_own = half_of(two_sum, y_rank, 0)
+    came, two_sent = tie(came, half_of(two_sum, other_y, 0))
+    qkv_sum = reduced(qkv_part, 0)
     branch_two = spread_three((*second[:2], *got))
     result = resid + RESIDUAL * own_mask * branch_two
-    norm_one = spread_one(terms, came)
-    qkv_sum = reduced(qkv_part, 0)
+    *norm_one, sums, two_other = spread_one(terms, came, sums, swap(two_sent, "y"))
     gains = jnp.stack((sums[:, 0] / gain_one, jnp.sum(gain_two_part, axis=0)))
-    gains = over_z(gains, jnp.add).reshape(2, lax.axis_size("z"), 2, 2, 2, -1)
+    gains = over_z(gains, jnp.add)
+    *got, gains, out_sum = tie(*norm_one[2:4], gains, out_sum)
+    gains = gains.reshape(2, lax.axis_size("z"), 2, 2, 2, -1)
 
     def halved(gains, dim, axis):
         at = lax.axis_index(axis)
         return (lax.dynamic_index_in_dim(gains, at, dim, keepdims=False),
                 lax.dynamic_index_in_dim(gains, 1 - at, dim, keepdims=False))
 
+    norm_one = spread_two((*norm_one[:2], *got), gains)
+    gains = norm_one[4]
+    out_own, out_sent = half_of(out_sum, y_rank, 0), half_of(out_sum, other_y, 0)
+    own, qkv_sent = half_of(qkv_sum, y_rank, 0), half_of(qkv_sum, other_y, 0)
     kept, sent = halved(gains, 4, "c")
     kept, sent = halved(kept + swap(sent, "c"), 3, "x")
-    *got, out_sum = tie(*norm_one[2:4], out_sum)
-    out_own, out_sent = half_of(out_sum, y_rank, 0), half_of(out_sum, other_y, 0)
-    norm_one = spread_two((*norm_one[:2], *got), sent, out_sent, two_sent)
-    sent, out_sent, two_sent = norm_one[4:]
-    kept, sent = halved(kept + swap(sent, "x"), 2, "y")
-    gains = kept + swap(sent, "y")
-    two_other, out_other = swap(two_sent, "y"), swap(out_sent, "y")
-    *norm_one, qkv_sum = tie(*norm_one[:4], qkv_sum)
-    own, other = traded(qkv_sum, 0)
+    *norm_one, qkv_sent, kept, sent, out_sent = tie(*norm_one[:4], qkv_sent, kept, sent, out_sent)
+    other, out_other = swap(qkv_sent, "y"), swap(out_sent, "y")
     (grad_input,) = row_call(
         input_back_kernel, (*norm_one, grad_resid, layer_in, scale_one, gain_one[None, :]),
         [((tok_rows, width), BF16)], "input_back",
     )
-    gains = lax.dynamic_index_in_dim(gains, z_rank, 1, keepdims=False)
+    kept, sent = halved(kept + swap(sent, "x"), 2, "y")
+    gains = lax.dynamic_index_in_dim(kept + swap(sent, "y"), z_rank, 1, keepdims=False)
 
     down_grad = ordered(down_own, down_other, y_rank, 0).astype(F32)
     gate_w_grad = ordered(one_own, one_other, y_rank, 1).astype(F32)

time: 696 us -> 676 us (0.971)
  Pallas kernels: 314 us -> 296 us
  local copies, waits for them, and re-layouts: 30.3 us -> 37.9 us
    pallas_call x4, Pallas kernels: 70.8 us -> 57.4 us  [call(): pl.pallas_call(kernel, out_shape=[jax.ShapeDtypeStruct(s, d) for s, d in...]
    ppermute x60, waiting for transfers between devices: 192 us -> 184 us  [swap(): return lax.ppermute(x, axis, [(0, 1), (1, 0)])]
    unnamed x119 -> x147, local copies, waits for them, and re-layouts: 13.1 us -> 19.9 us
  transfers between devices with their start and end apart: 74 -> 74, of which waited for: 38 -> 41; matrix products, arithmetic and copies ran while one was open for 9% -> 10% of each run, Pallas kernels for 46% -> 44%
where the time goes in v5:
time: 676 us; the launch traced here: 669 us
  Pallas kernels  296 us (44%)
  waiting for transfers between devices  209 us (31%)
  starting transfers between devices  59.4 us (9%)
  local copies, waits for them, and re-layouts  37.9 us (6%)
  other arithmetic  37.6 us (6%)
  between operations  16.3 us (2%)
  matrix products  13.8 us (2%)
    ppermute x60, waiting for transfers between devices, swap(): return lax.ppermute(x, axis, [(0, 1), (1, 0)])  184 us
    pallas_call x8, Pallas kernels, product(): pl.pallas_call(functools.partial(product_kernel, kinds, came is not None)...  76.3 us
    pallas_call x4, Pallas kernels, call(): pl.pallas_call(kernel, out_shape=[jax.ShapeDtypeStruct(s, d) for s, d in...  57.4 us
    pallas_call x5, Pallas kernels, outer(): pl.pallas_call(kernel, out_shape=outs, grid=(wide // cols, high // rows),...  56.9 us
    ppermute x60, starting transfers between devices, swap(): return lax.ppermute(x, axis, [(0, 1), (1, 0)])  49.2 us
    pallas_call x2, Pallas kernels, ffn_call(): pl.pallas_call(kernel, out_shape=[jax.ShapeDtypeStruct((rows.shape[0], wi...  43.9 us
    pallas_call x4, Pallas kernels, place(): pl.pallas_call(functools.partial(place_kernel, spots, number), out_shape=...  28.5 us
    ppermute x6, waiting for transfers between devices, along(): return lax.ppermute(x, 'z', [(i, (i + by) % peers) for i in range(peers)])  24.2 us
  transfers between devices with their start and end apart: 74, of which 41 were waited for; matrix products, arithmetic and copies ran while one was open for 10% of the time, Pallas kernels for 44%

profile of v5, /device:TPU:0, one launch (start us, length us, event | category | flops | bytes accessed | tf_op | source)
XLA Modules:
  0.0 669.1 jit_solution(13967085489181190049)
XLA Ops:
  9.8 3.0 collective-permute-start
  13.0 7.6 %collective-permute-done = bf16[256,640]{1,0:T(8,128)(2,1)S(1)} collective-permute-done((bf16[256,640]{1,0:T(8,128)(2,1)S(1)}, bf16[256,640]{1,0:T(8,128)(2,1)S(1)}, u32[]{:S(2)}, u32[]{:S(2)}) %collective-permute-start) | collective-permute-done | bytes 327712 | tf_op jit(solution)/shard_map/ppermute | solution.py:37
  27.9 9.1 %collective-permute-done.3.refs_2_ = bf16[256,1024]{1,0:T(8,128)(2,1)S(1)} collective-permute-done((bf16[256,1024]{1,0:T(8,128)(2,1)S(1)}, bf16[256,1024]{1,0:T(8,128)(2,1)S(1)}, u32[]{:S(2)}, u32[]{:S(2)}) %collective-permute-start.3) | collective-permute-done | bytes 524320 | tf_op jit(solution)/shard_map/ppermute | solution.py:37
  37.0 3.5 collective-permute-done.4.refs_3_
  44.5 18.5 %collective-permute-done.1 = bf16[256,2048]{1,0:T(8,128)(2,1)S(1)} collective-permute-done((bf16[256,2048]{1,0:T(8,128)(2,1)S(1)}, bf16[256,2048]{1,0:T(8,128)(2,1)S(1)}, u32[]{:S(2)}, u32[]{:S(2)}) %collective-permute-start.1) | collective-permute-done | bytes 1048608 | tf_op jit(solution)/shard_map/ppermute | solution.py:37
  63.0 2.4 maximum_select_fusion
  65.4 17.7 %collective-permute-done.6.refs_5_ = bf16[512,1024]{1,0:T(8,128)(2,1)S(1)} collective-permute-done((bf16[512,1024]{1,0:T(8,128)(2,1)}, bf16[512,1024]{1,0:T(8,128)(2,1)S(1)}, u32[]{:S(2)}, u32[]{:S(2)}) %collective-permute-start.6) | collective-permute-done | bytes 1048608 | tf_op jit(solution)/shard_map/ppermute | solution.py:37
  88.7 2.3 fusion.32
  95.5 7.4 %place.4.left = bf16[2048,2048]{1,0:T(8,128)(2,1)} custom-call(bf16[256,2048]{1,0:T(8,128)(2,1)} %copy-done.13, bf16[256,2048]{1,0:T(8,128)(2,1)} %collective-permute-done.2.refs_1_, bf16[256,1024]{1,0:T(8,128)(2,1)} %copy-done.27, bf16[256,1024]{1,0:T(8,128)(2,1)} %copy-done.28, bf16[512,1024]{1,0:T(8,128)(2,1)} %collective-permute-done.5.refs_4_, ...), custom_call_target="tpu_custom_call" | custom-call | tf_op jit(solution)/shard_map/place/pallas_call | solution.py:130
  102.9 6.1 fusion.6.qkv
  112.0 8.9 %collective-permute-done.9.halo = bf16[128,512]{1,0:T(8,128)(2,1)S(1)} collective-permute-done((bf16[128,512]{1,0:T(8,128)(2,1)S(1)}, bf16[128,512]{1,0:T(8,128)(2,1)S(1)}, u32[]{:S(2)}, u32[]{:S(2)}) %collective-permute-start.9) | collective-permute-done | bytes 131104 | tf_op jit(solution)/shard_map/ppermute | solution.py:42
  127.6 20.0 %attend.1 = (bf16[256,2048]{1,0:T(8,128)(2,1)S(1)}, f32[8,2048]{1,0:T(8,128)S(1)}, f32[8,128]{1,0:T(8,128)S(1)}) custom-call(s32[3]{0:T(128)S(1)} %pad_add_fusion.info, bf16[384,2048]{1,0:T(8,128)(2,1)S(1)} %rope.1.qkv, bf16[128,512]{1,0:T(8,128)(2,1)S(1)} %collective-permute-done.9.halo), custom_call_target="tpu_custom_call" | custom-call | tf_op jit(solution)/shard_map/attend/pallas_call | solution.py:599
  149.9 6.3 product.8
  156.2 4.5 collective-permute-done.16
  163.6 2.9 collective-permute-done.18
  168.2 2.0 copy-done.26
  170.2 7.4 %product.9 = (f32[2,256,1024]{2,1,0:T(8,128)}, f32[2,256,1024]{2,1,0:T(8,128)}, bf16[2,256,1024]{2,1,0:T(8,128)(2,1)}, bf16[2,256,1024]{2,1,0:T(8,128)(2,1)}) custom-call(bf16[256,2048]{1,0:T(8,128)(2,1)} %copy-done.1, bf16[2048,640]{1,0:T(8,128)(2,1)} %all-gather.4.cloned.1.call-done.refs_1_.weights, bf16[1024,2048]{1,0:T(8,128)(2,1)} %copy-done.26), custom_call_target="tpu_custom_call" | custom-call | tf_op jit(solution)/shard_map/product/pallas_call | solution.py:216
  179.7 8.3 %collective-permute-done.22 = f32[8,128]{1,0:T(8,128)S(1)} collective-permute-done((f32[8,128]{1,0:T(8,128)S(1)}, f32[8,128]{1,0:T(8,128)S(1)}, u32[]{:S(2)}, u32[]{:S(2)}) %collective-permute-start.22) | collective-permute-done | bytes 4128 | tf_op jit(solution)/shard_map/ppermute | solution.py:42
  188.1 2.5 maximum_select_fusion.1
  192.0 7.1 %place.5.right.rows = bf16[2048,2048]{1,0:T(8,128)(2,1)} custom-call(bf16[256,2048]{1,0:T(8,128)(2,1)} %multiply_convert_fusion.refs_0_, bf16[256,2048]{1,0:T(8,128)(2,1)} %collective-permute-done.10.refs_1_, bf16[256,1024]{1,0:T(8,128)(2,1)} %copy-done.29, bf16[256,1024]{1,0:T(8,128)(2,1)} %collective-permute-done.12.refs_3_, bf16[512,1024]{1,0:T(8,128)(2,1)} %copy-done.37, ...), custom_call_target="tpu_custom_call" | custom-call | tf_op jit(solution)/shard_map/place/pallas_call | solution.py:130
  199.1 3.8 collective-permute-done.19.left_x
  204.9 4.1 fold.4
  210.8 2.0 fusion.18.refs_5_.refs_8_
  212.8 9.2 %collective-permute-done.24.refs_2_ = bf16[256,1024]{1,0:T(8,128)(2,1)S(1)} collective-permute-done((bf16[256,1024]{1,0:T(8,128)(2,1)}, bf16[256,1024]{1,0:T(8,128)(2,1)S(1)}, u32[]{:S(2)}, u32[]{:S(2)}) %collective-permute-start.24) | collective-permute-done | bytes 524320 | tf_op jit(solution)/shard_map/ppermute | solution.py:37
  223.2 4.9 residual.1
  230.5 12.2 %collective-permute-done.27.refs_2_ = bf16[256,1024]{1,0:T(8,128)(2,1)S(1)} collective-permute-done((bf16[256,1024]{1,0:T(8,128)(2,1)}, bf16[256,1024]{1,0:T(8,128)(2,1)S(1)}, u32[]{:S(2)}, u32[]{:S(2)}) %collective-permute-start.27) | collective-permute-done | bytes 524320 | tf_op jit(solution)/shard_map/ppermute | solution.py:37
  248.1 22.9 %collective-permute-done.30.refs_5_ = bf16[512,1024]{1,0:T(8,128)(2,1)S(1)} collective-permute-done((bf16[512,1024]{1,0:T(8,128)(2,1)S(1)}, bf16[512,1024]{1,0:T(8,128)(2,1)S(1)}, u32[]{:S(2)}, u32[]{:S(2)}) %collective-permute-start.30) | collective-permute-done | bytes 1048608 | tf_op jit(solution)/shard_map/ppermute | solution.py:37
  273.2 4.3 collective-permute-done.32.refs_7_
  277.5 7.1 %place.6.rows.left = bf16[2048,2048]{1,0:T(8,128)(2,1)} custom-call(bf16[256,2048]{1,0:T(8,128)(2,1)} %get-tuple-element.256.refs_0_, bf16[256,2048]{1,0:T(8,128)(2,1)} %collective-permute-done.26.refs_1_, bf16[256,1024]{1,0:T(8,128)(2,1)} %copy-done.32, bf16[256,1024]{1,0:T(8,128)(2,1)} %copy-done.33, bf16[512,1024]{1,0:T(8,128)(2,1)} %copy-done.41, ...), custom_call_target="tpu_custom_call" | custom-call | tf_op jit(solution)/shard_map/place/pallas_call | solution.py:130
  284.6 23.9 %hidden.1 = (f32[2048,1024]{1,0:T(8,128)}, f32[2048,1024]{1,0:T(8,128)}, bf16[2048,1024]{1,0:T(8,128)(2,1)}) custom-call(bf16[2048,2048]{1,0:T(8,128)(2,1)} %place.6.rows.left, bf16[2048,2048]{1,0:T(8,128)(2,1)} %all-gather.6.cloned.1.call-done.gate_w.up_w.refs_1_.refs_3_, bf16[2048,2048]{1,0:T(8,128)(2,1)} %all-gather.6.cloned.1.call-done.gate_w.up_w.refs_1_.refs_3_), custom_call_target="tpu_custom_call" | custom-call | tf_op jit(solution)/shard_map/hidden/pallas_call | solution.py:634
  308.4 14.2 %outer.5 = bf16[1024,2048]{1,0:T(8,128)(2,1)} custom-call(bf16[2048,1024]{1,0:T(8,128)(2,1)} %get-tuple-element.292.left.refs_0_, bf16[2048,2048]{1,0:T(8,128)(2,1)} %place.5.right.rows), custom_call_target="tpu_custom_call" | custom-call | tf_op jit(solution)/shard_map/outer/pallas_call | solution.py:672
  322.9 20.0 %hidden_back.1 = (bf16[2048,1024]{1,0:T(8,128)(2,1)}, bf16[2048,1024]{1,0:T(8,128)(2,1)}) custom-call(bf16[2048,2048]{1,0:T(8,128)(2,1)} %place.5.right.rows, bf16[1024,2048]{1,0:T(8,128)(2,1)} %all-gather.8.cloned.1.call-done.weights.refs_1_, f32[2048,1024]{1,0:T(8,128)} %get-tuple-element.270.gates, f32[2048,1024]{1,0:T(8,128)} %get-tuple-element.271.ups), custom_call_target="tpu_custom_call" | custom-call | tf_op jit(solution)/shard_map/hidden_back/pallas_call | solution.py:634
  342.9 13.5 %product.10 = bf16[1024,2048]{1,0:T(8,128)(2,1)} custom-call(bf16[2048,1024]{1,0:T(8,128)(2,1)} %get-tuple-element.272.refs_0_.right, bf16[2048,2048]{1,0:T(8,128)(2,1)} %all-gather.6.cloned.1.call-done.gate_w.up_w.refs_1_.refs_3_, bf16[2048,1024]{1,0:T(8,128)(2,1)} %get-tuple-element.273.refs_2_.right, ...), custom_call_target="tpu_custom_call" | custom-call | tf_op jit(solution)/shard_map/product/pallas_call | solution.py:216
  356.4 7.4 %collective-permute-done.33.refs_4_ = bf16[1024,2048]{1,0:T(8,128)(2,1)S(1)} collective-permute-done((bf16[1024,2048]{1,0:T(8,128)(2,1)}, bf16[1024,2048]{1,0:T(8,128)(2,1)S(1)}, u32[]{:S(2)}, u32[]{:S(2)}) %collective-permute-start.33) | collective-permute-done | bytes 4194336 | tf_op jit(solution)/shard_map/ppermute | solution.py:37
  363.8 2.0 copy-done.15
  365.8 15.6 %product.11 = (f32[2,256,1024]{2,1,0:T(8,128)}, f32[2,256,1024]{2,1,0:T(8,128)}, bf16[2,256,1024]{2,1,0:T(8,128)(2,1)}, bf16[2,256,1024]{2,1,0:T(8,128)(2,1)}) custom-call(bf16[2048,1024]{1,0:T(8,128)(2,1)} %get-tuple-element.272.refs_0_.right, bf16[2048,2048]{1,0:T(8,128)(2,1)} %all-gather.6.cloned.1.call-done.gate_w.up_w.refs_1_.refs_3_, ...), custom_call_target="tpu_custom_call" | custom-call | tf_op jit(solution)/shard_map/product/pallas_call | solution.py:216
  383.4 13.4 %outer.7 = bf16[2048,1024]{1,0:T(8,128)(2,1)} custom-call(bf16[2048,2048]{1,0:T(8,128)(2,1)} %place.6.rows.left, bf16[2048,1024]{1,0:T(8,128)(2,1)} %get-tuple-element.273.refs_2_.right), custom_call_target="tpu_custom_call" | custom-call | tf_op jit(solution)/shard_map/outer/pallas_call | solution.py:672
  396.8 13.3 %outer.6 = bf16[2048,1024]{1,0:T(8,128)(2,1)} custom-call(bf16[2048,2048]{1,0:T(8,128)(2,1)} %place.6.rows.left, bf16[2048,1024]{1,0:T(8,128)(2,1)} %get-tuple-element.272.refs_0_.right), custom_call_target="tpu_custom_call" | custom-call | tf_op jit(solution)/shard_map/outer/pallas_call | solution.py:672
  411.5 4.1 fold.5
  417.6 11.7 %collective-permute-done.36.refs_2_ = bf16[256,1024]{1,0:T(8,128)(2,1)S(1)} collective-permute-done((bf16[256,1024]{1,0:T(8,128)(2,1)}, bf16[256,1024]{1,0:T(8,128)(2,1)S(1)}, u32[]{:S(2)}, u32[]{:S(2)}) %collective-permute-start.36) | collective-permute-done | bytes 524320 | tf_op jit(solution)/shard_map/ppermute | solution.py:37
  430.5 6.1 residual_back.1
  438.4 8.5 %product.12 = bf16[1024,2048]{1,0:T(8,128)(2,1)} custom-call(bf16[2048,1024]{1,0:T(8,128)(2,1)} %get-tuple-element.292.left.refs_0_, bf16[1024,2048]{1,0:T(8,128)(2,1)} %all-gather.8.cloned.1.call-done.weights.refs_1_), custom_call_target="tpu_custom_call" | custom-call | tf_op jit(solution)/shard_map/product/pallas_call | solution.py:216
  446.9 2.4 collective-permute-done.38.refs_2_
  455.0 2.6 collective-permute-done.42.refs_2_
  457.6 10.3 %product.13 = (f32[2,256,1024]{2,1,0:T(8,128)}, f32[2,256,1024]{2,1,0:T(8,128)}, bf16[2,256,1024]{2,1,0:T(8,128)(2,1)}, bf16[2,256,1024]{2,1,0:T(8,128)(2,1)}) custom-call(bf16[2048,1024]{1,0:T(8,128)(2,1)} %get-tuple-element.292.left.refs_0_, bf16[1024,2048]{1,0:T(8,128)(2,1)} %all-gather.8.cloned.1.call-done.weights.refs_1_, ...), custom_call_target="tpu_custom_call" | custom-call | tf_op jit(solution)/shard_map/product/pallas_call | solution.py:216
  467.9 9.9 %collective-permute-done.40.refs_5_ = bf16[512,1024]{1,0:T(8,128)(2,1)S(1)} collective-permute-done((bf16[512,1024]{1,0:T(8,128)(2,1)}, bf16[512,1024]{1,0:T(8,128)(2,1)S(1)}, u32[]{:S(2)}, u32[]{:S(2)}) %collective-permute-start.40) | collective-permute-done | bytes 1048608 | tf_op jit(solution)/shard_map/ppermute | solution.py:37
  482.0 2.1 collective-permute-done.45.refs_7_
  484.1 6.9 %place.7.left = bf16[2048,2048]{1,0:T(8,128)(2,1)} custom-call(bf16[256,2048]{1,0:T(8,128)(2,1)} %get-tuple-element.289.refs_0_, bf16[256,2048]{1,0:T(8,128)(2,1)} %copy-done.38, bf16[256,1024]{1,0:T(8,128)(2,1)} %copy-done.30, bf16[256,1024]{1,0:T(8,128)(2,1)} %copy-done.31, bf16[512,1024]{1,0:T(8,128)(2,1)} %copy-done.39, bf16[512,1024]{1,0:T(8,128)(2,1)} %copy-done.22, ...), custom_call_target="tpu_custom_call" | custom-call | tf_op jit(solution)/shard_map/place/pallas_call | solution.py:130
  495.4 7.7 %convolution_convert_fusion.upstream = bf16[256,2048]{1,0:T(8,128)(2,1)} fusion(bf16[2048,2048]{1,0:T(8,128)(2,1)} %place.7.left, bf16[2048,640]{1,0:T(8,128)(2,1)} %all-gather.4.cloned.1.call-done.refs_1_.weights), kind=kOutput, calls=%fused_computation.2 | convolution fusion | flops 2148007936 | bytes 10485760 | tf_op jit(solution)/shard_map/dot_general | solution.py:46
  503.1 35.8 %attend_back.1 = (bf16[256,2048]{1,0:T(8,128)(2,1)}, f32[128,2048]{1,0:T(8,128)}, bf16[128,512]{1,0:T(8,128)(2,1)}) custom-call(s32[3]{0:T(128)} %copy-done.9, bf16[384,2048]{1,0:T(8,128)(2,1)} %copy-done, bf16[128,512]{1,0:T(8,128)(2,1)} %copy-done.7, bf16[256,2048]{1,0:T(8,128)(2,1)} %convolution_convert_fusion.upstream, f32[8,2048]{1,0:T(8,128)} %copy-done.8, ...), custom_call_target="tpu_custom_call" | custom-call | tf_op jit(solution)/shard_map/attend_back/pallas_call | solution.py:599
  540.7 6.8 %collective-permute-start.50 = (bf16[128,512]{1,0:T(8,128)(2,1)}, bf16[128,512]{1,0:T(8,128)(2,1)S(1)}, u32[]{:S(2)}, u32[]{:S(2)}) collective-permute-start(bf16[128,512]{1,0:T(8,128)(2,1)} %get-tuple-element.323), channel_id=1, source_target_pairs={{0,24},{8,0},{16,8},{24,16},{1,25},{9,1},{17,9},{25,17},{2,26},{10... | collective-permute-start | bytes 393224 | tf_op jit(solution)/shard_map/ppermute | solution.py:42
  547.4 6.7 %outer.8 = bf16[2048,256]{1,0:T(8,128)(2,1)} custom-call(bf16[2048,2048]{1,0:T(8,128)(2,1)} %place.7.left, bf16[256,2048]{1,0:T(8,128)(2,1)} %copy-done.1), custom_call_target="tpu_custom_call" | custom-call | tf_op jit(solution)/shard_map/outer/pallas_call | solution.py:672
  554.2 4.3 fold.6
  561.0 6.4 product.14
  574.9 9.3 %outer.9 = (bf16[2048,384]{1,0:T(8,128)(2,1)}, f32[2048,128]{1,0:T(8,128)}) custom-call(bf16[2048,2048]{1,0:T(8,128)(2,1)} %place.4.left, bf16[384,2048]{1,0:T(8,128)(2,1)} %pad_maximum_fusion.4.refs_0_.right, bf16[2048,640]{1,0:T(8,128)(2,1)} %all-gather.4.cloned.1.call-done.refs_1_.weights), custom_call_target="tpu_custom_call" | custom-call | tf_op jit(solution)/shard_map/outer/pallas_call | solution.py:672
  585.0 2.1 constant_dynamic-slice_fusion.3
  589.8 8.3 %product.15 = (f32[2,256,1024]{2,1,0:T(8,128)}, f32[2,256,1024]{2,1,0:T(8,128)}, bf16[2,256,1024]{2,1,0:T(8,128)(2,1)}, bf16[2,256,1024]{2,1,0:T(8,128)(2,1)}) custom-call(bf16[384,2048]{1,0:T(8,128)(2,1)} %pad_maximum_fusion.4.refs_0_.right, bf16[2048,640]{1,0:T(8,128)(2,1)} %all-gather.4.cloned.1.call-done.refs_1_.weights, ...), custom_call_target="tpu_custom_call" | custom-call | tf_op jit(solution)/shard_map/product/pallas_call | solution.py:216
  603.7 3.5 collective-permute-done.57
  608.5 3.5 collective-permute-done.58
  612.1 14.2 %collective-permute-done.55.left_x = bf16[2,256,1024]{2,1,0:T(8,128)(2,1)S(1)} collective-permute-done((bf16[2,256,1024]{2,1,0:T(8,128)(2,1)}, bf16[2,256,1024]{2,1,0:T(8,128)(2,1)S(1)}, u32[]{:S(2)}, u32[]{:S(2)}) %collective-permute-start.55) | collective-permute-done | bytes 1048608 | tf_op jit(solution)/shard_map/ppermute | solution.py:37
  627.8 4.1 fold.7
  634.1 2.9 fusion.9
  639.3 4.8 collective-permute-done.59.refs_2_
  652.6 5.0 input_back.1
  (357 shorter events, 121.9 us)
Async XLA Ops:
  7.2 75.9 %all-gather.4.cloned.1.call-start = ((), (), s32[]{:S(2)}) async-start(), calls=%async_computation.5 | async-start | bytes 3276800 | tf_op jit(solution)/shard_map/all_gather | solution.py:720
  9.8 10.7 %collective-permute-start = (bf16[256,640]{1,0:T(8,128)(2,1)S(1)}, bf16[256,640]{1,0:T(8,128)(2,1)S(1)}, u32[]{:S(2)}, u32[]{:S(2)}) collective-permute-start(bf16[256,640]{1,0:T(8,128)(2,1)S(1)} %pad_maximum_fusion.19), channel_id=1, source_target_pairs={{0,4},{4,0},{1,5},{5,1},{2,6},{6,2},{3,7},{7,3},{8,12},{12,8},{9,1... | collective-permute-start | bytes 983048 | tf_op jit(solution)/shard_map/ppermute | solution.py:37
  21.8 221.6 %all-gather.6.cloned.1.call-start = ((), (), s32[]{:S(2)}) async-start(), calls=%async_computation.6 | async-start | bytes 10485760 | tf_op jit(solution)/shard_map/all_gather | solution.py:735
  23.9 13.2 %collective-permute-start.3 = (bf16[256,1024]{1,0:T(8,128)(2,1)S(1)}, bf16[256,1024]{1,0:T(8,128)(2,1)S(1)}, u32[]{:S(2)}, u32[]{:S(2)}) collective-permute-start(bf16[256,1024]{1,0:T(8,128)(2,1)S(1)} %get-tuple-element.448), channel_id=1, source_target_pairs={{0,2},{2,0},{1,3},{3,1},{4,6},{6,4},{5,7},{7,5},{8,10},{10,8},{9,1... | collective-permute-start | bytes 1572872 | tf_op jit(solution)/shard_map/ppermute | solution.py:37
  25.6 14.9 %collective-permute-start.4 = (bf16[256,1024]{1,0:T(8,128)(2,1)S(1)}, bf16[256,1024]{1,0:T(8,128)(2,1)S(1)}, u32[]{:S(2)}, u32[]{:S(2)}) collective-permute-start(bf16[256,1024]{1,0:T(8,128)(2,1)S(1)} %get-tuple-element.447), channel_id=1, source_target_pairs={{0,4},{4,0},{1,5},{5,1},{2,6},{6,2},{3,7},{7,3},{8,12},{12,8},{9,1... | collective-permute-start | bytes 1572872 | tf_op jit(solution)/shard_map/ppermute | solution.py:37
  27.3 35.7 %collective-permute-start.1 = (bf16[256,2048]{1,0:T(8,128)(2,1)S(1)}, bf16[256,2048]{1,0:T(8,128)(2,1)S(1)}, u32[]{:S(2)}, u32[]{:S(2)}) collective-permute-start(bf16[256,2048]{1,0:T(8,128)(2,1)S(1)} %pad_maximum_fusion.14), channel_id=1, source_target_pairs={{0,4},{4,0},{1,5},{5,1},{2,6},{6,2},{3,7},{7,3},{8,12},{12,8},{9,1... | collective-permute-start | bytes 3145736 | tf_op jit(solution)/shard_map/ppermute | solution.py:37
  27.9 37.5 %collective-permute-start.2 = (bf16[256,2048]{1,0:T(8,128)(2,1)S(1)}, bf16[256,2048]{1,0:T(8,128)(2,1)}, u32[]{:S(2)}, u32[]{:S(2)}) collective-permute-start(bf16[256,2048]{1,0:T(8,128)(2,1)S(1)} %fusion.3.refs_0_), channel_id=1, source_target_pairs={{0,1},{1,0},{2,3},{3,2},{4,5},{5,4},{6,7},{7,6},{8,9},{9,8},{10,11... | collective-permute-start | bytes 3145736 | tf_op jit(solution)/shard_map/ppermute | solution.py:37
  42.3 23.0 %collective-permute-start.5 = (bf16[512,1024]{1,0:T(8,128)(2,1)}, bf16[512,1024]{1,0:T(8,128)(2,1)}, u32[]{:S(2)}, u32[]{:S(2)}) collective-permute-start(bf16[512,1024]{1,0:T(8,128)(2,1)} %get-tuple-element.463), channel_id=1, source_target_pairs={{0,1},{1,0},{2,3},{3,2},{4,5},{5,4},{6,7},{7,6},{8,9},{9,8},{10,11... | collective-permute-start | bytes 3145736 | tf_op jit(solution)/shard_map/ppermute | solution.py:37
  42.4 40.7 %collective-permute-start.6 = (bf16[512,1024]{1,0:T(8,128)(2,1)}, bf16[512,1024]{1,0:T(8,128)(2,1)S(1)}, u32[]{:S(2)}, u32[]{:S(2)}) collective-permute-start(bf16[512,1024]{1,0:T(8,128)(2,1)} %get-tuple-element.464), channel_id=1, source_target_pairs={{0,4},{4,0},{1,5},{5,1},{2,6},{6,2},{3,7},{7,3},{8,12},{12,8},{9,1... | collective-permute-start | bytes 3145736 | tf_op jit(solution)/shard_map/ppermute | solution.py:37
  43.9 39.2 %collective-permute-start.7 = (bf16[512,1024]{1,0:T(8,128)(2,1)}, bf16[512,1024]{1,0:T(8,128)(2,1)S(1)}, u32[]{:S(2)}, u32[]{:S(2)}) collective-permute-start(bf16[512,1024]{1,0:T(8,128)(2,1)} %get-tuple-element.462), channel_id=1, source_target_pairs={{0,2},{2,0},{1,3},{3,1},{4,6},{6,4},{5,7},{7,5},{8,10},{10,8},{9,1... | collective-permute-start | bytes 3145736 | tf_op jit(solution)/shard_map/ppermute | solution.py:37
  83.2 239.7 %all-gather.8.cloned.1.call-start = ((), (), s32[]{:S(2)}) async-start(), calls=%async_computation.7 | async-start | bytes 5242880 | tf_op jit(solution)/shard_map/all_gather | solution.py:767
  85.1 10.4 %collective-permute-start.8 = (bf16[1024,1024]{1,0:T(8,128)(2,1)}, bf16[1024,1024]{1,0:T(8,128)(2,1)}, u32[]{:S(2)}, u32[]{:S(2)}) collective-permute-start(bf16[1024,1024]{1,0:T(8,128)(2,1)} %pad_maximum_fusion), channel_id=1, source_target_pairs={{0,1},{1,0},{2,3},{3,2},{4,5},{5,4},{6,7},{7,6},{8,9},{9,8},{10,11... | collective-permute-start | bytes 6291464 | tf_op jit(solution)/shard_map/ppermute | solution.py:37
  88.2 23.7 %collective-permute-start.10 = (bf16[256,2048]{1,0:T(8,128)(2,1)}, bf16[256,2048]{1,0:T(8,128)(2,1)}, u32[]{:S(2)}, u32[]{:S(2)}) collective-permute-start(bf16[256,2048]{1,0:T(8,128)(2,1)} %multiply_convert_fusion.refs_0_), channel_id=1, source_target_pairs={{0,1},{1,0},{2,3},{3,2},{4,5},{5,4},{6,7},{7,6},{8,9},{9,8},{10,11... | collective-permute-start | bytes 3145736 | tf_op jit(solution)/shard_map/ppermute | solution.py:37
  91.0 21.0 %collective-permute-start.11 = (bf16[256,1024]{1,0:T(8,128)(2,1)}, bf16[256,1024]{1,0:T(8,128)(2,1)S(1)}, u32[]{:S(2)}, u32[]{:S(2)}) collective-permute-start(bf16[256,1024]{1,0:T(8,128)(2,1)} %get-tuple-element.446), channel_id=1, source_target_pairs={{0,2},{2,0},{1,3},{3,1},{4,6},{6,4},{5,7},{7,5},{8,10},{10,8},{9,1... | collective-permute-start | bytes 1572872 | tf_op jit(solution)/shard_map/ppermute | solution.py:37
  91.6 20.4 %collective-permute-start.12 = (bf16[256,1024]{1,0:T(8,128)(2,1)}, bf16[256,1024]{1,0:T(8,128)(2,1)}, u32[]{:S(2)}, u32[]{:S(2)}) collective-permute-start(bf16[256,1024]{1,0:T(8,128)(2,1)} %get-tuple-element.445), channel_id=1, source_target_pairs={{0,4},{4,0},{1,5},{5,1},{2,6},{6,2},{3,7},{7,3},{8,12},{12,8},{9,1... | collective-permute-start | bytes 1572872 | tf_op jit(solution)/shard_map/ppermute | solution.py:37
  110.0 10.9 %collective-permute-start.9 = (bf16[128,512]{1,0:T(8,128)(2,1)S(1)}, bf16[128,512]{1,0:T(8,128)(2,1)S(1)}, u32[]{:S(2)}, u32[]{:S(2)}) collective-permute-start(bf16[128,512]{1,0:T(8,128)(2,1)S(1)} %slice.100), channel_id=1, source_target_pairs={{0,8},{8,16},{16,24},{24,0},{1,9},{9,17},{17,25},{25,1},{2,10},{10... | collective-permute-start | bytes 393224 | tf_op jit(solution)/shard_map/ppermute | solution.py:42
  123.8 25.4 %collective-permute-start.13 = (bf16[512,1024]{1,0:T(8,128)(2,1)S(1)}, bf16[512,1024]{1,0:T(8,128)(2,1)S(1)}, u32[]{:S(2)}, u32[]{:S(2)}) collective-permute-start(bf16[512,1024]{1,0:T(8,128)(2,1)S(1)} %get-tuple-element.460), channel_id=1, source_target_pairs={{0,1},{1,0},{2,3},{3,2},{4,5},{5,4},{6,7},{7,6},{8,9},{9,8},{10,11... | collective-permute-start | bytes 3145736 | tf_op jit(solution)/shard_map/ppermute | solution.py:37
  123.9 26.0 %collective-permute-start.14 = (bf16[512,1024]{1,0:T(8,128)(2,1)S(1)}, bf16[512,1024]{1,0:T(8,128)(2,1)S(1)}, u32[]{:S(2)}, u32[]{:S(2)}) collective-permute-start(bf16[512,1024]{1,0:T(8,128)(2,1)S(1)} %get-tuple-element.461), channel_id=1, source_target_pairs={{0,4},{4,0},{1,5},{5,1},{2,6},{6,2},{3,7},{7,3},{8,12},{12,8},{9,1... | collective-permute-start | bytes 3145736 | tf_op jit(solution)/shard_map/ppermute | solution.py:37
  124.7 25.2 %collective-permute-start.15 = (bf16[512,1024]{1,0:T(8,128)(2,1)S(1)}, bf16[512,1024]{1,0:T(8,128)(2,1)S(1)}, u32[]{:S(2)}, u32[]{:S(2)}) collective-permute-start(bf16[512,1024]{1,0:T(8,128)(2,1)S(1)} %get-tuple-element.459), channel_id=1, source_target_pairs={{0,2},{2,0},{1,3},{3,1},{4,6},{6,4},{5,7},{7,5},{8,10},{10,8},{9,1... | collective-permute-start | bytes 3145736 | tf_op jit(solution)/shard_map/ppermute | solution.py:37
  126.2 34.6 %collective-permute-start.16 = (bf16[1024,256]{1,0:T(8,128)(2,1)S(1)}, bf16[1024,256]{1,0:T(8,128)(2,1)}, u32[]{:S(2)}, u32[]{:S(2)}) collective-permute-start(bf16[1024,256]{1,0:T(8,128)(2,1)S(1)} %get-tuple-element.221), channel_id=1, source_target_pairs={{0,4},{4,0},{1,5},{5,1},{2,6},{6,2},{3,7},{7,3},{8,12},{12,8},{9,1... | collective-permute-start | bytes 1572872 | tf_op jit(solution)/shard_map/ppermute | solution.py:37
  160.8 7.4 %collective-permute-start.17 = (bf16[1024,2048]{1,0:T(8,128)(2,1)}, bf16[1024,2048]{1,0:T(8,128)(2,1)S(1)}, u32[]{:S(2)}, u32[]{:S(2)}) collective-permute-start(bf16[1024,2048]{1,0:T(8,128)(2,1)} %product.8), channel_id=1, source_target_pairs={{0,1},{1,0},{2,3},{3,2},{4,5},{5,4},{6,7},{7,6},{8,9},{9,8},{10,11... | collective-permute-start | bytes 12582920 | tf_op jit(solution)/shard_map/ppermute | solution.py:37
  162.4 28.3 %collective-permute-start.21 = (bf16[1024,1024]{1,0:T(8,128)(2,1)}, bf16[1024,1024]{1,0:T(8,128)(2,1)S(1)}, u32[]{:S(2)}, u32[]{:S(2)}) collective-permute-start(bf16[1024,1024]{1,0:T(8,128)(2,1)} %pad_maximum_fusion.1), channel_id=1, source_target_pairs={{0,1},{1,0},{2,3},{3,2},{4,5},{5,4},{6,7},{7,6},{8,9},{9,8},{10,11... | collective-permute-start | bytes 6291464 | tf_op jit(solution)/shard_map/ppermute | solution.py:37
  177.5 25.4 %collective-permute-start.19 = (bf16[2,256,1024]{2,1,0:T(8,128)(2,1)}, bf16[2,256,1024]{2,1,0:T(8,128)(2,1)S(1)}, u32[]{:S(2)}, u32[]{:S(2)}) collective-permute-start(bf16[2,256,1024]{2,1,0:T(8,128)(2,1)} %get-tuple-element.227), channel_id=1, source_target_pairs={{0,2},{2,0},{1,3},{3,1},{4,6},{6,4},{5,7},{7,5},{8,10},{10,8},{9,1... | collective-permute-start | bytes 3145736 | tf_op jit(solution)/shard_map/ppermute | solution.py:37
  179.1 25.2 %collective-permute-start.20 = (bf16[2,256,1024]{2,1,0:T(8,128)(2,1)}, bf16[2,256,1024]{2,1,0:T(8,128)(2,1)}, u32[]{:S(2)}, u32[]{:S(2)}) collective-permute-start(bf16[2,256,1024]{2,1,0:T(8,128)(2,1)} %get-tuple-element.228), channel_id=1, source_target_pairs={{0,4},{4,0},{1,5},{5,1},{2,6},{6,2},{3,7},{7,3},{8,12},{12,8},{9,1... | collective-permute-start | bytes 3145736 | tf_op jit(solution)/shard_map/ppermute | solution.py:37
  179.7 8.3 %collective-permute-start.22 = (f32[8,128]{1,0:T(8,128)S(1)}, f32[8,128]{1,0:T(8,128)S(1)}, u32[]{:S(2)}, u32[]{:S(2)}) collective-permute-start(f32[8,128]{1,0:T(8,128)S(1)} %maximum_select_fusion.10), channel_id=1, source_target_pairs={{0,8},{8,16},{16,24},{24,0},{1,9},{9,17},{17,25},{25,1},{2,10},{10... | collective-permute-start | bytes 12296 | tf_op jit(solution)/shard_map/ppermute | solution.py:42
  188.0 11.1 %collective-permute-start.23 = (f32[8,128]{1,0:T(8,128)S(1)}, f32[8,128]{1,0:T(8,128)S(1)}, u32[]{:S(2)}, u32[]{:S(2)}) collective-permute-start(f32[8,128]{1,0:T(8,128)S(1)} %max.17), channel_id=1, source_target_pairs={{0,16},{8,24},{16,0},{24,8},{1,17},{9,25},{17,1},{25,9},{2,18},{10... | collective-permute-start | bytes 12296 | tf_op jit(solution)/shard_map/ppermute | solution.py:42
  204.3 286.7 %reduce-scatter.6.cloned.1.call-start = ((), (), s32[]{:S(2)}) async-start(), calls=%async_computation.8 | async-start | bytes 5242880 | tf_op jit(solution)/shard_map/reduce_scatter | solution.py:786
  209.0 13.0 %collective-permute-start.24 = (bf16[256,1024]{1,0:T(8,128)(2,1)}, bf16[256,1024]{1,0:T(8,128)(2,1)S(1)}, u32[]{:S(2)}, u32[]{:S(2)}) collective-permute-start(bf16[256,1024]{1,0:T(8,128)(2,1)} %get-tuple-element.248), channel_id=1, source_target_pairs={{0,4},{4,0},{1,5},{5,1},{2,6},{6,2},{3,7},{7,3},{8,12},{12,8},{9,1... | collective-permute-start | bytes 1572872 | tf_op jit(solution)/shard_map/ppermute | solution.py:37
  209.6 12.7 %collective-permute-start.25 = (bf16[256,1024]{1,0:T(8,128)(2,1)}, bf16[256,1024]{1,0:T(8,128)(2,1)S(1)}, u32[]{:S(2)}, u32[]{:S(2)}) collective-permute-start(bf16[256,1024]{1,0:T(8,128)(2,1)} %get-tuple-element.249), channel_id=1, source_target_pairs={{0,2},{2,0},{1,3},{3,1},{4,6},{6,4},{5,7},{7,5},{8,10},{10,8},{9,1... | collective-permute-start | bytes 1572872 | tf_op jit(solution)/shard_map/ppermute | solution.py:37
  228.1 15.3 %collective-permute-start.26 = (bf16[256,2048]{1,0:T(8,128)(2,1)}, bf16[256,2048]{1,0:T(8,128)(2,1)}, u32[]{:S(2)}, u32[]{:S(2)}) collective-permute-start(bf16[256,2048]{1,0:T(8,128)(2,1)} %get-tuple-element.256.refs_0_), channel_id=1, source_target_pairs={{0,1},{1,0},{2,3},{3,2},{4,5},{5,4},{6,7},{7,6},{8,9},{9,8},{10,11... | collective-permute-start | bytes 3145736 | tf_op jit(solution)/shard_map/ppermute | solution.py:37
  228.2 14.5 %collective-permute-start.27 = (bf16[256,1024]{1,0:T(8,128)(2,1)}, bf16[256,1024]{1,0:T(8,128)(2,1)S(1)}, u32[]{:S(2)}, u32[]{:S(2)}) collective-permute-start(bf16[256,1024]{1,0:T(8,128)(2,1)} %get-tuple-element.254), channel_id=1, source_target_pairs={{0,2},{2,0},{1,3},{3,1},{4,6},{6,4},{5,7},{7,5},{8,10},{10,8},{9,1... | collective-permute-start | bytes 1572872 | tf_op jit(solution)/shard_map/ppermute | solution.py:37
  229.2 14.2 %collective-permute-start.28 = (bf16[256,1024]{1,0:T(8,128)(2,1)}, bf16[256,1024]{1,0:T(8,128)(2,1)S(1)}, u32[]{:S(2)}, u32[]{:S(2)}) collective-permute-start(bf16[256,1024]{1,0:T(8,128)(2,1)} %get-tuple-element.255), channel_id=1, source_target_pairs={{0,4},{4,0},{1,5},{5,1},{2,6},{6,2},{3,7},{7,3},{8,12},{12,8},{9,1... | collective-permute-start | bytes 1572872 | tf_op jit(solution)/shard_map/ppermute | solution.py:37
  245.5 25.6 %collective-permute-start.30 = (bf16[512,1024]{1,0:T(8,128)(2,1)S(1)}, bf16[512,1024]{1,0:T(8,128)(2,1)S(1)}, u32[]{:S(2)}, u32[]{:S(2)}) collective-permute-start(bf16[512,1024]{1,0:T(8,128)(2,1)S(1)} %get-tuple-element.458), channel_id=1, source_target_pairs={{0,4},{4,0},{1,5},{5,1},{2,6},{6,2},{3,7},{7,3},{8,12},{12,8},{9,1... | collective-permute-start | bytes 3145736 | tf_op jit(solution)/shard_map/ppermute | solution.py:37
  246.9 25.2 %collective-permute-start.31 = (bf16[512,1024]{1,0:T(8,128)(2,1)S(1)}, bf16[512,1024]{1,0:T(8,128)(2,1)S(1)}, u32[]{:S(2)}, u32[]{:S(2)}) collective-permute-start(bf16[512,1024]{1,0:T(8,128)(2,1)S(1)} %get-tuple-element.456), channel_id=1, source_target_pairs={{0,2},{2,0},{1,3},{3,1},{4,6},{6,4},{5,7},{7,5},{8,10},{10,8},{9,1... | collective-permute-start | bytes 3145736 | tf_op jit(solution)/shard_map/ppermute | solution.py:37
  322.6 168.4 %reduce-scatter.8.cloned.1.call-start = ((), (), s32[]{:S(2)}) async-start(), calls=%async_computation.9 | async-start | bytes 5242880 | tf_op jit(solution)/shard_map/reduce_scatter | solution.py:786
  381.4 28.7 %collective-permute-start.34 = (bf16[2,256,1024]{2,1,0:T(8,128)(2,1)}, bf16[2,256,1024]{2,1,0:T(8,128)(2,1)S(1)}, u32[]{:S(2)}, u32[]{:S(2)}) collective-permute-start(bf16[2,256,1024]{2,1,0:T(8,128)(2,1)} %get-tuple-element.278), channel_id=1, source_target_pairs={{0,2},{2,0},{1,3},{3,1},{4,6},{6,4},{5,7},{7,5},{8,10},{10,8},{9,1... | collective-permute-start | bytes 3145736 | tf_op jit(solution)/shard_map/ppermute | solution.py:37
  382.2 27.9 %collective-permute-start.35 = (bf16[2,256,1024]{2,1,0:T(8,128)(2,1)}, bf16[2,256,1024]{2,1,0:T(8,128)(2,1)S(1)}, u32[]{:S(2)}, u32[]{:S(2)}) collective-permute-start(bf16[2,256,1024]{2,1,0:T(8,128)(2,1)} %get-tuple-element.279), channel_id=1, source_target_pairs={{0,4},{4,0},{1,5},{5,1},{2,6},{6,2},{3,7},{7,3},{8,12},{12,8},{9,1... | collective-permute-start | bytes 3145736 | tf_op jit(solution)/shard_map/ppermute | solution.py:37
  411.4 172.8 %reduce-scatter.10.cloned.1.call-start = ((), (), s32[]{:S(2)}) async-start(), calls=%async_computation.10 | async-start | bytes 5242880 | tf_op jit(solution)/shard_map/reduce_scatter | solution.py:786
  415.5 13.7 %collective-permute-start.36 = (bf16[256,1024]{1,0:T(8,128)(2,1)}, bf16[256,1024]{1,0:T(8,128)(2,1)S(1)}, u32[]{:S(2)}, u32[]{:S(2)}) collective-permute-start(bf16[256,1024]{1,0:T(8,128)(2,1)} %get-tuple-element.285), channel_id=1, source_target_pairs={{0,4},{4,0},{1,5},{5,1},{2,6},{6,2},{3,7},{7,3},{8,12},{12,8},{9,1... | collective-permute-start | bytes 1572872 | tf_op jit(solution)/shard_map/ppermute | solution.py:37
  416.3 13.4 %collective-permute-start.37 = (bf16[256,1024]{1,0:T(8,128)(2,1)}, bf16[256,1024]{1,0:T(8,128)(2,1)S(1)}, u32[]{:S(2)}, u32[]{:S(2)}) collective-permute-start(bf16[256,1024]{1,0:T(8,128)(2,1)} %get-tuple-element.286), channel_id=1, source_target_pairs={{0,2},{2,0},{1,3},{3,1},{4,6},{6,4},{5,7},{7,5},{8,10},{10,8},{9,1... | collective-permute-start | bytes 1572872 | tf_op jit(solution)/shard_map/ppermute | solution.py:37
  436.6 12.7 %collective-permute-start.38 = (bf16[256,1024]{1,0:T(8,128)(2,1)}, bf16[256,1024]{1,0:T(8,128)(2,1)S(1)}, u32[]{:S(2)}, u32[]{:S(2)}) collective-permute-start(bf16[256,1024]{1,0:T(8,128)(2,1)} %get-tuple-element.290), channel_id=1, source_target_pairs={{0,2},{2,0},{1,3},{3,1},{4,6},{6,4},{5,7},{7,5},{8,10},{10,8},{9,1... | collective-permute-start | bytes 1572872 | tf_op jit(solution)/shard_map/ppermute | solution.py:37
  437.9 12.2 %collective-permute-start.39 = (bf16[256,1024]{1,0:T(8,128)(2,1)}, bf16[256,1024]{1,0:T(8,128)(2,1)S(1)}, u32[]{:S(2)}, u32[]{:S(2)}) collective-permute-start(bf16[256,1024]{1,0:T(8,128)(2,1)} %get-tuple-element.291), channel_id=1, source_target_pairs={{0,4},{4,0},{1,5},{5,1},{2,6},{6,2},{3,7},{7,3},{8,12},{12,8},{9,1... | collective-permute-start | bytes 1572872 | tf_op jit(solution)/shard_map/ppermute | solution.py:37
  450.1 7.5 %collective-permute-start.42 = (bf16[1024,2048]{1,0:T(8,128)(2,1)}, bf16[1024,2048]{1,0:T(8,128)(2,1)}, u32[]{:S(2)}, u32[]{:S(2)}) collective-permute-start(bf16[1024,2048]{1,0:T(8,128)(2,1)} %product.12), channel_id=1, source_target_pairs={{0,1},{1,0},{2,3},{3,2},{4,5},{5,4},{6,7},{7,6},{8,9},{9,8},{10,11... | collective-permute-start | bytes 12582920 | tf_op jit(solution)/shard_map/ppermute | solution.py:37
  450.1 161.9 %reduce-scatter.12.cloned.1.call-start = ((), (), s32[]{:S(2)}) async-start(), calls=%async_computation.11 | async-start | bytes 1310720 | tf_op jit(solution)/shard_map/reduce_scatter | solution.py:786
  452.3 25.4 %collective-permute-start.40 = (bf16[512,1024]{1,0:T(8,128)(2,1)}, bf16[512,1024]{1,0:T(8,128)(2,1)S(1)}, u32[]{:S(2)}, u32[]{:S(2)}) collective-permute-start(bf16[512,1024]{1,0:T(8,128)(2,1)} %get-tuple-element.454), channel_id=1, source_target_pairs={{0,4},{4,0},{1,5},{5,1},{2,6},{6,2},{3,7},{7,3},{8,12},{12,8},{9,1... | collective-permute-start | bytes 3145736 | tf_op jit(solution)/shard_map/ppermute | solution.py:37
  453.1 24.9 %collective-permute-start.41 = (bf16[512,1024]{1,0:T(8,128)(2,1)S(1)}, bf16[512,1024]{1,0:T(8,128)(2,1)S(1)}, u32[]{:S(2)}, u32[]{:S(2)}) collective-permute-start(bf16[512,1024]{1,0:T(8,128)(2,1)S(1)} %get-tuple-element.455), channel_id=1, source_target_pairs={{0,2},{2,0},{1,3},{3,1},{4,6},{6,4},{5,7},{7,5},{8,10},{10,8},{9,1... | collective-permute-start | bytes 3145736 | tf_op jit(solution)/shard_map/ppermute | solution.py:37
  454.5 23.5 %collective-permute-start.43 = (bf16[256,2048]{1,0:T(8,128)(2,1)S(1)}, bf16[256,2048]{1,0:T(8,128)(2,1)S(1)}, u32[]{:S(2)}, u32[]{:S(2)}) collective-permute-start(bf16[256,2048]{1,0:T(8,128)(2,1)S(1)} %copy-done.16), channel_id=1, source_target_pairs={{0,1},{1,0},{2,3},{3,2},{4,5},{5,4},{6,7},{7,6},{8,9},{9,8},{10,11... | collective-permute-start | bytes 3145736 | tf_op jit(solution)/shard_map/ppermute | solution.py:37
  454.5 23.5 %collective-permute-start.44 = (bf16[512,1024]{1,0:T(8,128)(2,1)S(1)}, bf16[512,1024]{1,0:T(8,128)(2,1)S(1)}, u32[]{:S(2)}, u32[]{:S(2)}) collective-permute-start(bf16[512,1024]{1,0:T(8,128)(2,1)S(1)} %get-tuple-element.453), channel_id=1, source_target_pairs={{0,1},{1,0},{2,3},{3,2},{4,5},{5,4},{6,7},{7,6},{8,9},{9,8},{10,11... | collective-permute-start | bytes 3145736 | tf_op jit(solution)/shard_map/ppermute | solution.py:37
  479.8 59.1 %collective-permute-start.48 = (bf16[2,256,1024]{2,1,0:T(8,128)(2,1)}, bf16[2,256,1024]{2,1,0:T(8,128)(2,1)S(1)}, u32[]{:S(2)}, u32[]{:S(2)}) collective-permute-start(bf16[2,256,1024]{2,1,0:T(8,128)(2,1)} %get-tuple-element.316), channel_id=1, source_target_pairs={{0,2},{2,0},{1,3},{3,1},{4,6},{6,4},{5,7},{7,5},{8,10},{10,8},{9,1... | collective-permute-start | bytes 3145736 | tf_op jit(solution)/shard_map/ppermute | solution.py:37
  481.1 57.8 %collective-permute-start.49 = (bf16[2,256,1024]{2,1,0:T(8,128)(2,1)}, bf16[2,256,1024]{2,1,0:T(8,128)(2,1)}, u32[]{:S(2)}, u32[]{:S(2)}) collective-permute-start(bf16[2,256,1024]{2,1,0:T(8,128)(2,1)} %get-tuple-element.317), channel_id=1, source_target_pairs={{0,4},{4,0},{1,5},{5,1},{2,6},{6,2},{3,7},{7,3},{8,12},{12,8},{9,1... | collective-permute-start | bytes 3145736 | tf_op jit(solution)/shard_map/ppermute | solution.py:37
  492.4 46.5 %collective-permute-start.46 = (bf16[1024,256]{1,0:T(8,128)(2,1)S(1)}, bf16[1024,256]{1,0:T(8,128)(2,1)S(1)}, u32[]{:S(2)}, u32[]{:S(2)}) collective-permute-start(bf16[1024,256]{1,0:T(8,128)(2,1)S(1)} %get-tuple-element.432), channel_id=1, source_target_pairs={{0,4},{4,0},{1,5},{5,1},{2,6},{6,2},{3,7},{7,3},{8,12},{12,8},{9,1... | collective-permute-start | bytes 1572872 | tf_op jit(solution)/shard_map/ppermute | solution.py:37
  494.6 44.4 %collective-permute-start.47 = (bf16[256,1024]{1,0:T(8,128)(2,1)}, bf16[256,1024]{1,0:T(8,128)(2,1)S(1)}, u32[]{:S(2)}, u32[]{:S(2)}) collective-permute-start(bf16[256,1024]{1,0:T(8,128)(2,1)} %get-tuple-element.436), channel_id=1, source_target_pairs={{0,4},{4,0},{1,5},{5,1},{2,6},{6,2},{3,7},{7,3},{8,12},{12,8},{9,1... | collective-permute-start | bytes 1572872 | tf_op jit(solution)/shard_map/ppermute | solution.py:37
  540.7 17.8 %collective-permute-start.50 = (bf16[128,512]{1,0:T(8,128)(2,1)}, bf16[128,512]{1,0:T(8,128)(2,1)S(1)}, u32[]{:S(2)}, u32[]{:S(2)}) collective-permute-start(bf16[128,512]{1,0:T(8,128)(2,1)} %get-tuple-element.323), channel_id=1, source_target_pairs={{0,24},{8,0},{16,8},{24,16},{1,25},{9,1},{17,9},{25,17},{2,26},{10... | collective-permute-start | bytes 393224 | tf_op jit(solution)/shard_map/ppermute | solution.py:42
  567.5 17.4 %collective-permute-start.51 = (bf16[1024,2048]{1,0:T(8,128)(2,1)}, bf16[1024,2048]{1,0:T(8,128)(2,1)}, u32[]{:S(2)}, u32[]{:S(2)}) collective-permute-start(bf16[1024,2048]{1,0:T(8,128)(2,1)} %product.14), channel_id=1, source_target_pairs={{0,1},{1,0},{2,3},{3,2},{4,5},{5,4},{6,7},{7,6},{8,9},{9,8},{10,11... | collective-permute-start | bytes 12582920 | tf_op jit(solution)/shard_map/ppermute | solution.py:37
  567.5 70.8 %reduce-scatter.14.cloned.1.call-start = ((), (), s32[]{:S(2)}) async-start(), calls=%async_computation.12 | async-start | bytes 1966080 | tf_op jit(solution)/shard_map/reduce_scatter | solution.py:786
  569.6 14.7 %collective-permute-start.52 = (bf16[256,1024]{1,0:T(8,128)(2,1)}, bf16[256,1024]{1,0:T(8,128)(2,1)S(1)}, u32[]{:S(2)}, u32[]{:S(2)}) collective-permute-start(bf16[256,1024]{1,0:T(8,128)(2,1)} %get-tuple-element.333), channel_id=1, source_target_pairs={{0,4},{4,0},{1,5},{5,1},{2,6},{6,2},{3,7},{7,3},{8,12},{12,8},{9,1... | collective-permute-start | bytes 1572872 | tf_op jit(solution)/shard_map/ppermute | solution.py:37
  570.7 14.3 %collective-permute-start.53 = (bf16[256,1024]{1,0:T(8,128)(2,1)}, bf16[256,1024]{1,0:T(8,128)(2,1)S(1)}, u32[]{:S(2)}, u32[]{:S(2)}) collective-permute-start(bf16[256,1024]{1,0:T(8,128)(2,1)} %get-tuple-element.334), channel_id=1, source_target_pairs={{0,2},{2,0},{1,3},{3,1},{4,6},{6,4},{5,7},{7,5},{8,10},{10,8},{9,1... | collective-permute-start | bytes 1572872 | tf_op jit(solution)/shard_map/ppermute | solution.py:37
  587.1 14.1 %collective-permute-start.54 = (bf16[256,1024]{1,0:T(8,128)(2,1)}, bf16[256,1024]{1,0:T(8,128)(2,1)}, u32[]{:S(2)}, u32[]{:S(2)}) collective-permute-start(bf16[256,1024]{1,0:T(8,128)(2,1)} %get-tuple-element.346), channel_id=1, source_target_pairs={{0,4},{4,0},{1,5},{5,1},{2,6},{6,2},{3,7},{7,3},{8,12},{12,8},{9,1... | collective-permute-start | bytes 1572872 | tf_op jit(solution)/shard_map/ppermute | solution.py:37
  601.8 24.5 %collective-permute-start.55 = (bf16[2,256,1024]{2,1,0:T(8,128)(2,1)}, bf16[2,256,1024]{2,1,0:T(8,128)(2,1)S(1)}, u32[]{:S(2)}, u32[]{:S(2)}) collective-permute-start(bf16[2,256,1024]{2,1,0:T(8,128)(2,1)} %get-tuple-element.347), channel_id=1, source_target_pairs={{0,2},{2,0},{1,3},{3,1},{4,6},{6,4},{5,7},{7,5},{8,10},{10,8},{9,1... | collective-permute-start | bytes 3145736 | tf_op jit(solution)/shard_map/ppermute | solution.py:37
  602.8 24.0 %collective-permute-start.56 = (bf16[2,256,1024]{2,1,0:T(8,128)(2,1)}, bf16[2,256,1024]{2,1,0:T(8,128)(2,1)S(1)}, u32[]{:S(2)}, u32[]{:S(2)}) collective-permute-start(bf16[2,256,1024]{2,1,0:T(8,128)(2,1)} %get-tuple-element.348), channel_id=1, source_target_pairs={{0,4},{4,0},{1,5},{5,1},{2,6},{6,2},{3,7},{7,3},{8,12},{12,8},{9,1... | collective-permute-start | bytes 3145736 | tf_op jit(solution)/shard_map/ppermute | solution.py:37
  631.9 12.2 %collective-permute-start.59 = (bf16[256,1024]{1,0:T(8,128)(2,1)}, bf16[256,1024]{1,0:T(8,128)(2,1)S(1)}, u32[]{:S(2)}, u32[]{:S(2)}) collective-permute-start(bf16[256,1024]{1,0:T(8,128)(2,1)} %get-tuple-element.359), channel_id=1, source_target_pairs={{0,4},{4,0},{1,5},{5,1},{2,6},{6,2},{3,7},{7,3},{8,12},{12,8},{9,1... | collective-permute-start | bytes 1572872 | tf_op jit(solution)/shard_map/ppermute | solution.py:37
  633.0 11.9 %collective-permute-start.60 = (bf16[256,1024]{1,0:T(8,128)(2,1)}, bf16[256,1024]{1,0:T(8,128)(2,1)S(1)}, u32[]{:S(2)}, u32[]{:S(2)}) collective-permute-start(bf16[256,1024]{1,0:T(8,128)(2,1)} %get-tuple-element.360), channel_id=1, source_target_pairs={{0,2},{2,0},{1,3},{3,1},{4,6},{6,4},{5,7},{7,5},{8,10},{10,8},{9,1... | collective-permute-start | bytes 1572872 | tf_op jit(solution)/shard_map/ppermute | solution.py:37
  644.9 13.3 %collective-permute-start.65 = (bf16[256,256]{1,0:T(8,128)(2,1)S(1)}, bf16[256,256]{1,0:T(8,128)(2,1)S(1)}, u32[]{:S(2)}, u32[]{:S(2)}) collective-permute-start(bf16[256,256]{1,0:T(8,128)(2,1)S(1)} %get-tuple-element.372), channel_id=1, source_target_pairs={{0,4},{4,0},{1,5},{5,1},{2,6},{6,2},{3,7},{7,3},{8,12},{12,8},{9,1... | collective-permute-start | bytes 393224 | tf_op jit(solution)/shard_map/ppermute | solution.py:37
  645.8 13.4 %collective-permute-start.64 = (bf16[256,384]{1,0:T(8,128)(2,1)S(1)}, bf16[256,384]{1,0:T(8,128)(2,1)S(1)}, u32[]{:S(2)}, u32[]{:S(2)}) collective-permute-start(bf16[256,384]{1,0:T(8,128)(2,1)S(1)} %constant_dynamic-slice_fusion.13), channel_id=1, source_target_pairs={{0,4},{4,0},{1,5},{5,1},{2,6},{6,2},{3,7},{7,3},{8,12},{12,8},{9,1... | collective-permute-start | bytes 589832 | tf_op jit(solution)/shard_map/ppermute | solution.py:37
  (82 other events, 421.3 us)
Sparse Core Ops, SparseCore 0:
  21.9 56.2 all-gather.3
  83.3 152.9 all-gather.5
  237.9 78.9 all-gather.7
  322.8 79.4 reduce-scatter.5
  410.3 79.4 reduce-scatter.7
  492.0 80.0 reduce-scatter.9
  574.5 27.6 reduce-scatter.11
  604.4 33.9 reduce-scatter.13

commit v6 on v5

--- a/solution.py
+++ b/solution.py
@@ -183,17 +183,20 @@
     tile = 512
     args, specs, kinds, scratch = [], [], [], []
     for left, right, left_dim, right_dim, cut, *block in terms:
-        rows = left.shape[1 - left_dim] // 2
+        whole = not isinstance(left, tuple)
+        at = part if whole else 0
+        left = left if whole else left[part]
+        rows = left.shape[1 - left_dim] // (2 if whole else 1)
         depth = left.shape[left_dim]
         if left_dim == 1:
-            specs.append(pl.BlockSpec((rows, depth), lambda n: (part, 0)))
+            specs.append(pl.BlockSpec((rows, depth), lambda n, at=at: (at, 0)))
         else:
             specs.append(pl.BlockSpec((depth, rows), lambda n: (0, part)))
             scratch.append(pltpu.VMEM((rows, depth), BF16))
         if right_dim == 1:
             width = right.shape[0]
             if block:
-                specs.append(pl.BlockSpec((tile, depth), lambda n, at=block[0]: (n, at)))
+                specs.append(pl.BlockSpec((tile, depth), lambda n, to=block[0]: (n, to)))
             else:
                 specs.append(pl.BlockSpec((tile, right.shape[1]), lambda n: (n, 0)))
         else:
@@ -234,6 +237,9 @@
     return left, right, swap(send_x, "x"), swap(send_y, "y"), *later
 
 
+ROWS = 64
+
+
 def fold_kernel(left, right, left_x, right_y, left_out, right_out, y_out, x_out):
     total = left[...] + left_x[...].astype(F32)
     left_out[...], y_out[...] = total[0], total[1].astype(BF16)
@@ -255,8 +261,36 @@
     )(*parts)
 
 
-def spread_two(state, *extra):
-    left, right, send_y, send_x = fold(*state[:4])
+def resident(kernel, args, outs, name):
+    spec = pl.BlockSpec(memory_space=pltpu.VMEM)
+    return pl.pallas_call(
+        kernel,
+        out_shape=[jax.ShapeDtypeStruct(shape, kind) for shape, kind in outs],
+        in_specs=[spec] * len(args),
+        out_specs=[spec] * len(outs),
+        compiler_params=pltpu.CompilerParams(vmem_limit_bytes=24 * 2**20),
+        cost_estimate=FREE,
+        name=name,
+    )(*args)
+
+
+def fold_loop_kernel(left, right, left_x, right_y, left_out, right_out, y_out, x_out):
+    @pl.loop(0, left.shape[1] // ROWS)
+    def _(i):
+        here = pl.ds(pl.multiple_of(i * ROWS, ROWS), ROWS)
+        total = left[:, here, :] + left_x[:, here, :].astype(F32)
+        left_out[here, :], y_out[here, :] = total[0], total[1].astype(BF16)
+        total = right[:, here, :] + right_y[:, here, :].astype(F32)
+        right_out[here, :], x_out[here, :] = total[0], total[1].astype(BF16)
+
+
+def fold_resident(*parts):
+    shape = parts[0].shape[1:]
+    return resident(fold_loop_kernel, parts, [(shape, d) for d in (F32, F32, BF16, BF16)], "fold")
+
+
+def spread_two(state, *extra, folding=fold_resident):
+    left, right, send_y, send_x = folding(*state[:4])
     if extra:
         send_y, send_x, *extra = tie(send_y, send_x, *extra)
     return left, right, swap(send_y, "y"), swap(send_x, "x"), *extra
@@ -293,11 +327,6 @@
     sums, grad_out = refs[9:11]
     upstream = joined(*refs[:4])
     normal = (values * scale).astype(BF16).astype(F32)
-
-    @pl.when(pl.program_id(0) == 0)
-    def _():
-        sums[...] = jnp.zeros(sums.shape, F32)
-
     share = normal * upstream
     sums[...] += jnp.sum(share.reshape(-1, 8, share.shape[1]), axis=0)
     grad = base.astype(F32) + norm_back(values, scale, gain * upstream)
@@ -311,24 +340,39 @@
     refs[8][...] = grad.astype(BF16)
 
 
+def input_back(*args):
+    rows, width = args[4].shape
+
+    def spec(shape):
+        if shape[0] == rows:
+            return pl.BlockSpec((ROWS, shape[1]), lambda i: (i, 0))
+        return pl.BlockSpec(shape, lambda i: (0, 0))
+
+    return pl.pallas_call(
+        input_back_kernel,
+        out_shape=jax.ShapeDtypeStruct((rows, width), BF16),
+        grid=(rows // ROWS,),
+        in_specs=[spec(arg.shape) for arg in args],
+        out_specs=spec((rows, width)),
+        cost_estimate=FREE,
+        name="input_back",
+    )(*args)
+
+
 def row_call(kernel, args, outs, name):
     rows = args[0].shape[0]
-    size = rows // 4
-
-    def spec(shape):
-        if shape[0] == rows:
-            return pl.BlockSpec((size, shape[1]), lambda i: (i, 0))
-        return pl.BlockSpec(shape, lambda i: (0, 0))
-
-    return pl.pallas_call(
-        kernel,
-        out_shape=[jax.ShapeDtypeStruct(shape, kind) for shape, kind in outs],
-        grid=(4,),
-        in_specs=[spec(arg.shape) for arg in args],
-        out_specs=[spec(shape) for shape, _ in outs],
-        cost_estimate=FREE,
-        name=name,
-    )(*args)
+
+    def looped(*refs):
+        for ref in refs[len(args) :]:
+            if ref.shape[0] == 8:
+                ref[...] = jnp.zeros(ref.shape, F32)
+
+        @pl.loop(0, rows // ROWS)
+        def _(i):
+            here = pl.ds(pl.multiple_of(i * ROWS, ROWS), ROWS)
+            kernel(*(ref.at[here, :] if ref.shape[0] == rows else ref for ref in refs))
+
+    return resident(looped, args, outs, name)
 
 
 def over_z(x, combine):
@@ -622,10 +666,13 @@
     up_out[...] = (grad * gate * sig).astype(BF16)
 
 
-def ffn_call(kernel, rows, weights, width, kinds, held, name):
+def ffn_call(kernel, rows, weights, width, kinds, held, name, part=0, parts=1):
     high, wide = min(256 if held else 512, rows.shape[0]), min(1024, width)
     depth, steps = rows.shape[1], width // wide
+    count = rows.shape[0] // parts
+    skip = part * (count // high)
     tile = pl.BlockSpec((high, wide), lambda n, m: (m, n))
+    held_tile = pl.BlockSpec((high, wide), lambda n, m: (m + skip, n))
     if held:
         specs = [pl.BlockSpec((wide, depth), lambda n, m: (n, 0))]
     else:
@@ -633,14 +680,38 @@
                  pl.BlockSpec((depth, wide), lambda n, m: (0, n + steps))]
     return pl.pallas_call(
         kernel,
-        out_shape=[jax.ShapeDtypeStruct((rows.shape[0], width), kind) for kind in kinds],
-        grid=(steps, rows.shape[0] // high),
-        in_specs=[pl.BlockSpec((high, depth), lambda n, m: (m, 0))] + specs + [tile] * len(held),
+        out_shape=[jax.ShapeDtypeStruct((count, width), kind) for kind in kinds],
+        grid=(steps, count // high),
+        in_specs=[pl.BlockSpec((high, depth), lambda n, m: (m + skip, 0))]
+        + specs
+        + [held_tile] * len(held),
         out_specs=[tile] * len(kinds),
         compiler_params=pltpu.CompilerParams(vmem_limit_bytes=56 * 2**20),
         cost_estimate=FREE,
         name=name,
     )(rows, *([weights] * len(specs)), *held)
+
+
+def outer_halves_kernel(left, low, high, out):
+    rows = low.shape[0]
+    total = dot(left[:rows], low[...], 0, 0) + dot(left[rows:], high[...], 0, 0)
+    out[...] = total.astype(BF16)
+
+
+def outer_halves(left, low, high):
+    (depth, tall), wide = left.shape, low.shape[1]
+    rows, cols = min(512, tall), min(1024, wide)
+    half = pl.BlockSpec((depth // 2, cols), lambda n, m: (0, n))
+    return pl.pallas_call(
+        outer_halves_kernel,
+        out_shape=jax.ShapeDtypeStruct((tall, wide), BF16),
+        grid=(wide // cols, tall // rows),
+        in_specs=[pl.BlockSpec((depth, rows), lambda n, m: (0, m)), half, half],
+        out_specs=pl.BlockSpec((rows, cols), lambda n, m: (m, n)),
+        compiler_params=pltpu.CompilerParams(vmem_limit_bytes=56 * 2**20),
+        cost_estimate=FREE,
+        name="outer_halves",
+    )(left, low, high)
 
 
 def outer_kernel(right_dim, left, right, out):
@@ -792,13 +863,23 @@
     (down_part,) = outer(hidden, down_rows, 0)
     down_sum = reduced(down_part, 1)
     down_rows = after(down_rows, down_part)
-    gate_grad, up_grad = ffn_call(
-        hidden_back_kernel, down_rows, full_down, hid, (BF16, BF16), (gate_proj, up_proj),
-        "hidden_back",
-    )
-    terms = [(gate_grad, full_ffn, 1, 1, None, 0), (up_grad, full_ffn, 1, 1, None, 1)]
-    *norm_two, acts_two = spread_one(terms, None, acts_two)
-    ffn_parts = [outer(acts_two, grad, 0)[0] for grad in (gate_grad, up_grad)]
+    def grads(part, rows):
+        return ffn_call(
+            hidden_back_kernel, rows, full_down, hid, (BF16, BF16), (gate_proj, up_proj),
+            "hidden_back", part, 2,
+        )
+
+    def back_terms(gate_grad, up_grad):
+        return [(gate_grad, full_ffn, 1, 1, None, 0), (up_grad, full_ffn, 1, 1, None, 1)]
+
+    high_grads = grads(1, down_rows)
+    high_part = product(back_terms(*((None, grad) for grad in high_grads)), 1)
+    high_part, down_rows = tie(high_part, down_rows)
+    low_grads = grads(0, down_rows)
+    came, *low_grads = tie(swap(high_part, "c"), *low_grads)
+    pairs = list(zip(low_grads, high_grads, strict=True))
+    *norm_two, acts_two = spread_one(back_terms(*pairs), came, acts_two)
+    ffn_parts = [outer_halves(acts_two, *pair) for pair in pairs]
     *got, ffn_parts[0], ffn_parts[1] = tie(*norm_two[2:4], *ffn_parts)
     one_sum, two_sum = [reduced(part, 0) for part in ffn_parts]
     norm_two = spread_two((*norm_two[:2], *got))
@@ -851,12 +932,22 @@
     two_own = half_of(two_sum, y_rank, 0)
     came, two_sent = tie(came, half_of(two_sum, other_y, 0))
     qkv_sum = reduced(qkv_part, 0)
-    branch_two = spread_three((*second[:2], *got))
-    result = resid + RESIDUAL * own_mask * branch_two
+    second = (*second[:2], *got)
     *norm_one, sums, two_other = spread_one(terms, came, sums, swap(two_sent, "y"))
     gains = jnp.stack((sums[:, 0] / gain_one, jnp.sum(gain_two_part, axis=0)))
     gains = over_z(gains, jnp.add)
-    *got, gains, out_sum = tie(*norm_one[2:4], gains, out_sum)
+    gains, down_own, down_other, one_own, one_other, head_peak, *second = tie(
+        gains, down_own, down_other, one_own, one_other, head_peak, *second
+    )
+    down_grad = ordered(down_own, down_other, y_rank, 0).astype(F32)
+    gate_w_grad = ordered(one_own, one_other, y_rank, 1).astype(F32)
+    level = clip_level[0].astype(F32) * LEVEL_UNIT
+    factor = level / jnp.maximum(level, head_peak)
+    query_clipped = w_query.astype(F32) * jnp.repeat(jnp.sqrt(factor), HD)[None, :]
+    result = (resid + RESIDUAL * own_mask * spread_three(second)).astype(BF16)
+    *got, gains, out_sum, down_grad, gate_w_grad, query_clipped, result = tie(
+        *norm_one[2:4], gains, out_sum, down_grad, gate_w_grad, query_clipped, result
+    )
     gains = gains.reshape(2, lax.axis_size("z"), 2, 2, 2, -1)
 
     def halved(gains, dim, axis):
@@ -864,7 +955,7 @@
         return (lax.dynamic_index_in_dim(gains, at, dim, keepdims=False),
                 lax.dynamic_index_in_dim(gains, 1 - at, dim, keepdims=False))
 
-    norm_one = spread_two((*norm_one[:2], *got), gains)
+    norm_one = spread_two((*norm_one[:2], *got), gains, folding=fold)
     gains = norm_one[4]
     out_own, out_sent = half_of(out_sum, y_rank, 0), half_of(out_sum, other_y, 0)
     own, qkv_sent = half_of(qkv_sum, y_rank, 0), half_of(qkv_sum, other_y, 0)
@@ -872,15 +963,10 @@
     kept, sent = halved(kept + swap(sent, "c"), 3, "x")
     *norm_one, qkv_sent, kept, sent, out_sent = tie(*norm_one[:4], qkv_sent, kept, sent, out_sent)
     other, out_other = swap(qkv_sent, "y"), swap(out_sent, "y")
-    (grad_input,) = row_call(
-        input_back_kernel, (*norm_one, grad_resid, layer_in, scale_one, gain_one[None, :]),
-        [((tok_rows, width), BF16)], "input_back",
-    )
+    grad_input = input_back(*norm_one, grad_resid, layer_in, scale_one, gain_one[None, :])
     kept, sent = halved(kept + swap(sent, "x"), 2, "y")
     gains = lax.dynamic_index_in_dim(kept + swap(sent, "y"), z_rank, 1, keepdims=False)
 
-    down_grad = ordered(down_own, down_other, y_rank, 0).astype(F32)
-    gate_w_grad = ordered(one_own, one_other, y_rank, 1).astype(F32)
     up_w_grad = ordered(two_own, two_other, y_rank, 1).astype(F32)
     out_grad = ordered(out_own.T, out_other.T, y_rank, 0).astype(F32)
 
@@ -891,13 +977,10 @@
     key_grad = columns(K_AT, V_AT)
     value_grad = columns(V_AT, V_AT + HD)
 
-    level = clip_level[0].astype(F32) * LEVEL_UNIT
-    factor = level / jnp.maximum(level, head_peak)
-    query_clipped = w_query.astype(F32) * jnp.repeat(jnp.sqrt(factor), HD)[None, :]
     kv_factor = jnp.min(factor.reshape(-1, HEADS), axis=1)
     key_clipped = w_key.astype(F32) * jnp.repeat(jnp.sqrt(kv_factor), HD)[None, :]
     return (
-        result.astype(BF16),
+        result,
         grad_input,
         gains[0],
         query_grad,

time: 676 us -> 661 us (0.978)
  Pallas kernels: 296 us -> 286 us
  waiting for transfers between devices: 209 us -> 199 us
    pallas_call x5 -> x3, Pallas kernels: 56.9 us -> 30 us  [outer(): pl.pallas_call(kernel, out_shape=outs, grid=(wide // cols, high // rows),...]
    pallas_call x5 -> x10, Pallas kernels: 60 us -> 86.1 us  [the longest x3 48 us: ffn_call(): pl.pallas_call(kernel, out_shape=[jax.ShapeDtypeStruct((count, width), ki...]
    ppermute x60, waiting for transfers between devices: 184 us -> 168 us  [swap(): return lax.ppermute(x, axis, [(0, 1), (1, 0)])]
    pallas_call x4 -> x2, Pallas kernels: 16.5 us -> 8.29 us  [fold(): pl.pallas_call(fold_kernel, out_shape=[jax.ShapeDtypeStruct((rows, cols),...]
    reduce_scatter x5, waiting for transfers between devices: 0.12 us -> 7.01 us  [reduced(): return lax.psum_scatter(grad, 'z', scatter_dimension=axis, tiled=True)]
    unnamed x147 -> x135, local copies, waits for them, and re-layouts: 19.9 us -> 22.3 us
  transfers between devices with their start and end apart: 74 -> 74, of which waited for: 41 -> 40; matrix products, arithmetic and copies ran while one was open for 10% -> 10% of each run, Pallas kernels for 44% -> 44%
where the time goes in v6:
time: 661 us; the launch traced here: 654 us
  Pallas kernels  286 us (43%)
  waiting for transfers between devices  199 us (30%)
  starting transfers between devices  60.1 us (9%)
  local copies, waits for them, and re-layouts  39.8 us (6%)
  other arithmetic  37.6 us (6%)
  between operations  16.3 us (2%)
  matrix products  14.4 us (2%)
    ppermute x60, waiting for transfers between devices, swap(): return lax.ppermute(x, axis, [(0, 1), (1, 0)])  168 us
    pallas_call x8, Pallas kernels, product(): pl.pallas_call(functools.partial(product_kernel, kinds, came is not None)...  76 us
    pallas_call x4, Pallas kernels, call(): pl.pallas_call(kernel, out_shape=[jax.ShapeDtypeStruct(s, d) for s, d in...  57.5 us
    ppermute x60, starting transfers between devices, swap(): return lax.ppermute(x, axis, [(0, 1), (1, 0)])  52.1 us
    pallas_call x3, Pallas kernels, ffn_call(): pl.pallas_call(kernel, out_shape=[jax.ShapeDtypeStruct((count, width), ki...  48 us
    pallas_call x3, Pallas kernels, outer(): pl.pallas_call(kernel, out_shape=outs, grid=(wide // cols, high // rows),...  30 us
    pallas_call x4, Pallas kernels, place(): pl.pallas_call(functools.partial(place_kernel, spots, number), out_shape=...  28.6 us
    pallas_call x2, Pallas kernels, outer_halves(): pl.pallas_call(outer_halves_kernel, out_shape=jax.ShapeDtypeStruct((tall,...  26.8 us
  transfers between devices with their start and end apart: 74, of which 40 were waited for; matrix products, arithmetic and copies ran while one was open for 10% of the time, Pallas kernels for 44%

profile of v6, /device:TPU:0, one launch (start us, length us, event | category | flops | bytes accessed | tf_op | source)
XLA Modules:
  0.0 653.8 jit_solution(12226621713519458807)
XLA Ops:
  9.8 3.0 collective-permute-start
  12.9 7.6 %collective-permute-done = bf16[256,640]{1,0:T(8,128)(2,1)S(1)} collective-permute-done((bf16[256,640]{1,0:T(8,128)(2,1)S(1)}, bf16[256,640]{1,0:T(8,128)(2,1)S(1)}, u32[]{:S(2)}, u32[]{:S(2)}) %collective-permute-start) | collective-permute-done | bytes 327712 | tf_op jit(solution)/shard_map/ppermute | solution.py:37
  24.1 1.8 collective-permute-start.4
  28.2 10.9 %collective-permute-done.4.refs_3_ = bf16[256,1024]{1,0:T(8,128)(2,1)S(1)} collective-permute-done((bf16[256,1024]{1,0:T(8,128)(2,1)S(1)}, bf16[256,1024]{1,0:T(8,128)(2,1)S(1)}, u32[]{:S(2)}, u32[]{:S(2)}) %collective-permute-start.4) | collective-permute-done | bytes 524320 | tf_op jit(solution)/shard_map/ppermute | solution.py:37
  39.0 2.0 pad_maximum_fusion.5
  44.3 17.2 %collective-permute-done.1 = bf16[256,2048]{1,0:T(8,128)(2,1)S(1)} collective-permute-done((bf16[256,2048]{1,0:T(8,128)(2,1)S(1)}, bf16[256,2048]{1,0:T(8,128)(2,1)S(1)}, u32[]{:S(2)}, u32[]{:S(2)}) %collective-permute-start.1) | collective-permute-done | bytes 1048608 | tf_op jit(solution)/shard_map/ppermute | solution.py:37
  61.5 2.3 maximum_select_fusion
  63.8 18.5 %collective-permute-done.6.refs_5_ = bf16[512,1024]{1,0:T(8,128)(2,1)} collective-permute-done((bf16[512,1024]{1,0:T(8,128)(2,1)}, bf16[512,1024]{1,0:T(8,128)(2,1)}, u32[]{:S(2)}, u32[]{:S(2)}) %collective-permute-start.6) | collective-permute-done | bytes 1048608 | tf_op jit(solution)/shard_map/ppermute | solution.py:37
  82.4 3.1 pad_maximum_fusion
  94.7 7.5 %place.4.left = bf16[2048,2048]{1,0:T(8,128)(2,1)} custom-call(bf16[256,2048]{1,0:T(8,128)(2,1)} %copy-done.22, bf16[256,2048]{1,0:T(8,128)(2,1)} %collective-permute-done.2.refs_1_, bf16[256,1024]{1,0:T(8,128)(2,1)} %copy-done.32, bf16[256,1024]{1,0:T(8,128)(2,1)} %copy-done.31, bf16[512,1024]{1,0:T(8,128)(2,1)} %collective-permute-done.5.refs_4_, ...), custom_call_target="tpu_custom_call" | custom-call | tf_op jit(solution)/shard_map/place/pallas_call | solution.py:130
  102.2 6.4 fusion.6.qkv
  109.7 2.1 collective-permute-start.9
  111.8 9.0 %collective-permute-done.9.halo = bf16[128,512]{1,0:T(8,128)(2,1)S(1)} collective-permute-done((bf16[128,512]{1,0:T(8,128)(2,1)S(1)}, bf16[128,512]{1,0:T(8,128)(2,1)S(1)}, u32[]{:S(2)}, u32[]{:S(2)}) %collective-permute-start.9) | collective-permute-done | bytes 131104 | tf_op jit(solution)/shard_map/ppermute | solution.py:42
  124.2 20.0 %attend.1 = (bf16[256,2048]{1,0:T(8,128)(2,1)S(1)}, f32[8,2048]{1,0:T(8,128)S(1)}, f32[8,128]{1,0:T(8,128)S(1)}) custom-call(s32[3]{0:T(128)S(1)} %pad_add_fusion.info, bf16[384,2048]{1,0:T(8,128)(2,1)S(1)} %rope.1.qkv, bf16[128,512]{1,0:T(8,128)(2,1)S(1)} %collective-permute-done.9.halo), custom_call_target="tpu_custom_call" | custom-call | tf_op jit(solution)/shard_map/attend/pallas_call | solution.py:643
  145.3 2.6 collective-permute-done.14.refs_5_
  147.9 5.9 product.8
  153.9 5.0 collective-permute-done.16
  161.8 2.8 collective-permute-done.18
  166.3 2.0 copy-done.29
  168.3 7.3 %product.9 = (f32[2,256,1024]{2,1,0:T(8,128)}, f32[2,256,1024]{2,1,0:T(8,128)}, bf16[2,256,1024]{2,1,0:T(8,128)(2,1)}, bf16[2,256,1024]{2,1,0:T(8,128)(2,1)}) custom-call(bf16[256,2048]{1,0:T(8,128)(2,1)} %copy-done.2, bf16[2048,640]{1,0:T(8,128)(2,1)} %all-gather.4.cloned.1.call-done.refs_1_.weights, bf16[1024,2048]{1,0:T(8,128)(2,1)} %copy-done.29), custom_call_target="tpu_custom_call" | custom-call | tf_op jit(solution)/shard_map/product/pallas_call | solution.py:219
  177.6 8.5 %collective-permute-done.22 = f32[8,128]{1,0:T(8,128)S(1)} collective-permute-done((f32[8,128]{1,0:T(8,128)S(1)}, f32[8,128]{1,0:T(8,128)S(1)}, u32[]{:S(2)}, u32[]{:S(2)}) %collective-permute-start.22) | collective-permute-done | bytes 4128 | tf_op jit(solution)/shard_map/ppermute | solution.py:42
  186.3 2.5 maximum_select_fusion.1
  188.8 7.1 %place.5.right.rows = bf16[2048,2048]{1,0:T(8,128)(2,1)} custom-call(bf16[256,2048]{1,0:T(8,128)(2,1)} %copy-done.21, bf16[256,2048]{1,0:T(8,128)(2,1)} %collective-permute-done.10.refs_1_, bf16[256,1024]{1,0:T(8,128)(2,1)} %copy-done.34, bf16[256,1024]{1,0:T(8,128)(2,1)} %copy-done.33, bf16[512,1024]{1,0:T(8,128)(2,1)} %copy-done.43, ...), custom_call_target="tpu_custom_call" | custom-call | tf_op jit(solution)/shard_map/place/pallas_call | solution.py:130
  195.9 5.3 collective-permute-done.19.left_x
  204.0 1.9 fold.4
  208.7 10.1 %collective-permute-done.24.refs_2_ = bf16[256,1024]{1,0:T(8,128)(2,1)S(1)} collective-permute-done((bf16[256,1024]{1,0:T(8,128)(2,1)S(1)}, bf16[256,1024]{1,0:T(8,128)(2,1)S(1)}, u32[]{:S(2)}, u32[]{:S(2)}) %collective-permute-start.24) | collective-permute-done | bytes 524320 | tf_op jit(solution)/shard_map/ppermute | solution.py:37
  223.3 12.2 %collective-permute-done.27.refs_2_ = bf16[256,1024]{1,0:T(8,128)(2,1)S(1)} collective-permute-done((bf16[256,1024]{1,0:T(8,128)(2,1)S(1)}, bf16[256,1024]{1,0:T(8,128)(2,1)S(1)}, u32[]{:S(2)}, u32[]{:S(2)}) %collective-permute-start.27) | collective-permute-done | bytes 524320 | tf_op jit(solution)/shard_map/ppermute | solution.py:37
  241.0 22.2 %collective-permute-done.31.refs_6_ = bf16[512,1024]{1,0:T(8,128)(2,1)S(1)} collective-permute-done((bf16[512,1024]{1,0:T(8,128)(2,1)S(1)}, bf16[512,1024]{1,0:T(8,128)(2,1)S(1)}, u32[]{:S(2)}, u32[]{:S(2)}) %collective-permute-start.31) | collective-permute-done | bytes 1048608 | tf_op jit(solution)/shard_map/ppermute | solution.py:37
  266.1 4.3 collective-permute-done.32.refs_7_
  270.4 6.9 %place.6.rows.left = bf16[2048,2048]{1,0:T(8,128)(2,1)} custom-call(bf16[256,2048]{1,0:T(8,128)(2,1)} %copy-done.4, bf16[256,2048]{1,0:T(8,128)(2,1)} %collective-permute-done.26.refs_1_, bf16[256,1024]{1,0:T(8,128)(2,1)} %copy-done.39, bf16[256,1024]{1,0:T(8,128)(2,1)} %copy-done.40, bf16[512,1024]{1,0:T(8,128)(2,1)} %copy-done.46, ...), custom_call_target="tpu_custom_call" | custom-call | tf_op jit(solution)/shard_map/place/pallas_call | solution.py:130
  277.3 23.9 %hidden.1 = (f32[2048,1024]{1,0:T(8,128)}, f32[2048,1024]{1,0:T(8,128)}, bf16[2048,1024]{1,0:T(8,128)(2,1)}) custom-call(bf16[2048,2048]{1,0:T(8,128)(2,1)} %place.6.rows.left, bf16[2048,2048]{1,0:T(8,128)(2,1)} %all-gather.6.cloned.1.call-done.gate_w.up_w.refs_1_.refs_3_, bf16[2048,2048]{1,0:T(8,128)(2,1)} %all-gather.6.cloned.1.call-done.gate_w.up_w.refs_1_.refs_3_), custom_call_target="tpu_custom_call" | custom-call | tf_op jit(solution)/shard_map/hidden/pallas_call | solution.py:681
  301.2 14.1 %outer.3 = bf16[1024,2048]{1,0:T(8,128)(2,1)} custom-call(bf16[2048,1024]{1,0:T(8,128)(2,1)} %get-tuple-element.320.left.refs_0_, bf16[2048,2048]{1,0:T(8,128)(2,1)} %place.5.right.rows), custom_call_target="tpu_custom_call" | custom-call | tf_op jit(solution)/shard_map/outer/pallas_call | solution.py:743
  316.9 12.3 %hidden_back.2 = (bf16[1024,1024]{1,0:T(8,128)(2,1)}, bf16[1024,1024]{1,0:T(8,128)(2,1)}) custom-call(bf16[2048,2048]{1,0:T(8,128)(2,1)} %place.5.right.rows, bf16[1024,2048]{1,0:T(8,128)(2,1)} %all-gather.8.cloned.1.call-done.weights.refs_1_, f32[2048,1024]{1,0:T(8,128)} %get-tuple-element.290.gates, f32[2048,1024]{1,0:T(8,128)} %get-tuple-element.291.ups), custom_call_target="tpu_custom_call" | custom-call | tf_op jit(solution)/shard_map/hidden_back/pallas_call | solution.py:681
  329.2 13.5 %product.10 = bf16[1024,2048]{1,0:T(8,128)(2,1)} custom-call(bf16[1024,1024]{1,0:T(8,128)(2,1)} %get-tuple-element.292.refs_0_.high, bf16[2048,2048]{1,0:T(8,128)(2,1)} %all-gather.6.cloned.1.call-done.gate_w.up_w.refs_1_.refs_3_, bf16[1024,1024]{1,0:T(8,128)(2,1)} %get-tuple-element.293.refs_2_.high, ...), custom_call_target="tpu_custom_call" | custom-call | tf_op jit(solution)/shard_map/product/pallas_call | solution.py:219
  342.7 11.9 %hidden_back.3 = (bf16[1024,1024]{1,0:T(8,128)(2,1)}, bf16[1024,1024]{1,0:T(8,128)(2,1)}) custom-call(bf16[2048,2048]{1,0:T(8,128)(2,1)} %place.5.right.rows, bf16[1024,2048]{1,0:T(8,128)(2,1)} %all-gather.8.cloned.1.call-done.weights.refs_1_, f32[2048,1024]{1,0:T(8,128)} %get-tuple-element.290.gates, f32[2048,1024]{1,0:T(8,128)} %get-tuple-element.291.ups), custom_call_target="tpu_custom_call" | custom-call | tf_op jit(solution)/shard_map/hidden_back/pallas_call | solution.py:681
  354.6 2.1 copy-done.30
  356.7 15.7 %product.11 = (f32[2,256,1024]{2,1,0:T(8,128)}, f32[2,256,1024]{2,1,0:T(8,128)}, bf16[2,256,1024]{2,1,0:T(8,128)(2,1)}, bf16[2,256,1024]{2,1,0:T(8,128)(2,1)}) custom-call(bf16[1024,1024]{1,0:T(8,128)(2,1)} %get-tuple-element.298.refs_0_.low, bf16[2048,2048]{1,0:T(8,128)(2,1)} %all-gather.6.cloned.1.call-done.gate_w.up_w.refs_1_.refs_3_, ...), custom_call_target="tpu_custom_call" | custom-call | tf_op jit(solution)/shard_map/product/pallas_call | solution.py:219
  375.4 13.4 %outer_halves.3 = bf16[2048,1024]{1,0:T(8,128)(2,1)} custom-call(bf16[2048,2048]{1,0:T(8,128)(2,1)} %place.6.rows.left, bf16[1024,1024]{1,0:T(8,128)(2,1)} %get-tuple-element.299.refs_2_.low, bf16[1024,1024]{1,0:T(8,128)(2,1)} %get-tuple-element.293.refs_2_.high), custom_call_target="tpu_custom_call" | custom-call | tf_op jit(solution)/shard_map/outer_halves/pallas_call | solution.py:705
  388.8 13.4 %outer_halves.2 = bf16[2048,1024]{1,0:T(8,128)(2,1)} custom-call(bf16[2048,2048]{1,0:T(8,128)(2,1)} %place.6.rows.left, bf16[1024,1024]{1,0:T(8,128)(2,1)} %get-tuple-element.298.refs_0_.low, bf16[1024,1024]{1,0:T(8,128)(2,1)} %get-tuple-element.292.refs_0_.high), custom_call_target="tpu_custom_call" | custom-call | tf_op jit(solution)/shard_map/outer_halves/pallas_call | solution.py:705
  408.1 12.9 %collective-permute-done.36.refs_2_ = bf16[256,1024]{1,0:T(8,128)(2,1)S(1)} collective-permute-done((bf16[256,1024]{1,0:T(8,128)(2,1)S(1)}, bf16[256,1024]{1,0:T(8,128)(2,1)S(1)}, u32[]{:S(2)}, u32[]{:S(2)}) %collective-permute-start.36) | collective-permute-done | bytes 524320 | tf_op jit(solution)/shard_map/ppermute | solution.py:37
  426.3 8.4 %product.12 = bf16[1024,2048]{1,0:T(8,128)(2,1)} custom-call(bf16[2048,1024]{1,0:T(8,128)(2,1)} %get-tuple-element.320.left.refs_0_, bf16[1024,2048]{1,0:T(8,128)(2,1)} %all-gather.8.cloned.1.call-done.weights.refs_1_), custom_call_target="tpu_custom_call" | custom-call | tf_op jit(solution)/shard_map/product/pallas_call | solution.py:219
  434.7 2.3 collective-permute-done.39.refs_2_
  446.1 10.2 %product.13 = (f32[2,256,1024]{2,1,0:T(8,128)}, f32[2,256,1024]{2,1,0:T(8,128)}, bf16[2,256,1024]{2,1,0:T(8,128)(2,1)}, bf16[2,256,1024]{2,1,0:T(8,128)(2,1)}) custom-call(bf16[2048,1024]{1,0:T(8,128)(2,1)} %get-tuple-element.320.left.refs_0_, bf16[1024,2048]{1,0:T(8,128)(2,1)} %all-gather.8.cloned.1.call-done.weights.refs_1_, ...), custom_call_target="tpu_custom_call" | custom-call | tf_op jit(solution)/shard_map/product/pallas_call | solution.py:219
  456.3 11.4 %collective-permute-done.43.refs_6_ = bf16[512,1024]{1,0:T(8,128)(2,1)S(1)} collective-permute-done((bf16[512,1024]{1,0:T(8,128)(2,1)}, bf16[512,1024]{1,0:T(8,128)(2,1)S(1)}, u32[]{:S(2)}, u32[]{:S(2)}) %collective-permute-start.43) | collective-permute-done | bytes 1048608 | tf_op jit(solution)/shard_map/ppermute | solution.py:37
  474.0 7.1 %place.7.left = bf16[2048,2048]{1,0:T(8,128)(2,1)} custom-call(bf16[256,2048]{1,0:T(8,128)(2,1)} %copy-done.3, bf16[256,2048]{1,0:T(8,128)(2,1)} %copy-done.44, bf16[256,1024]{1,0:T(8,128)(2,1)} %copy-done.35, bf16[256,1024]{1,0:T(8,128)(2,1)} %copy-done.37, bf16[512,1024]{1,0:T(8,128)(2,1)} %collective-permute-done.41.refs_4_, ...), custom_call_target="tpu_custom_call" | custom-call | tf_op jit(solution)/shard_map/place/pallas_call | solution.py:130
  481.1 2.2 constant_dynamic-slice_fusion.13
  486.4 7.9 %convolution_convert_fusion.upstream = bf16[256,2048]{1,0:T(8,128)(2,1)} fusion(bf16[2048,2048]{1,0:T(8,128)(2,1)} %place.7.left, bf16[2048,640]{1,0:T(8,128)(2,1)} %all-gather.4.cloned.1.call-done.refs_1_.weights), kind=kOutput, calls=%fused_computation.2 | convolution fusion | flops 2148007936 | bytes 10485760 | tf_op jit(solution)/shard_map/dot_general | solution.py:46
  494.3 35.8 %attend_back.1 = (bf16[256,2048]{1,0:T(8,128)(2,1)}, f32[128,2048]{1,0:T(8,128)}, bf16[128,512]{1,0:T(8,128)(2,1)}) custom-call(s32[3]{0:T(128)} %copy-done.19, bf16[384,2048]{1,0:T(8,128)(2,1)} %copy-done.1, bf16[128,512]{1,0:T(8,128)(2,1)} %copy-done.17, bf16[256,2048]{1,0:T(8,128)(2,1)} %convolution_convert_fusion.upstream, f32[8,2048]{1,0:T(8,128)} %copy-done.18, ...), custom_call_target="tpu_custom_call" | custom-call | tf_op jit(solution)/shard_map/attend_back/pallas_call | solution.py:643
  530.9 4.8 collective-permute-start.50
  535.7 6.7 %outer.4 = bf16[2048,256]{1,0:T(8,128)(2,1)} custom-call(bf16[2048,2048]{1,0:T(8,128)(2,1)} %place.7.left, bf16[256,2048]{1,0:T(8,128)(2,1)} %copy-done.2), custom_call_target="tpu_custom_call" | custom-call | tf_op jit(solution)/shard_map/outer/pallas_call | solution.py:743
  542.5 4.1 fold.6
  550.4 6.4 product.14
  559.0 9.1 %outer.5 = (bf16[2048,384]{1,0:T(8,128)(2,1)}, f32[2048,128]{1,0:T(8,128)}) custom-call(bf16[2048,2048]{1,0:T(8,128)(2,1)} %place.4.left, bf16[384,2048]{1,0:T(8,128)(2,1)} %pad_maximum_fusion.4.refs_0_.right, bf16[2048,640]{1,0:T(8,128)(2,1)} %all-gather.4.cloned.1.call-done.refs_1_.weights), custom_call_target="tpu_custom_call" | custom-call | tf_op jit(solution)/shard_map/outer/pallas_call | solution.py:743
  568.1 3.6 collective-permute-done.52
  572.9 2.1 constant_dynamic-slice_fusion.2
  577.6 8.4 %product.15 = (f32[2,256,1024]{2,1,0:T(8,128)}, f32[2,256,1024]{2,1,0:T(8,128)}, bf16[2,256,1024]{2,1,0:T(8,128)(2,1)}, bf16[2,256,1024]{2,1,0:T(8,128)(2,1)}) custom-call(bf16[384,2048]{1,0:T(8,128)(2,1)} %pad_maximum_fusion.4.refs_0_.right, bf16[2048,640]{1,0:T(8,128)(2,1)} %all-gather.4.cloned.1.call-done.refs_1_.weights, ...), custom_call_target="tpu_custom_call" | custom-call | tf_op jit(solution)/shard_map/product/pallas_call | solution.py:219
  586.1 2.6 collective-permute-done.54
  591.5 3.1 collective-permute-done.57
  594.7 2.9 fusion.10
  599.9 2.9 fusion.8
  608.1 5.2 collective-permute-done.55.left_x
  614.2 4.2 fold.7
  622.3 7.0 %reduce-scatter.14.cloned.1.call-done = bf16[512,384]{1,0:T(8,128)(2,1)} async-done(((bf16[2048,384]{1,0:T(8,128)(2,1)}), bf16[512,384]{1,0:T(8,128)(2,1)}) %reduce-scatter.14.cloned.1.call-update) | async-done | bytes 393232 | tf_op jit(solution)/shard_map/reduce_scatter | solution.py:857
  637.3 5.0 input_back.1
  (347 shorter events, 123.0 us)
Async XLA Ops:
  7.2 75.2 %all-gather.4.cloned.1.call-start = ((), (), s32[]{:S(2)}) async-start(), calls=%async_computation.5 | async-start | bytes 3276800 | tf_op jit(solution)/shard_map/all_gather | solution.py:791
  9.8 10.7 %collective-permute-start = (bf16[256,640]{1,0:T(8,128)(2,1)S(1)}, bf16[256,640]{1,0:T(8,128)(2,1)S(1)}, u32[]{:S(2)}, u32[]{:S(2)}) collective-permute-start(bf16[256,640]{1,0:T(8,128)(2,1)S(1)} %pad_maximum_fusion.19), channel_id=1, source_target_pairs={{0,4},{4,0},{1,5},{5,1},{2,6},{6,2},{3,7},{7,3},{8,12},{12,8},{9,1... | collective-permute-start | bytes 983048 | tf_op jit(solution)/shard_map/ppermute | solution.py:37
  21.7 214.6 %all-gather.6.cloned.1.call-start = ((), (), s32[]{:S(2)}) async-start(), calls=%async_computation.6 | async-start | bytes 10485760 | tf_op jit(solution)/shard_map/all_gather | solution.py:806
  24.1 14.9 %collective-permute-start.4 = (bf16[256,1024]{1,0:T(8,128)(2,1)S(1)}, bf16[256,1024]{1,0:T(8,128)(2,1)S(1)}, u32[]{:S(2)}, u32[]{:S(2)}) collective-permute-start(bf16[256,1024]{1,0:T(8,128)(2,1)S(1)} %get-tuple-element.489), channel_id=1, source_target_pairs={{0,4},{4,0},{1,5},{5,1},{2,6},{6,2},{3,7},{7,3},{8,12},{12,8},{9,1... | collective-permute-start | bytes 1572872 | tf_op jit(solution)/shard_map/ppermute | solution.py:37
  25.9 13.1 %collective-permute-start.3 = (bf16[256,1024]{1,0:T(8,128)(2,1)S(1)}, bf16[256,1024]{1,0:T(8,128)(2,1)S(1)}, u32[]{:S(2)}, u32[]{:S(2)}) collective-permute-start(bf16[256,1024]{1,0:T(8,128)(2,1)S(1)} %get-tuple-element.490), channel_id=1, source_target_pairs={{0,2},{2,0},{1,3},{3,1},{4,6},{6,4},{5,7},{7,5},{8,10},{10,8},{9,1... | collective-permute-start | bytes 1572872 | tf_op jit(solution)/shard_map/ppermute | solution.py:37
  27.6 33.9 %collective-permute-start.1 = (bf16[256,2048]{1,0:T(8,128)(2,1)S(1)}, bf16[256,2048]{1,0:T(8,128)(2,1)S(1)}, u32[]{:S(2)}, u32[]{:S(2)}) collective-permute-start(bf16[256,2048]{1,0:T(8,128)(2,1)S(1)} %pad_maximum_fusion.14), channel_id=1, source_target_pairs={{0,4},{4,0},{1,5},{5,1},{2,6},{6,2},{3,7},{7,3},{8,12},{12,8},{9,1... | collective-permute-start | bytes 3145736 | tf_op jit(solution)/shard_map/ppermute | solution.py:37
  28.2 35.7 %collective-permute-start.2 = (bf16[256,2048]{1,0:T(8,128)(2,1)S(1)}, bf16[256,2048]{1,0:T(8,128)(2,1)}, u32[]{:S(2)}, u32[]{:S(2)}) collective-permute-start(bf16[256,2048]{1,0:T(8,128)(2,1)S(1)} %fusion.3.refs_0_), channel_id=1, source_target_pairs={{0,1},{1,0},{2,3},{3,2},{4,5},{5,4},{6,7},{7,6},{8,9},{9,8},{10,11... | collective-permute-start | bytes 3145736 | tf_op jit(solution)/shard_map/ppermute | solution.py:37
  41.0 22.8 %collective-permute-start.7 = (bf16[512,1024]{1,0:T(8,128)(2,1)}, bf16[512,1024]{1,0:T(8,128)(2,1)}, u32[]{:S(2)}, u32[]{:S(2)}) collective-permute-start(bf16[512,1024]{1,0:T(8,128)(2,1)} %get-tuple-element.504), channel_id=1, source_target_pairs={{0,2},{2,0},{1,3},{3,1},{4,6},{6,4},{5,7},{7,5},{8,10},{10,8},{9,1... | collective-permute-start | bytes 3145736 | tf_op jit(solution)/shard_map/ppermute | solution.py:37
  42.8 21.1 %collective-permute-start.5 = (bf16[512,1024]{1,0:T(8,128)(2,1)}, bf16[512,1024]{1,0:T(8,128)(2,1)}, u32[]{:S(2)}, u32[]{:S(2)}) collective-permute-start(bf16[512,1024]{1,0:T(8,128)(2,1)} %get-tuple-element.505), channel_id=1, source_target_pairs={{0,1},{1,0},{2,3},{3,2},{4,5},{5,4},{6,7},{7,6},{8,9},{9,8},{10,11... | collective-permute-start | bytes 3145736 | tf_op jit(solution)/shard_map/ppermute | solution.py:37
  42.8 39.6 %collective-permute-start.6 = (bf16[512,1024]{1,0:T(8,128)(2,1)}, bf16[512,1024]{1,0:T(8,128)(2,1)}, u32[]{:S(2)}, u32[]{:S(2)}) collective-permute-start(bf16[512,1024]{1,0:T(8,128)(2,1)} %get-tuple-element.506), channel_id=1, source_target_pairs={{0,4},{4,0},{1,5},{5,1},{2,6},{6,2},{3,7},{7,3},{8,12},{12,8},{9,1... | collective-permute-start | bytes 3145736 | tf_op jit(solution)/shard_map/ppermute | solution.py:37
  82.4 234.5 %all-gather.8.cloned.1.call-start = ((), (), s32[]{:S(2)}) async-start(), calls=%async_computation.7 | async-start | bytes 5242880 | tf_op jit(solution)/shard_map/all_gather | solution.py:838
  85.5 9.1 %collective-permute-start.8 = (bf16[1024,1024]{1,0:T(8,128)(2,1)}, bf16[1024,1024]{1,0:T(8,128)(2,1)}, u32[]{:S(2)}, u32[]{:S(2)}) collective-permute-start(bf16[1024,1024]{1,0:T(8,128)(2,1)} %pad_maximum_fusion), channel_id=1, source_target_pairs={{0,1},{1,0},{2,3},{3,2},{4,5},{5,4},{6,7},{7,6},{8,9},{9,8},{10,11... | collective-permute-start | bytes 6291464 | tf_op jit(solution)/shard_map/ppermute | solution.py:37
  87.7 24.1 %collective-permute-start.10 = (bf16[256,2048]{1,0:T(8,128)(2,1)S(1)}, bf16[256,2048]{1,0:T(8,128)(2,1)}, u32[]{:S(2)}, u32[]{:S(2)}) collective-permute-start(bf16[256,2048]{1,0:T(8,128)(2,1)S(1)} %multiply_convert_fusion.refs_0_), channel_id=1, source_target_pairs={{0,1},{1,0},{2,3},{3,2},{4,5},{5,4},{6,7},{7,6},{8,9},{9,8},{10,11... | collective-permute-start | bytes 3145736 | tf_op jit(solution)/shard_map/ppermute | solution.py:37
  89.3 22.5 %collective-permute-start.12 = (bf16[256,1024]{1,0:T(8,128)(2,1)}, bf16[256,1024]{1,0:T(8,128)(2,1)S(1)}, u32[]{:S(2)}, u32[]{:S(2)}) collective-permute-start(bf16[256,1024]{1,0:T(8,128)(2,1)} %get-tuple-element.487), channel_id=1, source_target_pairs={{0,4},{4,0},{1,5},{5,1},{2,6},{6,2},{3,7},{7,3},{8,12},{12,8},{9,1... | collective-permute-start | bytes 1572872 | tf_op jit(solution)/shard_map/ppermute | solution.py:37
  90.7 21.1 %collective-permute-start.11 = (bf16[256,1024]{1,0:T(8,128)(2,1)}, bf16[256,1024]{1,0:T(8,128)(2,1)S(1)}, u32[]{:S(2)}, u32[]{:S(2)}) collective-permute-start(bf16[256,1024]{1,0:T(8,128)(2,1)} %get-tuple-element.488), channel_id=1, source_target_pairs={{0,2},{2,0},{1,3},{3,1},{4,6},{6,4},{5,7},{7,5},{8,10},{10,8},{9,1... | collective-permute-start | bytes 1572872 | tf_op jit(solution)/shard_map/ppermute | solution.py:37
  109.7 11.1 %collective-permute-start.9 = (bf16[128,512]{1,0:T(8,128)(2,1)S(1)}, bf16[128,512]{1,0:T(8,128)(2,1)S(1)}, u32[]{:S(2)}, u32[]{:S(2)}) collective-permute-start(bf16[128,512]{1,0:T(8,128)(2,1)S(1)} %slice.100), channel_id=1, source_target_pairs={{0,8},{8,16},{16,24},{24,0},{1,9},{9,17},{17,25},{25,1},{2,10},{10... | collective-permute-start | bytes 393224 | tf_op jit(solution)/shard_map/ppermute | solution.py:42
  121.3 24.0 %collective-permute-start.15 = (bf16[512,1024]{1,0:T(8,128)(2,1)S(1)}, bf16[512,1024]{1,0:T(8,128)(2,1)S(1)}, u32[]{:S(2)}, u32[]{:S(2)}) collective-permute-start(bf16[512,1024]{1,0:T(8,128)(2,1)S(1)} %get-tuple-element.501), channel_id=1, source_target_pairs={{0,2},{2,0},{1,3},{3,1},{4,6},{6,4},{5,7},{7,5},{8,10},{10,8},{9,1... | collective-permute-start | bytes 3145736 | tf_op jit(solution)/shard_map/ppermute | solution.py:37
  122.0 23.4 %collective-permute-start.13 = (bf16[512,1024]{1,0:T(8,128)(2,1)S(1)}, bf16[512,1024]{1,0:T(8,128)(2,1)S(1)}, u32[]{:S(2)}, u32[]{:S(2)}) collective-permute-start(bf16[512,1024]{1,0:T(8,128)(2,1)S(1)} %get-tuple-element.502), channel_id=1, source_target_pairs={{0,1},{1,0},{2,3},{3,2},{4,5},{5,4},{6,7},{7,6},{8,9},{9,8},{10,11... | collective-permute-start | bytes 3145736 | tf_op jit(solution)/shard_map/ppermute | solution.py:37
  122.0 26.0 %collective-permute-start.14 = (bf16[512,1024]{1,0:T(8,128)(2,1)S(1)}, bf16[512,1024]{1,0:T(8,128)(2,1)S(1)}, u32[]{:S(2)}, u32[]{:S(2)}) collective-permute-start(bf16[512,1024]{1,0:T(8,128)(2,1)S(1)} %get-tuple-element.503), channel_id=1, source_target_pairs={{0,4},{4,0},{1,5},{5,1},{2,6},{6,2},{3,7},{7,3},{8,12},{12,8},{9,1... | collective-permute-start | bytes 3145736 | tf_op jit(solution)/shard_map/ppermute | solution.py:37
  122.9 36.0 %collective-permute-start.16 = (bf16[1024,256]{1,0:T(8,128)(2,1)S(1)}, bf16[1024,256]{1,0:T(8,128)(2,1)}, u32[]{:S(2)}, u32[]{:S(2)}) collective-permute-start(bf16[1024,256]{1,0:T(8,128)(2,1)S(1)} %get-tuple-element.242), channel_id=1, source_target_pairs={{0,4},{4,0},{1,5},{5,1},{2,6},{6,2},{3,7},{7,3},{8,12},{12,8},{9,1... | collective-permute-start | bytes 1572872 | tf_op jit(solution)/shard_map/ppermute | solution.py:37
  160.4 28.3 %collective-permute-start.21 = (bf16[1024,1024]{1,0:T(8,128)(2,1)}, bf16[1024,1024]{1,0:T(8,128)(2,1)}, u32[]{:S(2)}, u32[]{:S(2)}) collective-permute-start(bf16[1024,1024]{1,0:T(8,128)(2,1)} %pad_maximum_fusion.1), channel_id=1, source_target_pairs={{0,1},{1,0},{2,3},{3,2},{4,5},{5,4},{6,7},{7,6},{8,9},{9,8},{10,11... | collective-permute-start | bytes 6291464 | tf_op jit(solution)/shard_map/ppermute | solution.py:37
  175.6 25.5 %collective-permute-start.19 = (bf16[2,256,1024]{2,1,0:T(8,128)(2,1)}, bf16[2,256,1024]{2,1,0:T(8,128)(2,1)}, u32[]{:S(2)}, u32[]{:S(2)}) collective-permute-start(bf16[2,256,1024]{2,1,0:T(8,128)(2,1)} %get-tuple-element.246), channel_id=1, source_target_pairs={{0,2},{2,0},{1,3},{3,1},{4,6},{6,4},{5,7},{7,5},{8,10},{10,8},{9,1... | collective-permute-start | bytes 3145736 | tf_op jit(solution)/shard_map/ppermute | solution.py:37
  177.1 25.3 %collective-permute-start.20 = (bf16[2,256,1024]{2,1,0:T(8,128)(2,1)}, bf16[2,256,1024]{2,1,0:T(8,128)(2,1)}, u32[]{:S(2)}, u32[]{:S(2)}) collective-permute-start(bf16[2,256,1024]{2,1,0:T(8,128)(2,1)} %get-tuple-element.247), channel_id=1, source_target_pairs={{0,4},{4,0},{1,5},{5,1},{2,6},{6,2},{3,7},{7,3},{8,12},{12,8},{9,1... | collective-permute-start | bytes 3145736 | tf_op jit(solution)/shard_map/ppermute | solution.py:37
  177.6 8.5 %collective-permute-start.22 = (f32[8,128]{1,0:T(8,128)S(1)}, f32[8,128]{1,0:T(8,128)S(1)}, u32[]{:S(2)}, u32[]{:S(2)}) collective-permute-start(f32[8,128]{1,0:T(8,128)S(1)} %maximum_select_fusion.10), channel_id=1, source_target_pairs={{0,8},{8,16},{16,24},{24,0},{1,9},{9,17},{17,25},{25,1},{2,10},{10... | collective-permute-start | bytes 12296 | tf_op jit(solution)/shard_map/ppermute | solution.py:42
  186.2 9.7 %collective-permute-start.23 = (f32[8,128]{1,0:T(8,128)S(1)}, f32[8,128]{1,0:T(8,128)S(1)}, u32[]{:S(2)}, u32[]{:S(2)}) collective-permute-start(f32[8,128]{1,0:T(8,128)S(1)} %max.10), channel_id=1, source_target_pairs={{0,16},{8,24},{16,0},{24,8},{1,17},{9,25},{17,1},{25,9},{2,18},{10... | collective-permute-start | bytes 12296 | tf_op jit(solution)/shard_map/ppermute | solution.py:42
  202.4 278.7 %reduce-scatter.6.cloned.1.call-start = ((), (), s32[]{:S(2)}) async-start(), calls=%async_computation.8 | async-start | bytes 5242880 | tf_op jit(solution)/shard_map/reduce_scatter | solution.py:857
  205.9 12.9 %collective-permute-start.24 = (bf16[256,1024]{1,0:T(8,128)(2,1)S(1)}, bf16[256,1024]{1,0:T(8,128)(2,1)S(1)}, u32[]{:S(2)}, u32[]{:S(2)}) collective-permute-start(bf16[256,1024]{1,0:T(8,128)(2,1)S(1)} %get-tuple-element.271), channel_id=1, source_target_pairs={{0,4},{4,0},{1,5},{5,1},{2,6},{6,2},{3,7},{7,3},{8,12},{12,8},{9,1... | collective-permute-start | bytes 1572872 | tf_op jit(solution)/shard_map/ppermute | solution.py:37
  206.5 12.5 %collective-permute-start.25 = (bf16[256,1024]{1,0:T(8,128)(2,1)S(1)}, bf16[256,1024]{1,0:T(8,128)(2,1)S(1)}, u32[]{:S(2)}, u32[]{:S(2)}) collective-permute-start(bf16[256,1024]{1,0:T(8,128)(2,1)S(1)} %get-tuple-element.272), channel_id=1, source_target_pairs={{0,2},{2,0},{1,3},{3,1},{4,6},{6,4},{5,7},{7,5},{8,10},{10,8},{9,1... | collective-permute-start | bytes 1572872 | tf_op jit(solution)/shard_map/ppermute | solution.py:37
  221.1 14.9 %collective-permute-start.26 = (bf16[256,2048]{1,0:T(8,128)(2,1)S(1)}, bf16[256,2048]{1,0:T(8,128)(2,1)}, u32[]{:S(2)}, u32[]{:S(2)}) collective-permute-start(bf16[256,2048]{1,0:T(8,128)(2,1)S(1)} %get-tuple-element.276.refs_0_), channel_id=1, source_target_pairs={{0,1},{1,0},{2,3},{3,2},{4,5},{5,4},{6,7},{7,6},{8,9},{9,8},{10,11... | collective-permute-start | bytes 3145736 | tf_op jit(solution)/shard_map/ppermute | solution.py:37
  221.2 14.3 %collective-permute-start.27 = (bf16[256,1024]{1,0:T(8,128)(2,1)S(1)}, bf16[256,1024]{1,0:T(8,128)(2,1)S(1)}, u32[]{:S(2)}, u32[]{:S(2)}) collective-permute-start(bf16[256,1024]{1,0:T(8,128)(2,1)S(1)} %get-tuple-element.274), channel_id=1, source_target_pairs={{0,2},{2,0},{1,3},{3,1},{4,6},{6,4},{5,7},{7,5},{8,10},{10,8},{9,1... | collective-permute-start | bytes 1572872 | tf_op jit(solution)/shard_map/ppermute | solution.py:37
  222.0 14.1 %collective-permute-start.28 = (bf16[256,1024]{1,0:T(8,128)(2,1)S(1)}, bf16[256,1024]{1,0:T(8,128)(2,1)S(1)}, u32[]{:S(2)}, u32[]{:S(2)}) collective-permute-start(bf16[256,1024]{1,0:T(8,128)(2,1)S(1)} %get-tuple-element.275), channel_id=1, source_target_pairs={{0,4},{4,0},{1,5},{5,1},{2,6},{6,2},{3,7},{7,3},{8,12},{12,8},{9,1... | collective-permute-start | bytes 1572872 | tf_op jit(solution)/shard_map/ppermute | solution.py:37
  238.0 25.2 %collective-permute-start.31 = (bf16[512,1024]{1,0:T(8,128)(2,1)S(1)}, bf16[512,1024]{1,0:T(8,128)(2,1)S(1)}, u32[]{:S(2)}, u32[]{:S(2)}) collective-permute-start(bf16[512,1024]{1,0:T(8,128)(2,1)S(1)} %get-tuple-element.498), channel_id=1, source_target_pairs={{0,2},{2,0},{1,3},{3,1},{4,6},{6,4},{5,7},{7,5},{8,10},{10,8},{9,1... | collective-permute-start | bytes 3145736 | tf_op jit(solution)/shard_map/ppermute | solution.py:37
  239.5 23.7 %collective-permute-start.29 = (bf16[512,1024]{1,0:T(8,128)(2,1)S(1)}, bf16[512,1024]{1,0:T(8,128)(2,1)S(1)}, u32[]{:S(2)}, u32[]{:S(2)}) collective-permute-start(bf16[512,1024]{1,0:T(8,128)(2,1)S(1)} %get-tuple-element.499), channel_id=1, source_target_pairs={{0,1},{1,0},{2,3},{3,2},{4,5},{5,4},{6,7},{7,6},{8,9},{9,8},{10,11... | collective-permute-start | bytes 3145736 | tf_op jit(solution)/shard_map/ppermute | solution.py:37
  239.5 25.6 %collective-permute-start.30 = (bf16[512,1024]{1,0:T(8,128)(2,1)S(1)}, bf16[512,1024]{1,0:T(8,128)(2,1)S(1)}, u32[]{:S(2)}, u32[]{:S(2)}) collective-permute-start(bf16[512,1024]{1,0:T(8,128)(2,1)S(1)} %get-tuple-element.500), channel_id=1, source_target_pairs={{0,4},{4,0},{1,5},{5,1},{2,6},{6,2},{3,7},{7,3},{8,12},{12,8},{9,1... | collective-permute-start | bytes 3145736 | tf_op jit(solution)/shard_map/ppermute | solution.py:37
  315.4 165.8 %reduce-scatter.8.cloned.1.call-start = ((), (), s32[]{:S(2)}) async-start(), calls=%async_computation.9 | async-start | bytes 5242880 | tf_op jit(solution)/shard_map/reduce_scatter | solution.py:857
  342.6 11.9 %collective-permute-start.33 = (bf16[1024,2048]{1,0:T(8,128)(2,1)}, bf16[1024,2048]{1,0:T(8,128)(2,1)S(1)}, u32[]{:S(2)}, u32[]{:S(2)}) collective-permute-start(bf16[1024,2048]{1,0:T(8,128)(2,1)} %product.10), channel_id=1, source_target_pairs={{0,1},{1,0},{2,3},{3,2},{4,5},{5,4},{6,7},{7,6},{8,9},{9,8},{10,11... | collective-permute-start | bytes 12582920 | tf_op jit(solution)/shard_map/ppermute | solution.py:37
  372.4 29.9 %collective-permute-start.34 = (bf16[2,256,1024]{2,1,0:T(8,128)(2,1)}, bf16[2,256,1024]{2,1,0:T(8,128)(2,1)S(1)}, u32[]{:S(2)}, u32[]{:S(2)}) collective-permute-start(bf16[2,256,1024]{2,1,0:T(8,128)(2,1)} %get-tuple-element.305), channel_id=1, source_target_pairs={{0,2},{2,0},{1,3},{3,1},{4,6},{6,4},{5,7},{7,5},{8,10},{10,8},{9,1... | collective-permute-start | bytes 3145736 | tf_op jit(solution)/shard_map/ppermute | solution.py:37
  373.9 28.3 %collective-permute-start.35 = (bf16[2,256,1024]{2,1,0:T(8,128)(2,1)}, bf16[2,256,1024]{2,1,0:T(8,128)(2,1)}, u32[]{:S(2)}, u32[]{:S(2)}) collective-permute-start(bf16[2,256,1024]{2,1,0:T(8,128)(2,1)} %get-tuple-element.306), channel_id=1, source_target_pairs={{0,4},{4,0},{1,5},{5,1},{2,6},{6,2},{3,7},{7,3},{8,12},{12,8},{9,1... | collective-permute-start | bytes 3145736 | tf_op jit(solution)/shard_map/ppermute | solution.py:37
  402.3 165.8 %reduce-scatter.10.cloned.1.call-start = ((), (), s32[]{:S(2)}) async-start(), calls=%async_computation.10 | async-start | bytes 5242880 | tf_op jit(solution)/shard_map/reduce_scatter | solution.py:857
  407.1 13.8 %collective-permute-start.36 = (bf16[256,1024]{1,0:T(8,128)(2,1)S(1)}, bf16[256,1024]{1,0:T(8,128)(2,1)S(1)}, u32[]{:S(2)}, u32[]{:S(2)}) collective-permute-start(bf16[256,1024]{1,0:T(8,128)(2,1)S(1)} %get-tuple-element.312), channel_id=1, source_target_pairs={{0,4},{4,0},{1,5},{5,1},{2,6},{6,2},{3,7},{7,3},{8,12},{12,8},{9,1... | collective-permute-start | bytes 1572872 | tf_op jit(solution)/shard_map/ppermute | solution.py:37
  407.7 13.5 %collective-permute-start.37 = (bf16[256,1024]{1,0:T(8,128)(2,1)S(1)}, bf16[256,1024]{1,0:T(8,128)(2,1)S(1)}, u32[]{:S(2)}, u32[]{:S(2)}) collective-permute-start(bf16[256,1024]{1,0:T(8,128)(2,1)S(1)} %get-tuple-element.313), channel_id=1, source_target_pairs={{0,2},{2,0},{1,3},{3,1},{4,6},{6,4},{5,7},{7,5},{8,10},{10,8},{9,1... | collective-permute-start | bytes 1572872 | tf_op jit(solution)/shard_map/ppermute | solution.py:37
  424.2 12.8 %collective-permute-start.39 = (bf16[256,1024]{1,0:T(8,128)(2,1)S(1)}, bf16[256,1024]{1,0:T(8,128)(2,1)S(1)}, u32[]{:S(2)}, u32[]{:S(2)}) collective-permute-start(bf16[256,1024]{1,0:T(8,128)(2,1)S(1)} %get-tuple-element.318), channel_id=1, source_target_pairs={{0,2},{2,0},{1,3},{3,1},{4,6},{6,4},{5,7},{7,5},{8,10},{10,8},{9,1... | collective-permute-start | bytes 1572872 | tf_op jit(solution)/shard_map/ppermute | solution.py:37
  424.6 12.7 %collective-permute-start.40 = (bf16[256,1024]{1,0:T(8,128)(2,1)S(1)}, bf16[256,1024]{1,0:T(8,128)(2,1)S(1)}, u32[]{:S(2)}, u32[]{:S(2)}) collective-permute-start(bf16[256,1024]{1,0:T(8,128)(2,1)S(1)} %get-tuple-element.319), channel_id=1, source_target_pairs={{0,4},{4,0},{1,5},{5,1},{2,6},{6,2},{3,7},{7,3},{8,12},{12,8},{9,1... | collective-permute-start | bytes 1572872 | tf_op jit(solution)/shard_map/ppermute | solution.py:37
  438.6 169.5 %reduce-scatter.12.cloned.1.call-start = ((), (), s32[]{:S(2)}) async-start(), calls=%async_computation.11 | async-start | bytes 1310720 | tf_op jit(solution)/shard_map/reduce_scatter | solution.py:857
  441.9 25.8 %collective-permute-start.43 = (bf16[512,1024]{1,0:T(8,128)(2,1)}, bf16[512,1024]{1,0:T(8,128)(2,1)S(1)}, u32[]{:S(2)}, u32[]{:S(2)}) collective-permute-start(bf16[512,1024]{1,0:T(8,128)(2,1)} %get-tuple-element.495), channel_id=1, source_target_pairs={{0,2},{2,0},{1,3},{3,1},{4,6},{6,4},{5,7},{7,5},{8,10},{10,8},{9,1... | collective-permute-start | bytes 3145736 | tf_op jit(solution)/shard_map/ppermute | solution.py:37
  442.9 25.5 %collective-permute-start.42 = (bf16[512,1024]{1,0:T(8,128)(2,1)}, bf16[512,1024]{1,0:T(8,128)(2,1)S(1)}, u32[]{:S(2)}, u32[]{:S(2)}) collective-permute-start(bf16[512,1024]{1,0:T(8,128)(2,1)} %get-tuple-element.497), channel_id=1, source_target_pairs={{0,4},{4,0},{1,5},{5,1},{2,6},{6,2},{3,7},{7,3},{8,12},{12,8},{9,1... | collective-permute-start | bytes 3145736 | tf_op jit(solution)/shard_map/ppermute | solution.py:37
  444.3 24.1 %collective-permute-start.38 = (bf16[256,2048]{1,0:T(8,128)(2,1)S(1)}, bf16[256,2048]{1,0:T(8,128)(2,1)S(1)}, u32[]{:S(2)}, u32[]{:S(2)}) collective-permute-start(bf16[256,2048]{1,0:T(8,128)(2,1)S(1)} %get-tuple-element.317.refs_0_), channel_id=1, source_target_pairs={{0,1},{1,0},{2,3},{3,2},{4,5},{5,4},{6,7},{7,6},{8,9},{9,8},{10,11... | collective-permute-start | bytes 3145736 | tf_op jit(solution)/shard_map/ppermute | solution.py:37
  444.3 25.1 %collective-permute-start.41 = (bf16[512,1024]{1,0:T(8,128)(2,1)S(1)}, bf16[512,1024]{1,0:T(8,128)(2,1)}, u32[]{:S(2)}, u32[]{:S(2)}) collective-permute-start(bf16[512,1024]{1,0:T(8,128)(2,1)S(1)} %get-tuple-element.496), channel_id=1, source_target_pairs={{0,1},{1,0},{2,3},{3,2},{4,5},{5,4},{6,7},{7,6},{8,9},{9,8},{10,11... | collective-permute-start | bytes 3145736 | tf_op jit(solution)/shard_map/ppermute | solution.py:37
  469.7 60.4 %collective-permute-start.48 = (bf16[2,256,1024]{2,1,0:T(8,128)(2,1)}, bf16[2,256,1024]{2,1,0:T(8,128)(2,1)}, u32[]{:S(2)}, u32[]{:S(2)}) collective-permute-start(bf16[2,256,1024]{2,1,0:T(8,128)(2,1)} %get-tuple-element.344), channel_id=1, source_target_pairs={{0,2},{2,0},{1,3},{3,1},{4,6},{6,4},{5,7},{7,5},{8,10},{10,8},{9,1... | collective-permute-start | bytes 3145736 | tf_op jit(solution)/shard_map/ppermute | solution.py:37
  470.9 59.2 %collective-permute-start.49 = (bf16[2,256,1024]{2,1,0:T(8,128)(2,1)}, bf16[2,256,1024]{2,1,0:T(8,128)(2,1)}, u32[]{:S(2)}, u32[]{:S(2)}) collective-permute-start(bf16[2,256,1024]{2,1,0:T(8,128)(2,1)} %get-tuple-element.345), channel_id=1, source_target_pairs={{0,4},{4,0},{1,5},{5,1},{2,6},{6,2},{3,7},{7,3},{8,12},{12,8},{9,1... | collective-permute-start | bytes 3145736 | tf_op jit(solution)/shard_map/ppermute | solution.py:37
  483.3 46.8 %collective-permute-start.46 = (bf16[1024,256]{1,0:T(8,128)(2,1)}, bf16[1024,256]{1,0:T(8,128)(2,1)S(1)}, u32[]{:S(2)}, u32[]{:S(2)}) collective-permute-start(bf16[1024,256]{1,0:T(8,128)(2,1)} %get-tuple-element.478), channel_id=1, source_target_pairs={{0,4},{4,0},{1,5},{5,1},{2,6},{6,2},{3,7},{7,3},{8,12},{12,8},{9,1... | collective-permute-start | bytes 1572872 | tf_op jit(solution)/shard_map/ppermute | solution.py:37
  485.8 44.4 %collective-permute-start.47 = (bf16[256,1024]{1,0:T(8,128)(2,1)}, bf16[256,1024]{1,0:T(8,128)(2,1)S(1)}, u32[]{:S(2)}, u32[]{:S(2)}) collective-permute-start(bf16[256,1024]{1,0:T(8,128)(2,1)} %get-tuple-element.476), channel_id=1, source_target_pairs={{0,4},{4,0},{1,5},{5,1},{2,6},{6,2},{3,7},{7,3},{8,12},{12,8},{9,1... | collective-permute-start | bytes 1572872 | tf_op jit(solution)/shard_map/ppermute | solution.py:37
  530.9 15.7 %collective-permute-start.50 = (bf16[128,512]{1,0:T(8,128)(2,1)}, bf16[128,512]{1,0:T(8,128)(2,1)S(1)}, u32[]{:S(2)}, u32[]{:S(2)}) collective-permute-start(bf16[128,512]{1,0:T(8,128)(2,1)} %get-tuple-element.346), channel_id=1, source_target_pairs={{0,24},{8,0},{16,8},{24,16},{1,25},{9,1},{17,9},{25,17},{2,26},{10... | collective-permute-start | bytes 393224 | tf_op jit(solution)/shard_map/ppermute | solution.py:42
  556.9 15.3 %collective-permute-start.51 = (bf16[1024,2048]{1,0:T(8,128)(2,1)}, bf16[1024,2048]{1,0:T(8,128)(2,1)}, u32[]{:S(2)}, u32[]{:S(2)}) collective-permute-start(bf16[1024,2048]{1,0:T(8,128)(2,1)} %product.14), channel_id=1, source_target_pairs={{0,1},{1,0},{2,3},{3,2},{4,5},{5,4},{6,7},{7,6},{8,9},{9,8},{10,11... | collective-permute-start | bytes 12582920 | tf_op jit(solution)/shard_map/ppermute | solution.py:37
  556.9 72.4 %reduce-scatter.14.cloned.1.call-start = ((), (), s32[]{:S(2)}) async-start(), calls=%async_computation.12 | async-start | bytes 1966080 | tf_op jit(solution)/shard_map/reduce_scatter | solution.py:857
  556.9 14.7 %collective-permute-start.52 = (bf16[256,1024]{1,0:T(8,128)(2,1)}, bf16[256,1024]{1,0:T(8,128)(2,1)}, u32[]{:S(2)}, u32[]{:S(2)}) collective-permute-start(bf16[256,1024]{1,0:T(8,128)(2,1)} %get-tuple-element.360), channel_id=1, source_target_pairs={{0,4},{4,0},{1,5},{5,1},{2,6},{6,2},{3,7},{7,3},{8,12},{12,8},{9,1... | collective-permute-start | bytes 1572872 | tf_op jit(solution)/shard_map/ppermute | solution.py:37
  557.9 14.3 %collective-permute-start.53 = (bf16[256,1024]{1,0:T(8,128)(2,1)}, bf16[256,1024]{1,0:T(8,128)(2,1)S(1)}, u32[]{:S(2)}, u32[]{:S(2)}) collective-permute-start(bf16[256,1024]{1,0:T(8,128)(2,1)} %get-tuple-element.361), channel_id=1, source_target_pairs={{0,2},{2,0},{1,3},{3,1},{4,6},{6,4},{5,7},{7,5},{8,10},{10,8},{9,1... | collective-permute-start | bytes 1572872 | tf_op jit(solution)/shard_map/ppermute | solution.py:37
  575.0 13.7 %collective-permute-start.54 = (bf16[256,1024]{1,0:T(8,128)(2,1)}, bf16[256,1024]{1,0:T(8,128)(2,1)}, u32[]{:S(2)}, u32[]{:S(2)}) collective-permute-start(bf16[256,1024]{1,0:T(8,128)(2,1)} %get-tuple-element.368), channel_id=1, source_target_pairs={{0,4},{4,0},{1,5},{5,1},{2,6},{6,2},{3,7},{7,3},{8,12},{12,8},{9,1... | collective-permute-start | bytes 1572872 | tf_op jit(solution)/shard_map/ppermute | solution.py:37
  589.2 24.0 %collective-permute-start.55 = (bf16[2,256,1024]{2,1,0:T(8,128)(2,1)}, bf16[2,256,1024]{2,1,0:T(8,128)(2,1)}, u32[]{:S(2)}, u32[]{:S(2)}) collective-permute-start(bf16[2,256,1024]{2,1,0:T(8,128)(2,1)} %get-tuple-element.369), channel_id=1, source_target_pairs={{0,2},{2,0},{1,3},{3,1},{4,6},{6,4},{5,7},{7,5},{8,10},{10,8},{9,1... | collective-permute-start | bytes 3145736 | tf_op jit(solution)/shard_map/ppermute | solution.py:37
  590.4 23.7 %collective-permute-start.56 = (bf16[2,256,1024]{2,1,0:T(8,128)(2,1)}, bf16[2,256,1024]{2,1,0:T(8,128)(2,1)}, u32[]{:S(2)}, u32[]{:S(2)}) collective-permute-start(bf16[2,256,1024]{2,1,0:T(8,128)(2,1)} %get-tuple-element.370), channel_id=1, source_target_pairs={{0,4},{4,0},{1,5},{5,1},{2,6},{6,2},{3,7},{7,3},{8,12},{12,8},{9,1... | collective-permute-start | bytes 3145736 | tf_op jit(solution)/shard_map/ppermute | solution.py:37
  618.4 11.8 %collective-permute-start.59 = (bf16[256,1024]{1,0:T(8,128)(2,1)}, bf16[256,1024]{1,0:T(8,128)(2,1)S(1)}, u32[]{:S(2)}, u32[]{:S(2)}) collective-permute-start(bf16[256,1024]{1,0:T(8,128)(2,1)} %get-tuple-element.401), channel_id=1, source_target_pairs={{0,4},{4,0},{1,5},{5,1},{2,6},{6,2},{3,7},{7,3},{8,12},{12,8},{9,1... | collective-permute-start | bytes 1572872 | tf_op jit(solution)/shard_map/ppermute | solution.py:37
  619.4 11.1 %collective-permute-start.60 = (bf16[256,1024]{1,0:T(8,128)(2,1)}, bf16[256,1024]{1,0:T(8,128)(2,1)S(1)}, u32[]{:S(2)}, u32[]{:S(2)}) collective-permute-start(bf16[256,1024]{1,0:T(8,128)(2,1)} %get-tuple-element.402), channel_id=1, source_target_pairs={{0,2},{2,0},{1,3},{3,1},{4,6},{6,4},{5,7},{7,5},{8,10},{10,8},{9,1... | collective-permute-start | bytes 1572872 | tf_op jit(solution)/shard_map/ppermute | solution.py:37
  631.8 11.1 %collective-permute-start.65 = (bf16[256,256]{1,0:T(8,128)(2,1)S(1)}, bf16[256,256]{1,0:T(8,128)(2,1)S(1)}, u32[]{:S(2)}, u32[]{:S(2)}) collective-permute-start(bf16[256,256]{1,0:T(8,128)(2,1)S(1)} %get-tuple-element.414), channel_id=1, source_target_pairs={{0,4},{4,0},{1,5},{5,1},{2,6},{6,2},{3,7},{7,3},{8,12},{12,8},{9,1... | collective-permute-start | bytes 393224 | tf_op jit(solution)/shard_map/ppermute | solution.py:37
  633.2 10.7 %collective-permute-start.64 = (bf16[256,384]{1,0:T(8,128)(2,1)S(1)}, bf16[256,384]{1,0:T(8,128)(2,1)S(1)}, u32[]{:S(2)}, u32[]{:S(2)}) collective-permute-start(bf16[256,384]{1,0:T(8,128)(2,1)S(1)} %constant_dynamic-slice_fusion.11), channel_id=1, source_target_pairs={{0,4},{4,0},{1,5},{5,1},{2,6},{6,2},{3,7},{7,3},{8,12},{12,8},{9,1... | collective-permute-start | bytes 589832 | tf_op jit(solution)/shard_map/ppermute | solution.py:37
  (76 other events, 436.1 us)
Sparse Core Ops, SparseCore 0:
  21.8 56.2 all-gather.3
  82.5 153.7 all-gather.5
  237.9 78.9 all-gather.7
  319.0 76.3 reduce-scatter.5
  402.4 77.9 reduce-scatter.7
  482.5 80.0 reduce-scatter.9
  565.0 27.6 reduce-scatter.11
  595.0 34.2 reduce-scatter.13

commit v7 on v6

--- a/solution.py
+++ b/solution.py
@@ -917,7 +917,6 @@
     left, right, *sent = fold(*second[:2], *got)
     (out_part,) = outer(mixed_rows, heads, 1)
     dkv, back_sent, out_part, *sent = tie(dkv, back_sent, out_part, *sent)
-    out_sum = reduced(out_part, 0)
     second = left, right, swap(sent[0], "y"), swap(sent[1], "x")
     (dkv_done,) = call(
         finish_kernel, info, (dkv, back_sent, cos, sin), [((2 * HD, rows), BF16)], [], "finish"
@@ -931,7 +930,7 @@
     )
     two_own = half_of(two_sum, y_rank, 0)
     came, two_sent = tie(came, half_of(two_sum, other_y, 0))
-    qkv_sum = reduced(qkv_part, 0)
+    heads_sum = reduced(jnp.concatenate((out_part, qkv_part), axis=1), 0)
     second = (*second[:2], *got)
     *norm_one, sums, two_other = spread_one(terms, came, sums, swap(two_sent, "y"))
     gains = jnp.stack((sums[:, 0] / gain_one, jnp.sum(gain_two_part, axis=0)))
@@ -945,8 +944,8 @@
     factor = level / jnp.maximum(level, head_peak)
     query_clipped = w_query.astype(F32) * jnp.repeat(jnp.sqrt(factor), HD)[None, :]
     result = (resid + RESIDUAL * own_mask * spread_three(second)).astype(BF16)
-    *got, gains, out_sum, down_grad, gate_w_grad, query_clipped, result = tie(
-        *norm_one[2:4], gains, out_sum, down_grad, gate_w_grad, query_clipped, result
+    *got, gains, down_grad, gate_w_grad, query_clipped, result = tie(
+        *norm_one[2:4], gains, down_grad, gate_w_grad, query_clipped, result
     )
     gains = gains.reshape(2, lax.axis_size("z"), 2, 2, 2, -1)
 
@@ -957,12 +956,13 @@
 
     norm_one = spread_two((*norm_one[:2], *got), gains, folding=fold)
     gains = norm_one[4]
-    out_own, out_sent = half_of(out_sum, y_rank, 0), half_of(out_sum, other_y, 0)
-    own, qkv_sent = half_of(qkv_sum, y_rank, 0), half_of(qkv_sum, other_y, 0)
+    own, heads_sent = half_of(heads_sum, y_rank, 0), half_of(heads_sum, other_y, 0)
     kept, sent = halved(gains, 4, "c")
     kept, sent = halved(kept + swap(sent, "c"), 3, "x")
-    *norm_one, qkv_sent, kept, sent, out_sent = tie(*norm_one[:4], qkv_sent, kept, sent, out_sent)
-    other, out_other = swap(qkv_sent, "y"), swap(out_sent, "y")
+    *norm_one, heads_sent, kept, sent = tie(*norm_one[:4], heads_sent, kept, sent)
+    other = swap(heads_sent, "y")
+    out_own, out_other = own[:, :out_cols], other[:, :out_cols]
+    own, other = own[:, out_cols:], other[:, out_cols:]
     grad_input = input_back(*norm_one, grad_resid, layer_in, scale_one, gain_one[None, :])
     kept, sent = halved(kept + swap(sent, "x"), 2, "y")
     gains = lax.dynamic_index_in_dim(kept + swap(sent, "y"), z_rank, 1, keepdims=False)

time: 661 us -> 661 us (level)
    unnamed x135 -> x125, local copies, waits for them, and re-layouts: 22.3 us -> 17.9 us
    ppermute x60 -> x59, waiting for transfers between devices: 168 us -> 172 us  [swap(): return lax.ppermute(x, axis, [(0, 1), (1, 0)])]
    ppermute x60 -> x59, starting transfers between devices: 52.1 us -> 49.4 us  [swap(): return lax.ppermute(x, axis, [(0, 1), (1, 0)])]
  transfers between devices with their start and end apart: 74 -> 72, of which waited for: 40 -> 42; matrix products, arithmetic and copies ran while one was open for 10% -> 10% of each run, Pallas kernels for 44% -> 44%
where the time goes in v7:
time: 661 us; the launch traced here: 654 us
  Pallas kernels  287 us (43%)
  waiting for transfers between devices  200 us (30%)
  starting transfers between devices  57.8 us (9%)
  other arithmetic  43.3 us (7%)
  local copies, waits for them, and re-layouts  35.9 us (5%)
  between operations  16.2 us (2%)
  matrix products  14 us (2%)
    ppermute x59, waiting for transfers between devices, swap(): return lax.ppermute(x, axis, [(0, 1), (1, 0)])  172 us
    pallas_call x8, Pallas kernels, product(): pl.pallas_call(functools.partial(product_kernel, kinds, came is not None)...  76 us
    pallas_call x4, Pallas kernels, call(): pl.pallas_call(kernel, out_shape=[jax.ShapeDtypeStruct(s, d) for s, d in...  57.4 us
    ppermute x59, starting transfers between devices, swap(): return lax.ppermute(x, axis, [(0, 1), (1, 0)])  49.4 us
    pallas_call x3, Pallas kernels, ffn_call(): pl.pallas_call(kernel, out_shape=[jax.ShapeDtypeStruct((count, width), ki...  48.3 us
    pallas_call x3, Pallas kernels, outer(): pl.pallas_call(kernel, out_shape=outs, grid=(wide // cols, high // rows),...  30.2 us
    pallas_call x4, Pallas kernels, place(): pl.pallas_call(functools.partial(place_kernel, spots, number), out_shape=...  28.6 us
    pallas_call x2, Pallas kernels, outer_halves(): pl.pallas_call(outer_halves_kernel, out_shape=jax.ShapeDtypeStruct((tall,...  26.8 us
  transfers between devices with their start and end apart: 72, of which 42 were waited for; matrix products, arithmetic and copies ran while one was open for 10% of the time, Pallas kernels for 44%

profile of v7, /device:TPU:0, one launch (start us, length us, event | category | flops | bytes accessed | tf_op | source)
XLA Modules:
  0.0 654.1 jit_solution(6772140130943164282)
XLA Ops:
  9.8 3.0 collective-permute-start
  12.9 7.6 %collective-permute-done = bf16[256,640]{1,0:T(8,128)(2,1)S(1)} collective-permute-done((bf16[256,640]{1,0:T(8,128)(2,1)S(1)}, bf16[256,640]{1,0:T(8,128)(2,1)S(1)}, u32[]{:S(2)}, u32[]{:S(2)}) %collective-permute-start) | collective-permute-done | bytes 327712 | tf_op jit(solution)/shard_map/ppermute | solution.py:37
  28.2 10.9 %collective-permute-done.4.refs_3_ = bf16[256,1024]{1,0:T(8,128)(2,1)S(1)} collective-permute-done((bf16[256,1024]{1,0:T(8,128)(2,1)S(1)}, bf16[256,1024]{1,0:T(8,128)(2,1)S(1)}, u32[]{:S(2)}, u32[]{:S(2)}) %collective-permute-start.4) | collective-permute-done | bytes 524320 | tf_op jit(solution)/shard_map/ppermute | solution.py:37
  44.3 17.2 %collective-permute-done.1 = bf16[256,2048]{1,0:T(8,128)(2,1)S(1)} collective-permute-done((bf16[256,2048]{1,0:T(8,128)(2,1)S(1)}, bf16[256,2048]{1,0:T(8,128)(2,1)S(1)}, u32[]{:S(2)}, u32[]{:S(2)}) %collective-permute-start.1) | collective-permute-done | bytes 1048608 | tf_op jit(solution)/shard_map/ppermute | solution.py:37
  61.5 2.3 maximum_select_fusion
  63.8 18.5 %collective-permute-done.6.refs_5_ = bf16[512,1024]{1,0:T(8,128)(2,1)} collective-permute-done((bf16[512,1024]{1,0:T(8,128)(2,1)}, bf16[512,1024]{1,0:T(8,128)(2,1)}, u32[]{:S(2)}, u32[]{:S(2)}) %collective-permute-start.6) | collective-permute-done | bytes 1048608 | tf_op jit(solution)/shard_map/ppermute | solution.py:37
  82.4 3.1 pad_maximum_fusion.1
  94.7 7.6 %place.4.left = bf16[2048,2048]{1,0:T(8,128)(2,1)} custom-call(bf16[256,2048]{1,0:T(8,128)(2,1)} %copy-done.22, bf16[256,2048]{1,0:T(8,128)(2,1)} %collective-permute-done.2.refs_1_, bf16[256,1024]{1,0:T(8,128)(2,1)} %copy-done.31, bf16[256,1024]{1,0:T(8,128)(2,1)} %copy-done.30, bf16[512,1024]{1,0:T(8,128)(2,1)} %collective-permute-done.5.refs_4_, ...), custom_call_target="tpu_custom_call" | custom-call | tf_op jit(solution)/shard_map/place/pallas_call | solution.py:130
  102.2 6.4 fusion.6.qkv
  111.7 9.0 %collective-permute-done.9.halo = bf16[128,512]{1,0:T(8,128)(2,1)S(1)} collective-permute-done((bf16[128,512]{1,0:T(8,128)(2,1)S(1)}, bf16[128,512]{1,0:T(8,128)(2,1)S(1)}, u32[]{:S(2)}, u32[]{:S(2)}) %collective-permute-start.9) | collective-permute-done | bytes 131104 | tf_op jit(solution)/shard_map/ppermute | solution.py:42
  124.0 20.0 %attend.1 = (bf16[256,2048]{1,0:T(8,128)(2,1)S(1)}, f32[8,2048]{1,0:T(8,128)S(1)}, f32[8,128]{1,0:T(8,128)S(1)}) custom-call(s32[3]{0:T(128)S(1)} %pad_add_fusion.info, bf16[384,2048]{1,0:T(8,128)(2,1)S(1)} %rope.1.qkv, bf16[128,512]{1,0:T(8,128)(2,1)S(1)} %collective-permute-done.9.halo), custom_call_target="tpu_custom_call" | custom-call | tf_op jit(solution)/shard_map/attend/pallas_call | solution.py:643
  145.2 2.6 collective-permute-done.14.refs_5_
  147.8 6.0 product.8
  153.8 4.9 collective-permute-done.16
  161.6 2.8 collective-permute-done.18
  166.1 2.0 copy-done.28
  168.1 7.4 %product.9 = (f32[2,256,1024]{2,1,0:T(8,128)}, f32[2,256,1024]{2,1,0:T(8,128)}, bf16[2,256,1024]{2,1,0:T(8,128)(2,1)}, bf16[2,256,1024]{2,1,0:T(8,128)(2,1)}) custom-call(bf16[256,2048]{1,0:T(8,128)(2,1)} %copy-done.2, bf16[2048,640]{1,0:T(8,128)(2,1)} %all-gather.4.cloned.1.call-done.refs_1_.weights, bf16[1024,2048]{1,0:T(8,128)(2,1)} %copy-done.28), custom_call_target="tpu_custom_call" | custom-call | tf_op jit(solution)/shard_map/product/pallas_call | solution.py:219
  177.5 8.6 %collective-permute-done.22 = f32[8,128]{1,0:T(8,128)S(1)} collective-permute-done((f32[8,128]{1,0:T(8,128)S(1)}, f32[8,128]{1,0:T(8,128)S(1)}, u32[]{:S(2)}, u32[]{:S(2)}) %collective-permute-start.22) | collective-permute-done | bytes 4128 | tf_op jit(solution)/shard_map/ppermute | solution.py:42
  186.3 2.4 maximum_select_fusion.1
  188.7 7.1 %place.5.right.rows = bf16[2048,2048]{1,0:T(8,128)(2,1)} custom-call(bf16[256,2048]{1,0:T(8,128)(2,1)} %copy-done.21, bf16[256,2048]{1,0:T(8,128)(2,1)} %collective-permute-done.10.refs_1_, bf16[256,1024]{1,0:T(8,128)(2,1)} %copy-done.33, bf16[256,1024]{1,0:T(8,128)(2,1)} %copy-done.32, bf16[512,1024]{1,0:T(8,128)(2,1)} %copy-done.41, ...), custom_call_target="tpu_custom_call" | custom-call | tf_op jit(solution)/shard_map/place/pallas_call | solution.py:130
  195.8 5.2 collective-permute-done.19.left_x
  209.1 10.1 %collective-permute-done.24.refs_2_ = bf16[256,1024]{1,0:T(8,128)(2,1)S(1)} collective-permute-done((bf16[256,1024]{1,0:T(8,128)(2,1)S(1)}, bf16[256,1024]{1,0:T(8,128)(2,1)S(1)}, u32[]{:S(2)}, u32[]{:S(2)}) %collective-permute-start.24) | collective-permute-done | bytes 524320 | tf_op jit(solution)/shard_map/ppermute | solution.py:37
  223.7 12.3 %collective-permute-done.27.refs_2_ = bf16[256,1024]{1,0:T(8,128)(2,1)S(1)} collective-permute-done((bf16[256,1024]{1,0:T(8,128)(2,1)S(1)}, bf16[256,1024]{1,0:T(8,128)(2,1)S(1)}, u32[]{:S(2)}, u32[]{:S(2)}) %collective-permute-start.27) | collective-permute-done | bytes 524320 | tf_op jit(solution)/shard_map/ppermute | solution.py:37
  241.1 22.1 %collective-permute-done.31.refs_6_ = bf16[512,1024]{1,0:T(8,128)(2,1)S(1)} collective-permute-done((bf16[512,1024]{1,0:T(8,128)(2,1)S(1)}, bf16[512,1024]{1,0:T(8,128)(2,1)S(1)}, u32[]{:S(2)}, u32[]{:S(2)}) %collective-permute-start.31) | collective-permute-done | bytes 1048608 | tf_op jit(solution)/shard_map/ppermute | solution.py:37
  266.2 4.3 collective-permute-done.32.refs_7_
  270.5 7.0 %place.6.rows.left = bf16[2048,2048]{1,0:T(8,128)(2,1)} custom-call(bf16[256,2048]{1,0:T(8,128)(2,1)} %copy-done.4, bf16[256,2048]{1,0:T(8,128)(2,1)} %collective-permute-done.26.refs_1_, bf16[256,1024]{1,0:T(8,128)(2,1)} %copy-done.36, bf16[256,1024]{1,0:T(8,128)(2,1)} %copy-done.37, bf16[512,1024]{1,0:T(8,128)(2,1)} %copy-done.43, ...), custom_call_target="tpu_custom_call" | custom-call | tf_op jit(solution)/shard_map/place/pallas_call | solution.py:130
  277.5 23.9 %hidden.1 = (f32[2048,1024]{1,0:T(8,128)}, f32[2048,1024]{1,0:T(8,128)}, bf16[2048,1024]{1,0:T(8,128)(2,1)}) custom-call(bf16[2048,2048]{1,0:T(8,128)(2,1)} %place.6.rows.left, bf16[2048,2048]{1,0:T(8,128)(2,1)} %all-gather.6.cloned.1.call-done.gate_w.up_w.refs_1_.refs_3_, bf16[2048,2048]{1,0:T(8,128)(2,1)} %all-gather.6.cloned.1.call-done.gate_w.up_w.refs_1_.refs_3_), custom_call_target="tpu_custom_call" | custom-call | tf_op jit(solution)/shard_map/hidden/pallas_call | solution.py:681
  301.4 14.1 %outer.3 = bf16[1024,2048]{1,0:T(8,128)(2,1)} custom-call(bf16[2048,1024]{1,0:T(8,128)(2,1)} %get-tuple-element.318.left.refs_0_, bf16[2048,2048]{1,0:T(8,128)(2,1)} %place.5.right.rows), custom_call_target="tpu_custom_call" | custom-call | tf_op jit(solution)/shard_map/outer/pallas_call | solution.py:743
  316.9 12.5 %hidden_back.2 = (bf16[1024,1024]{1,0:T(8,128)(2,1)}, bf16[1024,1024]{1,0:T(8,128)(2,1)}) custom-call(bf16[2048,2048]{1,0:T(8,128)(2,1)} %place.5.right.rows, bf16[1024,2048]{1,0:T(8,128)(2,1)} %all-gather.8.cloned.1.call-done.weights.refs_1_, f32[2048,1024]{1,0:T(8,128)} %get-tuple-element.288.gates, f32[2048,1024]{1,0:T(8,128)} %get-tuple-element.289.ups), custom_call_target="tpu_custom_call" | custom-call | tf_op jit(solution)/shard_map/hidden_back/pallas_call | solution.py:681
  329.4 13.5 %product.10 = bf16[1024,2048]{1,0:T(8,128)(2,1)} custom-call(bf16[1024,1024]{1,0:T(8,128)(2,1)} %get-tuple-element.290.refs_0_.high, bf16[2048,2048]{1,0:T(8,128)(2,1)} %all-gather.6.cloned.1.call-done.gate_w.up_w.refs_1_.refs_3_, bf16[1024,1024]{1,0:T(8,128)(2,1)} %get-tuple-element.291.refs_2_.high, ...), custom_call_target="tpu_custom_call" | custom-call | tf_op jit(solution)/shard_map/product/pallas_call | solution.py:219
  342.9 11.9 %hidden_back.3 = (bf16[1024,1024]{1,0:T(8,128)(2,1)}, bf16[1024,1024]{1,0:T(8,128)(2,1)}) custom-call(bf16[2048,2048]{1,0:T(8,128)(2,1)} %place.5.right.rows, bf16[1024,2048]{1,0:T(8,128)(2,1)} %all-gather.8.cloned.1.call-done.weights.refs_1_, f32[2048,1024]{1,0:T(8,128)} %get-tuple-element.288.gates, f32[2048,1024]{1,0:T(8,128)} %get-tuple-element.289.ups), custom_call_target="tpu_custom_call" | custom-call | tf_op jit(solution)/shard_map/hidden_back/pallas_call | solution.py:681
  354.8 2.0 copy-done.29
  356.9 15.7 %product.11 = (f32[2,256,1024]{2,1,0:T(8,128)}, f32[2,256,1024]{2,1,0:T(8,128)}, bf16[2,256,1024]{2,1,0:T(8,128)(2,1)}, bf16[2,256,1024]{2,1,0:T(8,128)(2,1)}) custom-call(bf16[1024,1024]{1,0:T(8,128)(2,1)} %get-tuple-element.296.refs_0_.low, bf16[2048,2048]{1,0:T(8,128)(2,1)} %all-gather.6.cloned.1.call-done.gate_w.up_w.refs_1_.refs_3_, ...), custom_call_target="tpu_custom_call" | custom-call | tf_op jit(solution)/shard_map/product/pallas_call | solution.py:219
  375.3 13.3 %outer_halves.3 = bf16[2048,1024]{1,0:T(8,128)(2,1)} custom-call(bf16[2048,2048]{1,0:T(8,128)(2,1)} %place.6.rows.left, bf16[1024,1024]{1,0:T(8,128)(2,1)} %get-tuple-element.297.refs_2_.low, bf16[1024,1024]{1,0:T(8,128)(2,1)} %get-tuple-element.291.refs_2_.high), custom_call_target="tpu_custom_call" | custom-call | tf_op jit(solution)/shard_map/outer_halves/pallas_call | solution.py:705
  388.6 13.4 %outer_halves.2 = bf16[2048,1024]{1,0:T(8,128)(2,1)} custom-call(bf16[2048,2048]{1,0:T(8,128)(2,1)} %place.6.rows.left, bf16[1024,1024]{1,0:T(8,128)(2,1)} %get-tuple-element.296.refs_0_.low, bf16[1024,1024]{1,0:T(8,128)(2,1)} %get-tuple-element.290.refs_0_.high), custom_call_target="tpu_custom_call" | custom-call | tf_op jit(solution)/shard_map/outer_halves/pallas_call | solution.py:705
  408.5 12.6 %collective-permute-done.36.refs_2_ = bf16[256,1024]{1,0:T(8,128)(2,1)S(1)} collective-permute-done((bf16[256,1024]{1,0:T(8,128)(2,1)S(1)}, bf16[256,1024]{1,0:T(8,128)(2,1)S(1)}, u32[]{:S(2)}, u32[]{:S(2)}) %collective-permute-start.36) | collective-permute-done | bytes 524320 | tf_op jit(solution)/shard_map/ppermute | solution.py:37
  426.3 8.4 %product.12 = bf16[1024,2048]{1,0:T(8,128)(2,1)} custom-call(bf16[2048,1024]{1,0:T(8,128)(2,1)} %get-tuple-element.318.left.refs_0_, bf16[1024,2048]{1,0:T(8,128)(2,1)} %all-gather.8.cloned.1.call-done.weights.refs_1_), custom_call_target="tpu_custom_call" | custom-call | tf_op jit(solution)/shard_map/product/pallas_call | solution.py:219
  434.7 2.4 collective-permute-done.39.refs_2_
  442.9 2.1 collective-permute-done.44.refs_2_
  445.0 10.2 %product.13 = (f32[2,256,1024]{2,1,0:T(8,128)}, f32[2,256,1024]{2,1,0:T(8,128)}, bf16[2,256,1024]{2,1,0:T(8,128)(2,1)}, bf16[2,256,1024]{2,1,0:T(8,128)(2,1)}) custom-call(bf16[2048,1024]{1,0:T(8,128)(2,1)} %get-tuple-element.318.left.refs_0_, bf16[1024,2048]{1,0:T(8,128)(2,1)} %all-gather.8.cloned.1.call-done.weights.refs_1_, ...), custom_call_target="tpu_custom_call" | custom-call | tf_op jit(solution)/shard_map/product/pallas_call | solution.py:219
  455.2 10.2 %collective-permute-done.43.refs_6_ = bf16[512,1024]{1,0:T(8,128)(2,1)} collective-permute-done((bf16[512,1024]{1,0:T(8,128)(2,1)}, bf16[512,1024]{1,0:T(8,128)(2,1)}, u32[]{:S(2)}, u32[]{:S(2)}) %collective-permute-start.43) | collective-permute-done | bytes 1048608 | tf_op jit(solution)/shard_map/ppermute | solution.py:37
  470.4 2.2 collective-permute-done.45.refs_7_
  472.6 6.9 %place.7.left = bf16[2048,2048]{1,0:T(8,128)(2,1)} custom-call(bf16[256,2048]{1,0:T(8,128)(2,1)} %copy-done.3, bf16[256,2048]{1,0:T(8,128)(2,1)} %collective-permute-done.38.refs_1_, bf16[256,1024]{1,0:T(8,128)(2,1)} %copy-done.34, bf16[256,1024]{1,0:T(8,128)(2,1)} %copy-done.35, bf16[512,1024]{1,0:T(8,128)(2,1)} %collective-permute-done.41.refs_4_, ...), custom_call_target="tpu_custom_call" | custom-call | tf_op jit(solution)/shard_map/place/pallas_call | solution.py:130
  480.9 2.3 constant_dynamic-slice_fusion.11
  486.3 7.6 %convolution_convert_fusion.upstream = bf16[256,2048]{1,0:T(8,128)(2,1)} fusion(bf16[2048,2048]{1,0:T(8,128)(2,1)} %place.7.left, bf16[2048,640]{1,0:T(8,128)(2,1)} %all-gather.4.cloned.1.call-done.refs_1_.weights), kind=kOutput, calls=%fused_computation.3 | convolution fusion | flops 2148007936 | bytes 10485760 | tf_op jit(solution)/shard_map/dot_general | solution.py:46
  493.9 35.8 %attend_back.1 = (bf16[256,2048]{1,0:T(8,128)(2,1)}, f32[128,2048]{1,0:T(8,128)}, bf16[128,512]{1,0:T(8,128)(2,1)}) custom-call(s32[3]{0:T(128)} %copy-done.19, bf16[384,2048]{1,0:T(8,128)(2,1)} %copy-done.1, bf16[128,512]{1,0:T(8,128)(2,1)} %copy-done.17, bf16[256,2048]{1,0:T(8,128)(2,1)} %convolution_convert_fusion.upstream, f32[8,2048]{1,0:T(8,128)} %copy-done.18, ...), custom_call_target="tpu_custom_call" | custom-call | tf_op jit(solution)/shard_map/attend_back/pallas_call | solution.py:643
  529.7 4.4 collective-permute-start.50
  534.2 6.8 %outer.4 = bf16[2048,256]{1,0:T(8,128)(2,1)} custom-call(bf16[2048,2048]{1,0:T(8,128)(2,1)} %place.7.left, bf16[256,2048]{1,0:T(8,128)(2,1)} %copy-done.2), custom_call_target="tpu_custom_call" | custom-call | tf_op jit(solution)/shard_map/outer/pallas_call | solution.py:743
  540.9 4.1 fold.6
  548.9 6.4 product.14
  556.5 9.3 %outer.5 = (bf16[2048,384]{1,0:T(8,128)(2,1)}, f32[2048,128]{1,0:T(8,128)}) custom-call(bf16[2048,2048]{1,0:T(8,128)(2,1)} %place.4.left, bf16[384,2048]{1,0:T(8,128)(2,1)} %pad_maximum_fusion.5.refs_0_.right, bf16[2048,640]{1,0:T(8,128)(2,1)} %all-gather.4.cloned.1.call-done.refs_1_.weights), custom_call_target="tpu_custom_call" | custom-call | tf_op jit(solution)/shard_map/outer/pallas_call | solution.py:743
  565.8 4.2 collective-permute-done.52
  570.1 3.1 pad_maximum_fusion
  573.2 2.1 constant_dynamic-slice_fusion.1
  578.4 8.4 %product.15 = (f32[2,256,1024]{2,1,0:T(8,128)}, f32[2,256,1024]{2,1,0:T(8,128)}, bf16[2,256,1024]{2,1,0:T(8,128)(2,1)}, bf16[2,256,1024]{2,1,0:T(8,128)(2,1)}) custom-call(bf16[384,2048]{1,0:T(8,128)(2,1)} %pad_maximum_fusion.5.refs_0_.right, bf16[2048,640]{1,0:T(8,128)(2,1)} %all-gather.4.cloned.1.call-done.refs_1_.weights, ...), custom_call_target="tpu_custom_call" | custom-call | tf_op jit(solution)/shard_map/product/pallas_call | solution.py:219
  586.8 2.1 collective-permute-done.54
  592.5 3.6 collective-permute-done.57
  596.3 2.9 fusion.10
  599.2 3.3 collective-permute-done.58
  603.0 2.8 fusion.8
  612.1 2.5 collective-permute-done.55.left_x
  615.4 4.1 fold.7
  625.4 5.6 collective-permute-done.59.refs_2_
  637.6 5.0 input_back.1
  (332 shorter events, 125.8 us)
Async XLA Ops:
  7.2 75.2 %all-gather.4.cloned.1.call-start = ((), (), s32[]{:S(2)}) async-start(), calls=%async_computation.4 | async-start | bytes 3276800 | tf_op jit(solution)/shard_map/all_gather | solution.py:791
  9.8 10.7 %collective-permute-start = (bf16[256,640]{1,0:T(8,128)(2,1)S(1)}, bf16[256,640]{1,0:T(8,128)(2,1)S(1)}, u32[]{:S(2)}, u32[]{:S(2)}) collective-permute-start(bf16[256,640]{1,0:T(8,128)(2,1)S(1)} %pad_maximum_fusion.20), channel_id=1, source_target_pairs={{0,4},{4,0},{1,5},{5,1},{2,6},{6,2},{3,7},{7,3},{8,12},{12,8},{9,1... | collective-permute-start | bytes 983048 | tf_op jit(solution)/shard_map/ppermute | solution.py:37
  21.7 214.8 %all-gather.6.cloned.1.call-start = ((), (), s32[]{:S(2)}) async-start(), calls=%async_computation.5 | async-start | bytes 10485760 | tf_op jit(solution)/shard_map/all_gather | solution.py:806
  24.1 14.9 %collective-permute-start.4 = (bf16[256,1024]{1,0:T(8,128)(2,1)S(1)}, bf16[256,1024]{1,0:T(8,128)(2,1)S(1)}, u32[]{:S(2)}, u32[]{:S(2)}) collective-permute-start(bf16[256,1024]{1,0:T(8,128)(2,1)S(1)} %get-tuple-element.485), channel_id=1, source_target_pairs={{0,4},{4,0},{1,5},{5,1},{2,6},{6,2},{3,7},{7,3},{8,12},{12,8},{9,1... | collective-permute-start | bytes 1572872 | tf_op jit(solution)/shard_map/ppermute | solution.py:37
  25.9 13.1 %collective-permute-start.3 = (bf16[256,1024]{1,0:T(8,128)(2,1)S(1)}, bf16[256,1024]{1,0:T(8,128)(2,1)S(1)}, u32[]{:S(2)}, u32[]{:S(2)}) collective-permute-start(bf16[256,1024]{1,0:T(8,128)(2,1)S(1)} %get-tuple-element.486), channel_id=1, source_target_pairs={{0,2},{2,0},{1,3},{3,1},{4,6},{6,4},{5,7},{7,5},{8,10},{10,8},{9,1... | collective-permute-start | bytes 1572872 | tf_op jit(solution)/shard_map/ppermute | solution.py:37
  27.6 33.9 %collective-permute-start.1 = (bf16[256,2048]{1,0:T(8,128)(2,1)S(1)}, bf16[256,2048]{1,0:T(8,128)(2,1)S(1)}, u32[]{:S(2)}, u32[]{:S(2)}) collective-permute-start(bf16[256,2048]{1,0:T(8,128)(2,1)S(1)} %pad_maximum_fusion.15), channel_id=1, source_target_pairs={{0,4},{4,0},{1,5},{5,1},{2,6},{6,2},{3,7},{7,3},{8,12},{12,8},{9,1... | collective-permute-start | bytes 3145736 | tf_op jit(solution)/shard_map/ppermute | solution.py:37
  28.1 35.7 %collective-permute-start.2 = (bf16[256,2048]{1,0:T(8,128)(2,1)S(1)}, bf16[256,2048]{1,0:T(8,128)(2,1)}, u32[]{:S(2)}, u32[]{:S(2)}) collective-permute-start(bf16[256,2048]{1,0:T(8,128)(2,1)S(1)} %fusion.3.refs_0_), channel_id=1, source_target_pairs={{0,1},{1,0},{2,3},{3,2},{4,5},{5,4},{6,7},{7,6},{8,9},{9,8},{10,11... | collective-permute-start | bytes 3145736 | tf_op jit(solution)/shard_map/ppermute | solution.py:37
  41.0 22.8 %collective-permute-start.7 = (bf16[512,1024]{1,0:T(8,128)(2,1)}, bf16[512,1024]{1,0:T(8,128)(2,1)}, u32[]{:S(2)}, u32[]{:S(2)}) collective-permute-start(bf16[512,1024]{1,0:T(8,128)(2,1)} %get-tuple-element.504), channel_id=1, source_target_pairs={{0,2},{2,0},{1,3},{3,1},{4,6},{6,4},{5,7},{7,5},{8,10},{10,8},{9,1... | collective-permute-start | bytes 3145736 | tf_op jit(solution)/shard_map/ppermute | solution.py:37
  42.8 21.1 %collective-permute-start.5 = (bf16[512,1024]{1,0:T(8,128)(2,1)}, bf16[512,1024]{1,0:T(8,128)(2,1)}, u32[]{:S(2)}, u32[]{:S(2)}) collective-permute-start(bf16[512,1024]{1,0:T(8,128)(2,1)} %get-tuple-element.505), channel_id=1, source_target_pairs={{0,1},{1,0},{2,3},{3,2},{4,5},{5,4},{6,7},{7,6},{8,9},{9,8},{10,11... | collective-permute-start | bytes 3145736 | tf_op jit(solution)/shard_map/ppermute | solution.py:37
  42.8 39.6 %collective-permute-start.6 = (bf16[512,1024]{1,0:T(8,128)(2,1)}, bf16[512,1024]{1,0:T(8,128)(2,1)}, u32[]{:S(2)}, u32[]{:S(2)}) collective-permute-start(bf16[512,1024]{1,0:T(8,128)(2,1)} %get-tuple-element.506), channel_id=1, source_target_pairs={{0,4},{4,0},{1,5},{5,1},{2,6},{6,2},{3,7},{7,3},{8,12},{12,8},{9,1... | collective-permute-start | bytes 3145736 | tf_op jit(solution)/shard_map/ppermute | solution.py:37
  82.4 234.5 %all-gather.8.cloned.1.call-start = ((), (), s32[]{:S(2)}) async-start(), calls=%async_computation.6 | async-start | bytes 5242880 | tf_op jit(solution)/shard_map/all_gather | solution.py:838
  85.5 9.1 %collective-permute-start.8 = (bf16[1024,1024]{1,0:T(8,128)(2,1)}, bf16[1024,1024]{1,0:T(8,128)(2,1)}, u32[]{:S(2)}, u32[]{:S(2)}) collective-permute-start(bf16[1024,1024]{1,0:T(8,128)(2,1)} %pad_maximum_fusion.1), channel_id=1, source_target_pairs={{0,1},{1,0},{2,3},{3,2},{4,5},{5,4},{6,7},{7,6},{8,9},{9,8},{10,11... | collective-permute-start | bytes 6291464 | tf_op jit(solution)/shard_map/ppermute | solution.py:37
  87.7 24.0 %collective-permute-start.10 = (bf16[256,2048]{1,0:T(8,128)(2,1)S(1)}, bf16[256,2048]{1,0:T(8,128)(2,1)}, u32[]{:S(2)}, u32[]{:S(2)}) collective-permute-start(bf16[256,2048]{1,0:T(8,128)(2,1)S(1)} %multiply_convert_fusion.refs_0_), channel_id=1, source_target_pairs={{0,1},{1,0},{2,3},{3,2},{4,5},{5,4},{6,7},{7,6},{8,9},{9,8},{10,11... | collective-permute-start | bytes 3145736 | tf_op jit(solution)/shard_map/ppermute | solution.py:37
  89.3 22.3 %collective-permute-start.12 = (bf16[256,1024]{1,0:T(8,128)(2,1)}, bf16[256,1024]{1,0:T(8,128)(2,1)S(1)}, u32[]{:S(2)}, u32[]{:S(2)}) collective-permute-start(bf16[256,1024]{1,0:T(8,128)(2,1)} %get-tuple-element.483), channel_id=1, source_target_pairs={{0,4},{4,0},{1,5},{5,1},{2,6},{6,2},{3,7},{7,3},{8,12},{12,8},{9,1... | collective-permute-start | bytes 1572872 | tf_op jit(solution)/shard_map/ppermute | solution.py:37
  90.7 20.9 %collective-permute-start.11 = (bf16[256,1024]{1,0:T(8,128)(2,1)}, bf16[256,1024]{1,0:T(8,128)(2,1)S(1)}, u32[]{:S(2)}, u32[]{:S(2)}) collective-permute-start(bf16[256,1024]{1,0:T(8,128)(2,1)} %get-tuple-element.484), channel_id=1, source_target_pairs={{0,2},{2,0},{1,3},{3,1},{4,6},{6,4},{5,7},{7,5},{8,10},{10,8},{9,1... | collective-permute-start | bytes 1572872 | tf_op jit(solution)/shard_map/ppermute | solution.py:37
  109.7 10.9 %collective-permute-start.9 = (bf16[128,512]{1,0:T(8,128)(2,1)S(1)}, bf16[128,512]{1,0:T(8,128)(2,1)S(1)}, u32[]{:S(2)}, u32[]{:S(2)}) collective-permute-start(bf16[128,512]{1,0:T(8,128)(2,1)S(1)} %slice.116), channel_id=1, source_target_pairs={{0,8},{8,16},{16,24},{24,0},{1,9},{9,17},{17,25},{25,1},{2,10},{10... | collective-permute-start | bytes 393224 | tf_op jit(solution)/shard_map/ppermute | solution.py:42
  121.2 24.0 %collective-permute-start.15 = (bf16[512,1024]{1,0:T(8,128)(2,1)S(1)}, bf16[512,1024]{1,0:T(8,128)(2,1)S(1)}, u32[]{:S(2)}, u32[]{:S(2)}) collective-permute-start(bf16[512,1024]{1,0:T(8,128)(2,1)S(1)} %get-tuple-element.501), channel_id=1, source_target_pairs={{0,2},{2,0},{1,3},{3,1},{4,6},{6,4},{5,7},{7,5},{8,10},{10,8},{9,1... | collective-permute-start | bytes 3145736 | tf_op jit(solution)/shard_map/ppermute | solution.py:37
  121.8 23.4 %collective-permute-start.13 = (bf16[512,1024]{1,0:T(8,128)(2,1)S(1)}, bf16[512,1024]{1,0:T(8,128)(2,1)S(1)}, u32[]{:S(2)}, u32[]{:S(2)}) collective-permute-start(bf16[512,1024]{1,0:T(8,128)(2,1)S(1)} %get-tuple-element.502), channel_id=1, source_target_pairs={{0,1},{1,0},{2,3},{3,2},{4,5},{5,4},{6,7},{7,6},{8,9},{9,8},{10,11... | collective-permute-start | bytes 3145736 | tf_op jit(solution)/shard_map/ppermute | solution.py:37
  121.8 26.0 %collective-permute-start.14 = (bf16[512,1024]{1,0:T(8,128)(2,1)S(1)}, bf16[512,1024]{1,0:T(8,128)(2,1)S(1)}, u32[]{:S(2)}, u32[]{:S(2)}) collective-permute-start(bf16[512,1024]{1,0:T(8,128)(2,1)S(1)} %get-tuple-element.503), channel_id=1, source_target_pairs={{0,4},{4,0},{1,5},{5,1},{2,6},{6,2},{3,7},{7,3},{8,12},{12,8},{9,1... | collective-permute-start | bytes 3145736 | tf_op jit(solution)/shard_map/ppermute | solution.py:37
  122.7 36.0 %collective-permute-start.16 = (bf16[1024,256]{1,0:T(8,128)(2,1)S(1)}, bf16[1024,256]{1,0:T(8,128)(2,1)}, u32[]{:S(2)}, u32[]{:S(2)}) collective-permute-start(bf16[1024,256]{1,0:T(8,128)(2,1)S(1)} %get-tuple-element.240), channel_id=1, source_target_pairs={{0,4},{4,0},{1,5},{5,1},{2,6},{6,2},{3,7},{7,3},{8,12},{12,8},{9,1... | collective-permute-start | bytes 1572872 | tf_op jit(solution)/shard_map/ppermute | solution.py:37
  158.7 7.4 %collective-permute-start.17 = (bf16[1024,2048]{1,0:T(8,128)(2,1)}, bf16[1024,2048]{1,0:T(8,128)(2,1)S(1)}, u32[]{:S(2)}, u32[]{:S(2)}) collective-permute-start(bf16[1024,2048]{1,0:T(8,128)(2,1)} %product.8), channel_id=1, source_target_pairs={{0,1},{1,0},{2,3},{3,2},{4,5},{5,4},{6,7},{7,6},{8,9},{9,8},{10,11... | collective-permute-start | bytes 12582920 | tf_op jit(solution)/shard_map/ppermute | solution.py:37
  160.3 28.4 %collective-permute-start.21 = (bf16[1024,1024]{1,0:T(8,128)(2,1)}, bf16[1024,1024]{1,0:T(8,128)(2,1)}, u32[]{:S(2)}, u32[]{:S(2)}) collective-permute-start(bf16[1024,1024]{1,0:T(8,128)(2,1)} %pad_maximum_fusion.2), channel_id=1, source_target_pairs={{0,1},{1,0},{2,3},{3,2},{4,5},{5,4},{6,7},{7,6},{8,9},{9,8},{10,11... | collective-permute-start | bytes 6291464 | tf_op jit(solution)/shard_map/ppermute | solution.py:37
  175.5 25.5 %collective-permute-start.19 = (bf16[2,256,1024]{2,1,0:T(8,128)(2,1)}, bf16[2,256,1024]{2,1,0:T(8,128)(2,1)}, u32[]{:S(2)}, u32[]{:S(2)}) collective-permute-start(bf16[2,256,1024]{2,1,0:T(8,128)(2,1)} %get-tuple-element.244), channel_id=1, source_target_pairs={{0,2},{2,0},{1,3},{3,1},{4,6},{6,4},{5,7},{7,5},{8,10},{10,8},{9,1... | collective-permute-start | bytes 3145736 | tf_op jit(solution)/shard_map/ppermute | solution.py:37
  176.9 25.2 %collective-permute-start.20 = (bf16[2,256,1024]{2,1,0:T(8,128)(2,1)}, bf16[2,256,1024]{2,1,0:T(8,128)(2,1)}, u32[]{:S(2)}, u32[]{:S(2)}) collective-permute-start(bf16[2,256,1024]{2,1,0:T(8,128)(2,1)} %get-tuple-element.245), channel_id=1, source_target_pairs={{0,4},{4,0},{1,5},{5,1},{2,6},{6,2},{3,7},{7,3},{8,12},{12,8},{9,1... | collective-permute-start | bytes 3145736 | tf_op jit(solution)/shard_map/ppermute | solution.py:37
  177.5 8.6 %collective-permute-start.22 = (f32[8,128]{1,0:T(8,128)S(1)}, f32[8,128]{1,0:T(8,128)S(1)}, u32[]{:S(2)}, u32[]{:S(2)}) collective-permute-start(f32[8,128]{1,0:T(8,128)S(1)} %maximum_select_fusion.10), channel_id=1, source_target_pairs={{0,8},{8,16},{16,24},{24,0},{1,9},{9,17},{17,25},{25,1},{2,10},{10... | collective-permute-start | bytes 12296 | tf_op jit(solution)/shard_map/ppermute | solution.py:42
  186.1 9.7 %collective-permute-start.23 = (f32[8,128]{1,0:T(8,128)S(1)}, f32[8,128]{1,0:T(8,128)S(1)}, u32[]{:S(2)}, u32[]{:S(2)}) collective-permute-start(f32[8,128]{1,0:T(8,128)S(1)} %max.10), channel_id=1, source_target_pairs={{0,16},{8,24},{16,0},{24,8},{1,17},{9,25},{17,1},{25,9},{2,18},{10... | collective-permute-start | bytes 12296 | tf_op jit(solution)/shard_map/ppermute | solution.py:42
  202.2 277.3 %reduce-scatter.5.cloned.1.call-start = ((), (), s32[]{:S(2)}) async-start(), calls=%async_computation.7 | async-start | bytes 5242880 | tf_op jit(solution)/shard_map/reduce_scatter | solution.py:857
  206.3 12.9 %collective-permute-start.24 = (bf16[256,1024]{1,0:T(8,128)(2,1)S(1)}, bf16[256,1024]{1,0:T(8,128)(2,1)S(1)}, u32[]{:S(2)}, u32[]{:S(2)}) collective-permute-start(bf16[256,1024]{1,0:T(8,128)(2,1)S(1)} %get-tuple-element.269), channel_id=1, source_target_pairs={{0,4},{4,0},{1,5},{5,1},{2,6},{6,2},{3,7},{7,3},{8,12},{12,8},{9,1... | collective-permute-start | bytes 1572872 | tf_op jit(solution)/shard_map/ppermute | solution.py:37
  206.9 12.5 %collective-permute-start.25 = (bf16[256,1024]{1,0:T(8,128)(2,1)S(1)}, bf16[256,1024]{1,0:T(8,128)(2,1)S(1)}, u32[]{:S(2)}, u32[]{:S(2)}) collective-permute-start(bf16[256,1024]{1,0:T(8,128)(2,1)S(1)} %get-tuple-element.270), channel_id=1, source_target_pairs={{0,2},{2,0},{1,3},{3,1},{4,6},{6,4},{5,7},{7,5},{8,10},{10,8},{9,1... | collective-permute-start | bytes 1572872 | tf_op jit(solution)/shard_map/ppermute | solution.py:37
  221.6 14.9 %collective-permute-start.26 = (bf16[256,2048]{1,0:T(8,128)(2,1)S(1)}, bf16[256,2048]{1,0:T(8,128)(2,1)}, u32[]{:S(2)}, u32[]{:S(2)}) collective-permute-start(bf16[256,2048]{1,0:T(8,128)(2,1)S(1)} %get-tuple-element.274.refs_0_), channel_id=1, source_target_pairs={{0,1},{1,0},{2,3},{3,2},{4,5},{5,4},{6,7},{7,6},{8,9},{9,8},{10,11... | collective-permute-start | bytes 3145736 | tf_op jit(solution)/shard_map/ppermute | solution.py:37
  221.6 14.3 %collective-permute-start.27 = (bf16[256,1024]{1,0:T(8,128)(2,1)S(1)}, bf16[256,1024]{1,0:T(8,128)(2,1)S(1)}, u32[]{:S(2)}, u32[]{:S(2)}) collective-permute-start(bf16[256,1024]{1,0:T(8,128)(2,1)S(1)} %get-tuple-element.272), channel_id=1, source_target_pairs={{0,2},{2,0},{1,3},{3,1},{4,6},{6,4},{5,7},{7,5},{8,10},{10,8},{9,1... | collective-permute-start | bytes 1572872 | tf_op jit(solution)/shard_map/ppermute | solution.py:37
  222.4 14.1 %collective-permute-start.28 = (bf16[256,1024]{1,0:T(8,128)(2,1)S(1)}, bf16[256,1024]{1,0:T(8,128)(2,1)S(1)}, u32[]{:S(2)}, u32[]{:S(2)}) collective-permute-start(bf16[256,1024]{1,0:T(8,128)(2,1)S(1)} %get-tuple-element.273), channel_id=1, source_target_pairs={{0,4},{4,0},{1,5},{5,1},{2,6},{6,2},{3,7},{7,3},{8,12},{12,8},{9,1... | collective-permute-start | bytes 1572872 | tf_op jit(solution)/shard_map/ppermute | solution.py:37
  238.4 24.8 %collective-permute-start.31 = (bf16[512,1024]{1,0:T(8,128)(2,1)S(1)}, bf16[512,1024]{1,0:T(8,128)(2,1)S(1)}, u32[]{:S(2)}, u32[]{:S(2)}) collective-permute-start(bf16[512,1024]{1,0:T(8,128)(2,1)S(1)} %get-tuple-element.498), channel_id=1, source_target_pairs={{0,2},{2,0},{1,3},{3,1},{4,6},{6,4},{5,7},{7,5},{8,10},{10,8},{9,1... | collective-permute-start | bytes 3145736 | tf_op jit(solution)/shard_map/ppermute | solution.py:37
  239.7 23.6 %collective-permute-start.29 = (bf16[512,1024]{1,0:T(8,128)(2,1)S(1)}, bf16[512,1024]{1,0:T(8,128)(2,1)S(1)}, u32[]{:S(2)}, u32[]{:S(2)}) collective-permute-start(bf16[512,1024]{1,0:T(8,128)(2,1)S(1)} %get-tuple-element.499), channel_id=1, source_target_pairs={{0,1},{1,0},{2,3},{3,2},{4,5},{5,4},{6,7},{7,6},{8,9},{9,8},{10,11... | collective-permute-start | bytes 3145736 | tf_op jit(solution)/shard_map/ppermute | solution.py:37
  239.7 25.6 %collective-permute-start.30 = (bf16[512,1024]{1,0:T(8,128)(2,1)S(1)}, bf16[512,1024]{1,0:T(8,128)(2,1)S(1)}, u32[]{:S(2)}, u32[]{:S(2)}) collective-permute-start(bf16[512,1024]{1,0:T(8,128)(2,1)S(1)} %get-tuple-element.500), channel_id=1, source_target_pairs={{0,4},{4,0},{1,5},{5,1},{2,6},{6,2},{3,7},{7,3},{8,12},{12,8},{9,1... | collective-permute-start | bytes 3145736 | tf_op jit(solution)/shard_map/ppermute | solution.py:37
  315.5 165.4 %reduce-scatter.7.cloned.1.call-start = ((), (), s32[]{:S(2)}) async-start(), calls=%async_computation.8 | async-start | bytes 5242880 | tf_op jit(solution)/shard_map/reduce_scatter | solution.py:857
  342.9 11.9 %collective-permute-start.33 = (bf16[1024,2048]{1,0:T(8,128)(2,1)}, bf16[1024,2048]{1,0:T(8,128)(2,1)S(1)}, u32[]{:S(2)}, u32[]{:S(2)}) collective-permute-start(bf16[1024,2048]{1,0:T(8,128)(2,1)} %product.10), channel_id=1, source_target_pairs={{0,1},{1,0},{2,3},{3,2},{4,5},{5,4},{6,7},{7,6},{8,9},{9,8},{10,11... | collective-permute-start | bytes 12582920 | tf_op jit(solution)/shard_map/ppermute | solution.py:37
  372.6 29.5 %collective-permute-start.34 = (bf16[2,256,1024]{2,1,0:T(8,128)(2,1)}, bf16[2,256,1024]{2,1,0:T(8,128)(2,1)S(1)}, u32[]{:S(2)}, u32[]{:S(2)}) collective-permute-start(bf16[2,256,1024]{2,1,0:T(8,128)(2,1)} %get-tuple-element.303), channel_id=1, source_target_pairs={{0,2},{2,0},{1,3},{3,1},{4,6},{6,4},{5,7},{7,5},{8,10},{10,8},{9,1... | collective-permute-start | bytes 3145736 | tf_op jit(solution)/shard_map/ppermute | solution.py:37
  373.8 28.2 %collective-permute-start.35 = (bf16[2,256,1024]{2,1,0:T(8,128)(2,1)}, bf16[2,256,1024]{2,1,0:T(8,128)(2,1)}, u32[]{:S(2)}, u32[]{:S(2)}) collective-permute-start(bf16[2,256,1024]{2,1,0:T(8,128)(2,1)} %get-tuple-element.304), channel_id=1, source_target_pairs={{0,4},{4,0},{1,5},{5,1},{2,6},{6,2},{3,7},{7,3},{8,12},{12,8},{9,1... | collective-permute-start | bytes 3145736 | tf_op jit(solution)/shard_map/ppermute | solution.py:37
  402.1 163.7 %reduce-scatter.9.cloned.1.call-start = ((), (), s32[]{:S(2)}) async-start(), calls=%async_computation.9 | async-start | bytes 5242880 | tf_op jit(solution)/shard_map/reduce_scatter | solution.py:857
  407.2 13.9 %collective-permute-start.36 = (bf16[256,1024]{1,0:T(8,128)(2,1)S(1)}, bf16[256,1024]{1,0:T(8,128)(2,1)S(1)}, u32[]{:S(2)}, u32[]{:S(2)}) collective-permute-start(bf16[256,1024]{1,0:T(8,128)(2,1)S(1)} %get-tuple-element.310), channel_id=1, source_target_pairs={{0,4},{4,0},{1,5},{5,1},{2,6},{6,2},{3,7},{7,3},{8,12},{12,8},{9,1... | collective-permute-start | bytes 1572872 | tf_op jit(solution)/shard_map/ppermute | solution.py:37
  407.7 13.6 %collective-permute-start.37 = (bf16[256,1024]{1,0:T(8,128)(2,1)S(1)}, bf16[256,1024]{1,0:T(8,128)(2,1)S(1)}, u32[]{:S(2)}, u32[]{:S(2)}) collective-permute-start(bf16[256,1024]{1,0:T(8,128)(2,1)S(1)} %get-tuple-element.311), channel_id=1, source_target_pairs={{0,2},{2,0},{1,3},{3,1},{4,6},{6,4},{5,7},{7,5},{8,10},{10,8},{9,1... | collective-permute-start | bytes 1572872 | tf_op jit(solution)/shard_map/ppermute | solution.py:37
  424.3 12.9 %collective-permute-start.39 = (bf16[256,1024]{1,0:T(8,128)(2,1)S(1)}, bf16[256,1024]{1,0:T(8,128)(2,1)S(1)}, u32[]{:S(2)}, u32[]{:S(2)}) collective-permute-start(bf16[256,1024]{1,0:T(8,128)(2,1)S(1)} %get-tuple-element.316), channel_id=1, source_target_pairs={{0,2},{2,0},{1,3},{3,1},{4,6},{6,4},{5,7},{7,5},{8,10},{10,8},{9,1... | collective-permute-start | bytes 1572872 | tf_op jit(solution)/shard_map/ppermute | solution.py:37
  425.0 12.5 %collective-permute-start.40 = (bf16[256,1024]{1,0:T(8,128)(2,1)S(1)}, bf16[256,1024]{1,0:T(8,128)(2,1)S(1)}, u32[]{:S(2)}, u32[]{:S(2)}) collective-permute-start(bf16[256,1024]{1,0:T(8,128)(2,1)S(1)} %get-tuple-element.317), channel_id=1, source_target_pairs={{0,4},{4,0},{1,5},{5,1},{2,6},{6,2},{3,7},{7,3},{8,12},{12,8},{9,1... | collective-permute-start | bytes 1572872 | tf_op jit(solution)/shard_map/ppermute | solution.py:37
  437.5 7.5 %collective-permute-start.44 = (bf16[1024,2048]{1,0:T(8,128)(2,1)}, bf16[1024,2048]{1,0:T(8,128)(2,1)}, u32[]{:S(2)}, u32[]{:S(2)}) collective-permute-start(bf16[1024,2048]{1,0:T(8,128)(2,1)} %product.12), channel_id=1, source_target_pairs={{0,1},{1,0},{2,3},{3,2},{4,5},{5,4},{6,7},{7,6},{8,9},{9,8},{10,11... | collective-permute-start | bytes 12582920 | tf_op jit(solution)/shard_map/ppermute | solution.py:37
  439.5 25.9 %collective-permute-start.43 = (bf16[512,1024]{1,0:T(8,128)(2,1)}, bf16[512,1024]{1,0:T(8,128)(2,1)}, u32[]{:S(2)}, u32[]{:S(2)}) collective-permute-start(bf16[512,1024]{1,0:T(8,128)(2,1)} %get-tuple-element.495), channel_id=1, source_target_pairs={{0,2},{2,0},{1,3},{3,1},{4,6},{6,4},{5,7},{7,5},{8,10},{10,8},{9,1... | collective-permute-start | bytes 3145736 | tf_op jit(solution)/shard_map/ppermute | solution.py:37
  440.9 25.6 %collective-permute-start.42 = (bf16[512,1024]{1,0:T(8,128)(2,1)}, bf16[512,1024]{1,0:T(8,128)(2,1)}, u32[]{:S(2)}, u32[]{:S(2)}) collective-permute-start(bf16[512,1024]{1,0:T(8,128)(2,1)} %get-tuple-element.497), channel_id=1, source_target_pairs={{0,4},{4,0},{1,5},{5,1},{2,6},{6,2},{3,7},{7,3},{8,12},{12,8},{9,1... | collective-permute-start | bytes 3145736 | tf_op jit(solution)/shard_map/ppermute | solution.py:37
  442.3 24.2 %collective-permute-start.38 = (bf16[256,2048]{1,0:T(8,128)(2,1)S(1)}, bf16[256,2048]{1,0:T(8,128)(2,1)}, u32[]{:S(2)}, u32[]{:S(2)}) collective-permute-start(bf16[256,2048]{1,0:T(8,128)(2,1)S(1)} %get-tuple-element.315.refs_0_), channel_id=1, source_target_pairs={{0,1},{1,0},{2,3},{3,2},{4,5},{5,4},{6,7},{7,6},{8,9},{9,8},{10,11... | collective-permute-start | bytes 3145736 | tf_op jit(solution)/shard_map/ppermute | solution.py:37
  442.3 24.2 %collective-permute-start.41 = (bf16[512,1024]{1,0:T(8,128)(2,1)}, bf16[512,1024]{1,0:T(8,128)(2,1)}, u32[]{:S(2)}, u32[]{:S(2)}) collective-permute-start(bf16[512,1024]{1,0:T(8,128)(2,1)} %get-tuple-element.496), channel_id=1, source_target_pairs={{0,1},{1,0},{2,3},{3,2},{4,5},{5,4},{6,7},{7,6},{8,9},{9,8},{10,11... | collective-permute-start | bytes 3145736 | tf_op jit(solution)/shard_map/ppermute | solution.py:37
  442.9 181.5 %reduce-scatter.11.cloned.1.call-start = ((), (), s32[]{:S(2)}) async-start(), calls=%async_computation.10 | async-start | bytes 3276800 | tf_op jit(solution)/shard_map/reduce_scatter | solution.py:857
  468.3 61.3 %collective-permute-start.48 = (bf16[2,256,1024]{2,1,0:T(8,128)(2,1)}, bf16[2,256,1024]{2,1,0:T(8,128)(2,1)}, u32[]{:S(2)}, u32[]{:S(2)}) collective-permute-start(bf16[2,256,1024]{2,1,0:T(8,128)(2,1)} %get-tuple-element.342), channel_id=1, source_target_pairs={{0,2},{2,0},{1,3},{3,1},{4,6},{6,4},{5,7},{7,5},{8,10},{10,8},{9,1... | collective-permute-start | bytes 3145736 | tf_op jit(solution)/shard_map/ppermute | solution.py:37
  469.0 60.7 %collective-permute-start.49 = (bf16[2,256,1024]{2,1,0:T(8,128)(2,1)}, bf16[2,256,1024]{2,1,0:T(8,128)(2,1)}, u32[]{:S(2)}, u32[]{:S(2)}) collective-permute-start(bf16[2,256,1024]{2,1,0:T(8,128)(2,1)} %get-tuple-element.343), channel_id=1, source_target_pairs={{0,4},{4,0},{1,5},{5,1},{2,6},{6,2},{3,7},{7,3},{8,12},{12,8},{9,1... | collective-permute-start | bytes 3145736 | tf_op jit(solution)/shard_map/ppermute | solution.py:37
  483.2 46.4 %collective-permute-start.46 = (bf16[1024,256]{1,0:T(8,128)(2,1)}, bf16[1024,256]{1,0:T(8,128)(2,1)S(1)}, u32[]{:S(2)}, u32[]{:S(2)}) collective-permute-start(bf16[1024,256]{1,0:T(8,128)(2,1)} %get-tuple-element.474), channel_id=1, source_target_pairs={{0,4},{4,0},{1,5},{5,1},{2,6},{6,2},{3,7},{7,3},{8,12},{12,8},{9,1... | collective-permute-start | bytes 1572872 | tf_op jit(solution)/shard_map/ppermute | solution.py:37
  485.8 43.9 %collective-permute-start.47 = (bf16[256,1024]{1,0:T(8,128)(2,1)}, bf16[256,1024]{1,0:T(8,128)(2,1)S(1)}, u32[]{:S(2)}, u32[]{:S(2)}) collective-permute-start(bf16[256,1024]{1,0:T(8,128)(2,1)} %get-tuple-element.472), channel_id=1, source_target_pairs={{0,4},{4,0},{1,5},{5,1},{2,6},{6,2},{3,7},{7,3},{8,12},{12,8},{9,1... | collective-permute-start | bytes 1572872 | tf_op jit(solution)/shard_map/ppermute | solution.py:37
  529.7 15.3 %collective-permute-start.50 = (bf16[128,512]{1,0:T(8,128)(2,1)}, bf16[128,512]{1,0:T(8,128)(2,1)S(1)}, u32[]{:S(2)}, u32[]{:S(2)}) collective-permute-start(bf16[128,512]{1,0:T(8,128)(2,1)} %get-tuple-element.344), channel_id=1, source_target_pairs={{0,24},{8,0},{16,8},{24,16},{1,25},{9,1},{17,9},{25,17},{2,26},{10... | collective-permute-start | bytes 393224 | tf_op jit(solution)/shard_map/ppermute | solution.py:42
  555.3 14.8 %collective-permute-start.51 = (bf16[1024,2048]{1,0:T(8,128)(2,1)}, bf16[1024,2048]{1,0:T(8,128)(2,1)}, u32[]{:S(2)}, u32[]{:S(2)}) collective-permute-start(bf16[1024,2048]{1,0:T(8,128)(2,1)} %product.14), channel_id=1, source_target_pairs={{0,1},{1,0},{2,3},{3,2},{4,5},{5,4},{6,7},{7,6},{8,9},{9,8},{10,11... | collective-permute-start | bytes 12582920 | tf_op jit(solution)/shard_map/ppermute | solution.py:37
  555.3 14.7 %collective-permute-start.52 = (bf16[256,1024]{1,0:T(8,128)(2,1)}, bf16[256,1024]{1,0:T(8,128)(2,1)}, u32[]{:S(2)}, u32[]{:S(2)}) collective-permute-start(bf16[256,1024]{1,0:T(8,128)(2,1)} %get-tuple-element.358), channel_id=1, source_target_pairs={{0,4},{4,0},{1,5},{5,1},{2,6},{6,2},{3,7},{7,3},{8,12},{12,8},{9,1... | collective-permute-start | bytes 1572872 | tf_op jit(solution)/shard_map/ppermute | solution.py:37
  555.7 14.4 %collective-permute-start.53 = (bf16[256,1024]{1,0:T(8,128)(2,1)}, bf16[256,1024]{1,0:T(8,128)(2,1)}, u32[]{:S(2)}, u32[]{:S(2)}) collective-permute-start(bf16[256,1024]{1,0:T(8,128)(2,1)} %get-tuple-element.359), channel_id=1, source_target_pairs={{0,2},{2,0},{1,3},{3,1},{4,6},{6,4},{5,7},{7,5},{8,10},{10,8},{9,1... | collective-permute-start | bytes 1572872 | tf_op jit(solution)/shard_map/ppermute | solution.py:37
  575.3 13.6 %collective-permute-start.54 = (bf16[256,1024]{1,0:T(8,128)(2,1)}, bf16[256,1024]{1,0:T(8,128)(2,1)S(1)}, u32[]{:S(2)}, u32[]{:S(2)}) collective-permute-start(bf16[256,1024]{1,0:T(8,128)(2,1)} %get-tuple-element.366), channel_id=1, source_target_pairs={{0,4},{4,0},{1,5},{5,1},{2,6},{6,2},{3,7},{7,3},{8,12},{12,8},{9,1... | collective-permute-start | bytes 1572872 | tf_op jit(solution)/shard_map/ppermute | solution.py:37
  590.9 23.7 %collective-permute-start.55 = (bf16[2,256,1024]{2,1,0:T(8,128)(2,1)}, bf16[2,256,1024]{2,1,0:T(8,128)(2,1)}, u32[]{:S(2)}, u32[]{:S(2)}) collective-permute-start(bf16[2,256,1024]{2,1,0:T(8,128)(2,1)} %get-tuple-element.367), channel_id=1, source_target_pairs={{0,2},{2,0},{1,3},{3,1},{4,6},{6,4},{5,7},{7,5},{8,10},{10,8},{9,1... | collective-permute-start | bytes 3145736 | tf_op jit(solution)/shard_map/ppermute | solution.py:37
  591.5 23.8 %collective-permute-start.56 = (bf16[2,256,1024]{2,1,0:T(8,128)(2,1)}, bf16[2,256,1024]{2,1,0:T(8,128)(2,1)}, u32[]{:S(2)}, u32[]{:S(2)}) collective-permute-start(bf16[2,256,1024]{2,1,0:T(8,128)(2,1)} %get-tuple-element.368), channel_id=1, source_target_pairs={{0,4},{4,0},{1,5},{5,1},{2,6},{6,2},{3,7},{7,3},{8,12},{12,8},{9,1... | collective-permute-start | bytes 3145736 | tf_op jit(solution)/shard_map/ppermute | solution.py:37
  619.5 11.5 %collective-permute-start.59 = (bf16[256,1024]{1,0:T(8,128)(2,1)}, bf16[256,1024]{1,0:T(8,128)(2,1)S(1)}, u32[]{:S(2)}, u32[]{:S(2)}) collective-permute-start(bf16[256,1024]{1,0:T(8,128)(2,1)} %get-tuple-element.398), channel_id=1, source_target_pairs={{0,4},{4,0},{1,5},{5,1},{2,6},{6,2},{3,7},{7,3},{8,12},{12,8},{9,1... | collective-permute-start | bytes 1572872 | tf_op jit(solution)/shard_map/ppermute | solution.py:37
  620.5 11.3 %collective-permute-start.60 = (bf16[256,1024]{1,0:T(8,128)(2,1)}, bf16[256,1024]{1,0:T(8,128)(2,1)S(1)}, u32[]{:S(2)}, u32[]{:S(2)}) collective-permute-start(bf16[256,1024]{1,0:T(8,128)(2,1)} %get-tuple-element.399), channel_id=1, source_target_pairs={{0,2},{2,0},{1,3},{3,1},{4,6},{6,4},{5,7},{7,5},{8,10},{10,8},{9,1... | collective-permute-start | bytes 1572872 | tf_op jit(solution)/shard_map/ppermute | solution.py:37
  633.0 10.2 %collective-permute-start.64 = (bf16[256,640]{1,0:T(8,128)(2,1)S(1)}, bf16[256,640]{1,0:T(8,128)(2,1)S(1)}, u32[]{:S(2)}, u32[]{:S(2)}) collective-permute-start(bf16[256,640]{1,0:T(8,128)(2,1)S(1)} %constant_dynamic-slice_fusion.9), channel_id=1, source_target_pairs={{0,4},{4,0},{1,5},{5,1},{2,6},{6,2},{3,7},{7,3},{8,12},{12,8},{9,1... | collective-permute-start | bytes 983048 | tf_op jit(solution)/shard_map/ppermute | solution.py:37
  (69 other events, 432.9 us)
Sparse Core Ops, SparseCore 0:
  21.8 56.2 all-gather.3
  82.5 153.7 all-gather.5
  237.9 78.9 all-gather.7
  319.0 76.8 reduce-scatter.4
  402.2 78.6 reduce-scatter.6
  483.1 80.0 reduce-scatter.8
  573.4 50.9 reduce-scatter.10
